TPU v7x, 32 devices: a whole 2x2x4 slice. The times are simulated.
32 devices in a mesh: col: 16 (over z, y, x), row: 2 (over core).
Axes of the slice: x: 2, y: 2, z: 4, core: 2. Of those that a mesh axis runs over, the one named last changes fastest.
Arguments:
- rhs: bfloat16 [4, 16, 256, 512], P(None, 'col', 'row'), may hold values from -4 to 4
- leaf_rhs: bfloat16 [128, 256, 512], P(('col', 'row')), may hold values from -6 to 6
- leaf_inverse: bfloat16 [128, 256, 256], P(('col', 'row')), may hold values from -1 to 1.5
- leaf_lower: bfloat16 [4, 128, 256, 256], P(None, ('col', 'row')), may hold values from -0.0625 to 0.0625
- inverse_0: bfloat16 [4096, 256], P('col'), may hold values from -1 to 1.5
- inverse_1: bfloat16 [2048, 256], P('col'), may hold values from -1 to 1.5
- inverse_2: bfloat16 [1024, 256], P('col'), may hold values from -1 to 1.5
- inverse_3: bfloat16 [512, 256], P('col'), may hold values from -1 to 1.5
- lower_0: bfloat16 [3, 256, 4096], P(None, 'row', 'col'), may hold values from -0.1875 to 0.1875
- lower_1: bfloat16 [2, 256, 2048], P(None, 'row', 'col'), may hold values from -0.1875 to 0.1875
- lower_2: bfloat16 [1, 256, 1024], P(None, 'row', 'col'), may hold values from -0.1875 to 0.1875
- sparsity: int32 [6, 16, 8], P(None, 'col', 'row'), may hold values 0 or 1
Outputs:
- solution_0: bfloat16 [4096, 512], P('col')
- solution_1: bfloat16 [2048, 512], P('col')
- solution_2: bfloat16 [1024, 512], P('col')
- solution_3: bfloat16 [512, 512], P('col')
All inputs are finite; a program needn't handle non-finite values. No bound on the sum of `sparsity` on one device may be relied on, other than what follows from the above.
Results may differ from a plain program's by a relative error of at most 0.015.
Values may be sent and summed in bfloat16 or wider, within the bound.
No kernel may reach another device: no remote copies, remote signals or barrier semaphores. Data moves between devices by JAX's collectives and lax.ppermute only.
A program may use at most 64 MiB of HBM per device.

v0:
```python
import jax
import jax.numpy as jnp
from jax import lax
from jax.sharding import PartitionSpec as P


def from_partner(block, axis, stride):
    count = lax.axis_size(axis)
    route = []
    for low in range(count):
        high = low | 1 << stride
        if high != low and high < count:
            route += [(low, high), (high, low)]
    return lax.ppermute(block, axis, route)


def body(
    rhs,
    leaf_rhs,
    leaf_inverse,
    leaf_lower,
    inverse_0,
    inverse_1,
    inverse_2,
    inverse_3,
    lower_0,
    lower_1,
    lower_2,
    sparsity,
):
    inverses = [inverse_0, inverse_1, inverse_2, inverse_3]
    lowers = [lower_0, lower_1, lower_2]
    bases = [0, 3, 5]
    levels = rhs.shape[0]
    row_count = rhs.shape[2]
    width = rhs.shape[3]
    leaf_solution = jnp.einsum(
        "vrs,vsk->vrk", leaf_inverse, leaf_rhs, preferred_element_type=jnp.float32
    ).astype(jnp.bfloat16)
    pending = jnp.transpose(rhs[:, 0], (1, 0, 2)).astype(jnp.float32)
    terms = jnp.einsum(
        "mvrs,vsk->rmk", leaf_lower, leaf_solution, preferred_element_type=jnp.float32
    )
    scattered = lax.psum_scatter(
        terms.reshape(row_count * lax.axis_size("row"), (levels - 0) * width).astype(jnp.bfloat16),
        "row",
        scatter_dimension=0,
        tiled=True,
    ).astype(jnp.float32)
    pending = pending - scattered.reshape(row_count, levels, width)
    outputs = []
    for height in range(levels):
        inverse = inverses[height]
        residual = pending[:, height, :]
        for bit in range(height):
            residual = residual + from_partner(residual.astype(jnp.bfloat16), "col", bit).astype(
                residual.dtype
            )
        residual_half = residual.astype(jnp.bfloat16)

        def fold_rows(running, gathered, offset, inverse=inverse):
            return jnp.dot(inverse, gathered, preferred_element_type=jnp.float32)

        initial = jnp.zeros((inverse.shape[0], width), jnp.float32)
        solved = fold_rows(
            initial, lax.all_gather(residual_half, "row", axis=0, tiled=True), jnp.int32(0)
        ).astype(jnp.bfloat16)
        outputs.append(solved)
        if height + 1 < levels:
            lower_blocks = lowers[height]
            ancestors = levels - 1 - height
            pattern = sparsity[bases[height] : bases[height] + ancestors, 0, :].astype(jnp.float32)
            spread = row_count // pattern.shape[1]
            row_pattern = jnp.broadcast_to(
                pattern[:, :, None], (ancestors, pattern.shape[1], spread)
            ).reshape(ancestors, row_count)
            updates = jnp.einsum(
                "mrc,ck->rmk", lower_blocks, solved, preferred_element_type=jnp.float32
            )
            updates = updates * jnp.transpose(row_pattern)[:, :, None]
            pending = pending.at[:, height + 1 :, :].add(-updates)
    return (outputs[0], outputs[1], outputs[2], outputs[3])


def solution(mesh):
    return jax.shard_map(
        body,
        mesh=mesh,
        in_specs=(
            P(None, "col", "row", None),
            P(("col", "row"), None, None),
            P(("col", "row"), None, None),
            P(None, ("col", "row"), None, None),
            P("col", None),
            P("col", None),
            P("col", None),
            P("col", None),
            P(None, "row", "col"),
            P(None, "row", "col"),
            P(None, "row", "col"),
            P(None, "col", "row"),
        ),
        out_specs=(P("col", None), P("col", None), P("col", None), P("col", None)),
        check_vma=False,
    )
```

profile of v0, /device:TPU:0, one launch (start us, length us, event | category | flops | bytes accessed | tf_op | source)
XLA Modules:
  0.0 76.9 jit_solution(1997259431066418957)
XLA Ops:
  7.2 1.5 %copy-done = bf16[4,4,256,256]{3,2,1,0:T(8,128)(2,1)S(1)} copy-done((bf16[4,4,256,256]{3,2,1,0:T(8,128)(2,1)S(1)}, bf16[4,4,256,256]{3,2,1,0:T(8,128)(2,1)}, u32[]{:S(2)}) %copy-start) | copy-done | bytes 2097176
  8.8 3.0 %bitcast_convert_fusion = bf16[512,4,256]{2,0,1:T(8,128)(2,1)S(1)} fusion(bf16[4,4,256,256]{3,2,1,0:T(8,128)(2,1)S(1)} %copy-done, bf16[4,256,256]{2,1,0:T(8,128)(2,1)} %param.20, bf16[4,256,512]{2,1,0:T(8,128)(2,1)} %param.19), kind=kOutput, calls=%fused_computation | convolution fusion | flops 1343225856 | bytes 4718592 | tf_op jit(solution)/shard_map/mvrs,vsk->rmk/dot_general | solution.py:41
  11.7 1.4 %copy.27 = bf16[256,2048]{1,0:T(8,128)(2,1)} copy(bf16[256,2048]{0,1:T(8,128)(2,1)S(1)} %bitcast.111) | data formatting | bytes 2097152
  13.2 1.3 %copy.21 = bf16[4,1,128,512]{2,3,0,1:T(8,128)(2,1)S(1)} copy(bf16[4,1,128,512]{3,2,1,0:T(8,128)(2,1)} %param.18) | data formatting | bytes 1048576 | tf_op args[0]
  14.8 9.7 %reduce-scatter.4.cloned.1.call-done = bf16[128,2048]{1,0:T(8,128)(2,1)} async-done(((bf16[256,2048]{1,0:T(8,128)(2,1)}), bf16[128,2048]{1,0:T(8,128)(2,1)}) %reduce-scatter.4.cloned.1.call-update) | async-done | bytes 524304
  24.5 1.3 %copy.28 = bf16[128,2048]{0,1:T(8,128)(2,1)S(1)} copy(bf16[128,2048]{1,0:T(8,128)(2,1)} %reduce-scatter.4.cloned.1.call-done) | data formatting | bytes 1048576
  25.9 2.2 %all-gather = bf16[256,1,512]{0,2,1:T(8,128)(2,1)S(1)} all-gather(bf16[128,1,512]{0,2,1:T(8,128)(2,1)S(1)} %slice.132), channel_id=2, replica_groups=mesh['col'=16,'row'=2] {'row'}, dimensions={0}, use_global_device_ids=true | all-gather | bytes 393216 | tf_op jit(solution)/shard_map/all_gather | solution.py:66
  28.1 0.3 convolution_convert_fusion.1
  28.4 0.3 fusion.3
  28.7 1.9 %collective-permute-start = (bf16[128,512]{0,1:T(8,128)(2,1)S(1)}, bf16[128,512]{0,1:T(8,128)(2,1)S(1)}, u32[]{:S(2)}, u32[]{:S(2)}) collective-permute-start(bf16[128,512]{0,1:T(8,128)(2,1)S(1)} %fusion.15), channel_id=1, source_target_pairs={{0,2},{2,0},{4,6},{6,4},{8,10},{10,8},{12,14},{14,12},{16,18},{18,... | collective-permute-start | bytes 393224 | tf_op jit(solution)/shard_map/ppermute | solution.py:14
  30.9 3.6 %collective-permute-done = bf16[128,512]{0,1:T(8,128)(2,1)S(1)} collective-permute-done((bf16[128,512]{0,1:T(8,128)(2,1)S(1)}, bf16[128,512]{0,1:T(8,128)(2,1)S(1)}, u32[]{:S(2)}, u32[]{:S(2)}) %collective-permute-start) | collective-permute-done | bytes 131104 | tf_op jit(solution)/shard_map/ppermute | solution.py:14
  34.5 2.0 %all_gather.13 = bf16[256,512]{0,1:T(8,128)(2,1)S(1)} all-gather(bf16[128,512]{0,1:T(8,128)(2,1)S(1)} %add_convert_fusion.2), channel_id=1, replica_groups=mesh['col'=16,'row'=2] {'row'}, dimensions={0}, use_global_device_ids=true | all-gather | bytes 393216 | tf_op jit(solution)/shard_map/all_gather | solution.py:66
  36.6 0.2 convolution_convert_fusion.2
  36.8 1.3 %fusion.6 = f32[128,2,512]{0,2,1:T(8,128)S(1)} fusion(bf16[2,128,128]{2,1,0:T(8,128)(2,1)} %param.27, f32[128,3,512]{0,2,1:T(8,128)} %copy-done.1, f32[128,2]{0,1:T(2,128)S(1)} %bitcast.116, bf16[512,128]{1,0:T(8,128)(2,1)S(1)} %convolution_convert_fusion.2), kind=kOutput, calls=%fused_computation.10 | convolution fusion | flops 33947648 | bytes 1246208 | tf_op jit(solution)/shard_map/mrc,ck->rmk/dot_general | solution.py:77
  38.1 1.8 %collective-permute-start.1 = (bf16[128,512]{0,1:T(8,128)(2,1)S(1)}, bf16[128,512]{0,1:T(8,128)(2,1)S(1)}, u32[]{:S(2)}, u32[]{:S(2)}) collective-permute-start(bf16[128,512]{0,1:T(8,128)(2,1)S(1)} %fusion.16), channel_id=1, source_target_pairs={{0,2},{2,0},{4,6},{6,4},{8,10},{10,8},{12,14},{14,12},{16,18},{18,... | collective-permute-start | bytes 393224 | tf_op jit(solution)/shard_map/ppermute | solution.py:14
  39.9 3.8 %collective-permute-done.1 = bf16[128,512]{0,1:T(8,128)(2,1)S(1)} collective-permute-done((bf16[128,512]{0,1:T(8,128)(2,1)S(1)}, bf16[128,512]{0,1:T(8,128)(2,1)S(1)}, u32[]{:S(2)}, u32[]{:S(2)}) %collective-permute-start.1) | collective-permute-done | bytes 131104 | tf_op jit(solution)/shard_map/ppermute | solution.py:14
  43.8 1.8 %collective-permute-start.2 = (bf16[128,512]{0,1:T(8,128)(2,1)S(1)}, bf16[128,512]{0,1:T(8,128)(2,1)S(1)}, u32[]{:S(2)}, u32[]{:S(2)}) collective-permute-start(bf16[128,512]{0,1:T(8,128)(2,1)S(1)} %fusion.18), channel_id=1, source_target_pairs={{0,4},{4,0},{2,6},{6,2},{8,12},{12,8},{10,14},{14,10},{16,20},{20,... | collective-permute-start | bytes 393224 | tf_op jit(solution)/shard_map/ppermute | solution.py:14
  45.6 0.2 convert_reduce_fusion
  45.9 2.9 %collective-permute-done.2 = bf16[128,512]{0,1:T(8,128)(2,1)S(1)} collective-permute-done((bf16[128,512]{0,1:T(8,128)(2,1)S(1)}, bf16[128,512]{0,1:T(8,128)(2,1)S(1)}, u32[]{:S(2)}, u32[]{:S(2)}) %collective-permute-start.2) | collective-permute-done | bytes 131104 | tf_op jit(solution)/shard_map/ppermute | solution.py:14
  48.9 2.0 %all_gather.14 = bf16[256,512]{0,1:T(8,128)(2,1)S(1)} all-gather(bf16[128,512]{0,1:T(8,128)(2,1)S(1)} %add_convert_fusion.1), channel_id=1, replica_groups=mesh['col'=16,'row'=2] {'row'}, dimensions={0}, use_global_device_ids=true | all-gather | bytes 393216 | tf_op jit(solution)/shard_map/all_gather | solution.py:66
  50.9 0.2 convolution_convert_fusion.3
  51.1 0.2 fusion.22
  51.4 1.8 %collective-permute-start.3 = (bf16[128,512]{0,1:T(8,128)(2,1)S(1)}, bf16[128,512]{0,1:T(8,128)(2,1)S(1)}, u32[]{:S(2)}, u32[]{:S(2)}) collective-permute-start(bf16[128,512]{0,1:T(8,128)(2,1)S(1)} %get-tuple-element.48), channel_id=1, source_target_pairs={{0,2},{2,0},{4,6},{6,4},{8,10},{10,8},{12,14},{14,12},{16,18},{18,... | collective-permute-start | bytes 393224 | tf_op jit(solution)/shard_map/ppermute | solution.py:14
  53.2 3.8 %collective-permute-done.3 = bf16[128,512]{0,1:T(8,128)(2,1)S(1)} collective-permute-done((bf16[128,512]{0,1:T(8,128)(2,1)S(1)}, bf16[128,512]{0,1:T(8,128)(2,1)S(1)}, u32[]{:S(2)}, u32[]{:S(2)}) %collective-permute-start.3) | collective-permute-done | bytes 131104 | tf_op jit(solution)/shard_map/ppermute | solution.py:14
  57.0 1.8 %collective-permute-start.4 = (bf16[128,512]{0,1:T(8,128)(2,1)S(1)}, bf16[128,512]{0,1:T(8,128)(2,1)S(1)}, u32[]{:S(2)}, u32[]{:S(2)}) collective-permute-start(bf16[128,512]{0,1:T(8,128)(2,1)S(1)} %fusion.17), channel_id=1, source_target_pairs={{0,4},{4,0},{2,6},{6,2},{8,12},{12,8},{10,14},{14,10},{16,20},{20,... | collective-permute-start | bytes 393224 | tf_op jit(solution)/shard_map/ppermute | solution.py:14
  58.8 3.2 %collective-permute-done.4 = bf16[128,512]{0,1:T(8,128)(2,1)S(1)} collective-permute-done((bf16[128,512]{0,1:T(8,128)(2,1)S(1)}, bf16[128,512]{0,1:T(8,128)(2,1)S(1)}, u32[]{:S(2)}, u32[]{:S(2)}) %collective-permute-start.4) | collective-permute-done | bytes 131104 | tf_op jit(solution)/shard_map/ppermute | solution.py:14
  62.1 1.8 %collective-permute-start.5 = (bf16[128,512]{0,1:T(8,128)(2,1)S(1)}, bf16[128,512]{0,1:T(8,128)(2,1)S(1)}, u32[]{:S(2)}, u32[]{:S(2)}) collective-permute-start(bf16[128,512]{0,1:T(8,128)(2,1)S(1)} %fusion.20), channel_id=1, source_target_pairs={{0,8},{8,0},{2,10},{10,2},{4,12},{12,4},{6,14},{14,6},{16,24},{24,... | collective-permute-start | bytes 393224 | tf_op jit(solution)/shard_map/ppermute | solution.py:14
  63.9 0.8 %copy.24 = bf16[256,512]{1,0:T(8,128)(2,1)} copy(bf16[256,512]{0,1:T(8,128)(2,1)S(1)} %bitcast.108) | data formatting | bytes 524288
  64.8 0.8 %copy.25 = bf16[128,512]{1,0:T(8,128)(2,1)} copy(bf16[128,512]{0,1:T(8,128)(2,1)S(1)} %bitcast.110) | data formatting | bytes 262144
  65.5 1.6 %collective-permute-done.5 = bf16[128,512]{0,1:T(8,128)(2,1)S(1)} collective-permute-done((bf16[128,512]{0,1:T(8,128)(2,1)S(1)}, bf16[128,512]{0,1:T(8,128)(2,1)S(1)}, u32[]{:S(2)}, u32[]{:S(2)}) %collective-permute-start.5) | collective-permute-done | bytes 131104 | tf_op jit(solution)/shard_map/ppermute | solution.py:14
  67.2 2.0 %all_gather.15 = bf16[256,512]{0,1:T(8,128)(2,1)S(1)} all-gather(bf16[128,512]{0,1:T(8,128)(2,1)S(1)} %add_convert_fusion), channel_id=1, replica_groups=mesh['col'=16,'row'=2] {'row'}, dimensions={0}, use_global_device_ids=true | all-gather | bytes 393216 | tf_op jit(solution)/shard_map/all_gather | solution.py:66
  69.2 0.8 %fusion.12 = bf16[32,512]{1,0:T(8,128)(2,1)} fusion(bf16[256,512]{0,1:T(8,128)(2,1)S(1)} %all_gather.15, bf16[32,256]{1,0:T(8,128)(2,1)S(1)} %copy-done.9), kind=kOutput, calls=%fused_computation.21 | convolution fusion | flops 8404992 | bytes 311296 | tf_op jit(solution)/shard_map/dot_general | solution.py:62
  (41 shorter events, 1.3 us)
Async XLA Ops:
  7.2 1.6 %copy-start = (bf16[4,4,256,256]{3,2,1,0:T(8,128)(2,1)S(1)}, bf16[4,4,256,256]{3,2,1,0:T(8,128)(2,1)}, u32[]{:S(2)}) copy-start(bf16[4,4,256,256]{3,2,1,0:T(8,128)(2,1)} %param.21) | copy-start | bytes 6291460
  7.2 17.3 %reduce-scatter.4.cloned.1.call-start = ((), (), s32[]{:S(2)}) async-start(), calls=%async_computation.1 | async-start | bytes 1572864
  11.7 2.8 %copy-start.7 = (s32[6,1,4]{0,2,1:T(4,128)S(1)}, s32[6,1,4]{0,2,1:T(4,128)}, u32[]{:S(2)}) copy-start(s32[6,1,4]{0,2,1:T(4,128)} %param.29) | copy-start | bytes 292
  14.5 13.6 %copy-start.4 = (bf16[256,256]{1,0:T(8,128)(2,1)S(1)}, bf16[256,256]{1,0:T(8,128)(2,1)}, u32[]{:S(2)}) copy-start(bf16[256,256]{1,0:T(8,128)(2,1)} %param.22) | copy-start | bytes 393220
  14.8 13.5 %copy-start.3 = (bf16[3,128,256]{2,1,0:T(8,128)(2,1)S(1)}, bf16[3,128,256]{2,1,0:T(8,128)(2,1)}, u32[]{:S(2)}) copy-start(bf16[3,128,256]{2,1,0:T(8,128)(2,1)} %param.26) | copy-start | bytes 589828
  25.9 10.6 %copy-start.5 = (bf16[128,256]{1,0:T(8,128)(2,1)S(1)}, bf16[128,256]{1,0:T(8,128)(2,1)}, u32[]{:S(2)}) copy-start(bf16[128,256]{1,0:T(8,128)(2,1)} %param.23) | copy-start | bytes 196612
  28.7 8.1 %copy-start.1 = (f32[128,3,512]{0,2,1:T(8,128)}, f32[128,3,512]{0,2,1:T(8,128)S(1)}, u32[]{:S(2)}) copy-start(f32[128,3,512]{0,2,1:T(8,128)S(1)} %fusion.3) | copy-start | bytes 2359300
  28.7 5.7 %collective-permute-start = (bf16[128,512]{0,1:T(8,128)(2,1)S(1)}, bf16[128,512]{0,1:T(8,128)(2,1)S(1)}, u32[]{:S(2)}, u32[]{:S(2)}) collective-permute-start(bf16[128,512]{0,1:T(8,128)(2,1)S(1)} %fusion.15), channel_id=1, source_target_pairs={{0,2},{2,0},{4,6},{6,4},{8,10},{10,8},{12,14},{14,12},{16,18},{18,... | collective-permute-start | bytes 393224 | tf_op jit(solution)/shard_map/ppermute | solution.py:14
  34.5 16.4 %copy-start.6 = (bf16[64,256]{1,0:T(8,128)(2,1)S(1)}, bf16[64,256]{1,0:T(8,128)(2,1)}, u32[]{:S(2)}) copy-start(bf16[64,256]{1,0:T(8,128)(2,1)} %param.24) | copy-start | bytes 98308
  34.5 16.6 %copy-start.8 = (bf16[1,128,64]{1,2,0:T(8,128)(2,1)S(1)}, bf16[1,128,64]{1,2,0:T(8,128)(2,1)}, u32[]{:S(2)}) copy-start(bf16[1,128,64]{1,2,0:T(8,128)(2,1)} %param.28) | copy-start | bytes 49156
  38.1 5.6 %collective-permute-start.1 = (bf16[128,512]{0,1:T(8,128)(2,1)S(1)}, bf16[128,512]{0,1:T(8,128)(2,1)S(1)}, u32[]{:S(2)}, u32[]{:S(2)}) collective-permute-start(bf16[128,512]{0,1:T(8,128)(2,1)S(1)} %fusion.16), channel_id=1, source_target_pairs={{0,2},{2,0},{4,6},{6,4},{8,10},{10,8},{12,14},{14,12},{16,18},{18,... | collective-permute-start | bytes 393224 | tf_op jit(solution)/shard_map/ppermute | solution.py:14
  43.8 5.0 %collective-permute-start.2 = (bf16[128,512]{0,1:T(8,128)(2,1)S(1)}, bf16[128,512]{0,1:T(8,128)(2,1)S(1)}, u32[]{:S(2)}, u32[]{:S(2)}) collective-permute-start(bf16[128,512]{0,1:T(8,128)(2,1)S(1)} %fusion.18), channel_id=1, source_target_pairs={{0,4},{4,0},{2,6},{6,2},{8,12},{12,8},{10,14},{14,10},{16,20},{20,... | collective-permute-start | bytes 393224 | tf_op jit(solution)/shard_map/ppermute | solution.py:14
  50.9 18.3 %copy-start.9 = (bf16[32,256]{1,0:T(8,128)(2,1)S(1)}, bf16[32,256]{1,0:T(8,128)(2,1)}, u32[]{:S(2)}) copy-start(bf16[32,256]{1,0:T(8,128)(2,1)} %param.25) | copy-start | bytes 49156
  51.1 18.9 %copy-start.2 = (bf16[512,64]{0,1:T(8,128)(2,1)}, bf16[512,64]{0,1:T(8,128)(2,1)S(1)}, u32[]{:S(2)}) copy-start(bf16[512,64]{0,1:T(8,128)(2,1)S(1)} %convolution_convert_fusion.3) | copy-start | bytes 196612
  51.4 5.6 %collective-permute-start.3 = (bf16[128,512]{0,1:T(8,128)(2,1)S(1)}, bf16[128,512]{0,1:T(8,128)(2,1)S(1)}, u32[]{:S(2)}, u32[]{:S(2)}) collective-permute-start(bf16[128,512]{0,1:T(8,128)(2,1)S(1)} %get-tuple-element.48), channel_id=1, source_target_pairs={{0,2},{2,0},{4,6},{6,4},{8,10},{10,8},{12,14},{14,12},{16,18},{18,... | collective-permute-start | bytes 393224 | tf_op jit(solution)/shard_map/ppermute | solution.py:14
  57.0 5.0 %collective-permute-start.4 = (bf16[128,512]{0,1:T(8,128)(2,1)S(1)}, bf16[128,512]{0,1:T(8,128)(2,1)S(1)}, u32[]{:S(2)}, u32[]{:S(2)}) collective-permute-start(bf16[128,512]{0,1:T(8,128)(2,1)S(1)} %fusion.17), channel_id=1, source_target_pairs={{0,4},{4,0},{2,6},{6,2},{8,12},{12,8},{10,14},{14,10},{16,20},{20,... | collective-permute-start | bytes 393224 | tf_op jit(solution)/shard_map/ppermute | solution.py:14
  62.1 5.0 %collective-permute-start.5 = (bf16[128,512]{0,1:T(8,128)(2,1)S(1)}, bf16[128,512]{0,1:T(8,128)(2,1)S(1)}, u32[]{:S(2)}, u32[]{:S(2)}) collective-permute-start(bf16[128,512]{0,1:T(8,128)(2,1)S(1)} %fusion.20), channel_id=1, source_target_pairs={{0,8},{8,0},{2,10},{10,2},{4,12},{12,4},{6,14},{14,6},{16,24},{24,... | collective-permute-start | bytes 393224 | tf_op jit(solution)/shard_map/ppermute | solution.py:14
Sparse Core Ops, SparseCore 0:
  13.3 11.1 reduce-scatter.3
where the time goes:
time: 77.3 us; the launch traced here: 76.9 us
  waiting for transfers between devices  28.6 us (37%)
  between operations  14.3 us (18%)
  starting transfers between devices  10.9 us (14%)
  blocking collectives  8.23 us (11%)
  local copies, waits for them, and re-layouts  7.97 us (10%)
  matrix products  6.28 us (8%)
    ppermute x6, waiting for transfers between devices, from_partner(): return lax.ppermute(block, axis, route)  18.9 us
    ppermute x6, starting transfers between devices, from_partner(): return lax.ppermute(block, axis, route)  10.9 us
    unnamed x2, waiting for transfers between devices  9.68 us
    all_gather x4, blocking collectives, body(): lax.all_gather(residual_half, 'row', axis=0, tiled=True)  8.23 us
    unnamed x25, local copies, waits for them, and re-layouts  7.26 us
    dot_general x1, matrix products, body(): jnp.einsum('mvrs,vsk->rmk', leaf_lower, leaf_solution, preferred_element_...  2.96 us
    dot_general x3, matrix products, body(): jnp.einsum('mrc,ck->rmk', lower_blocks, solved, preferred_element_type=jn...  1.85 us
  transfers between devices with their start and end apart: 7, of which 7 were waited for; matrix products, arithmetic and copies ran while one was open for 5% of the time, Pallas kernels for 0%

commit v1 on v0

v1 whole, which is shorter than its diff:
```python
import functools

import jax
import jax.numpy as jnp
from jax import lax
from jax.experimental import pallas as pl
from jax.experimental.pallas import tpu as pltpu
from jax.sharding import PartitionSpec as P

F32, BF16 = jnp.float32, jnp.bfloat16
WHOLE = pl.BlockSpec(memory_space=pltpu.VMEM)


def dot(a, b):
    return jnp.dot(a, b, preferred_element_type=F32)


def call(kernel, outs, *args, scratch=(), flops=0, name=None):
    outs = [jax.ShapeDtypeStruct(shape, dtype) for shape, dtype in outs]
    moved = sum(a.size * a.dtype.itemsize for a in (*args, *outs))
    single = len(outs) == 1
    return pl.pallas_call(
        kernel,
        out_shape=outs[0] if single else outs,
        in_specs=[WHOLE] * len(args),
        out_specs=WHOLE if single else [WHOLE] * len(outs),
        scratch_shapes=list(scratch),
        cost_estimate=pl.CostEstimate(flops=flops, bytes_accessed=moved, transcendentals=0),
        compiler_params=pltpu.CompilerParams(vmem_limit_bytes=16 << 20),
        name=name,
    )(*args)


def partner(block, axis, stride):
    count = lax.axis_size(axis)
    return lax.ppermute(block, axis, [(low, low ^ stride) for low in range(count)])


def halves(ref_like, half):
    me = lax.axis_index("row")
    return pl.ds(pl.multiple_of(me * half, half), half), pl.ds(
        pl.multiple_of((1 - me) * half, half), half
    )


def leaf_first(inverse, right, lower, top, solution_out, keep, send, total):
    leaves, size, _ = inverse.shape
    rows = top.shape[0]
    half = keep.shape[1]
    me = lax.axis_index("row")
    for v in range(leaves):
        solved = dot(inverse[v], right[v]).astype(BF16)
        solution_out[v] = solved
        term = dot(lower[v], solved)
        total[...] = -term if v == 0 else total[...] - term
    mine = pl.ds(pl.multiple_of(me * rows, rows), rows)
    total[mine, :] = total[mine, :] + top[...].astype(F32)
    own, other = halves(total, half)
    keep[...] = total[:, own]
    send[...] = total[:, other].astype(BF16)


def leaf_rest(solved, lower, top, keep, send, total):
    levels, leaves, size, _ = lower.shape
    rows = top.shape[1]
    half = keep.shape[2]
    me = lax.axis_index("row")
    mine = pl.ds(pl.multiple_of(me * rows, rows), rows)
    own, other = halves(total, half)
    for m in range(levels):
        acc = dot(lower[m, 0], solved[0])
        for v in range(1, leaves):
            acc = acc + dot(lower[m, v], solved[v])
        total[...] = -acc
        total[mine, :] = total[mine, :] + top[m].astype(F32)
        keep[m] = total[:, own]
        send[m] = total[:, other].astype(BF16)


def mask_lower(lower_0, lower_1, lower_2, pattern, out_0, out_1, out_2):
    rows = lower_0.shape[1]
    blocks = pattern.shape[2]
    spread = rows // blocks
    p = 0
    for lower, out in ((lower_0, out_0), (lower_1, out_1), (lower_2, out_2)):
        for m in range(lower.shape[0]):
            for b in range(blocks):
                at = pl.ds(b * spread, spread)
                factor = pattern[p, 0, b].astype(F32)
                out[m, at, :] = (lower[m, at, :].astype(F32) * factor).astype(BF16)
            p += 1


def by_core(own, other):
    first = lax.axis_index("row") == 0
    return jnp.where(first, own, other), jnp.where(first, other, own)


def level_zero(keep, got, inverse, low_own, low_other, keep_rest, got_rest, solved_out, p1, p2, p3):
    rows = low_own.shape[1]
    residual = (keep[...] + got[...].astype(F32)).astype(BF16)
    solved = dot(inverse[...], residual).astype(BF16)
    solved_out[...] = solved
    me = lax.axis_index("row")
    mine = pl.ds(pl.multiple_of(me * rows, rows), rows)
    theirs = pl.ds(pl.multiple_of((1 - me) * rows, rows), rows)
    for m, out in enumerate((p1, p2, p3)):
        for low, at in ((low_own, mine), (low_other, theirs)):
            total = keep_rest[m, at, :] + got_rest[m, at, :].astype(F32)
            out[at, :] = (total - dot(low[m], solved)).astype(out.dtype)


def level_one(own, got, inv_own, inv_x, low_oo, low_or, low_xo, low_xr, solved_out, u2, u3):
    part, size = inv_own.shape
    rows = low_oo.shape[1]
    residual = (own[...].astype(F32) + got[...].astype(F32)).astype(BF16)
    solved_own = dot(inv_own[...], residual).astype(BF16)
    solved_x = dot(inv_x[...], residual).astype(BF16)
    solved_out[...] = solved_own
    me = lax.axis_index("row")
    mine = pl.ds(pl.multiple_of(me * rows, rows), rows)
    theirs = pl.ds(pl.multiple_of((1 - me) * rows, rows), rows)
    for m, out in enumerate((u2, u3)):
        for low_a, low_b, at in ((low_oo, low_xo, mine), (low_or, low_xr, theirs)):
            out[at, :] = (dot(low_a[m], solved_own) + dot(low_b[m], solved_x)).astype(BF16)


def level_two(base, got, u_own, u_got, inv, low_own, low_other, rest, solved_out, v3):
    rows = low_own.shape[1]
    part = inv.shape[1]
    residual = (
        base[...].astype(F32) + got[...].astype(F32) - u_own[...].astype(F32) - u_got[...].astype(F32)
    ).astype(BF16)
    solved = [dot(inv[i], residual).astype(BF16) for i in range(inv.shape[0])]
    solved_out[...] = solved[0]
    me = lax.axis_index("row")
    mine = pl.ds(pl.multiple_of(me * rows, rows), rows)
    theirs = pl.ds(pl.multiple_of((1 - me) * rows, rows), rows)
    for low, at in ((low_own, mine), (low_other, theirs)):
        total = rest[at, :]
        for i in range(inv.shape[0]):
            total = total - dot(low[i], solved[i])
        v3[at, :] = total.astype(BF16)


def level_three(own, got, inverse, solved_out):
    residual = (own[...].astype(F32) + got[...].astype(F32)).astype(BF16)
    solved_out[...] = dot(inverse[...], residual).astype(BF16)


def join_halves(own, got, out):
    half = own.shape[1]
    mine, theirs = halves(out, half)
    out[:, mine] = own[...]
    out[:, theirs] = got[...]


def body(
    rhs, leaf_rhs, leaf_inverse, leaf_lower,
    inverse_0, inverse_1, inverse_2, inverse_3,
    lower_0, lower_1, lower_2, sparsity,
):
    levels, _, rows, width = rhs.shape
    leaves, size, _ = leaf_inverse.shape
    half = width // lax.axis_size("row")

    inv1_x = partner(inverse_1, "col", 1)
    inv2_x = partner(inverse_2, "col", 1)

    solved_leaf, keep0, send0 = call(
        leaf_first,
        [((leaves, size, width), BF16), ((size, half), F32), ((size, half), BF16)],
        leaf_inverse, leaf_rhs, leaf_lower[0], rhs[0, 0],
        scratch=[pltpu.VMEM((size, width), F32)],
        flops=4 * leaves * size * size * width, name="leaf_first",
    )
    low0, low1, low2 = pl.pallas_call(
        mask_lower,
        out_shape=[jax.ShapeDtypeStruct(x.shape, BF16) for x in (lower_0, lower_1, lower_2)],
        in_specs=[WHOLE] * 3 + [pl.BlockSpec(memory_space=pltpu.SMEM)],
        out_specs=[WHOLE] * 3,
        compiler_params=pltpu.CompilerParams(vmem_limit_bytes=16 << 20),
        name="mask_lower",
    )(lower_0, lower_1, lower_2, sparsity)
    low1_x = partner(low1, "col", 1)
    low2_x = partner(low2, "col", 1)
    low0_r = partner(low0, "row", 1)

    got0 = partner(send0, "row", 1)
    keep, send = call(
        leaf_rest,
        [((levels - 1, size, half), F32), ((levels - 1, size, half), BF16)],
        solved_leaf, leaf_lower[1:], rhs[1:, 0],
        scratch=[pltpu.VMEM((size, width), F32)],
        flops=2 * (levels - 1) * leaves * size * size * width, name="leaf_rest",
    )
    got = partner(send, "row", 1)
    sol0, p1, p2, p3 = call(
        level_zero,
        [((size, half), BF16)] * 4,
        keep0, got0, inverse_0, low0, low0_r, keep, got,
        flops=8 * size * size * half, name="level_zero",
    )
    p1_x = partner(p1, "col", 1)
    p2_y = partner(p2, "col", 2)
    p3_x = partner(p3, "col", 1)

    low1_r = partner(low1, "row", 1)
    low1_xr = partner(low1_x, "row", 1)
    inv2_y = partner(jnp.stack([inverse_2, inv2_x]), "col", 2)
    low2_y = partner(jnp.concatenate([low2, low2_x]), "col", 2)
    inv2 = jnp.concatenate([inverse_2[None], inv2_x[None], inv2_y])
    low2_all = jnp.concatenate([low2, low2_x, low2_y])
    low2_r = partner(low2_all, "row", 1)

    sol1, u2, u3 = call(
        level_one,
        [((inverse_1.shape[0], half), BF16)] + [((size, half), BF16)] * 2,
        p1, p1_x, inverse_1, inv1_x, low1, low1_r, low1_x, low1_xr,
        flops=6 * size * size * half, name="level_one",
    )
    u2_y = partner(u2, "col", 2)
    s2 = (p2.astype(F32) + p2_y.astype(F32)).astype(BF16)
    s2_x = partner(s2, "col", 1)
    s3 = (p3.astype(F32) + p3_x.astype(F32) - u3.astype(F32)).astype(BF16)
    s3_y = partner(s3, "col", 2)
    rest = s3.astype(F32) + s3_y.astype(F32)
    sol2, v3 = call(
        level_two,
        [((inverse_2.shape[0], half), BF16), ((size, half), BF16)],
        s2, s2_x, u2, u2_y, inv2, low2_all, low2_r, rest,
        flops=4 * size * size * half, name="level_two",
    )
    v3_z = partner(v3, "col", 4)
    sol3 = call(
        level_three,
        [((inverse_3.shape[0], half), BF16)],
        v3, v3_z, inverse_3, flops=2 * inverse_3.size * half, name="level_three",
    )
    outs = []
    for solved in (sol0, sol1, sol2, sol3):
        got_half = partner(solved, "row", 1)
        outs.append(call(join_halves, [((solved.shape[0], width), BF16)], solved, got_half, name="join"))
    return tuple(outs)


def solution(mesh):
    return jax.shard_map(
        body,
        mesh=mesh,
        in_specs=(
            P(None, "col", "row", None),
            P(("col", "row"), None, None),
            P(("col", "row"), None, None),
            P(None, ("col", "row"), None, None),
            P("col", None),
            P("col", None),
            P("col", None),
            P("col", None),
            P(None, "row", "col"),
            P(None, "row", "col"),
            P(None, "row", "col"),
            P(None, "col", "row"),
        ),
        out_specs=(P("col", None), P("col", None), P("col", None), P("col", None)),
        check_vma=False,
    )
```

time: 77.3 us -> 51 us (0.66)
  between operations: 14.3 us -> 0.89 us
  blocking collectives: 8.23 us -> 0 us
  waiting for transfers between devices: 28.6 us -> 21 us
  Pallas kernels: 0 us -> 7.46 us
  starting transfers between devices: 10.9 us -> 18.1 us
  matrix products: 6.28 us -> 0 us
  local copies, waits for them, and re-layouts: 7.97 us -> 3.2 us
    unnamed x2 -> x0, waiting for transfers between devices: 9.68 us -> none
    all_gather x4 -> x0, blocking collectives: 8.23 us -> none  [body(): lax.all_gather(residual_half, 'row', axis=0, tiled=True)]
    pallas_call x0 -> x11, Pallas kernels: none -> 7.46 us  [the longest x10 6.82 us: call(): pl.pallas_call(kernel, out_shape=outs[0] if single else outs, in_specs=[W...]
    ppermute x6 -> x23, starting transfers between devices: 10.9 us -> 18.1 us  [partner(): lax.ppermute(block, axis, [(low, low ^ stride) for low in range(count)])]
    unnamed x25 -> x26, local copies, waits for them, and re-layouts: 7.26 us -> 0.39 us
    dot_general x8 -> x0, matrix products: 6.28 us -> none  [the longest x1 2.96 us: body(): jnp.einsum('mvrs,vsk->rmk', leaf_lower, leaf_solution, preferred_element_...]
    ppermute x6 -> x23, waiting for transfers between devices: 18.9 us -> 21 us  [partner(): lax.ppermute(block, axis, [(low, low ^ stride) for low in range(count)])]
    slice x1, local copies, waits for them, and re-layouts: 0.02 us -> 1.63 us  [body(): leaf_lower[1:]]
  transfers between devices with their start and end apart: 7 -> 23, of which waited for: 7 -> 9; matrix products, arithmetic and copies ran while one was open for 5% -> 1% of each run, Pallas kernels for 0% -> 7%
where the time goes in v1:
time: 51 us; the launch traced here: 50.8 us
  waiting for transfers between devices  21 us (41%)
  starting transfers between devices  18.1 us (35%)
  Pallas kernels  7.46 us (15%)
  local copies, waits for them, and re-layouts  3.2 us (6%)
  between operations  0.89 us (2%)
    ppermute x23, waiting for transfers between devices, partner(): lax.ppermute(block, axis, [(low, low ^ stride) for low in range(count)])  21 us
    ppermute x23, starting transfers between devices, partner(): lax.ppermute(block, axis, [(low, low ^ stride) for low in range(count)])  18.1 us
    pallas_call x10, Pallas kernels, call(): pl.pallas_call(kernel, out_shape=outs[0] if single else outs, in_specs=[W...  6.82 us
    slice x1, local copies, waits for them, and re-layouts, body(): leaf_lower[1:]  1.63 us
    squeeze x1, local copies, waits for them, and re-layouts, body(): leaf_lower[0]  1.14 us
  transfers between devices with their start and end apart: 23, of which 9 were waited for; matrix products, arithmetic and copies ran while one was open for 1% of the time, Pallas kernels for 7%

profile of v1, /device:TPU:0, one launch (start us, length us, event | category | flops | bytes accessed | tf_op | source)
XLA Modules:
  0.0 50.8 jit_solution(15012955525708646610)
XLA Ops:
  0.6 1.1 %slice_bitcast_fusion.lower = bf16[4,256,256]{2,1,0:T(8,128)(2,1)S(1)} fusion(bf16[4,4,256,256]{3,2,1,0:T(8,128)(2,1)} %param.15), kind=kLoop, calls=%fused_computation | loop fusion | bytes 1048576 | tf_op jit(solution)/shard_map/squeeze | solution.py:173
  1.8 1.6 %slice.14.lower = bf16[3,4,256,256]{3,2,1,0:T(8,128)(2,1)S(1)} slice(bf16[4,4,256,256]{3,2,1,0:T(8,128)(2,1)} %param.15), slice={[1:4], [0:4], [0:256], [0:256]} | slice | bytes 3145728 | tf_op jit(solution)/shard_map/slice | solution.py:193
  3.6 1.3 %leaf_first.1 = (bf16[4,256,512]{2,1,0:T(8,128)(2,1)S(1)}, f32[256,256]{1,0:T(8,128)S(1)}, bf16[256,256]{1,0:T(8,128)(2,1)S(1)}) custom-call(bf16[4,256,256]{2,1,0:T(8,128)(2,1)S(1)} %copy-done.1, bf16[4,256,512]{2,1,0:T(8,128)(2,1)S(1)} %copy-done, bf16[4,256,256]{2,1,0:T(8,128)(2,1)S(1)} %slice_bitcast_fusion.lower, ...), custom_call_target="tpu_custom_call" | custom-call | flops 536870912 | bytes 3670016 | tf_op jit(solution)/shard_map/leaf_first/pallas_call | solution.py:22
  5.0 1.2 %leaf_rest.1 = (f32[3,256,256]{2,1,0:T(8,128)S(1)}, bf16[3,256,256]{2,1,0:T(8,128)(2,1)S(1)}) custom-call(bf16[4,256,512]{2,1,0:T(8,128)(2,1)S(1)} %get-tuple-element.24.solved, bf16[3,4,256,256]{3,2,1,0:T(8,128)(2,1)S(1)} %slice.14.lower, bf16[3,128,512]{2,1,0:T(8,128)(2,1)S(1)} %slice_bitcast_fusion.1.top), custom_call_target="tpu_custom_call" | custom-call | flops 805306368 | bytes 4194304 | tf_op jit(solution)/shard_map/leaf_rest/pallas_call | solution.py:22
  6.2 0.6 %collective-permute-start.2 = (bf16[3,256,256]{2,1,0:T(8,128)(2,1)S(1)}, bf16[3,256,256]{2,1,0:T(8,128)(2,1)S(1)}, u32[]{:S(2)}, u32[]{:S(2)}) collective-permute-start(bf16[3,256,256]{2,1,0:T(8,128)(2,1)S(1)} %get-tuple-element.26), channel_id=1, source_target_pairs={{0,1},{1,0},{2,3},{3,2},{4,5},{5,4},{6,7},{7,6},{8,9},{9,8},{10,11... | collective-permute-start | bytes 1179656 | tf_op jit(solution)/shard_map/ppermute | solution.py:36
  7.1 0.6 %mask_lower.1 = (bf16[3,128,256]{2,1,0:T(8,128)(2,1)S(1)}, bf16[2,128,128]{2,1,0:T(8,128)(2,1)S(1)}, bf16[1,128,64]{2,1,0:T(8,128)(2,1)S(1)}) custom-call(bf16[3,128,256]{2,1,0:T(8,128)(2,1)S(1)} %copy-done.2, bf16[2,128,128]{2,1,0:T(8,128)(2,1)S(1)} %copy-done.5, bf16[1,128,64]{2,1,0:T(8,128)(2,1)S(1)} %copy.16.lower_2, s32[6,1,4]{2,1,0:T(1,128)S(1)} %copy.17.pattern), custom_call_target="tpu_custom_call" | custom-call | tf_op jit(solution)/shard_map/mask_lower/pallas_call | solution.py:177
  8.3 2.5 %collective-permute-start.7 = (bf16[2,128,128]{2,1,0:T(8,128)(2,1)S(1)}, bf16[2,128,128]{2,1,0:T(8,128)(2,1)S(1)}, u32[]{:S(2)}, u32[]{:S(2)}) collective-permute-start(bf16[2,128,128]{2,1,0:T(8,128)(2,1)S(1)} %get-tuple-element.29.low_oo), channel_id=1, source_target_pairs={{0,2},{2,0},{4,6},{6,4},{8,10},{10,8},{12,14},{14,12},{16,18},{18,... | collective-permute-start | bytes 196616 | tf_op jit(solution)/shard_map/ppermute | solution.py:36
  10.8 3.9 %collective-permute-done.15 = bf16[1,128,64]{2,1,0:T(8,128)(2,1)S(1)} collective-permute-done((bf16[1,128,64]{2,1,0:T(8,128)(2,1)S(1)}, bf16[1,128,64]{2,1,0:T(8,128)(2,1)S(1)}, u32[]{:S(2)}, u32[]{:S(2)}) %collective-permute-start.15) | collective-permute-done | bytes 16416 | tf_op jit(solution)/shard_map/ppermute | solution.py:36
  14.7 1.2 %collective-permute-start.13 = (bf16[64,256]{1,0:T(8,128)(2,1)S(1)}, bf16[64,256]{1,0:T(8,128)(2,1)S(1)}, u32[]{:S(2)}, u32[]{:S(2)}) collective-permute-start(bf16[64,256]{1,0:T(8,128)(2,1)S(1)} %copy-done.8), channel_id=1, source_target_pairs={{0,2},{2,0},{4,6},{6,4},{8,10},{10,8},{12,14},{14,12},{16,18},{18,... | collective-permute-start | bytes 98312 | tf_op jit(solution)/shard_map/ppermute | solution.py:36
  16.0 2.7 %collective-permute-done.13 = bf16[64,256]{1,0:T(8,128)(2,1)S(1)} collective-permute-done((bf16[64,256]{1,0:T(8,128)(2,1)S(1)}, bf16[64,256]{1,0:T(8,128)(2,1)S(1)}, u32[]{:S(2)}, u32[]{:S(2)}) %collective-permute-start.13) | collective-permute-done | bytes 32800 | tf_op jit(solution)/shard_map/ppermute | solution.py:36
  18.7 1.5 %collective-permute-start.16 = (bf16[2,128,64]{2,1,0:T(8,128)(2,1)S(1)}, bf16[2,128,64]{2,1,0:T(8,128)(2,1)S(1)}, u32[]{:S(2)}, u32[]{:S(2)}) collective-permute-start(bf16[2,128,64]{2,1,0:T(8,128)(2,1)S(1)} %pad_maximum_fusion.2), channel_id=1, source_target_pairs={{0,4},{2,6},{4,0},{6,2},{8,12},{10,14},{12,8},{14,10},{16,20},{18,... | collective-permute-start | bytes 98312 | tf_op jit(solution)/shard_map/ppermute | solution.py:36
  20.3 0.6 %collective-permute-start.14 = (bf16[2,64,256]{2,1,0:T(8,128)(2,1)S(1)}, bf16[2,64,256]{2,1,0:T(8,128)(2,1)S(1)}, u32[]{:S(2)}, u32[]{:S(2)}) collective-permute-start(bf16[2,64,256]{2,1,0:T(8,128)(2,1)S(1)} %pad_maximum_fusion.1), channel_id=1, source_target_pairs={{0,4},{2,6},{4,0},{6,2},{8,12},{10,14},{12,8},{14,10},{16,20},{18,... | collective-permute-start | bytes 196616 | tf_op jit(solution)/shard_map/ppermute | solution.py:36
  21.4 1.3 %collective-permute-start.4 = (bf16[256,256]{1,0:T(8,128)(2,1)S(1)}, bf16[256,256]{1,0:T(8,128)(2,1)S(1)}, u32[]{:S(2)}, u32[]{:S(2)}) collective-permute-start(bf16[256,256]{1,0:T(8,128)(2,1)S(1)} %get-tuple-element.28.own), channel_id=1, source_target_pairs={{0,2},{2,0},{4,6},{6,4},{8,10},{10,8},{12,14},{14,12},{16,18},{18,... | collective-permute-start | bytes 393224 | tf_op jit(solution)/shard_map/ppermute | solution.py:36
  22.9 1.2 %collective-permute-start.18 = (bf16[256,256]{1,0:T(8,128)(2,1)S(1)}, bf16[256,256]{1,0:T(8,128)(2,1)S(1)}, u32[]{:S(2)}, u32[]{:S(2)}) collective-permute-start(bf16[256,256]{1,0:T(8,128)(2,1)S(1)} %get-tuple-element.34), channel_id=1, source_target_pairs={{0,2},{2,0},{4,6},{6,4},{8,10},{10,8},{12,14},{14,12},{16,18},{18,... | collective-permute-start | bytes 393224 | tf_op jit(solution)/shard_map/ppermute | solution.py:36
  24.2 0.9 %collective-permute-start.5 = (bf16[128,256]{1,0:T(8,128)(2,1)S(1)}, bf16[128,256]{1,0:T(8,128)(2,1)S(1)}, u32[]{:S(2)}, u32[]{:S(2)}) collective-permute-start(bf16[128,256]{1,0:T(8,128)(2,1)S(1)} %copy-done.4), channel_id=1, source_target_pairs={{0,2},{2,0},{4,6},{6,4},{8,10},{10,8},{12,14},{14,12},{16,18},{18,... | collective-permute-start | bytes 196616 | tf_op jit(solution)/shard_map/ppermute | solution.py:36
  25.1 0.6 %collective-permute-start.17 = (bf16[4,128,64]{2,1,0:T(8,128)(2,1)S(1)}, bf16[4,128,64]{2,1,0:T(8,128)(2,1)S(1)}, u32[]{:S(2)}, u32[]{:S(2)}) collective-permute-start(bf16[4,128,64]{2,1,0:T(8,128)(2,1)S(1)} %constant_dynamic-update-slice_fusion.low_own), channel_id=1, source_target_pairs={{0,1},{1,0},{2,3},{3,2},{4,5},{5,4},{6,7},{7,6},{8,9},{9,8},{10,11... | collective-permute-start | bytes 196616 | tf_op jit(solution)/shard_map/ppermute | solution.py:36
  25.7 5.5 %collective-permute-done.5.inv_x = bf16[128,256]{1,0:T(8,128)(2,1)S(1)} collective-permute-done((bf16[128,256]{1,0:T(8,128)(2,1)S(1)}, bf16[128,256]{1,0:T(8,128)(2,1)S(1)}, u32[]{:S(2)}, u32[]{:S(2)}) %collective-permute-start.5) | collective-permute-done | bytes 65568 | tf_op jit(solution)/shard_map/ppermute | solution.py:36
  31.2 1.5 %collective-permute-start.10 = (bf16[256,256]{1,0:T(8,128)(2,1)S(1)}, bf16[256,256]{1,0:T(8,128)(2,1)S(1)}, u32[]{:S(2)}, u32[]{:S(2)}) collective-permute-start(bf16[256,256]{1,0:T(8,128)(2,1)S(1)} %get-tuple-element.31), channel_id=1, source_target_pairs={{0,4},{2,6},{4,0},{6,2},{8,12},{10,14},{12,8},{14,10},{16,20},{18,... | collective-permute-start | bytes 393224 | tf_op jit(solution)/shard_map/ppermute | solution.py:36
  33.3 0.6 %collective-permute-start.19 = (bf16[256,256]{1,0:T(8,128)(2,1)S(1)}, bf16[256,256]{1,0:T(8,128)(2,1)S(1)}, u32[]{:S(2)}, u32[]{:S(2)}) collective-permute-start(bf16[256,256]{1,0:T(8,128)(2,1)S(1)} %subtract_convert_fusion), channel_id=1, source_target_pairs={{0,4},{2,6},{4,0},{6,2},{8,12},{10,14},{12,8},{14,10},{16,20},{18,... | collective-permute-start | bytes 393224 | tf_op jit(solution)/shard_map/ppermute | solution.py:36
  33.8 1.5 %collective-permute-start.12 = (bf16[256,256]{1,0:T(8,128)(2,1)S(1)}, bf16[256,256]{1,0:T(8,128)(2,1)S(1)}, u32[]{:S(2)}, u32[]{:S(2)}) collective-permute-start(bf16[256,256]{1,0:T(8,128)(2,1)S(1)} %get-tuple-element.32.u_own), channel_id=1, source_target_pairs={{0,4},{2,6},{4,0},{6,2},{8,12},{10,14},{12,8},{14,10},{16,20},{18,... | collective-permute-start | bytes 393224 | tf_op jit(solution)/shard_map/ppermute | solution.py:36
  35.3 2.0 %collective-permute-done.10 = bf16[256,256]{1,0:T(8,128)(2,1)S(1)} collective-permute-done((bf16[256,256]{1,0:T(8,128)(2,1)S(1)}, bf16[256,256]{1,0:T(8,128)(2,1)S(1)}, u32[]{:S(2)}, u32[]{:S(2)}) %collective-permute-start.10) | collective-permute-done | bytes 131104 | tf_op jit(solution)/shard_map/ppermute | solution.py:36
  37.4 1.3 %collective-permute-start.11 = (bf16[256,256]{1,0:T(8,128)(2,1)S(1)}, bf16[256,256]{1,0:T(8,128)(2,1)S(1)}, u32[]{:S(2)}, u32[]{:S(2)}) collective-permute-start(bf16[256,256]{1,0:T(8,128)(2,1)S(1)} %add_convert_fusion.base), channel_id=1, source_target_pairs={{0,2},{2,0},{4,6},{6,4},{8,10},{10,8},{12,14},{14,12},{16,18},{18,... | collective-permute-start | bytes 393224 | tf_op jit(solution)/shard_map/ppermute | solution.py:36
  38.7 1.5 %collective-permute-done.19 = bf16[256,256]{1,0:T(8,128)(2,1)S(1)} collective-permute-done((bf16[256,256]{1,0:T(8,128)(2,1)S(1)}, bf16[256,256]{1,0:T(8,128)(2,1)S(1)}, u32[]{:S(2)}, u32[]{:S(2)}) %collective-permute-start.19) | collective-permute-done | bytes 131104 | tf_op jit(solution)/shard_map/ppermute | solution.py:36
  40.2 1.5 %collective-permute-done.12.u_got = bf16[256,256]{1,0:T(8,128)(2,1)S(1)} collective-permute-done((bf16[256,256]{1,0:T(8,128)(2,1)S(1)}, bf16[256,256]{1,0:T(8,128)(2,1)S(1)}, u32[]{:S(2)}, u32[]{:S(2)}) %collective-permute-start.12) | collective-permute-done | bytes 131104 | tf_op jit(solution)/shard_map/ppermute | solution.py:36
  41.8 0.7 %collective-permute-done.11.got = bf16[256,256]{1,0:T(8,128)(2,1)S(1)} collective-permute-done((bf16[256,256]{1,0:T(8,128)(2,1)S(1)}, bf16[256,256]{1,0:T(8,128)(2,1)S(1)}, u32[]{:S(2)}, u32[]{:S(2)}) %collective-permute-start.11) | collective-permute-done | bytes 131104 | tf_op jit(solution)/shard_map/ppermute | solution.py:36
  42.9 1.6 %collective-permute-start.21 = (bf16[256,256]{1,0:T(8,128)(2,1)S(1)}, bf16[256,256]{1,0:T(8,128)(2,1)S(1)}, u32[]{:S(2)}, u32[]{:S(2)}) collective-permute-start(bf16[256,256]{1,0:T(8,128)(2,1)S(1)} %get-tuple-element.37.own), channel_id=1, source_target_pairs={{0,8},{2,10},{4,12},{6,14},{8,0},{10,2},{12,4},{14,6},{16,24},{18,... | collective-permute-start | bytes 393224 | tf_op jit(solution)/shard_map/ppermute | solution.py:36
  44.6 0.5 collective-permute-start.9
  45.1 2.9 %collective-permute-done.21.got = bf16[256,256]{1,0:T(8,128)(2,1)S(1)} collective-permute-done((bf16[256,256]{1,0:T(8,128)(2,1)S(1)}, bf16[256,256]{1,0:T(8,128)(2,1)S(1)}, u32[]{:S(2)}, u32[]{:S(2)}) %collective-permute-start.21) | collective-permute-done | bytes 131104 | tf_op jit(solution)/shard_map/ppermute | solution.py:36
  48.1 0.7 %join.4 = bf16[256,512]{1,0:T(8,128)(2,1)} custom-call(bf16[256,256]{1,0:T(8,128)(2,1)S(1)} %get-tuple-element.27.own, bf16[256,256]{1,0:T(8,128)(2,1)S(1)} %collective-permute-done.3.got), custom_call_target="tpu_custom_call" | custom-call | bytes 524288 | tf_op jit(solution)/shard_map/join/pallas_call | solution.py:22
  48.9 0.7 %join.5 = bf16[128,512]{1,0:T(8,128)(2,1)} custom-call(bf16[128,256]{1,0:T(8,128)(2,1)S(1)} %get-tuple-element.30.own, bf16[128,256]{1,0:T(8,128)(2,1)S(1)} %collective-permute-done.9.got), custom_call_target="tpu_custom_call" | custom-call | bytes 262144 | tf_op jit(solution)/shard_map/join/pallas_call | solution.py:22
  49.6 0.6 %join.6 = bf16[64,512]{1,0:T(8,128)(2,1)} custom-call(bf16[64,256]{1,0:T(8,128)(2,1)S(1)} %get-tuple-element.36.own, bf16[64,256]{1,0:T(8,128)(2,1)S(1)} %collective-permute-done.20.got), custom_call_target="tpu_custom_call" | custom-call | bytes 131072 | tf_op jit(solution)/shard_map/join/pallas_call | solution.py:22
  50.2 0.6 %join.7 = bf16[32,512]{1,0:T(8,128)(2,1)} custom-call(bf16[32,256]{1,0:T(8,128)(2,1)S(1)} %level_three.1.own, bf16[32,256]{1,0:T(8,128)(2,1)S(1)} %collective-permute-done.22.got), custom_call_target="tpu_custom_call" | custom-call | bytes 65536 | tf_op jit(solution)/shard_map/join/pallas_call | solution.py:22
  (62 shorter events, 3.2 us)
Async XLA Ops:
  0.6 2.8 %copy-start.7 = (bf16[4,1,128,512]{3,2,1,0:T(8,128)(2,1)S(1)}, bf16[4,1,128,512]{3,2,1,0:T(8,128)(2,1)}, u32[]{:S(2)}) copy-start(bf16[4,1,128,512]{3,2,1,0:T(8,128)(2,1)} %param.12) | copy-start | bytes 1572868
  3.6 3.2 %copy-start.9 = (bf16[1,128,64]{1,2,0:T(8,128)(2,1)S(1)}, bf16[1,128,64]{1,2,0:T(8,128)(2,1)}, u32[]{:S(2)}) copy-start(bf16[1,128,64]{1,2,0:T(8,128)(2,1)} %param.22) | copy-start | bytes 49156
  3.6 3.3 %copy-start.10 = (s32[6,1,4]{0,2,1:T(4,128)S(1)}, s32[6,1,4]{0,2,1:T(4,128)}, u32[]{:S(2)}) copy-start(s32[6,1,4]{0,2,1:T(4,128)} %param.23) | copy-start | bytes 292
  3.6 3.4 %copy-start.2 = (bf16[3,128,256]{2,1,0:T(8,128)(2,1)S(1)}, bf16[3,128,256]{2,1,0:T(8,128)(2,1)}, u32[]{:S(2)}) copy-start(bf16[3,128,256]{2,1,0:T(8,128)(2,1)} %lower_0.1) | copy-start | bytes 589828
  3.6 3.4 %copy-start.5 = (bf16[2,128,128]{2,1,0:T(8,128)(2,1)S(1)}, bf16[2,128,128]{2,1,0:T(8,128)(2,1)}, u32[]{:S(2)}) copy-start(bf16[2,128,128]{2,1,0:T(8,128)(2,1)} %lower_1.1) | copy-start | bytes 196612
  5.0 9.8 %copy-start.8 = (bf16[64,256]{1,0:T(8,128)(2,1)S(1)}, bf16[64,256]{1,0:T(8,128)(2,1)}, u32[]{:S(2)}) copy-start(bf16[64,256]{1,0:T(8,128)(2,1)} %param.18) | copy-start | bytes 98308
  5.0 15.9 %copy-start.3 = (bf16[256,256]{1,0:T(8,128)(2,1)S(1)}, bf16[256,256]{1,0:T(8,128)(2,1)}, u32[]{:S(2)}) copy-start(bf16[256,256]{1,0:T(8,128)(2,1)} %inverse.4) | copy-start | bytes 393220
  6.2 17.9 %copy-start.4 = (bf16[128,256]{1,0:T(8,128)(2,1)S(1)}, bf16[128,256]{1,0:T(8,128)(2,1)}, u32[]{:S(2)}) copy-start(bf16[128,256]{1,0:T(8,128)(2,1)} %inv_own.1) | copy-start | bytes 196612
  6.2 14.6 %collective-permute-start.2 = (bf16[3,256,256]{2,1,0:T(8,128)(2,1)S(1)}, bf16[3,256,256]{2,1,0:T(8,128)(2,1)S(1)}, u32[]{:S(2)}, u32[]{:S(2)}) collective-permute-start(bf16[3,256,256]{2,1,0:T(8,128)(2,1)S(1)} %get-tuple-element.26), channel_id=1, source_target_pairs={{0,1},{1,0},{2,3},{3,2},{4,5},{5,4},{6,7},{7,6},{8,9},{9,8},{10,11... | collective-permute-start | bytes 1179656 | tf_op jit(solution)/shard_map/ppermute | solution.py:36
  7.7 12.6 %collective-permute-start.1 = (bf16[3,128,256]{2,1,0:T(8,128)(2,1)S(1)}, bf16[3,128,256]{2,1,0:T(8,128)(2,1)S(1)}, u32[]{:S(2)}, u32[]{:S(2)}) collective-permute-start(bf16[3,128,256]{2,1,0:T(8,128)(2,1)S(1)} %get-tuple-element.23.low_own), channel_id=1, source_target_pairs={{0,1},{1,0},{2,3},{3,2},{4,5},{5,4},{6,7},{7,6},{8,9},{9,8},{10,11... | collective-permute-start | bytes 589832 | tf_op jit(solution)/shard_map/ppermute | solution.py:36
  7.8 12.4 %collective-permute-start = (bf16[256,256]{1,0:T(8,128)(2,1)S(1)}, bf16[256,256]{1,0:T(8,128)(2,1)S(1)}, u32[]{:S(2)}, u32[]{:S(2)}) collective-permute-start(bf16[256,256]{1,0:T(8,128)(2,1)S(1)} %get-tuple-element.22), channel_id=1, source_target_pairs={{0,1},{1,0},{2,3},{3,2},{4,5},{5,4},{6,7},{7,6},{8,9},{9,8},{10,11... | collective-permute-start | bytes 393224 | tf_op jit(solution)/shard_map/ppermute | solution.py:36
  8.3 15.9 %collective-permute-start.7 = (bf16[2,128,128]{2,1,0:T(8,128)(2,1)S(1)}, bf16[2,128,128]{2,1,0:T(8,128)(2,1)S(1)}, u32[]{:S(2)}, u32[]{:S(2)}) collective-permute-start(bf16[2,128,128]{2,1,0:T(8,128)(2,1)S(1)} %get-tuple-element.29.low_oo), channel_id=1, source_target_pairs={{0,2},{2,0},{4,6},{6,4},{8,10},{10,8},{12,14},{14,12},{16,18},{18,... | collective-permute-start | bytes 196616 | tf_op jit(solution)/shard_map/ppermute | solution.py:36
  10.8 3.9 %collective-permute-start.15 = (bf16[1,128,64]{2,1,0:T(8,128)(2,1)S(1)}, bf16[1,128,64]{2,1,0:T(8,128)(2,1)S(1)}, u32[]{:S(2)}, u32[]{:S(2)}) collective-permute-start(bf16[1,128,64]{2,1,0:T(8,128)(2,1)S(1)} %get-tuple-element.33), channel_id=1, source_target_pairs={{0,2},{2,0},{4,6},{6,4},{8,10},{10,8},{12,14},{14,12},{16,18},{18,... | collective-permute-start | bytes 49160 | tf_op jit(solution)/shard_map/ppermute | solution.py:36
  14.7 3.9 %collective-permute-start.13 = (bf16[64,256]{1,0:T(8,128)(2,1)S(1)}, bf16[64,256]{1,0:T(8,128)(2,1)S(1)}, u32[]{:S(2)}, u32[]{:S(2)}) collective-permute-start(bf16[64,256]{1,0:T(8,128)(2,1)S(1)} %copy-done.8), channel_id=1, source_target_pairs={{0,2},{2,0},{4,6},{6,4},{8,10},{10,8},{12,14},{14,12},{16,18},{18,... | collective-permute-start | bytes 98312 | tf_op jit(solution)/shard_map/ppermute | solution.py:36
  18.7 4.3 %collective-permute-start.16 = (bf16[2,128,64]{2,1,0:T(8,128)(2,1)S(1)}, bf16[2,128,64]{2,1,0:T(8,128)(2,1)S(1)}, u32[]{:S(2)}, u32[]{:S(2)}) collective-permute-start(bf16[2,128,64]{2,1,0:T(8,128)(2,1)S(1)} %pad_maximum_fusion.2), channel_id=1, source_target_pairs={{0,4},{2,6},{4,0},{6,2},{8,12},{10,14},{12,8},{14,10},{16,20},{18,... | collective-permute-start | bytes 98312 | tf_op jit(solution)/shard_map/ppermute | solution.py:36
  20.2 4.9 %collective-permute-start.6 = (bf16[2,128,128]{2,1,0:T(8,128)(2,1)S(1)}, bf16[2,128,128]{2,1,0:T(8,128)(2,1)S(1)}, u32[]{:S(2)}, u32[]{:S(2)}) collective-permute-start(bf16[2,128,128]{2,1,0:T(8,128)(2,1)S(1)} %get-tuple-element.29.low_oo), channel_id=1, source_target_pairs={{0,1},{1,0},{2,3},{3,2},{4,5},{5,4},{6,7},{7,6},{8,9},{9,8},{10,11... | collective-permute-start | bytes 196616 | tf_op jit(solution)/shard_map/ppermute | solution.py:36
  20.3 4.8 %collective-permute-start.14 = (bf16[2,64,256]{2,1,0:T(8,128)(2,1)S(1)}, bf16[2,64,256]{2,1,0:T(8,128)(2,1)S(1)}, u32[]{:S(2)}, u32[]{:S(2)}) collective-permute-start(bf16[2,64,256]{2,1,0:T(8,128)(2,1)S(1)} %pad_maximum_fusion.1), channel_id=1, source_target_pairs={{0,4},{2,6},{4,0},{6,2},{8,12},{10,14},{12,8},{14,10},{16,20},{18,... | collective-permute-start | bytes 196616 | tf_op jit(solution)/shard_map/ppermute | solution.py:36
  21.4 26.6 %copy-start.6 = (bf16[32,256]{1,0:T(8,128)(2,1)S(1)}, bf16[32,256]{1,0:T(8,128)(2,1)}, u32[]{:S(2)}) copy-start(bf16[32,256]{1,0:T(8,128)(2,1)} %inverse.5) | copy-start | bytes 49156
  21.4 11.4 %collective-permute-start.4 = (bf16[256,256]{1,0:T(8,128)(2,1)S(1)}, bf16[256,256]{1,0:T(8,128)(2,1)S(1)}, u32[]{:S(2)}, u32[]{:S(2)}) collective-permute-start(bf16[256,256]{1,0:T(8,128)(2,1)S(1)} %get-tuple-element.28.own), channel_id=1, source_target_pairs={{0,2},{2,0},{4,6},{6,4},{8,10},{10,8},{12,14},{14,12},{16,18},{18,... | collective-permute-start | bytes 393224 | tf_op jit(solution)/shard_map/ppermute | solution.py:36
  22.9 10.3 %collective-permute-start.18 = (bf16[256,256]{1,0:T(8,128)(2,1)S(1)}, bf16[256,256]{1,0:T(8,128)(2,1)S(1)}, u32[]{:S(2)}, u32[]{:S(2)}) collective-permute-start(bf16[256,256]{1,0:T(8,128)(2,1)S(1)} %get-tuple-element.34), channel_id=1, source_target_pairs={{0,2},{2,0},{4,6},{6,4},{8,10},{10,8},{12,14},{14,12},{16,18},{18,... | collective-permute-start | bytes 393224 | tf_op jit(solution)/shard_map/ppermute | solution.py:36
  24.2 7.0 %collective-permute-start.5 = (bf16[128,256]{1,0:T(8,128)(2,1)S(1)}, bf16[128,256]{1,0:T(8,128)(2,1)S(1)}, u32[]{:S(2)}, u32[]{:S(2)}) collective-permute-start(bf16[128,256]{1,0:T(8,128)(2,1)S(1)} %copy-done.4), channel_id=1, source_target_pairs={{0,2},{2,0},{4,6},{6,4},{8,10},{10,8},{12,14},{14,12},{16,18},{18,... | collective-permute-start | bytes 196616 | tf_op jit(solution)/shard_map/ppermute | solution.py:36
  25.0 7.7 %collective-permute-start.8 = (bf16[2,128,128]{2,1,0:T(8,128)(2,1)S(1)}, bf16[2,128,128]{2,1,0:T(8,128)(2,1)S(1)}, u32[]{:S(2)}, u32[]{:S(2)}) collective-permute-start(bf16[2,128,128]{2,1,0:T(8,128)(2,1)S(1)} %collective-permute-done.7.low_xo), channel_id=1, source_target_pairs={{0,1},{1,0},{2,3},{3,2},{4,5},{5,4},{6,7},{7,6},{8,9},{9,8},{10,11... | collective-permute-start | bytes 196616 | tf_op jit(solution)/shard_map/ppermute | solution.py:36
  25.1 15.2 %collective-permute-start.17 = (bf16[4,128,64]{2,1,0:T(8,128)(2,1)S(1)}, bf16[4,128,64]{2,1,0:T(8,128)(2,1)S(1)}, u32[]{:S(2)}, u32[]{:S(2)}) collective-permute-start(bf16[4,128,64]{2,1,0:T(8,128)(2,1)S(1)} %constant_dynamic-update-slice_fusion.low_own), channel_id=1, source_target_pairs={{0,1},{1,0},{2,3},{3,2},{4,5},{5,4},{6,7},{7,6},{8,9},{9,8},{10,11... | collective-permute-start | bytes 196616 | tf_op jit(solution)/shard_map/ppermute | solution.py:36
  31.2 6.2 %collective-permute-start.10 = (bf16[256,256]{1,0:T(8,128)(2,1)S(1)}, bf16[256,256]{1,0:T(8,128)(2,1)S(1)}, u32[]{:S(2)}, u32[]{:S(2)}) collective-permute-start(bf16[256,256]{1,0:T(8,128)(2,1)S(1)} %get-tuple-element.31), channel_id=1, source_target_pairs={{0,4},{2,6},{4,0},{6,2},{8,12},{10,14},{12,8},{14,10},{16,20},{18,... | collective-permute-start | bytes 393224 | tf_op jit(solution)/shard_map/ppermute | solution.py:36
  33.3 6.9 %collective-permute-start.19 = (bf16[256,256]{1,0:T(8,128)(2,1)S(1)}, bf16[256,256]{1,0:T(8,128)(2,1)S(1)}, u32[]{:S(2)}, u32[]{:S(2)}) collective-permute-start(bf16[256,256]{1,0:T(8,128)(2,1)S(1)} %subtract_convert_fusion), channel_id=1, source_target_pairs={{0,4},{2,6},{4,0},{6,2},{8,12},{10,14},{12,8},{14,10},{16,20},{18,... | collective-permute-start | bytes 393224 | tf_op jit(solution)/shard_map/ppermute | solution.py:36
  33.8 8.0 %collective-permute-start.12 = (bf16[256,256]{1,0:T(8,128)(2,1)S(1)}, bf16[256,256]{1,0:T(8,128)(2,1)S(1)}, u32[]{:S(2)}, u32[]{:S(2)}) collective-permute-start(bf16[256,256]{1,0:T(8,128)(2,1)S(1)} %get-tuple-element.32.u_own), channel_id=1, source_target_pairs={{0,4},{2,6},{4,0},{6,2},{8,12},{10,14},{12,8},{14,10},{16,20},{18,... | collective-permute-start | bytes 393224 | tf_op jit(solution)/shard_map/ppermute | solution.py:36
  37.4 5.0 %collective-permute-start.11 = (bf16[256,256]{1,0:T(8,128)(2,1)S(1)}, bf16[256,256]{1,0:T(8,128)(2,1)S(1)}, u32[]{:S(2)}, u32[]{:S(2)}) collective-permute-start(bf16[256,256]{1,0:T(8,128)(2,1)S(1)} %add_convert_fusion.base), channel_id=1, source_target_pairs={{0,2},{2,0},{4,6},{6,4},{8,10},{10,8},{12,14},{14,12},{16,18},{18,... | collective-permute-start | bytes 393224 | tf_op jit(solution)/shard_map/ppermute | solution.py:36
  42.9 5.0 %collective-permute-start.21 = (bf16[256,256]{1,0:T(8,128)(2,1)S(1)}, bf16[256,256]{1,0:T(8,128)(2,1)S(1)}, u32[]{:S(2)}, u32[]{:S(2)}) collective-permute-start(bf16[256,256]{1,0:T(8,128)(2,1)S(1)} %get-tuple-element.37.own), channel_id=1, source_target_pairs={{0,8},{2,10},{4,12},{6,14},{8,0},{10,2},{12,4},{14,6},{16,24},{18,... | collective-permute-start | bytes 393224 | tf_op jit(solution)/shard_map/ppermute | solution.py:36
  44.6 3.5 %collective-permute-start.3 = (bf16[256,256]{1,0:T(8,128)(2,1)S(1)}, bf16[256,256]{1,0:T(8,128)(2,1)S(1)}, u32[]{:S(2)}, u32[]{:S(2)}) collective-permute-start(bf16[256,256]{1,0:T(8,128)(2,1)S(1)} %get-tuple-element.27.own), channel_id=1, source_target_pairs={{0,1},{1,0},{2,3},{3,2},{4,5},{5,4},{6,7},{7,6},{8,9},{9,8},{10,11... | collective-permute-start | bytes 393224 | tf_op jit(solution)/shard_map/ppermute | solution.py:36
  44.6 4.3 %collective-permute-start.9 = (bf16[128,256]{1,0:T(8,128)(2,1)S(1)}, bf16[128,256]{1,0:T(8,128)(2,1)S(1)}, u32[]{:S(2)}, u32[]{:S(2)}) collective-permute-start(bf16[128,256]{1,0:T(8,128)(2,1)S(1)} %get-tuple-element.30.own), channel_id=1, source_target_pairs={{0,1},{1,0},{2,3},{3,2},{4,5},{5,4},{6,7},{7,6},{8,9},{9,8},{10,11... | collective-permute-start | bytes 196616 | tf_op jit(solution)/shard_map/ppermute | solution.py:36
  45.1 4.5 %collective-permute-start.20 = (bf16[64,256]{1,0:T(8,128)(2,1)S(1)}, bf16[64,256]{1,0:T(8,128)(2,1)S(1)}, u32[]{:S(2)}, u32[]{:S(2)}) collective-permute-start(bf16[64,256]{1,0:T(8,128)(2,1)S(1)} %get-tuple-element.36.own), channel_id=1, source_target_pairs={{0,1},{1,0},{2,3},{3,2},{4,5},{5,4},{6,7},{7,6},{8,9},{9,8},{10,11... | collective-permute-start | bytes 98312 | tf_op jit(solution)/shard_map/ppermute | solution.py:36
  48.1 2.1 %collective-permute-start.22 = (bf16[32,256]{1,0:T(8,128)(2,1)S(1)}, bf16[32,256]{1,0:T(8,128)(2,1)S(1)}, u32[]{:S(2)}, u32[]{:S(2)}) collective-permute-start(bf16[32,256]{1,0:T(8,128)(2,1)S(1)} %level_three.1.own), channel_id=1, source_target_pairs={{0,1},{1,0},{2,3},{3,2},{4,5},{5,4},{6,7},{7,6},{8,9},{9,8},{10,11... | collective-permute-start | bytes 49160 | tf_op jit(solution)/shard_map/ppermute | solution.py:36
  (2 other events, 3.6 us)

commit v2 on v0

v2 whole, which is shorter than its diff:
```python
import jax
import jax.numpy as jnp
from jax import lax
from jax.experimental import pallas as pl
from jax.experimental.pallas import tpu as pltpu
from jax.sharding import PartitionSpec as P

F32, BF16 = jnp.float32, jnp.bfloat16
WHOLE = pl.BlockSpec(memory_space=pltpu.VMEM)
SCALARS = pl.BlockSpec(memory_space=pltpu.SMEM)


def dot(a, b):
    return jnp.dot(a, b, preferred_element_type=F32)


def dot_t(a, b):
    return lax.dot_general(a, b, (((0,), (0,)), ((), ())), preferred_element_type=F32)


def call(kernel, outs, *args, scratch=(), flops=0, specs=None):
    outs = [jax.ShapeDtypeStruct(shape, dtype) for shape, dtype in outs]
    moved = sum(a.size * a.dtype.itemsize for a in (*args, *outs))
    single = len(outs) == 1
    return pl.pallas_call(
        kernel,
        out_shape=outs[0] if single else outs,
        in_specs=specs or [WHOLE] * len(args),
        out_specs=WHOLE if single else [WHOLE] * len(outs),
        scratch_shapes=list(scratch),
        cost_estimate=pl.CostEstimate(flops=flops, bytes_accessed=moved, transcendentals=0),
        compiler_params=pltpu.CompilerParams(vmem_limit_bytes=16 << 20),
    )(*args)


def swap(block, axis, stride):
    count = lax.axis_size(axis)
    return lax.ppermute(block, axis, [(low, low ^ stride) for low in range(count)])


def own_and_other(part):
    me = lax.axis_index("row")
    return (
        pl.ds(pl.multiple_of(me * part, part), part),
        pl.ds(pl.multiple_of((1 - me) * part, part), part),
    )


def prepare(lower_0, lower_1, lower_2t, pattern, inv_1, inv_2, across, along):
    rows = lower_0.shape[1]
    blocks = pattern.shape[1]
    spread = rows // blocks
    size = lower_0.shape[2]
    n0, n1 = lower_0.shape[0], lower_1.shape[0]
    part_1, part_2 = lower_1.shape[2], lower_2t.shape[1]
    for b in range(blocks):
        at = pl.ds(b * spread, spread)
        for m in range(n0):
            factor = pattern[0, b, m].astype(BF16)
            across[at, pl.ds(m * size, size)] = lower_0[m, at, :] * factor
        for m in range(n1):
            factor = pattern[0, b, n0 + m].astype(BF16)
            masked = lower_1[m, at, :] * factor
            across[at, pl.ds(n0 * size + m * part_1, part_1)] = masked
            along[at, pl.ds(size + m * part_1, part_1)] = masked
    lane = lax.broadcasted_iota(jnp.int32, (1, rows), 1) // spread
    keep = jnp.zeros((1, rows), F32)
    for b in range(blocks):
        keep = jnp.where(lane == b, pattern[0, b, n0 + n1].astype(F32), keep)
    masked = (lower_2t[0].astype(F32) * keep).astype(BF16)
    start = n0 * size + n1 * part_1
    across[pl.ds(0, part_2), pl.ds(start, rows)] = masked
    across[pl.ds(part_2, rows - part_2), pl.ds(start, rows)] = jnp.zeros((rows - part_2, rows), BF16)
    along[pl.ds(0, part_1), pl.ds(0, size)] = inv_1[...]
    along[pl.ds(part_1, part_2), pl.ds(0, size)] = inv_2[...]
    along[pl.ds(part_1, part_2), pl.ds(size, rows)] = masked
    wide = along.shape[1] - size - rows
    along[pl.ds(part_1, part_2), pl.ds(size + rows, wide)] = jnp.zeros((part_2, wide), BF16)


def leaf_sums(solved, lower, rhs, keep, send, total, ready=None):
    leaves = lower.shape[1]
    mine, _ = own_and_other(rhs.shape[2])
    own, other = own_and_other(keep.shape[2])
    for m in range(keep.shape[0]):
        if ready:
            ready(m)
        acc = dot(lower[m, 0], solved[0])
        for v in range(1, leaves):
            acc = acc + dot(lower[m, v], solved[v])
        total[...] = -acc
        total[mine, :] = total[mine, :] + rhs[m, 0].astype(F32)
        keep[m] = total[:, own]
        send[m] = total[:, other].astype(BF16)


def opening(
    inverse, right, lower, rhs, lower_0, lower_1, lower_2t, pattern, inv_1, inv_2,
    solved, keep, send, across, along, lower_late, rhs_late,
    total, inverse_v, right_v, lower_v, rhs_v, low0_v, low1_v, low2_v, inv1_v, inv2_v, pattern_s, sems,
):
    leaves = inverse.shape[0]
    early = keep.shape[0]
    late = lower_late.shape[0]
    copies = []

    def fetch(source, target):
        copy = pltpu.make_async_copy(source, target, sems.at[len(copies)])
        copy.start()
        copies.append(copy)
        return copy

    leaf = []
    for v in range(leaves):
        leaf.append((fetch(inverse.at[v], inverse_v.at[v]), fetch(right.at[v], right_v.at[v])))
    sums = [fetch(lower.at[m], lower_v.at[m]) for m in range(early)]
    tops = fetch(rhs.at[pl.ds(0, early)], rhs_v)
    small = [
        fetch(source, target)
        for source, target in (
            (lower_0, low0_v), (lower_1, low1_v), (lower_2t, low2_v), (pattern, pattern_s),
            (inv_1, inv1_v), (inv_2, inv2_v),
        )
    ]
    last = [
        fetch(lower.at[pl.ds(early, late)], lower_late),
        fetch(rhs.at[pl.ds(early, late)], rhs_late),
    ]
    for v in range(leaves):
        for copy in leaf[v]:
            copy.wait()
        solved[v] = dot(inverse_v[v], right_v[v]).astype(BF16)
    tops.wait()
    leaf_sums(solved, lower_v, rhs_v, keep, send, total, lambda m: sums[m].wait())
    for copy in small:
        copy.wait()
    prepare(low0_v, low1_v, low2_v, pattern_s, inv1_v, inv2_v, across, along)
    for copy in last:
        copy.wait()


def leaf_b(solved, lower, rhs, keep, send, total):
    leaf_sums(solved, lower, rhs, keep, send, total)


def zero_a(keep, got, inverse, across, across_o, solved_out, p1):
    size = inverse.shape[1]
    residual = (keep[0] + got[0].astype(F32)).astype(BF16)
    solved = dot(inverse[...], residual).astype(BF16)
    solved_out[...] = solved
    for low, at in zip((across, across_o), own_and_other(across.shape[0])):
        total = keep[1, at, :] + got[1, at, :].astype(F32)
        p1[at, :] = (total - dot(low[:, pl.ds(0, size)], solved)).astype(BF16)


def zero_b(keep, got, solved, across, across_o, p2, p3):
    size = solved.shape[0]
    for low, at in zip((across, across_o), own_and_other(across.shape[0])):
        for m, out in enumerate((p2, p3)):
            total = keep[m, at, :] + got[m, at, :].astype(F32)
            low_m = low[:, pl.ds((m + 1) * size, size)]
            out[at, :] = (total - dot(low_m, solved[...])).astype(BF16)


def one(p1, p1_x, along, along_x, across_o, along_xo, solved_out, u2, u3):
    size = p1.shape[0]
    part = solved_out.shape[0]
    first = across_o.shape[1] - along_x.shape[1] + size - part
    residual = (p1[...].astype(F32) + p1_x[...].astype(F32)).astype(BF16)
    solved = dot(along[pl.ds(0, part), pl.ds(0, size)], residual).astype(BF16)
    solved_x = dot(along_x[pl.ds(0, part), pl.ds(0, size)], residual).astype(BF16)
    solved_out[...] = solved
    first = 3 * size
    mine, theirs = own_and_other(across_o.shape[0])
    for m, out in enumerate((u2, u3)):
        at = pl.ds(size + m * part, part)
        out[mine, :] = (
            dot(along[pl.ds(0, part), at], solved) + dot(along_x[pl.ds(0, part), at], solved_x)
        ).astype(BF16)
        out[theirs, :] = (
            dot(across_o[:, pl.ds(first + m * part, part)], solved)
            + dot(along_xo[pl.ds(0, part), at], solved_x)
        ).astype(BF16)


def two(s2, s2_x, u2, u2_y, along, along_x, side, across_o, along_xo, side_o, s3, s3_y, solved_out, v3):
    size = s2.shape[0]
    part = solved_out.shape[0]
    rows = across_o.shape[0]
    top = along.shape[0] - part
    residual = (
        s2[...].astype(F32) + s2_x[...].astype(F32) - (u2[...].astype(F32) + u2_y[...].astype(F32))
    ).astype(BF16)
    pieces = [(along, top), (along_x, top), (side, 0), (side, part)]
    others = [(across_o, 0, across_o.shape[1] - rows)] + [
        (ref, at, size) for ref, at in ((along_xo, top), (side_o, 0), (side_o, part))
    ]
    mine, theirs = own_and_other(rows)
    total = [s3[at, :].astype(F32) + s3_y[at, :].astype(F32) for at in (mine, theirs)]
    for i, ((ref, at), (ref_o, at_o, lane_o)) in enumerate(zip(pieces, others)):
        solved = dot(ref[pl.ds(at, part), pl.ds(0, size)], residual).astype(BF16)
        if i == 0:
            solved_out[...] = solved
        total[0] = total[0] - dot_t(ref[pl.ds(at, part), pl.ds(size, rows)], solved)
        total[1] = total[1] - dot_t(ref_o[pl.ds(at_o, part), pl.ds(lane_o, rows)], solved)
    v3[mine, :] = total[0].astype(BF16)
    v3[theirs, :] = total[1].astype(BF16)


def three(v3, v3_z, inverse, solved_out):
    residual = (v3[...].astype(F32) + v3_z[...].astype(F32)).astype(BF16)
    solved_out[...] = dot(inverse[...], residual).astype(BF16)


def add_2(a, b, out):
    out[...] = (a[...].astype(F32) + b[...].astype(F32)).astype(BF16)


def add_3(a, b, c, out):
    out[...] = (a[...].astype(F32) + b[...].astype(F32) - c[...].astype(F32)).astype(BF16)


def join(own, got, out):
    mine, theirs = own_and_other(own.shape[1])
    out[:, mine] = own[...]
    out[:, theirs] = got[...]


def body(
    rhs, leaf_rhs, leaf_inverse, leaf_lower,
    inverse_0, inverse_1, inverse_2, inverse_3,
    lower_0, lower_1, lower_2, sparsity,
):
    levels, _, rows, width = rhs.shape
    leaves, size, _ = leaf_inverse.shape
    half = width // lax.axis_size("row")
    n0, n1 = lower_0.shape[0], lower_1.shape[0]
    part_1, part_2 = inverse_1.shape[0], inverse_2.shape[0]
    block = ((size, half), BF16)
    full = [pltpu.VMEM((size, width), F32)]

    early = 2
    late = levels - early
    lower_2t, pattern = jnp.swapaxes(lower_2, 1, 2), jnp.transpose(sparsity, (1, 2, 0))
    sources = (leaf_inverse, leaf_rhs, leaf_lower, rhs, lower_0, lower_1, lower_2t, pattern, inverse_1, inverse_2)
    solved_leaf, keep_a, send_a, across, along, lower_late, rhs_late = call(
        opening,
        [
            ((leaves, size, width), BF16),
            ((early, size, half), F32),
            ((early, size, half), BF16),
            ((rows, n0 * size + n1 * part_1 + rows), BF16),
            ((part_1 + part_2, size + n1 * part_1), BF16),
            ((late, leaves, size, size), BF16),
            ((late, 1, rows, width), BF16),
        ],
        *(pltpu.with_memory_space_constraint(x, pltpu.HBM) for x in sources),
        specs=[pl.BlockSpec(memory_space=pltpu.HBM)] * len(sources),
        scratch=[pltpu.VMEM((size, width), F32)]
        + [pltpu.VMEM(x.shape, BF16) for x in (leaf_inverse, leaf_rhs)]
        + [pltpu.VMEM((early, *x.shape[1:]), BF16) for x in (leaf_lower, rhs)]
        + [pltpu.VMEM(x.shape, BF16) for x in (lower_0, lower_1, lower_2t, inverse_1, inverse_2)]
        + [pltpu.SMEM(pattern.shape, jnp.int32), pltpu.SemaphoreType.DMA((2 * leaves + early + 9,))],
        flops=6 * leaves * size * size * width,
    )
    got_a = swap(send_a, "row", 1)
    across_o = swap(across, "row", 1)
    along_x = swap(along, "col", 1)
    keep_b, send_b = call(
        leaf_b,
        [((late, size, half), F32), ((late, size, half), BF16)],
        solved_leaf, lower_late, rhs_late,
        scratch=full, flops=2 * late * leaves * size * size * width,
    )
    got_b = swap(send_b, "row", 1)
    sol0, p1 = call(
        zero_a, [block] * 2, keep_a, got_a, inverse_0, across, across_o,
        flops=4 * size * size * half,
    )
    p1_x = swap(p1, "col", 1)
    p2, p3 = call(
        zero_b, [block] * 2, keep_b, got_b, sol0, across, across_o,
        flops=4 * size * size * half,
    )
    p2_y = swap(p2, "col", 2)
    p3_x = swap(p3, "col", 1)
    along_xo = swap(along_x, "row", 1)
    side = swap(
        jnp.concatenate([along[part_1:, : size + rows], along_x[part_1:, : size + rows]]),
        "col", 2,
    )
    sol1, u2, u3 = call(
        one, [((part_1, half), BF16), block, block],
        p1, p1_x, along, along_x, across_o, along_xo,
        flops=6 * size * size * half,
    )
    u2_y = swap(u2, "col", 2)
    s2 = call(add_2, [block], p2, p2_y)
    s2_x = swap(s2, "col", 1)
    s3 = call(add_3, [block], p3, p3_x, u3)
    s3_y = swap(s3, "col", 2)
    side_o = swap(side, "row", 1)
    sol2, v3 = call(
        two, [((part_2, half), BF16), block],
        s2, s2_x, u2, u2_y, along, along_x, side, across_o, along_xo, side_o, s3, s3_y,
        flops=4 * size * size * half,
    )
    v3_z = swap(v3, "col", 4)
    sol3 = call(
        three, [((inverse_3.shape[0], half), BF16)], v3, v3_z, inverse_3,
        flops=2 * inverse_3.size * half,
    )
    outs = []
    for solved in (sol0, sol1, sol2, sol3):
        got = swap(solved, "row", 1)
        outs.append(call(join, [((solved.shape[0], width), BF16)], solved, got))
    return tuple(outs)


def solution(mesh):
    return jax.shard_map(
        body,
        mesh=mesh,
        in_specs=(
            P(None, "col", "row", None),
            P(("col", "row"), None, None),
            P(("col", "row"), None, None),
            P(None, ("col", "row"), None, None),
            P("col", None),
            P("col", None),
            P("col", None),
            P("col", None),
            P(None, "row", "col"),
            P(None, "row", "col"),
            P(None, "row", "col"),
            P(None, "col", "row"),
        ),
        out_specs=(P("col", None), P("col", None), P("col", None), P("col", None)),
        check_vma=False,
    )
```

time: 77.3 us -> 41.3 us (0.53)
  between operations: 14.3 us -> 0.77 us
  waiting for transfers between devices: 28.6 us -> 17.4 us
  Pallas kernels: 0 us -> 8.96 us
  blocking collectives: 8.23 us -> 0 us
  local copies, waits for them, and re-layouts: 7.97 us -> 0.03 us
  matrix products: 6.28 us -> 0 us
  starting transfers between devices: 10.9 us -> 13.9 us
    unnamed x2 -> x0, waiting for transfers between devices: 9.68 us -> none
    pallas_call x0 -> x13, Pallas kernels: none -> 8.96 us  [call(): pl.pallas_call(kernel, out_shape=outs[0] if single else outs, in_specs=sp...]
    all_gather x4 -> x0, blocking collectives: 8.23 us -> none  [body(): lax.all_gather(residual_half, 'row', axis=0, tiled=True)]
    unnamed x25 -> x4, local copies, waits for them, and re-layouts: 7.26 us -> 0.01 us
    dot_general x8 -> x0, matrix products: 6.28 us -> none  [the longest x1 2.96 us: body(): jnp.einsum('mvrs,vsk->rmk', leaf_lower, leaf_solution, preferred_element_...]
    ppermute x6 -> x18, starting transfers between devices: 10.9 us -> 13.9 us  [swap(): lax.ppermute(block, axis, [(low, low ^ stride) for low in range(count)])]
    ppermute x6 -> x18, waiting for transfers between devices: 18.9 us -> 17.4 us  [swap(): lax.ppermute(block, axis, [(low, low ^ stride) for low in range(count)])]
  transfers between devices with their start and end apart: 7 -> 18, of which waited for: 7 -> 7; matrix products, arithmetic and copies ran while one was open for 5% -> 0% of each run, Pallas kernels for 0% -> 10%
where the time goes in v2:
time: 41.3 us; the launch traced here: 41.1 us
  waiting for transfers between devices  17.4 us (42%)
  starting transfers between devices  13.9 us (34%)
  Pallas kernels  8.96 us (22%)
  between operations  0.77 us (2%)
    ppermute x18, waiting for transfers between devices, swap(): lax.ppermute(block, axis, [(low, low ^ stride) for low in range(count)])  17.4 us
    ppermute x18, starting transfers between devices, swap(): lax.ppermute(block, axis, [(low, low ^ stride) for low in range(count)])  13.9 us
    pallas_call x13, Pallas kernels, call(): pl.pallas_call(kernel, out_shape=outs[0] if single else outs, in_specs=sp...  8.96 us
  transfers between devices with their start and end apart: 18, of which 7 were waited for; matrix products, arithmetic and copies ran while one was open for 0% of the time, Pallas kernels for 10%

profile of v2, /device:TPU:0, one launch (start us, length us, event | category | flops | bytes accessed | tf_op | source)
XLA Modules:
  0.0 41.1 jit_solution(15163297871157802327)
XLA Ops:
  0.6 3.3 %shard_map.147 = (bf16[4,256,512]{2,1,0:T(8,128)(2,1)S(1)}, f32[2,256,256]{2,1,0:T(8,128)S(1)}, bf16[2,256,256]{2,1,0:T(8,128)(2,1)S(1)}, bf16[128,1152]{1,0:T(8...) custom-call(bf16[4,256,256]{2,1,0:T(8,128)(2,1)} %inverse.3, ...), custom_call_target="tpu_custom_call" | custom-call | flops 805306368 | bytes 8208480 | tf_op jit(solution)/shard_map/pallas_call | solution.py:25
  3.9 0.5 %collective-permute-start.1 = (bf16[128,1152]{1,0:T(8,128)(2,1)S(1)}, bf16[128,1152]{1,0:T(8,128)(2,1)S(1)}, u32[]{:S(2)}, u32[]{:S(2)}) collective-permute-start(bf16[128,1152]{1,0:T(8,128)(2,1)S(1)} %get-tuple-element.24.across), channel_id=1, source_target_pairs={{0,1},{1,0},{2,3},{3,2},{4,5},{5,4},{6,7},{7,6},{8,9},{9,8},{10,11... | collective-permute-start | bytes 884744 | tf_op jit(solution)/shard_map/ppermute | solution.py:38
  4.5 0.1 collective-permute-start
  4.5 0.9 %shard_map.152 = (f32[2,256,256]{2,1,0:T(8,128)S(1)}, bf16[2,256,256]{2,1,0:T(8,128)(2,1)S(1)}) custom-call(bf16[4,256,512]{2,1,0:T(8,128)(2,1)S(1)} %get-tuple-element.29.solved, bf16[2,4,256,256]{3,2,1,0:T(8,128)(2,1)S(1)} %get-tuple-element.30.lower, bf16[2,1,128,512]{3,2,1,0:T(8,128)(2,1)S(1)} %get-tuple-element.31.rhs), custom_call_target="tpu_custom_call" | custom-call | flops 536870912 | bytes 3145728 | tf_op jit(solution)/shard_map/pallas_call | solution.py:25
  5.4 0.5 %collective-permute-start.7 = (bf16[2,256,256]{2,1,0:T(8,128)(2,1)S(1)}, bf16[2,256,256]{2,1,0:T(8,128)(2,1)S(1)}, u32[]{:S(2)}, u32[]{:S(2)}) collective-permute-start(bf16[2,256,256]{2,1,0:T(8,128)(2,1)S(1)} %get-tuple-element.33), channel_id=1, source_target_pairs={{0,1},{1,0},{2,3},{3,2},{4,5},{5,4},{6,7},{7,6},{8,9},{9,8},{10,11... | collective-permute-start | bytes 786440 | tf_op jit(solution)/shard_map/ppermute | solution.py:38
  5.9 2.6 %collective-permute-start.4 = (bf16[192,512]{1,0:T(8,128)(2,1)S(1)}, bf16[192,512]{1,0:T(8,128)(2,1)S(1)}, u32[]{:S(2)}, u32[]{:S(2)}) collective-permute-start(bf16[192,512]{1,0:T(8,128)(2,1)S(1)} %get-tuple-element.27.along), channel_id=1, source_target_pairs={{0,2},{2,0},{4,6},{6,4},{8,10},{10,8},{12,14},{14,12},{16,18},{18,... | collective-permute-start | bytes 589832 | tf_op jit(solution)/shard_map/ppermute | solution.py:38
  8.5 5.5 %collective-permute-done.4.along_x = bf16[192,512]{1,0:T(8,128)(2,1)S(1)} collective-permute-done((bf16[192,512]{1,0:T(8,128)(2,1)S(1)}, bf16[192,512]{1,0:T(8,128)(2,1)S(1)}, u32[]{:S(2)}, u32[]{:S(2)}) %collective-permute-start.4) | collective-permute-done | bytes 196640 | tf_op jit(solution)/shard_map/ppermute | solution.py:38
  14.0 0.4 shard_map.148
  14.5 0.2 shard_map.153
  14.7 1.8 %collective-permute-start.13 = (bf16[256,256]{1,0:T(8,128)(2,1)S(1)}, bf16[256,256]{1,0:T(8,128)(2,1)S(1)}, u32[]{:S(2)}, u32[]{:S(2)}) collective-permute-start(bf16[256,256]{1,0:T(8,128)(2,1)S(1)} %get-tuple-element.36.a), channel_id=1, source_target_pairs={{0,2},{2,0},{4,6},{6,4},{8,10},{10,8},{12,14},{14,12},{16,18},{18,... | collective-permute-start | bytes 393224 | tf_op jit(solution)/shard_map/ppermute | solution.py:38
  16.5 0.3 collective-permute-start.3
  16.8 1.8 %collective-permute-start.8 = (bf16[256,256]{1,0:T(8,128)(2,1)S(1)}, bf16[256,256]{1,0:T(8,128)(2,1)S(1)}, u32[]{:S(2)}, u32[]{:S(2)}) collective-permute-start(bf16[256,256]{1,0:T(8,128)(2,1)S(1)} %get-tuple-element.34.a), channel_id=1, source_target_pairs={{0,4},{2,6},{4,0},{6,2},{8,12},{10,14},{12,8},{14,10},{16,20},{18,... | collective-permute-start | bytes 393224 | tf_op jit(solution)/shard_map/ppermute | solution.py:38
  18.6 0.3 collective-permute-start.11
  18.9 4.6 %collective-permute-done.3.p1_x = bf16[256,256]{1,0:T(8,128)(2,1)S(1)} collective-permute-done((bf16[256,256]{1,0:T(8,128)(2,1)S(1)}, bf16[256,256]{1,0:T(8,128)(2,1)S(1)}, u32[]{:S(2)}, u32[]{:S(2)}) %collective-permute-start.3) | collective-permute-done | bytes 131104 | tf_op jit(solution)/shard_map/ppermute | solution.py:38
  23.5 0.5 %shard_map.150 = (bf16[128,256]{1,0:T(8,128)(2,1)S(1)}, bf16[256,256]{1,0:T(8,128)(2,1)S(1)}, bf16[256,256]{1,0:T(8,128)(2,1)S(1)}) custom-call(bf16[256,256]{1,0:T(8,128)(2,1)S(1)} %get-tuple-element.26.p1, bf16[256,256]{1,0:T(8,128)(2,1)S(1)} %collective-permute-done.3.p1_x, bf16[192,512]{1,0:T(8,128)(2,1)S(1)} %get-tuple-element.27.along, ...), custom_call_target="tpu_custom_call" | custom-call | flops 100663296 | bytes 1474560 | tf_op jit(solution)/shard_map/pallas_call | solution.py:25
  24.0 0.1 shard_map.155.s3
  24.0 1.8 %collective-permute-start.14 = (bf16[256,256]{1,0:T(8,128)(2,1)S(1)}, bf16[256,256]{1,0:T(8,128)(2,1)S(1)}, u32[]{:S(2)}, u32[]{:S(2)}) collective-permute-start(bf16[256,256]{1,0:T(8,128)(2,1)S(1)} %shard_map.155.s3), channel_id=1, source_target_pairs={{0,4},{2,6},{4,0},{6,2},{8,12},{10,14},{12,8},{14,10},{16,20},{18,... | collective-permute-start | bytes 393224 | tf_op jit(solution)/shard_map/ppermute | solution.py:38
  25.9 1.5 %collective-permute-start.9 = (bf16[256,256]{1,0:T(8,128)(2,1)S(1)}, bf16[256,256]{1,0:T(8,128)(2,1)S(1)}, u32[]{:S(2)}, u32[]{:S(2)}) collective-permute-start(bf16[256,256]{1,0:T(8,128)(2,1)S(1)} %shard_map.154.s2), channel_id=1, source_target_pairs={{0,2},{2,0},{4,6},{6,4},{8,10},{10,8},{12,14},{14,12},{16,18},{18,... | collective-permute-start | bytes 393224 | tf_op jit(solution)/shard_map/ppermute | solution.py:38
  27.5 0.5 %collective-permute-start.10 = (bf16[256,256]{1,0:T(8,128)(2,1)S(1)}, bf16[256,256]{1,0:T(8,128)(2,1)S(1)}, u32[]{:S(2)}, u32[]{:S(2)}) collective-permute-start(bf16[256,256]{1,0:T(8,128)(2,1)S(1)} %get-tuple-element.35.u2), channel_id=1, source_target_pairs={{0,4},{2,6},{4,0},{6,2},{8,12},{10,14},{12,8},{14,10},{16,20},{18,... | collective-permute-start | bytes 393224 | tf_op jit(solution)/shard_map/ppermute | solution.py:38
  28.0 1.3 %collective-permute-done.12.side_o = bf16[128,384]{1,0:T(8,128)(2,1)S(1)} collective-permute-done((bf16[128,384]{1,0:T(8,128)(2,1)S(1)}, bf16[128,384]{1,0:T(8,128)(2,1)S(1)}, u32[]{:S(2)}, u32[]{:S(2)}) %collective-permute-start.12) | collective-permute-done | bytes 98336 | tf_op jit(solution)/shard_map/ppermute | solution.py:38
  29.3 0.4 %collective-permute-done.14.s3_y = bf16[256,256]{1,0:T(8,128)(2,1)S(1)} collective-permute-done((bf16[256,256]{1,0:T(8,128)(2,1)S(1)}, bf16[256,256]{1,0:T(8,128)(2,1)S(1)}, u32[]{:S(2)}, u32[]{:S(2)}) %collective-permute-start.14) | collective-permute-done | bytes 131104 | tf_op jit(solution)/shard_map/ppermute | solution.py:38
  29.7 1.2 %collective-permute-done.9.s2_x = bf16[256,256]{1,0:T(8,128)(2,1)S(1)} collective-permute-done((bf16[256,256]{1,0:T(8,128)(2,1)S(1)}, bf16[256,256]{1,0:T(8,128)(2,1)S(1)}, u32[]{:S(2)}, u32[]{:S(2)}) %collective-permute-start.9) | collective-permute-done | bytes 131104 | tf_op jit(solution)/shard_map/ppermute | solution.py:38
  30.9 1.5 %collective-permute-done.10.u2_y = bf16[256,256]{1,0:T(8,128)(2,1)S(1)} collective-permute-done((bf16[256,256]{1,0:T(8,128)(2,1)S(1)}, bf16[256,256]{1,0:T(8,128)(2,1)S(1)}, u32[]{:S(2)}, u32[]{:S(2)}) %collective-permute-start.10) | collective-permute-done | bytes 131104 | tf_op jit(solution)/shard_map/ppermute | solution.py:38
  32.4 0.8 %shard_map.156 = (bf16[64,256]{1,0:T(8,128)(2,1)S(1)}, bf16[256,256]{1,0:T(8,128)(2,1)S(1)}) custom-call(bf16[256,256]{1,0:T(8,128)(2,1)S(1)} %shard_map.154.s2, bf16[256,256]{1,0:T(8,128)(2,1)S(1)} %collective-permute-done.9.s2_x, bf16[256,256]{1,0:T(8,128)(2,1)S(1)} %get-tuple-element.35.u2, bf16[256,256]{1,0:T(8,128)(2,1)S(1)} %collective-permute-done.10.u2_y, ...), custom_call_target="tpu_custom_call" | custom-call | flops 67108864 | bytes 2031616 | tf_op jit(solution)/shard_map/pallas_call | solution.py:25
  33.2 1.7 %collective-permute-start.16 = (bf16[256,256]{1,0:T(8,128)(2,1)S(1)}, bf16[256,256]{1,0:T(8,128)(2,1)S(1)}, u32[]{:S(2)}, u32[]{:S(2)}) collective-permute-start(bf16[256,256]{1,0:T(8,128)(2,1)S(1)} %get-tuple-element.39.v3), channel_id=1, source_target_pairs={{0,8},{2,10},{4,12},{6,14},{8,0},{10,2},{12,4},{14,6},{16,24},{18,... | collective-permute-start | bytes 393224 | tf_op jit(solution)/shard_map/ppermute | solution.py:38
  34.9 0.5 %collective-permute-start.6 = (bf16[128,256]{1,0:T(8,128)(2,1)S(1)}, bf16[128,256]{1,0:T(8,128)(2,1)S(1)}, u32[]{:S(2)}, u32[]{:S(2)}) collective-permute-start(bf16[128,256]{1,0:T(8,128)(2,1)S(1)} %get-tuple-element.28.own), channel_id=1, source_target_pairs={{0,1},{1,0},{2,3},{3,2},{4,5},{5,4},{6,7},{7,6},{8,9},{9,8},{10,11... | collective-permute-start | bytes 196616 | tf_op jit(solution)/shard_map/ppermute | solution.py:38
  35.4 2.9 %collective-permute-done.16.v3_z = bf16[256,256]{1,0:T(8,128)(2,1)S(1)} collective-permute-done((bf16[256,256]{1,0:T(8,128)(2,1)S(1)}, bf16[256,256]{1,0:T(8,128)(2,1)S(1)}, u32[]{:S(2)}, u32[]{:S(2)}) %collective-permute-start.16) | collective-permute-done | bytes 131104 | tf_op jit(solution)/shard_map/ppermute | solution.py:38
  38.3 0.1 shard_map.158.own
  38.4 0.7 %shard_map.149 = bf16[256,512]{1,0:T(8,128)(2,1)} custom-call(bf16[256,256]{1,0:T(8,128)(2,1)S(1)} %get-tuple-element.25.own.solved, bf16[256,256]{1,0:T(8,128)(2,1)S(1)} %collective-permute-done.2.got), custom_call_target="tpu_custom_call" | custom-call | bytes 524288 | tf_op jit(solution)/shard_map/pallas_call | solution.py:25
  39.2 0.7 %shard_map.151 = bf16[128,512]{1,0:T(8,128)(2,1)} custom-call(bf16[128,256]{1,0:T(8,128)(2,1)S(1)} %get-tuple-element.28.own, bf16[128,256]{1,0:T(8,128)(2,1)S(1)} %collective-permute-done.6.got), custom_call_target="tpu_custom_call" | custom-call | bytes 262144 | tf_op jit(solution)/shard_map/pallas_call | solution.py:25
  39.8 0.6 %shard_map.157 = bf16[64,512]{1,0:T(8,128)(2,1)} custom-call(bf16[64,256]{1,0:T(8,128)(2,1)S(1)} %get-tuple-element.38.own, bf16[64,256]{1,0:T(8,128)(2,1)S(1)} %collective-permute-done.15.got), custom_call_target="tpu_custom_call" | custom-call | bytes 131072 | tf_op jit(solution)/shard_map/pallas_call | solution.py:25
  40.5 0.6 %shard_map.159 = bf16[32,512]{1,0:T(8,128)(2,1)} custom-call(bf16[32,256]{1,0:T(8,128)(2,1)S(1)} %shard_map.158.own, bf16[32,256]{1,0:T(8,128)(2,1)S(1)} %collective-permute-done.17.got), custom_call_target="tpu_custom_call" | custom-call | bytes 65536 | tf_op jit(solution)/shard_map/pallas_call | solution.py:25
  (24 shorter events, 0.1 us)
Async XLA Ops:
  3.9 10.1 %copy-start = (bf16[256,256]{1,0:T(8,128)(2,1)S(1)}, bf16[256,256]{1,0:T(8,128)(2,1)}, u32[]{:S(2)}) copy-start(bf16[256,256]{1,0:T(8,128)(2,1)} %inverse.4) | copy-start | bytes 393220
  3.9 10.1 %collective-permute-start.1 = (bf16[128,1152]{1,0:T(8,128)(2,1)S(1)}, bf16[128,1152]{1,0:T(8,128)(2,1)S(1)}, u32[]{:S(2)}, u32[]{:S(2)}) collective-permute-start(bf16[128,1152]{1,0:T(8,128)(2,1)S(1)} %get-tuple-element.24.across), channel_id=1, source_target_pairs={{0,1},{1,0},{2,3},{3,2},{4,5},{5,4},{6,7},{7,6},{8,9},{9,8},{10,11... | collective-permute-start | bytes 884744 | tf_op jit(solution)/shard_map/ppermute | solution.py:38
  4.5 9.5 %collective-permute-start = (bf16[2,256,256]{2,1,0:T(8,128)(2,1)S(1)}, bf16[2,256,256]{2,1,0:T(8,128)(2,1)S(1)}, u32[]{:S(2)}, u32[]{:S(2)}) collective-permute-start(bf16[2,256,256]{2,1,0:T(8,128)(2,1)S(1)} %get-tuple-element.23), channel_id=1, source_target_pairs={{0,1},{1,0},{2,3},{3,2},{4,5},{5,4},{6,7},{7,6},{8,9},{9,8},{10,11... | collective-permute-start | bytes 786440 | tf_op jit(solution)/shard_map/ppermute | solution.py:38
  5.4 9.0 %collective-permute-start.7 = (bf16[2,256,256]{2,1,0:T(8,128)(2,1)S(1)}, bf16[2,256,256]{2,1,0:T(8,128)(2,1)S(1)}, u32[]{:S(2)}, u32[]{:S(2)}) collective-permute-start(bf16[2,256,256]{2,1,0:T(8,128)(2,1)S(1)} %get-tuple-element.33), channel_id=1, source_target_pairs={{0,1},{1,0},{2,3},{3,2},{4,5},{5,4},{6,7},{7,6},{8,9},{9,8},{10,11... | collective-permute-start | bytes 786440 | tf_op jit(solution)/shard_map/ppermute | solution.py:38
  5.9 8.0 %collective-permute-start.4 = (bf16[192,512]{1,0:T(8,128)(2,1)S(1)}, bf16[192,512]{1,0:T(8,128)(2,1)S(1)}, u32[]{:S(2)}, u32[]{:S(2)}) collective-permute-start(bf16[192,512]{1,0:T(8,128)(2,1)S(1)} %get-tuple-element.27.along), channel_id=1, source_target_pairs={{0,2},{2,0},{4,6},{6,4},{8,10},{10,8},{12,14},{14,12},{16,18},{18,... | collective-permute-start | bytes 589832 | tf_op jit(solution)/shard_map/ppermute | solution.py:38
  14.0 4.9 %collective-permute-start.5 = (bf16[192,512]{1,0:T(8,128)(2,1)S(1)}, bf16[192,512]{1,0:T(8,128)(2,1)S(1)}, u32[]{:S(2)}, u32[]{:S(2)}) collective-permute-start(bf16[192,512]{1,0:T(8,128)(2,1)S(1)} %collective-permute-done.4.along_x), channel_id=1, source_target_pairs={{0,1},{1,0},{2,3},{3,2},{4,5},{5,4},{6,7},{7,6},{8,9},{9,8},{10,11... | collective-permute-start | bytes 589832 | tf_op jit(solution)/shard_map/ppermute | solution.py:38
  14.7 23.6 %copy-start.1 = (bf16[32,256]{1,0:T(8,128)(2,1)S(1)}, bf16[32,256]{1,0:T(8,128)(2,1)}, u32[]{:S(2)}) copy-start(bf16[32,256]{1,0:T(8,128)(2,1)} %inverse.5) | copy-start | bytes 49156
  14.7 9.2 %collective-permute-start.13 = (bf16[256,256]{1,0:T(8,128)(2,1)S(1)}, bf16[256,256]{1,0:T(8,128)(2,1)S(1)}, u32[]{:S(2)}, u32[]{:S(2)}) collective-permute-start(bf16[256,256]{1,0:T(8,128)(2,1)S(1)} %get-tuple-element.36.a), channel_id=1, source_target_pairs={{0,2},{2,0},{4,6},{6,4},{8,10},{10,8},{12,14},{14,12},{16,18},{18,... | collective-permute-start | bytes 393224 | tf_op jit(solution)/shard_map/ppermute | solution.py:38
  16.5 7.0 %collective-permute-start.3 = (bf16[256,256]{1,0:T(8,128)(2,1)S(1)}, bf16[256,256]{1,0:T(8,128)(2,1)S(1)}, u32[]{:S(2)}, u32[]{:S(2)}) collective-permute-start(bf16[256,256]{1,0:T(8,128)(2,1)S(1)} %get-tuple-element.26.p1), channel_id=1, source_target_pairs={{0,2},{2,0},{4,6},{6,4},{8,10},{10,8},{12,14},{14,12},{16,18},{18,... | collective-permute-start | bytes 393224 | tf_op jit(solution)/shard_map/ppermute | solution.py:38
  16.8 9.1 %collective-permute-start.8 = (bf16[256,256]{1,0:T(8,128)(2,1)S(1)}, bf16[256,256]{1,0:T(8,128)(2,1)S(1)}, u32[]{:S(2)}, u32[]{:S(2)}) collective-permute-start(bf16[256,256]{1,0:T(8,128)(2,1)S(1)} %get-tuple-element.34.a), channel_id=1, source_target_pairs={{0,4},{2,6},{4,0},{6,2},{8,12},{10,14},{12,8},{14,10},{16,20},{18,... | collective-permute-start | bytes 393224 | tf_op jit(solution)/shard_map/ppermute | solution.py:38
  18.6 9.4 %collective-permute-start.11 = (bf16[128,384]{1,0:T(8,128)(2,1)S(1)}, bf16[128,384]{1,0:T(8,128)(2,1)S(1)}, u32[]{:S(2)}, u32[]{:S(2)}) collective-permute-start(bf16[128,384]{1,0:T(8,128)(2,1)S(1)} %pad_maximum_fusion), channel_id=1, source_target_pairs={{0,4},{2,6},{4,0},{6,2},{8,12},{10,14},{12,8},{14,10},{16,20},{18,... | collective-permute-start | bytes 294920 | tf_op jit(solution)/shard_map/ppermute | solution.py:38
  24.0 5.7 %collective-permute-start.14 = (bf16[256,256]{1,0:T(8,128)(2,1)S(1)}, bf16[256,256]{1,0:T(8,128)(2,1)S(1)}, u32[]{:S(2)}, u32[]{:S(2)}) collective-permute-start(bf16[256,256]{1,0:T(8,128)(2,1)S(1)} %shard_map.155.s3), channel_id=1, source_target_pairs={{0,4},{2,6},{4,0},{6,2},{8,12},{10,14},{12,8},{14,10},{16,20},{18,... | collective-permute-start | bytes 393224 | tf_op jit(solution)/shard_map/ppermute | solution.py:38
  25.9 5.0 %collective-permute-start.9 = (bf16[256,256]{1,0:T(8,128)(2,1)S(1)}, bf16[256,256]{1,0:T(8,128)(2,1)S(1)}, u32[]{:S(2)}, u32[]{:S(2)}) collective-permute-start(bf16[256,256]{1,0:T(8,128)(2,1)S(1)} %shard_map.154.s2), channel_id=1, source_target_pairs={{0,2},{2,0},{4,6},{6,4},{8,10},{10,8},{12,14},{14,12},{16,18},{18,... | collective-permute-start | bytes 393224 | tf_op jit(solution)/shard_map/ppermute | solution.py:38
  27.5 5.0 %collective-permute-start.10 = (bf16[256,256]{1,0:T(8,128)(2,1)S(1)}, bf16[256,256]{1,0:T(8,128)(2,1)S(1)}, u32[]{:S(2)}, u32[]{:S(2)}) collective-permute-start(bf16[256,256]{1,0:T(8,128)(2,1)S(1)} %get-tuple-element.35.u2), channel_id=1, source_target_pairs={{0,4},{2,6},{4,0},{6,2},{8,12},{10,14},{12,8},{14,10},{16,20},{18,... | collective-permute-start | bytes 393224 | tf_op jit(solution)/shard_map/ppermute | solution.py:38
  28.0 1.3 %collective-permute-start.12 = (bf16[128,384]{1,0:T(8,128)(2,1)S(1)}, bf16[128,384]{1,0:T(8,128)(2,1)S(1)}, u32[]{:S(2)}, u32[]{:S(2)}) collective-permute-start(bf16[128,384]{1,0:T(8,128)(2,1)S(1)} %collective-permute-done.11.side), channel_id=1, source_target_pairs={{0,1},{1,0},{2,3},{3,2},{4,5},{5,4},{6,7},{7,6},{8,9},{9,8},{10,11... | collective-permute-start | bytes 294920 | tf_op jit(solution)/shard_map/ppermute | solution.py:38
  33.2 5.0 %collective-permute-start.16 = (bf16[256,256]{1,0:T(8,128)(2,1)S(1)}, bf16[256,256]{1,0:T(8,128)(2,1)S(1)}, u32[]{:S(2)}, u32[]{:S(2)}) collective-permute-start(bf16[256,256]{1,0:T(8,128)(2,1)S(1)} %get-tuple-element.39.v3), channel_id=1, source_target_pairs={{0,8},{2,10},{4,12},{6,14},{8,0},{10,2},{12,4},{14,6},{16,24},{18,... | collective-permute-start | bytes 393224 | tf_op jit(solution)/shard_map/ppermute | solution.py:38
  34.9 3.5 %collective-permute-start.2 = (bf16[256,256]{1,0:T(8,128)(2,1)S(1)}, bf16[256,256]{1,0:T(8,128)(2,1)S(1)}, u32[]{:S(2)}, u32[]{:S(2)}) collective-permute-start(bf16[256,256]{1,0:T(8,128)(2,1)S(1)} %get-tuple-element.25.own.solved), channel_id=1, source_target_pairs={{0,1},{1,0},{2,3},{3,2},{4,5},{5,4},{6,7},{7,6},{8,9},{9,8},{10,11... | collective-permute-start | bytes 393224 | tf_op jit(solution)/shard_map/ppermute | solution.py:38
  34.9 4.3 %collective-permute-start.6 = (bf16[128,256]{1,0:T(8,128)(2,1)S(1)}, bf16[128,256]{1,0:T(8,128)(2,1)S(1)}, u32[]{:S(2)}, u32[]{:S(2)}) collective-permute-start(bf16[128,256]{1,0:T(8,128)(2,1)S(1)} %get-tuple-element.28.own), channel_id=1, source_target_pairs={{0,1},{1,0},{2,3},{3,2},{4,5},{5,4},{6,7},{7,6},{8,9},{9,8},{10,11... | collective-permute-start | bytes 196616 | tf_op jit(solution)/shard_map/ppermute | solution.py:38
  35.4 4.5 %collective-permute-start.15 = (bf16[64,256]{1,0:T(8,128)(2,1)S(1)}, bf16[64,256]{1,0:T(8,128)(2,1)S(1)}, u32[]{:S(2)}, u32[]{:S(2)}) collective-permute-start(bf16[64,256]{1,0:T(8,128)(2,1)S(1)} %get-tuple-element.38.own), channel_id=1, source_target_pairs={{0,1},{1,0},{2,3},{3,2},{4,5},{5,4},{6,7},{7,6},{8,9},{9,8},{10,11... | collective-permute-start | bytes 98312 | tf_op jit(solution)/shard_map/ppermute | solution.py:38
  38.4 2.1 %collective-permute-start.17 = (bf16[32,256]{1,0:T(8,128)(2,1)S(1)}, bf16[32,256]{1,0:T(8,128)(2,1)S(1)}, u32[]{:S(2)}, u32[]{:S(2)}) collective-permute-start(bf16[32,256]{1,0:T(8,128)(2,1)S(1)} %shard_map.158.own), channel_id=1, source_target_pairs={{0,1},{1,0},{2,3},{3,2},{4,5},{5,4},{6,7},{7,6},{8,9},{9,8},{10,11... | collective-permute-start | bytes 49160 | tf_op jit(solution)/shard_map/ppermute | solution.py:38

commit v3 on v2

v3 whole, which is shorter than its diff:
```python
import jax
import jax.numpy as jnp
from jax import lax
from jax.experimental import pallas as pl
from jax.experimental.pallas import tpu as pltpu
from jax.sharding import PartitionSpec as P

F32, BF16 = jnp.float32, jnp.bfloat16
WHOLE = pl.BlockSpec(memory_space=pltpu.VMEM)
SCALARS = pl.BlockSpec(memory_space=pltpu.SMEM)


def dot(a, b):
    return jnp.dot(a, b, preferred_element_type=F32)


def dot_t(a, b):
    return lax.dot_general(a, b, (((0,), (0,)), ((), ())), preferred_element_type=F32)


def call(kernel, outs, *args, scratch=(), flops=0, specs=None):
    outs = [jax.ShapeDtypeStruct(shape, dtype) for shape, dtype in outs]
    moved = sum(a.size * a.dtype.itemsize for a in (*args, *outs))
    single = len(outs) == 1
    return pl.pallas_call(
        kernel,
        out_shape=outs[0] if single else outs,
        in_specs=specs or [WHOLE] * len(args),
        out_specs=WHOLE if single else [WHOLE] * len(outs),
        scratch_shapes=list(scratch),
        cost_estimate=pl.CostEstimate(flops=flops, bytes_accessed=moved, transcendentals=0),
        compiler_params=pltpu.CompilerParams(vmem_limit_bytes=16 << 20),
    )(*args)


def swap(block, axis, stride):
    count = lax.axis_size(axis)
    return lax.ppermute(block, axis, [(low, low ^ stride) for low in range(count)])


def own_and_other(part):
    me = lax.axis_index("row")
    return (
        pl.ds(pl.multiple_of(me * part, part), part),
        pl.ds(pl.multiple_of((1 - me) * part, part), part),
    )


def prepare(lower_0, lower_1, lower_2t, pattern, inv_1, inv_2, across, along_1, along_2):
    rows = lower_0.shape[1]
    blocks = pattern.shape[1]
    spread = rows // blocks
    size = lower_0.shape[2]
    n0, n1 = lower_0.shape[0], lower_1.shape[0]
    part_1, part_2 = lower_1.shape[2], lower_2t.shape[1]
    for b in range(blocks):
        at = pl.ds(b * spread, spread)
        for m in range(n0):
            factor = pattern[0, b, m].astype(BF16)
            across[at, pl.ds(m * size, size)] = lower_0[m, at, :] * factor
        for m in range(n1):
            factor = pattern[0, b, n0 + m].astype(BF16)
            masked = lower_1[m, at, :] * factor
            across[at, pl.ds(n0 * size + m * part_1, part_1)] = masked
            along_1[at, pl.ds(m * part_1, part_1)] = masked
    lane = lax.broadcasted_iota(jnp.int32, (1, rows), 1) // spread
    keep = jnp.zeros((1, rows), F32)
    for b in range(blocks):
        keep = jnp.where(lane == b, pattern[0, b, n0 + n1].astype(F32), keep)
    masked = (lower_2t[0].astype(F32) * keep).astype(BF16)
    start = n0 * size + n1 * part_1
    across[pl.ds(0, part_2), pl.ds(start, rows)] = masked
    across[pl.ds(part_2, rows - part_2), pl.ds(start, rows)] = jnp.zeros((rows - part_2, rows), BF16)
    cut = along_1.shape[0] - rows
    mine, _ = own_and_other(cut)
    along_1[pl.ds(rows, cut), :] = inv_1[mine, :]
    along_2[:, pl.ds(0, size)] = inv_2[...]
    along_2[:, pl.ds(size, rows)] = masked


def leaf_sums(solved, lower, rhs, keep, send, total, ready=None):
    leaves = lower.shape[1]
    mine, _ = own_and_other(rhs.shape[2])
    own, other = own_and_other(keep.shape[2])
    for m in range(keep.shape[0]):
        if ready:
            ready(m)
        acc = dot(lower[m, 0], solved[0])
        for v in range(1, leaves):
            acc = acc + dot(lower[m, v], solved[v])
        total[...] = -acc
        total[mine, :] = total[mine, :] + rhs[m, 0].astype(F32)
        keep[m] = total[:, own]
        send[m] = total[:, other].astype(BF16)


def opening(
    inverse, right, lower, rhs, lower_0, lower_1, lower_2t, pattern, inv_1, inv_2,
    solved, keep, send, across, along_1, along_2, lower_late, rhs_late,
    total, inverse_v, right_v, lower_v, rhs_v, low0_v, low1_v, low2_v, inv1_v, inv2_v, pattern_s, sems,
):
    leaves = inverse.shape[0]
    early = keep.shape[0]
    late = lower_late.shape[0]
    copies = []

    def fetch(source, target):
        copy = pltpu.make_async_copy(source, target, sems.at[len(copies)])
        copy.start()
        copies.append(copy)
        return copy

    leaf = []
    for v in range(leaves):
        leaf.append((fetch(inverse.at[v], inverse_v.at[v]), fetch(right.at[v], right_v.at[v])))
    sums = [fetch(lower.at[m], lower_v.at[m]) for m in range(early)]
    tops = fetch(rhs.at[pl.ds(0, early)], rhs_v)
    small = [
        fetch(source, target)
        for source, target in (
            (lower_0, low0_v), (lower_1, low1_v), (lower_2t, low2_v), (pattern, pattern_s),
            (inv_1, inv1_v), (inv_2, inv2_v),
        )
    ]
    last = [
        fetch(lower.at[pl.ds(early, late)], lower_late),
        fetch(rhs.at[pl.ds(early, late)], rhs_late),
    ]
    for v in range(leaves):
        for copy in leaf[v]:
            copy.wait()
        solved[v] = dot(inverse_v[v], right_v[v]).astype(BF16)
    tops.wait()
    leaf_sums(solved, lower_v, rhs_v, keep, send, total, lambda m: sums[m].wait())
    for copy in small:
        copy.wait()
    prepare(low0_v, low1_v, low2_v, pattern_s, inv1_v, inv2_v, across, along_1, along_2)
    for copy in last:
        copy.wait()


def leaf_b(solved, lower, rhs, keep, send, total):
    leaf_sums(solved, lower, rhs, keep, send, total)


def quarters(half):
    part = half // 2
    bit = lax.rem(lax.axis_index("col"), 2)
    return (
        pl.ds(pl.multiple_of(bit * part, part), part),
        pl.ds(pl.multiple_of((1 - bit) * part, part), part),
    )


def zero_a(keep, got, inverse, across, across_o, solved_out, kept, sent, total):
    size = inverse.shape[1]
    residual = (keep[0] + got[0].astype(F32)).astype(BF16)
    solved = dot(inverse[...], residual).astype(BF16)
    solved_out[...] = solved
    for low, at in zip((across, across_o), own_and_other(across.shape[0])):
        before = keep[1, at, :] + got[1, at, :].astype(F32)
        total[at, :] = before - dot(low[:, pl.ds(0, size)], solved)
    own, other = quarters(total.shape[1])
    kept[...] = total[:, own]
    sent[...] = total[:, other].astype(BF16)


def zero_b(keep, got, solved, across, across_o, kept_2, sent_2, kept_3, sent_3, total):
    size = solved.shape[0]
    own, other = quarters(total.shape[1])
    for m, (kept, sent) in enumerate(((kept_2, sent_2), (kept_3, sent_3))):
        for low, at in zip((across, across_o), own_and_other(across.shape[0])):
            before = keep[m, at, :] + got[m, at, :].astype(F32)
            total[at, :] = before - dot(low[:, pl.ds((m + 1) * size, size)], solved[...])
        kept[...] = total[:, own]
        sent[...] = total[:, other].astype(BF16)


def one(kept, got, inverse, along, along_x, across_o, along_xo, solved_own, solved_x, u2, u3):
    size, part = kept.shape[0], inverse.shape[0]
    rows = across_o.shape[0]
    residual = (kept[...] + got[...].astype(F32)).astype(BF16)
    solved_own[...] = dot(inverse[...], residual).astype(BF16)
    cut = along.shape[0] - rows
    for ref, at in zip((along_x, along_xo), own_and_other(cut)):
        solved_x[at, :] = dot(ref[pl.ds(rows, cut), :], residual).astype(BF16)
    own, other = solved_own[...], solved_x[...]
    first = 3 * size
    mine, theirs = own_and_other(rows)
    for m, out in enumerate((u2, u3)):
        at = pl.ds(m * part, part)
        out[mine, :] = dot(along[pl.ds(0, rows), at], own) + dot(along_x[pl.ds(0, rows), at], other)
        out[theirs, :] = dot(across_o[:, pl.ds(first + m * part, part)], own) + dot(
            along_xo[pl.ds(0, rows), at], other
        )


def difference(kept, got, update, out):
    out[...] = (kept[...] + got[...].astype(F32) - update[...]).astype(BF16)


def two(w2, w2_y, along, along_x, side, across_o, along_xo, side_o, s3, s3_y, solved_own, solved_x, v3):
    part = along.shape[0]
    size = w2.shape[0]
    rows = across_o.shape[0]
    residual = (w2[...].astype(F32) + w2_y[...].astype(F32)).astype(BF16)
    pieces = ((along, 0), (along_x, 0), (side, 0), (side, part))
    others = (
        (across_o, 0, across_o.shape[1] - rows), (along_xo, 0, size), (side_o, 0, size), (side_o, part, size),
    )
    mine, theirs = own_and_other(rows)
    total = [s3[at, :].astype(F32) + s3_y[at, :].astype(F32) for at in (mine, theirs)]
    for i, ((ref, at), (ref_o, at_o, lane_o)) in enumerate(zip(pieces, others)):
        solved = dot(ref[pl.ds(at, part), pl.ds(0, size)], residual).astype(BF16)
        if i < 2:
            (solved_own, solved_x)[i][...] = solved
        total[0] = total[0] - dot_t(ref[pl.ds(at, part), pl.ds(size, rows)], solved)
        total[1] = total[1] - dot_t(ref_o[pl.ds(at_o, part), pl.ds(lane_o, rows)], solved)
    v3[mine, :] = total[0].astype(BF16)
    v3[theirs, :] = total[1].astype(BF16)


def three(v3, v3_x, v3_z, v3_xz, inverse, sol1, sol1_x, sol2, sol2_x, out, full):
    own, other = quarters(out.shape[1])
    full[:, own] = (v3[...].astype(F32) + v3_z[...].astype(F32)).astype(BF16)
    full[:, other] = (v3_x[...].astype(F32) + v3_xz[...].astype(F32)).astype(BF16)
    n1, n2 = sol1.shape[0], sol2.shape[0]
    out[pl.ds(0, n1), own] = sol1[...]
    out[pl.ds(0, n1), other] = sol1_x[...]
    out[pl.ds(n1, n2), own] = sol2[...]
    out[pl.ds(n1, n2), other] = sol2_x[...]
    out[pl.ds(n1 + n2, inverse.shape[0]), :] = dot(inverse[...], full[...]).astype(BF16)


def join(own, got, *outs):
    mine, theirs = own_and_other(own.shape[1])
    first = 0
    for out in outs:
        at = pl.ds(first, out.shape[0])
        out[:, mine] = own[at, :]
        out[:, theirs] = got[at, :]
        first += out.shape[0]


def body(
    rhs, leaf_rhs, leaf_inverse, leaf_lower,
    inverse_0, inverse_1, inverse_2, inverse_3,
    lower_0, lower_1, lower_2, sparsity,
):
    levels, _, rows, width = rhs.shape
    leaves, size, _ = leaf_inverse.shape
    half = width // lax.axis_size("row")
    n0, n1 = lower_0.shape[0], lower_1.shape[0]
    part_1, part_2 = inverse_1.shape[0], inverse_2.shape[0]
    full = [pltpu.VMEM((size, width), F32)]

    early = 2
    late = levels - early
    lower_2t, pattern = jnp.swapaxes(lower_2, 1, 2), jnp.transpose(sparsity, (1, 2, 0))
    sources = (leaf_inverse, leaf_rhs, leaf_lower, rhs, lower_0, lower_1, lower_2t, pattern, inverse_1, inverse_2)
    solved_leaf, keep_a, send_a, across, along_1, along_2, lower_late, rhs_late = call(
        opening,
        [
            ((leaves, size, width), BF16),
            ((early, size, half), F32),
            ((early, size, half), BF16),
            ((rows, n0 * size + n1 * part_1 + rows), BF16),
            ((rows + part_1 // 2, n1 * part_1), BF16),
            ((part_2, size + rows), BF16),
            ((late, leaves, size, size), BF16),
            ((late, 1, rows, width), BF16),
        ],
        *(pltpu.with_memory_space_constraint(x, pltpu.HBM) for x in sources),
        specs=[pl.BlockSpec(memory_space=pltpu.HBM)] * len(sources),
        scratch=[pltpu.VMEM((size, width), F32)]
        + [pltpu.VMEM(x.shape, BF16) for x in (leaf_inverse, leaf_rhs)]
        + [pltpu.VMEM((early, *x.shape[1:]), BF16) for x in (leaf_lower, rhs)]
        + [pltpu.VMEM(x.shape, BF16) for x in (lower_0, lower_1, lower_2t, inverse_1, inverse_2)]
        + [pltpu.SMEM(pattern.shape, jnp.int32), pltpu.SemaphoreType.DMA((2 * leaves + early + 9,))],
        flops=6 * leaves * size * size * width,
    )
    got_a = swap(send_a, "row", 1)
    across_o = swap(across, "row", 1)
    along_2x = swap(along_2, "col", 1)
    along_1x = swap(along_1, "col", 1)
    keep_b, send_b = call(
        leaf_b,
        [((late, size, half), F32), ((late, size, half), BF16)],
        solved_leaf, lower_late, rhs_late,
        scratch=full, flops=2 * late * leaves * size * size * width,
    )
    got_b = swap(send_b, "row", 1)
    quarter = half // 2
    square = pltpu.VMEM((size, half), F32)
    kept, sent = ((size, quarter), F32), ((size, quarter), BF16)
    sol0, kept1, sent1 = call(
        zero_a, [((size, half), BF16), kept, sent], keep_a, got_a, inverse_0, across, across_o,
        scratch=[square], flops=4 * size * size * half,
    )
    got1 = swap(sent1, "col", 1)
    kept2, sent2, kept3, sent3 = call(
        zero_b, [kept, sent, kept, sent], keep_b, got_b, sol0, across, across_o,
        scratch=[square], flops=4 * size * size * half,
    )
    got2 = swap(sent2, "col", 1)
    side = swap(jnp.concatenate([along_2, along_2x]), "col", 2)
    got3 = swap(sent3, "col", 1)
    along_2xo = swap(along_2x, "row", 1)
    along_1xo = swap(along_1x, "row", 1)
    sol1, sol1_for_x, u2, u3 = call(
        one, [((part_1, quarter), BF16)] * 2 + [kept] * 2,
        kept1, got1, inverse_1, along_1, along_1x, across_o, along_1xo,
        flops=6 * size * size * quarter,
    )
    w2 = call(difference, [sent], kept2, got2, u2)
    w2_y = swap(w2, "col", 2)
    sol0_o = swap(sol0, "row", 1)
    side_o = swap(side, "row", 1)
    s3 = call(difference, [sent], kept3, got3, u3)
    s3_y = swap(s3, "col", 2)
    out0 = call(join, [((size, width), BF16)], sol0, sol0_o)
    sol2, sol2_for_x, v3 = call(
        two, [((part_2, quarter), BF16)] * 2 + [sent],
        w2, w2_y, along_2, along_2x, side, across_o, along_2xo, side_o, s3, s3_y,
        flops=4 * size * size * quarter,
    )
    v3_xz = swap(v3, "col", 5)
    v3_x = swap(v3, "col", 1)
    v3_z = swap(v3, "col", 4)
    sol1_x = swap(sol1_for_x, "col", 1)
    sol2_x = swap(sol2_for_x, "col", 1)
    part_3 = inverse_3.shape[0]
    last = call(
        three, [((part_1 + part_2 + part_3, half), BF16)],
        v3, v3_x, v3_z, v3_xz, inverse_3, sol1, sol1_x, sol2, sol2_x,
        scratch=[pltpu.VMEM((size, half), BF16)], flops=2 * inverse_3.size * half,
    )
    last_o = swap(last, "row", 1)
    rest = call(join, [((part, width), BF16) for part in (part_1, part_2, part_3)], last, last_o)
    return (out0, *rest)


def solution(mesh):
    return jax.shard_map(
        body,
        mesh=mesh,
        in_specs=(
            P(None, "col", "row", None),
            P(("col", "row"), None, None),
            P(("col", "row"), None, None),
            P(None, ("col", "row"), None, None),
            P("col", None),
            P("col", None),
            P("col", None),
            P("col", None),
            P(None, "row", "col"),
            P(None, "row", "col"),
            P(None, "row", "col"),
            P(None, "col", "row"),
        ),
        out_specs=(P("col", None), P("col", None), P("col", None), P("col", None)),
        check_vma=False,
    )
```

time: 41.3 us -> 38.3 us (0.927)
  waiting for transfers between devices: 17.4 us -> 12.4 us
  starting transfers between devices: 13.9 us -> 17.3 us
  Pallas kernels: 8.96 us -> 7.64 us
    ppermute x18 -> x21, waiting for transfers between devices: 17.4 us -> 12.4 us  [swap(): lax.ppermute(block, axis, [(low, low ^ stride) for low in range(count)])]
    ppermute x18 -> x21, starting transfers between devices: 13.9 us -> 17.3 us  [swap(): lax.ppermute(block, axis, [(low, low ^ stride) for low in range(count)])]
    pallas_call x13 -> x11, Pallas kernels: 8.96 us -> 7.64 us  [call(): pl.pallas_call(kernel, out_shape=outs[0] if single else outs, in_specs=sp...]
  transfers between devices with their start and end apart: 18 -> 21, of which waited for: 7 -> 10; matrix products, arithmetic and copies ran while one was open for 0% -> 0% of each run, Pallas kernels for 10% -> 8%
where the time goes in v3:
time: 38.3 us; the launch traced here: 38.1 us
  starting transfers between devices  17.3 us (45%)
  waiting for transfers between devices  12.4 us (32%)
  Pallas kernels  7.64 us (20%)
  between operations  0.75 us (2%)
    ppermute x21, starting transfers between devices, swap(): lax.ppermute(block, axis, [(low, low ^ stride) for low in range(count)])  17.3 us
    ppermute x21, waiting for transfers between devices, swap(): lax.ppermute(block, axis, [(low, low ^ stride) for low in range(count)])  12.4 us
    pallas_call x11, Pallas kernels, call(): pl.pallas_call(kernel, out_shape=outs[0] if single else outs, in_specs=sp...  7.64 us
  transfers between devices with their start and end apart: 21, of which 10 were waited for; matrix products, arithmetic and copies ran while one was open for 0% of the time, Pallas kernels for 8%

profile of v3, /device:TPU:0, one launch (start us, length us, event | category | flops | bytes accessed | tf_op | source)
XLA Modules:
  0.0 38.1 jit_solution(11648885627737463603)
XLA Ops:
  0.6 3.3 %shard_map.147 = (bf16[4,256,512]{2,1,0:T(8,128)(2,1)S(1)}, f32[2,256,256]{2,1,0:T(8,128)S(1)}, bf16[2,256,256]{2,1,0:T(8,128)(2,1)S(1)}, bf16[128,1152]{1,0:T(8...) custom-call(bf16[4,256,256]{2,1,0:T(8,128)(2,1)} %inverse.4, ...), custom_call_target="tpu_custom_call" | custom-call | flops 805306368 | bytes 8159328 | tf_op jit(solution)/shard_map/pallas_call | solution.py:25
  3.9 0.6 %collective-permute-start.1 = (bf16[128,1152]{1,0:T(8,128)(2,1)S(1)}, bf16[128,1152]{1,0:T(8,128)(2,1)S(1)}, u32[]{:S(2)}, u32[]{:S(2)}) collective-permute-start(bf16[128,1152]{1,0:T(8,128)(2,1)S(1)} %get-tuple-element.33.across), channel_id=1, source_target_pairs={{0,1},{1,0},{2,3},{3,2},{4,5},{5,4},{6,7},{7,6},{8,9},{9,8},{10,11... | collective-permute-start | bytes 884744 | tf_op jit(solution)/shard_map/ppermute | solution.py:38
  4.6 0.9 %shard_map.150 = (f32[2,256,256]{2,1,0:T(8,128)S(1)}, bf16[2,256,256]{2,1,0:T(8,128)(2,1)S(1)}) custom-call(bf16[4,256,512]{2,1,0:T(8,128)(2,1)S(1)} %get-tuple-element.35.solved, bf16[2,4,256,256]{3,2,1,0:T(8,128)(2,1)S(1)} %get-tuple-element.36.lower, bf16[2,1,128,512]{3,2,1,0:T(8,128)(2,1)S(1)} %get-tuple-element.37.rhs), custom_call_target="tpu_custom_call" | custom-call | flops 536870912 | bytes 3145728 | tf_op jit(solution)/shard_map/pallas_call | solution.py:25
  5.5 0.5 %collective-permute-start.3 = (bf16[2,256,256]{2,1,0:T(8,128)(2,1)S(1)}, bf16[2,256,256]{2,1,0:T(8,128)(2,1)S(1)}, u32[]{:S(2)}, u32[]{:S(2)}) collective-permute-start(bf16[2,256,256]{2,1,0:T(8,128)(2,1)S(1)} %get-tuple-element.39), channel_id=1, source_target_pairs={{0,1},{1,0},{2,3},{3,2},{4,5},{5,4},{6,7},{7,6},{8,9},{9,8},{10,11... | collective-permute-start | bytes 786440 | tf_op jit(solution)/shard_map/ppermute | solution.py:38
  6.0 2.5 %collective-permute-start.9 = (bf16[64,384]{1,0:T(8,128)(2,1)S(1)}, bf16[64,384]{1,0:T(8,128)(2,1)S(1)}, u32[]{:S(2)}, u32[]{:S(2)}) collective-permute-start(bf16[64,384]{1,0:T(8,128)(2,1)S(1)} %get-tuple-element.46.along), channel_id=1, source_target_pairs={{0,2},{2,0},{4,6},{6,4},{8,10},{10,8},{12,14},{14,12},{16,18},{18,... | collective-permute-start | bytes 147464 | tf_op jit(solution)/shard_map/ppermute | solution.py:38
  8.6 2.3 %collective-permute-done.9.along_x = bf16[64,384]{1,0:T(8,128)(2,1)S(1)} collective-permute-done((bf16[64,384]{1,0:T(8,128)(2,1)S(1)}, bf16[64,384]{1,0:T(8,128)(2,1)S(1)}, u32[]{:S(2)}, u32[]{:S(2)}) %collective-permute-start.9) | collective-permute-done | bytes 49184 | tf_op jit(solution)/shard_map/ppermute | solution.py:38
  10.8 1.9 %collective-permute-start.10 = (bf16[128,384]{1,0:T(8,128)(2,1)S(1)}, bf16[128,384]{1,0:T(8,128)(2,1)S(1)}, u32[]{:S(2)}, u32[]{:S(2)}) collective-permute-start(bf16[128,384]{1,0:T(8,128)(2,1)S(1)} %pad_maximum_fusion), channel_id=1, source_target_pairs={{0,4},{2,6},{4,0},{6,2},{8,12},{10,14},{12,8},{14,10},{16,20},{18,... | collective-permute-start | bytes 294920 | tf_op jit(solution)/shard_map/ppermute | solution.py:38
  12.7 0.6 %collective-permute-done.6.along_x = bf16[192,256]{1,0:T(8,128)(2,1)S(1)} collective-permute-done((bf16[192,256]{1,0:T(8,128)(2,1)S(1)}, bf16[192,256]{1,0:T(8,128)(2,1)S(1)}, u32[]{:S(2)}, u32[]{:S(2)}) %collective-permute-start.6) | collective-permute-done | bytes 98336 | tf_op jit(solution)/shard_map/ppermute | solution.py:38
  13.4 0.4 %shard_map.148 = (bf16[256,256]{1,0:T(8,128)(2,1)S(1)}, f32[256,128]{1,0:T(8,128)S(1)}, bf16[256,128]{1,0:T(8,128)(2,1)S(1)}) custom-call(f32[2,256,256]{2,1,0:T(8,128)S(1)} %get-tuple-element.31.keep, bf16[2,256,256]{2,1,0:T(8,128)(2,1)S(1)} %collective-permute-done.got, bf16[256,256]{1,0:T(8,128)(2,1)S(1)} %copy-done.1, ...), custom_call_target="tpu_custom_call" | custom-call | flops 67108864 | bytes 1835008 | tf_op jit(solution)/shard_map/pallas_call | solution.py:25
  13.8 1.4 %collective-permute-start.5 = (bf16[256,128]{1,0:T(8,128)(2,1)S(1)}, bf16[256,128]{1,0:T(8,128)(2,1)S(1)}, u32[]{:S(2)}, u32[]{:S(2)}) collective-permute-start(bf16[256,128]{1,0:T(8,128)(2,1)S(1)} %get-tuple-element.43), channel_id=1, source_target_pairs={{0,2},{2,0},{4,6},{6,4},{8,10},{10,8},{12,14},{14,12},{16,18},{18,... | collective-permute-start | bytes 196616 | tf_op jit(solution)/shard_map/ppermute | solution.py:38
  15.3 0.3 shard_map.151
  15.6 0.7 %collective-permute-start.13 = (bf16[256,128]{1,0:T(8,128)(2,1)S(1)}, bf16[256,128]{1,0:T(8,128)(2,1)S(1)}, u32[]{:S(2)}, u32[]{:S(2)}) collective-permute-start(bf16[256,128]{1,0:T(8,128)(2,1)S(1)} %get-tuple-element.48), channel_id=1, source_target_pairs={{0,2},{2,0},{4,6},{6,4},{8,10},{10,8},{12,14},{14,12},{16,18},{18,... | collective-permute-start | bytes 196616 | tf_op jit(solution)/shard_map/ppermute | solution.py:38
  16.3 1.4 %collective-permute-start.4 = (bf16[256,128]{1,0:T(8,128)(2,1)S(1)}, bf16[256,128]{1,0:T(8,128)(2,1)S(1)}, u32[]{:S(2)}, u32[]{:S(2)}) collective-permute-start(bf16[256,128]{1,0:T(8,128)(2,1)S(1)} %get-tuple-element.41), channel_id=1, source_target_pairs={{0,2},{2,0},{4,6},{6,4},{8,10},{10,8},{12,14},{14,12},{16,18},{18,... | collective-permute-start | bytes 196616 | tf_op jit(solution)/shard_map/ppermute | solution.py:38
  17.7 0.7 %collective-permute-done.5.got = bf16[256,128]{1,0:T(8,128)(2,1)S(1)} collective-permute-done((bf16[256,128]{1,0:T(8,128)(2,1)S(1)}, bf16[256,128]{1,0:T(8,128)(2,1)S(1)}, u32[]{:S(2)}, u32[]{:S(2)}) %collective-permute-start.5) | collective-permute-done | bytes 65568 | tf_op jit(solution)/shard_map/ppermute | solution.py:38
  18.4 0.4 %shard_map.152 = (bf16[128,128]{1,0:T(8,128)(2,1)S(1)}, bf16[128,128]{1,0:T(8,128)(2,1)S(1)}, f32[256,128]{1,0:T(8,128)S(1)}, f32[256,128]{1,0:T(8,128)S(1)}) custom-call(f32[256,128]{1,0:T(8,128)S(1)} %get-tuple-element.42.kept, bf16[256,128]{1,0:T(8,128)(2,1)S(1)} %collective-permute-done.5.got, bf16[128,256]{1,0:T(8,128)(2,1)S(1)} %copy-done, ...), custom_call_target="tpu_custom_call" | custom-call | flops 50331648 | bytes 1179648 | tf_op jit(solution)/shard_map/pallas_call | solution.py:25
  18.8 1.8 %collective-permute-done.13.got = bf16[256,128]{1,0:T(8,128)(2,1)S(1)} collective-permute-done((bf16[256,128]{1,0:T(8,128)(2,1)S(1)}, bf16[256,128]{1,0:T(8,128)(2,1)S(1)}, u32[]{:S(2)}, u32[]{:S(2)}) %collective-permute-start.13) | collective-permute-done | bytes 65568 | tf_op jit(solution)/shard_map/ppermute | solution.py:38
  20.6 1.5 %collective-permute-start.14 = (bf16[256,128]{1,0:T(8,128)(2,1)S(1)}, bf16[256,128]{1,0:T(8,128)(2,1)S(1)}, u32[]{:S(2)}, u32[]{:S(2)}) collective-permute-start(bf16[256,128]{1,0:T(8,128)(2,1)S(1)} %shard_map.154.s3), channel_id=1, source_target_pairs={{0,4},{2,6},{4,0},{6,2},{8,12},{10,14},{12,8},{14,10},{16,20},{18,... | collective-permute-start | bytes 196616 | tf_op jit(solution)/shard_map/ppermute | solution.py:38
  22.2 0.7 %collective-permute-start.8 = (bf16[256,128]{1,0:T(8,128)(2,1)S(1)}, bf16[256,128]{1,0:T(8,128)(2,1)S(1)}, u32[]{:S(2)}, u32[]{:S(2)}) collective-permute-start(bf16[256,128]{1,0:T(8,128)(2,1)S(1)} %shard_map.153.w2), channel_id=1, source_target_pairs={{0,4},{2,6},{4,0},{6,2},{8,12},{10,14},{12,8},{14,10},{16,20},{18,... | collective-permute-start | bytes 196616 | tf_op jit(solution)/shard_map/ppermute | solution.py:38
  22.8 1.2 %collective-permute-done.11.along_xo = bf16[64,384]{1,0:T(8,128)(2,1)S(1)} collective-permute-done((bf16[64,384]{1,0:T(8,128)(2,1)S(1)}, bf16[64,384]{1,0:T(8,128)(2,1)S(1)}, u32[]{:S(2)}, u32[]{:S(2)}) %collective-permute-start.11) | collective-permute-done | bytes 49184 | tf_op jit(solution)/shard_map/ppermute | solution.py:38
  24.1 0.9 %collective-permute-done.14.s3_y = bf16[256,128]{1,0:T(8,128)(2,1)S(1)} collective-permute-done((bf16[256,128]{1,0:T(8,128)(2,1)S(1)}, bf16[256,128]{1,0:T(8,128)(2,1)S(1)}, u32[]{:S(2)}, u32[]{:S(2)}) %collective-permute-start.14) | collective-permute-done | bytes 65568 | tf_op jit(solution)/shard_map/ppermute | solution.py:38
  24.9 1.6 %collective-permute-done.8.w2_y = bf16[256,128]{1,0:T(8,128)(2,1)S(1)} collective-permute-done((bf16[256,128]{1,0:T(8,128)(2,1)S(1)}, bf16[256,128]{1,0:T(8,128)(2,1)S(1)}, u32[]{:S(2)}, u32[]{:S(2)}) %collective-permute-start.8) | collective-permute-done | bytes 65568 | tf_op jit(solution)/shard_map/ppermute | solution.py:38
  26.5 0.6 %shard_map.155 = (bf16[64,128]{1,0:T(8,128)(2,1)S(1)}, bf16[64,128]{1,0:T(8,128)(2,1)S(1)}, bf16[256,128]{1,0:T(8,128)(2,1)S(1)}) custom-call(bf16[256,128]{1,0:T(8,128)(2,1)S(1)} %shard_map.153.w2, bf16[256,128]{1,0:T(8,128)(2,1)S(1)} %collective-permute-done.8.w2_y, bf16[64,384]{1,0:T(8,128)(2,1)S(1)} %get-tuple-element.46.along, ...), custom_call_target="tpu_custom_call" | custom-call | flops 33554432 | bytes 999424 | tf_op jit(solution)/shard_map/pallas_call | solution.py:25
  27.1 1.1 %collective-permute-start.15 = (bf16[256,128]{1,0:T(8,128)(2,1)S(1)}, bf16[256,128]{1,0:T(8,128)(2,1)S(1)}, u32[]{:S(2)}, u32[]{:S(2)}) collective-permute-start(bf16[256,128]{1,0:T(8,128)(2,1)S(1)} %get-tuple-element.50.v3), channel_id=1, source_target_pairs={{0,2},{2,0},{4,6},{6,4},{8,10},{10,8},{12,14},{14,12},{16,18},{18,... | collective-permute-start | bytes 196616 | tf_op jit(solution)/shard_map/ppermute | solution.py:38
  28.3 1.6 %collective-permute-start.16 = (bf16[256,128]{1,0:T(8,128)(2,1)S(1)}, bf16[256,128]{1,0:T(8,128)(2,1)S(1)}, u32[]{:S(2)}, u32[]{:S(2)}) collective-permute-start(bf16[256,128]{1,0:T(8,128)(2,1)S(1)} %get-tuple-element.50.v3), channel_id=1, source_target_pairs={{0,8},{2,10},{4,12},{6,14},{8,0},{10,2},{12,4},{14,6},{16,24},{18,... | collective-permute-start | bytes 196616 | tf_op jit(solution)/shard_map/ppermute | solution.py:38
  29.8 0.8 %collective-permute-start.17 = (bf16[256,128]{1,0:T(8,128)(2,1)S(1)}, bf16[256,128]{1,0:T(8,128)(2,1)S(1)}, u32[]{:S(2)}, u32[]{:S(2)}) collective-permute-start(bf16[256,128]{1,0:T(8,128)(2,1)S(1)} %get-tuple-element.50.v3), channel_id=1, source_target_pairs={{0,10},{2,8},{4,14},{6,12},{8,2},{10,0},{12,6},{14,4},{16,26},{18,... | collective-permute-start | bytes 196616 | tf_op jit(solution)/shard_map/ppermute | solution.py:38
  30.7 1.1 %collective-permute-start.18 = (bf16[128,128]{1,0:T(8,128)(2,1)S(1)}, bf16[128,128]{1,0:T(8,128)(2,1)S(1)}, u32[]{:S(2)}, u32[]{:S(2)}) collective-permute-start(bf16[128,128]{1,0:T(8,128)(2,1)S(1)} %get-tuple-element.52), channel_id=1, source_target_pairs={{0,2},{2,0},{4,6},{6,4},{8,10},{10,8},{12,14},{14,12},{16,18},{18,... | collective-permute-start | bytes 98312 | tf_op jit(solution)/shard_map/ppermute | solution.py:38
  31.7 1.0 %collective-permute-start.19 = (bf16[64,128]{1,0:T(8,128)(2,1)S(1)}, bf16[64,128]{1,0:T(8,128)(2,1)S(1)}, u32[]{:S(2)}, u32[]{:S(2)}) collective-permute-start(bf16[64,128]{1,0:T(8,128)(2,1)S(1)} %get-tuple-element.54), channel_id=1, source_target_pairs={{0,2},{2,0},{4,6},{6,4},{8,10},{10,8},{12,14},{14,12},{16,18},{18,... | collective-permute-start | bytes 49160 | tf_op jit(solution)/shard_map/ppermute | solution.py:38
  32.7 2.6 %collective-permute-done.18.sol1_x = bf16[128,128]{1,0:T(8,128)(2,1)S(1)} collective-permute-done((bf16[128,128]{1,0:T(8,128)(2,1)S(1)}, bf16[128,128]{1,0:T(8,128)(2,1)S(1)}, u32[]{:S(2)}, u32[]{:S(2)}) %collective-permute-start.18) | collective-permute-done | bytes 32800 | tf_op jit(solution)/shard_map/ppermute | solution.py:38
  35.7 0.4 collective-permute-start.20
  36.1 0.6 %collective-permute-done.2.got = bf16[256,256]{1,0:T(8,128)(2,1)S(1)} collective-permute-done((bf16[256,256]{1,0:T(8,128)(2,1)S(1)}, bf16[256,256]{1,0:T(8,128)(2,1)S(1)}, u32[]{:S(2)}, u32[]{:S(2)}) %collective-permute-start.2) | collective-permute-done | bytes 131104 | tf_op jit(solution)/shard_map/ppermute | solution.py:38
  36.7 0.7 %shard_map.149 = bf16[256,512]{1,0:T(8,128)(2,1)} custom-call(bf16[256,256]{1,0:T(8,128)(2,1)S(1)} %get-tuple-element.34.own.solved, bf16[256,256]{1,0:T(8,128)(2,1)S(1)} %collective-permute-done.2.got), custom_call_target="tpu_custom_call" | custom-call | bytes 524288 | tf_op jit(solution)/shard_map/pallas_call | solution.py:25
  37.4 0.7 %shard_map.157 = (bf16[128,512]{1,0:T(8,128)(2,1)}, bf16[64,512]{1,0:T(8,128)(2,1)}, bf16[32,512]{1,0:T(8,128)(2,1)}) custom-call(bf16[224,256]{1,0:T(8,128)(2,1)S(1)} %shard_map.156.own, bf16[224,256]{1,0:T(8,128)(2,1)S(1)} %collective-permute-done.20.got), custom_call_target="tpu_custom_call" | custom-call | bytes 458752 | tf_op jit(solution)/shard_map/pallas_call | solution.py:25
  (28 shorter events, 0.6 us)
Async XLA Ops:
  3.9 9.4 %copy-start.1 = (bf16[256,256]{1,0:T(8,128)(2,1)S(1)}, bf16[256,256]{1,0:T(8,128)(2,1)}, u32[]{:S(2)}) copy-start(bf16[256,256]{1,0:T(8,128)(2,1)} %inverse.5) | copy-start | bytes 393220
  3.9 9.4 %collective-permute-start.1 = (bf16[128,1152]{1,0:T(8,128)(2,1)S(1)}, bf16[128,1152]{1,0:T(8,128)(2,1)S(1)}, u32[]{:S(2)}, u32[]{:S(2)}) collective-permute-start(bf16[128,1152]{1,0:T(8,128)(2,1)S(1)} %get-tuple-element.33.across), channel_id=1, source_target_pairs={{0,1},{1,0},{2,3},{3,2},{4,5},{5,4},{6,7},{7,6},{8,9},{9,8},{10,11... | collective-permute-start | bytes 884744 | tf_op jit(solution)/shard_map/ppermute | solution.py:38
  4.5 8.9 %collective-permute-start = (bf16[2,256,256]{2,1,0:T(8,128)(2,1)S(1)}, bf16[2,256,256]{2,1,0:T(8,128)(2,1)S(1)}, u32[]{:S(2)}, u32[]{:S(2)}) collective-permute-start(bf16[2,256,256]{2,1,0:T(8,128)(2,1)S(1)} %get-tuple-element.32), channel_id=1, source_target_pairs={{0,1},{1,0},{2,3},{3,2},{4,5},{5,4},{6,7},{7,6},{8,9},{9,8},{10,11... | collective-permute-start | bytes 786440 | tf_op jit(solution)/shard_map/ppermute | solution.py:38
  5.5 12.9 %copy-start = (bf16[128,256]{1,0:T(8,128)(2,1)S(1)}, bf16[128,256]{1,0:T(8,128)(2,1)}, u32[]{:S(2)}) copy-start(bf16[128,256]{1,0:T(8,128)(2,1)} %inverse.6) | copy-start | bytes 196612
  5.5 9.8 %collective-permute-start.3 = (bf16[2,256,256]{2,1,0:T(8,128)(2,1)S(1)}, bf16[2,256,256]{2,1,0:T(8,128)(2,1)S(1)}, u32[]{:S(2)}, u32[]{:S(2)}) collective-permute-start(bf16[2,256,256]{2,1,0:T(8,128)(2,1)S(1)} %get-tuple-element.39), channel_id=1, source_target_pairs={{0,1},{1,0},{2,3},{3,2},{4,5},{5,4},{6,7},{7,6},{8,9},{9,8},{10,11... | collective-permute-start | bytes 786440 | tf_op jit(solution)/shard_map/ppermute | solution.py:38
  6.0 4.8 %collective-permute-start.9 = (bf16[64,384]{1,0:T(8,128)(2,1)S(1)}, bf16[64,384]{1,0:T(8,128)(2,1)S(1)}, u32[]{:S(2)}, u32[]{:S(2)}) collective-permute-start(bf16[64,384]{1,0:T(8,128)(2,1)S(1)} %get-tuple-element.46.along), channel_id=1, source_target_pairs={{0,2},{2,0},{4,6},{6,4},{8,10},{10,8},{12,14},{14,12},{16,18},{18,... | collective-permute-start | bytes 147464 | tf_op jit(solution)/shard_map/ppermute | solution.py:38
  8.5 4.8 %collective-permute-start.6 = (bf16[192,256]{1,0:T(8,128)(2,1)S(1)}, bf16[192,256]{1,0:T(8,128)(2,1)S(1)}, u32[]{:S(2)}, u32[]{:S(2)}) collective-permute-start(bf16[192,256]{1,0:T(8,128)(2,1)S(1)} %get-tuple-element.44.along), channel_id=1, source_target_pairs={{0,2},{2,0},{4,6},{6,4},{8,10},{10,8},{12,14},{14,12},{16,18},{18,... | collective-permute-start | bytes 294920 | tf_op jit(solution)/shard_map/ppermute | solution.py:38
  10.8 6.8 %collective-permute-start.10 = (bf16[128,384]{1,0:T(8,128)(2,1)S(1)}, bf16[128,384]{1,0:T(8,128)(2,1)S(1)}, u32[]{:S(2)}, u32[]{:S(2)}) collective-permute-start(bf16[128,384]{1,0:T(8,128)(2,1)S(1)} %pad_maximum_fusion), channel_id=1, source_target_pairs={{0,4},{2,6},{4,0},{6,2},{8,12},{10,14},{12,8},{14,10},{16,20},{18,... | collective-permute-start | bytes 294920 | tf_op jit(solution)/shard_map/ppermute | solution.py:38
  13.3 4.3 %collective-permute-start.7 = (bf16[192,256]{1,0:T(8,128)(2,1)S(1)}, bf16[192,256]{1,0:T(8,128)(2,1)S(1)}, u32[]{:S(2)}, u32[]{:S(2)}) collective-permute-start(bf16[192,256]{1,0:T(8,128)(2,1)S(1)} %collective-permute-done.6.along_x), channel_id=1, source_target_pairs={{0,1},{1,0},{2,3},{3,2},{4,5},{5,4},{6,7},{7,6},{8,9},{9,8},{10,11... | collective-permute-start | bytes 294920 | tf_op jit(solution)/shard_map/ppermute | solution.py:38
  13.8 21.7 %copy-start.2 = (bf16[32,256]{1,0:T(8,128)(2,1)S(1)}, bf16[32,256]{1,0:T(8,128)(2,1)}, u32[]{:S(2)}) copy-start(bf16[32,256]{1,0:T(8,128)(2,1)} %inverse.7) | copy-start | bytes 49156
  13.8 4.6 %collective-permute-start.5 = (bf16[256,128]{1,0:T(8,128)(2,1)S(1)}, bf16[256,128]{1,0:T(8,128)(2,1)S(1)}, u32[]{:S(2)}, u32[]{:S(2)}) collective-permute-start(bf16[256,128]{1,0:T(8,128)(2,1)S(1)} %get-tuple-element.43), channel_id=1, source_target_pairs={{0,2},{2,0},{4,6},{6,4},{8,10},{10,8},{12,14},{14,12},{16,18},{18,... | collective-permute-start | bytes 196616 | tf_op jit(solution)/shard_map/ppermute | solution.py:38
  15.6 5.0 %collective-permute-start.13 = (bf16[256,128]{1,0:T(8,128)(2,1)S(1)}, bf16[256,128]{1,0:T(8,128)(2,1)S(1)}, u32[]{:S(2)}, u32[]{:S(2)}) collective-permute-start(bf16[256,128]{1,0:T(8,128)(2,1)S(1)} %get-tuple-element.48), channel_id=1, source_target_pairs={{0,2},{2,0},{4,6},{6,4},{8,10},{10,8},{12,14},{14,12},{16,18},{18,... | collective-permute-start | bytes 196616 | tf_op jit(solution)/shard_map/ppermute | solution.py:38
  16.3 5.8 %collective-permute-start.4 = (bf16[256,128]{1,0:T(8,128)(2,1)S(1)}, bf16[256,128]{1,0:T(8,128)(2,1)S(1)}, u32[]{:S(2)}, u32[]{:S(2)}) collective-permute-start(bf16[256,128]{1,0:T(8,128)(2,1)S(1)} %get-tuple-element.41), channel_id=1, source_target_pairs={{0,2},{2,0},{4,6},{6,4},{8,10},{10,8},{12,14},{14,12},{16,18},{18,... | collective-permute-start | bytes 196616 | tf_op jit(solution)/shard_map/ppermute | solution.py:38
  17.7 6.4 %collective-permute-start.12 = (bf16[128,384]{1,0:T(8,128)(2,1)S(1)}, bf16[128,384]{1,0:T(8,128)(2,1)S(1)}, u32[]{:S(2)}, u32[]{:S(2)}) collective-permute-start(bf16[128,384]{1,0:T(8,128)(2,1)S(1)} %collective-permute-done.10.side), channel_id=1, source_target_pairs={{0,1},{1,0},{2,3},{3,2},{4,5},{5,4},{6,7},{7,6},{8,9},{9,8},{10,11... | collective-permute-start | bytes 294920 | tf_op jit(solution)/shard_map/ppermute | solution.py:38
  20.6 4.3 %collective-permute-start.14 = (bf16[256,128]{1,0:T(8,128)(2,1)S(1)}, bf16[256,128]{1,0:T(8,128)(2,1)S(1)}, u32[]{:S(2)}, u32[]{:S(2)}) collective-permute-start(bf16[256,128]{1,0:T(8,128)(2,1)S(1)} %shard_map.154.s3), channel_id=1, source_target_pairs={{0,4},{2,6},{4,0},{6,2},{8,12},{10,14},{12,8},{14,10},{16,20},{18,... | collective-permute-start | bytes 196616 | tf_op jit(solution)/shard_map/ppermute | solution.py:38
  22.2 4.3 %collective-permute-start.8 = (bf16[256,128]{1,0:T(8,128)(2,1)S(1)}, bf16[256,128]{1,0:T(8,128)(2,1)S(1)}, u32[]{:S(2)}, u32[]{:S(2)}) collective-permute-start(bf16[256,128]{1,0:T(8,128)(2,1)S(1)} %shard_map.153.w2), channel_id=1, source_target_pairs={{0,4},{2,6},{4,0},{6,2},{8,12},{10,14},{12,8},{14,10},{16,20},{18,... | collective-permute-start | bytes 196616 | tf_op jit(solution)/shard_map/ppermute | solution.py:38
  22.8 1.2 %collective-permute-start.11 = (bf16[64,384]{1,0:T(8,128)(2,1)S(1)}, bf16[64,384]{1,0:T(8,128)(2,1)S(1)}, u32[]{:S(2)}, u32[]{:S(2)}) collective-permute-start(bf16[64,384]{1,0:T(8,128)(2,1)S(1)} %collective-permute-done.9.along_x), channel_id=1, source_target_pairs={{0,1},{1,0},{2,3},{3,2},{4,5},{5,4},{6,7},{7,6},{8,9},{9,8},{10,11... | collective-permute-start | bytes 147464 | tf_op jit(solution)/shard_map/ppermute | solution.py:38
  27.1 8.4 %collective-permute-start.15 = (bf16[256,128]{1,0:T(8,128)(2,1)S(1)}, bf16[256,128]{1,0:T(8,128)(2,1)S(1)}, u32[]{:S(2)}, u32[]{:S(2)}) collective-permute-start(bf16[256,128]{1,0:T(8,128)(2,1)S(1)} %get-tuple-element.50.v3), channel_id=1, source_target_pairs={{0,2},{2,0},{4,6},{6,4},{8,10},{10,8},{12,14},{14,12},{16,18},{18,... | collective-permute-start | bytes 196616 | tf_op jit(solution)/shard_map/ppermute | solution.py:38
  28.3 7.2 %collective-permute-start.16 = (bf16[256,128]{1,0:T(8,128)(2,1)S(1)}, bf16[256,128]{1,0:T(8,128)(2,1)S(1)}, u32[]{:S(2)}, u32[]{:S(2)}) collective-permute-start(bf16[256,128]{1,0:T(8,128)(2,1)S(1)} %get-tuple-element.50.v3), channel_id=1, source_target_pairs={{0,8},{2,10},{4,12},{6,14},{8,0},{10,2},{12,4},{14,6},{16,24},{18,... | collective-permute-start | bytes 196616 | tf_op jit(solution)/shard_map/ppermute | solution.py:38
  29.8 5.7 %collective-permute-start.17 = (bf16[256,128]{1,0:T(8,128)(2,1)S(1)}, bf16[256,128]{1,0:T(8,128)(2,1)S(1)}, u32[]{:S(2)}, u32[]{:S(2)}) collective-permute-start(bf16[256,128]{1,0:T(8,128)(2,1)S(1)} %get-tuple-element.50.v3), channel_id=1, source_target_pairs={{0,10},{2,8},{4,14},{6,12},{8,2},{10,0},{12,6},{14,4},{16,26},{18,... | collective-permute-start | bytes 196616 | tf_op jit(solution)/shard_map/ppermute | solution.py:38
  30.7 4.6 %collective-permute-start.18 = (bf16[128,128]{1,0:T(8,128)(2,1)S(1)}, bf16[128,128]{1,0:T(8,128)(2,1)S(1)}, u32[]{:S(2)}, u32[]{:S(2)}) collective-permute-start(bf16[128,128]{1,0:T(8,128)(2,1)S(1)} %get-tuple-element.52), channel_id=1, source_target_pairs={{0,2},{2,0},{4,6},{6,4},{8,10},{10,8},{12,14},{14,12},{16,18},{18,... | collective-permute-start | bytes 98312 | tf_op jit(solution)/shard_map/ppermute | solution.py:38
  31.7 3.7 %collective-permute-start.19 = (bf16[64,128]{1,0:T(8,128)(2,1)S(1)}, bf16[64,128]{1,0:T(8,128)(2,1)S(1)}, u32[]{:S(2)}, u32[]{:S(2)}) collective-permute-start(bf16[64,128]{1,0:T(8,128)(2,1)S(1)} %get-tuple-element.54), channel_id=1, source_target_pairs={{0,2},{2,0},{4,6},{6,4},{8,10},{10,8},{12,14},{14,12},{16,18},{18,... | collective-permute-start | bytes 49160 | tf_op jit(solution)/shard_map/ppermute | solution.py:38
  35.3 1.3 %collective-permute-start.2 = (bf16[256,256]{1,0:T(8,128)(2,1)S(1)}, bf16[256,256]{1,0:T(8,128)(2,1)S(1)}, u32[]{:S(2)}, u32[]{:S(2)}) collective-permute-start(bf16[256,256]{1,0:T(8,128)(2,1)S(1)} %get-tuple-element.34.own.solved), channel_id=1, source_target_pairs={{0,1},{1,0},{2,3},{3,2},{4,5},{5,4},{6,7},{7,6},{8,9},{9,8},{10,11... | collective-permute-start | bytes 393224 | tf_op jit(solution)/shard_map/ppermute | solution.py:38
  35.7 1.7 %collective-permute-start.20 = (bf16[224,256]{1,0:T(8,128)(2,1)S(1)}, bf16[224,256]{1,0:T(8,128)(2,1)S(1)}, u32[]{:S(2)}, u32[]{:S(2)}) collective-permute-start(bf16[224,256]{1,0:T(8,128)(2,1)S(1)} %shard_map.156.own), channel_id=1, source_target_pairs={{0,1},{1,0},{2,3},{3,2},{4,5},{5,4},{6,7},{7,6},{8,9},{9,8},{10,11... | collective-permute-start | bytes 344072 | tf_op jit(solution)/shard_map/ppermute | solution.py:38

commit v4 on v3

v4 whole, which is shorter than its diff:
```python
import jax
import jax.numpy as jnp
from jax import lax
from jax.experimental import pallas as pl
from jax.experimental.pallas import tpu as pltpu
from jax.sharding import PartitionSpec as P

F32, BF16 = jnp.float32, jnp.bfloat16
WHOLE = pl.BlockSpec(memory_space=pltpu.VMEM)
SCALARS = pl.BlockSpec(memory_space=pltpu.SMEM)


def dot(a, b):
    return jnp.dot(a, b, preferred_element_type=F32)


def dot_t(a, b):
    return lax.dot_general(a, b, (((0,), (0,)), ((), ())), preferred_element_type=F32)


def call(kernel, outs, *args, scratch=(), flops=0, specs=None):
    outs = [jax.ShapeDtypeStruct(shape, dtype) for shape, dtype in outs]
    moved = sum(a.size * a.dtype.itemsize for a in (*args, *outs))
    single = len(outs) == 1
    return pl.pallas_call(
        kernel,
        out_shape=outs[0] if single else outs,
        in_specs=specs or [WHOLE] * len(args),
        out_specs=WHOLE if single else [WHOLE] * len(outs),
        scratch_shapes=list(scratch),
        cost_estimate=pl.CostEstimate(flops=flops, bytes_accessed=moved, transcendentals=0),
        compiler_params=pltpu.CompilerParams(vmem_limit_bytes=16 << 20),
    )(*args)


def swap(block, axis, stride):
    count = lax.axis_size(axis)
    return lax.ppermute(block, axis, [(low, low ^ stride) for low in range(count)])


def own_and_other(part):
    me = lax.axis_index("row")
    return (
        pl.ds(pl.multiple_of(me * part, part), part),
        pl.ds(pl.multiple_of((1 - me) * part, part), part),
    )


def prepare(lower_0, lower_1, lower_2t, pattern, inv_1, inv_2, pack, first, along):
    rows = lower_0.shape[1]
    blocks = pattern.shape[1]
    spread = rows // blocks
    n0, n1 = lower_0.shape[0], lower_1.shape[0]
    part_1, part_2 = lower_1.shape[2], lower_2t.shape[1]
    for b in range(blocks):
        at = pl.ds(b * spread, spread)
        for m in range(n0):
            factor = pattern[0, b, m].astype(BF16)
            pack[pl.ds(first + m * rows + b * spread, spread), :] = lower_0[m, at, :] * factor
        for m in range(n1):
            factor = pattern[0, b, n0 + m].astype(BF16)
            masked = lower_1[m, at, :] * factor
            lanes = pl.ds(m * part_1, part_1)
            pack[pl.ds(first + n0 * rows + b * spread, spread), lanes] = masked
            along[at, lanes] = masked
    lane = lax.broadcasted_iota(jnp.int32, (1, rows), 1) // spread
    keep = jnp.zeros((1, rows), F32)
    for b in range(blocks):
        keep = jnp.where(lane == b, pattern[0, b, n0 + n1].astype(F32), keep)
    short = part_2 // 2
    cut = part_1 // 2
    last = rows + cut + part_2
    for i in range(2):
        masked = (lower_2t[0, pl.ds(i * short, short), :].astype(F32) * keep).astype(BF16)
        pack[pl.ds(first + (n0 + 1) * rows, short), pl.ds(i * rows, rows)] = masked
        along[pl.ds(last, short), pl.ds(i * rows, rows)] = masked
    mine, _ = own_and_other(cut)
    along[pl.ds(rows, cut), :] = inv_1[mine, :]
    along[pl.ds(rows + cut, part_2), :] = inv_2[...]


def leaf_sum(m, solved, lower, rhs, keep, send, total):
    leaves = lower.shape[1]
    mine, _ = own_and_other(rhs.shape[2])
    own, other = own_and_other(keep.shape[2])
    acc = dot(lower[m, 0], solved[0])
    for v in range(1, leaves):
        acc = acc + dot(lower[m, v], solved[v])
    total[...] = -acc
    total[mine, :] = total[mine, :] + rhs[m, 0].astype(F32)
    keep[m] = total[:, own]
    size = total.shape[0]
    send[pl.ds(m * size, size), :] = total[:, other].astype(BF16)


def opening(
    inverse, right, lower, rhs, lower_0, lower_1, lower_2t, pattern, inv_1, inv_2,
    solved, keep, pack, along, lower_late, rhs_late,
    total, inverse_v, right_v, lower_v, rhs_v, low0_v, low1_v, low2_v, inv1_v, inv2_v, pattern_s, sems,
):
    leaves, size, _ = inverse.shape
    early = keep.shape[0]
    late = lower_late.shape[0]
    copies = []

    def fetch(source, target):
        copy = pltpu.make_async_copy(source, target, sems.at[len(copies)])
        copy.start()
        copies.append(copy)
        return copy

    leaf = []
    for v in range(leaves):
        leaf.append((fetch(inverse.at[v], inverse_v.at[v]), fetch(right.at[v], right_v.at[v])))
    sums = [fetch(lower.at[0], lower_v.at[0]), fetch(rhs.at[pl.ds(0, early)], rhs_v)]
    small = [
        fetch(source, target)
        for source, target in (
            (lower_0, low0_v), (lower_1, low1_v), (lower_2t, low2_v), (pattern, pattern_s),
            (inv_1, inv1_v), (inv_2, inv2_v),
        )
    ]
    small += [fetch(lower.at[m], lower_v.at[m]) for m in range(1, early)]
    last = [
        fetch(lower.at[pl.ds(early, late)], lower_late),
        fetch(rhs.at[pl.ds(early, late)], rhs_late),
    ]
    for v in range(leaves):
        for copy in leaf[v]:
            copy.wait()
        solved[v] = dot(inverse_v[v], right_v[v]).astype(BF16)
    for copy in sums:
        copy.wait()
    leaf_sum(0, solved, lower_v, rhs_v, keep, pack, total)
    for copy in small:
        copy.wait()
    prepare(low0_v, low1_v, low2_v, pattern_s, inv1_v, inv2_v, pack, early * size, along)
    for m in range(1, early):
        leaf_sum(m, solved, lower_v, rhs_v, keep, pack, total)
    for copy in last:
        copy.wait()


def leaf_b(solved, lower, rhs, keep, send, total):
    for m in range(lower.shape[0]):
        leaf_sum(m, solved, lower, rhs, keep, send, total)


def quarters(half):
    part = half // 2
    bit = lax.rem(lax.axis_index("col"), 2)
    return (
        pl.ds(pl.multiple_of(bit * part, part), part),
        pl.ds(pl.multiple_of((1 - bit) * part, part), part),
    )


def zero_a(keep, pack, pack_o, inverse, solved_out, kept, sent, total):
    size = inverse.shape[1]
    rows = size // 2
    early = keep.shape[0]
    residual = (keep[0] + pack_o[pl.ds(0, size), :].astype(F32)).astype(BF16)
    solved = dot(inverse[...], residual).astype(BF16)
    solved_out[...] = solved
    total[...] = keep[1] + pack_o[pl.ds(size, size), :].astype(F32)
    for ref, at in zip((pack, pack_o), own_and_other(rows)):
        total[at, :] = total[at, :] - dot(ref[pl.ds(early * size, rows), :], solved)
    own, other = quarters(total.shape[1])
    kept[...] = total[:, own]
    sent[...] = total[:, other].astype(BF16)


def zero_b(keep, got, solved, pack, pack_o, kept, sent, total):
    size = solved.shape[0]
    rows = size // 2
    first = 2 * size + rows
    own, other = quarters(total.shape[1])
    for m in range(keep.shape[0]):
        total[...] = keep[m] + got[pl.ds(m * size, size), :].astype(F32)
        for ref, at in zip((pack, pack_o), own_and_other(rows)):
            total[at, :] = total[at, :] - dot(ref[pl.ds(first + m * rows, rows), :], solved[...])
        kept[m] = total[:, own]
        sent[m] = total[:, other].astype(BF16)


def one(kept, got, inverse, pack, pack_o, along, along_x, along_xo, solved_own, solved_x, u):
    size, part = kept.shape[0], inverse.shape[0]
    rows = size // 2
    first = 2 * size + 3 * rows
    residual = (kept[...] + got[...].astype(F32)).astype(BF16)
    solved_own[...] = dot(inverse[...], residual).astype(BF16)
    cut = part // 2
    for ref, at in zip((along_x, along_xo), own_and_other(cut)):
        solved_x[at, :] = dot(ref[pl.ds(rows, cut), :], residual).astype(BF16)
    own, other = solved_own[...], solved_x[...]
    for m in range(u.shape[0]):
        lanes = pl.ds(m * part, part)
        for ref, ref_x, at in zip((pack, pack_o), (along_x, along_xo), own_and_other(rows)):
            u[m, at, :] = dot(ref[pl.ds(first, rows), lanes], own) + dot(ref_x[pl.ds(0, rows), lanes], other)


def stack(along, along_x, out):
    part = out.shape[0] // 2
    at = pl.ds(along.shape[0] - part, part)
    out[pl.ds(0, part), :] = along[at, :]
    out[pl.ds(part, part), :] = along_x[at, :]


def differences(kept, got, update, out):
    out[...] = (kept[...] + got[...].astype(F32) - update[...]).astype(BF16)


def two(w, w_y, pack, pack_o, along, along_x, along_xo, side, side_o, sol1_x, solved_own, v3, to_x):
    size = w.shape[1]
    rows = size // 2
    part = solved_own.shape[0]
    short = part // 2
    residual = (w[0].astype(F32) + w_y[0].astype(F32)).astype(BF16)
    top = along.shape[0] - part - short
    step = part + short
    inverses = ((along, top), (along_x, top), (side, 0), (side, step))
    mine_at = ((along, top + part), (along_x, top + part), (side, part), (side, step + part))
    their_at = (
        (pack_o, pack_o.shape[0] - short), (along_xo, top + part), (side_o, part), (side_o, step + part),
    )
    ranges = own_and_other(rows)
    total = [w[1, at, :].astype(F32) + w_y[1, at, :].astype(F32) for at in ranges]
    for i, (ref, at) in enumerate(inverses):
        solved = dot(ref[pl.ds(at, part), :], residual).astype(BF16)
        if i == 0:
            solved_own[...] = solved
        if i == 1:
            to_x[pl.ds(size + rows, part), :] = solved
        for j, (low, start) in enumerate((mine_at[i], their_at[i])):
            block = low[pl.ds(start, short), :]
            total[j] = total[j] - dot_t(block[:, :rows], solved[:short]) - dot_t(block[:, rows:], solved[short:])
    for at, value in zip(ranges, total):
        v3[at, :] = value.astype(BF16)
        to_x[at, :] = value.astype(BF16)
    to_x[pl.ds(size, rows), :] = sol1_x[...]


def three(v3, v3_z, v3_xz, from_x, inverse, sol1, sol2, out, full):
    size = v3.shape[0]
    own, other = quarters(out.shape[1])
    full[:, own] = (v3[...].astype(F32) + v3_z[...].astype(F32)).astype(BF16)
    full[:, other] = (from_x[pl.ds(0, size), :].astype(F32) + v3_xz[...].astype(F32)).astype(BF16)
    n1, n2 = sol1.shape[0], sol2.shape[0]
    out[pl.ds(0, n1), own] = sol1[...]
    out[pl.ds(n1, n2), own] = sol2[...]
    out[pl.ds(0, n1 + n2), other] = from_x[pl.ds(size, n1 + n2), :]
    out[pl.ds(n1 + n2, inverse.shape[0]), :] = dot(inverse[...], full[...]).astype(BF16)


def join(own, got, *outs):
    mine, theirs = own_and_other(own.shape[1])
    first = 0
    for out in outs:
        at = pl.ds(first, out.shape[0])
        out[:, mine] = own[at, :]
        out[:, theirs] = got[at, :]
        first += out.shape[0]


def body(
    rhs, leaf_rhs, leaf_inverse, leaf_lower,
    inverse_0, inverse_1, inverse_2, inverse_3,
    lower_0, lower_1, lower_2, sparsity,
):
    levels, _, rows, width = rhs.shape
    leaves, size, _ = leaf_inverse.shape
    half = width // lax.axis_size("row")
    n0 = lower_0.shape[0]
    part_1, part_2 = inverse_1.shape[0], inverse_2.shape[0]
    full = [pltpu.VMEM((size, width), F32)]

    early = 2
    late = levels - early
    lower_2t, pattern = jnp.swapaxes(lower_2, 1, 2), jnp.transpose(sparsity, (1, 2, 0))
    sources = (leaf_inverse, leaf_rhs, leaf_lower, rhs, lower_0, lower_1, lower_2t, pattern, inverse_1, inverse_2)
    short = part_2 // 2
    solved_leaf, keep_a, pack, along, lower_late, rhs_late = call(
        opening,
        [
            ((leaves, size, width), BF16),
            ((early, size, half), F32),
            ((early * size + (n0 + 1) * rows + short, half), BF16),
            ((rows + part_1 // 2 + part_2 + short, half), BF16),
            ((late, leaves, size, size), BF16),
            ((late, 1, rows, width), BF16),
        ],
        *(pltpu.with_memory_space_constraint(x, pltpu.HBM) for x in sources),
        specs=[pl.BlockSpec(memory_space=pltpu.HBM)] * len(sources),
        scratch=[pltpu.VMEM((size, width), F32)]
        + [pltpu.VMEM(x.shape, BF16) for x in (leaf_inverse, leaf_rhs)]
        + [pltpu.VMEM((early, *x.shape[1:]), BF16) for x in (leaf_lower, rhs)]
        + [pltpu.VMEM(x.shape, BF16) for x in (lower_0, lower_1, lower_2t, inverse_1, inverse_2)]
        + [pltpu.SMEM(pattern.shape, jnp.int32), pltpu.SemaphoreType.DMA((2 * leaves + early + 9,))],
        flops=6 * leaves * size * size * width,
    )
    pack_o = swap(pack, "row", 1)
    along_x = swap(along, "col", 1)
    keep_b, send_b = call(
        leaf_b,
        [((late, size, half), F32), ((late * size, half), BF16)],
        solved_leaf, lower_late, rhs_late,
        scratch=full, flops=2 * late * leaves * size * size * width,
    )
    got_b = swap(send_b, "row", 1)
    quarter = half // 2
    square = pltpu.VMEM((size, half), F32)
    sol0, kept1, sent1 = call(
        zero_a, [((size, half), BF16), ((size, quarter), F32), ((size, quarter), BF16)],
        keep_a, pack, pack_o, inverse_0,
        scratch=[square], flops=4 * size * size * half,
    )
    got1 = swap(sent1, "col", 1)
    kept23, sent23 = call(
        zero_b, [((late, size, quarter), F32), ((late, size, quarter), BF16)],
        keep_b, got_b, sol0, pack, pack_o,
        scratch=[square], flops=4 * size * size * half,
    )
    got23 = swap(sent23, "col", 1)
    along_xo = swap(along_x, "row", 1)
    side = swap(call(stack, [((2 * (part_2 + short), half), BF16)], along, along_x), "col", 2)
    sol1, sol1_for_x, u = call(
        one, [((part_1, quarter), BF16)] * 2 + [((late, size, quarter), F32)],
        kept1, got1, inverse_1, pack, pack_o, along, along_x, along_xo,
        flops=6 * size * size * quarter,
    )
    w = call(differences, [((late, size, quarter), BF16)], kept23, got23, u)
    w_y = swap(w, "col", 2)
    sol0_o = swap(sol0, "row", 1)
    side_o = swap(side, "row", 1)
    out0 = call(join, [((size, width), BF16)], sol0, sol0_o)
    sol2, v3, to_x = call(
        two,
        [((part_2, quarter), BF16), ((size, quarter), BF16), ((size + part_1 + part_2, quarter), BF16)],
        w, w_y, pack, pack_o, along, along_x, along_xo, side, side_o, sol1_for_x,
        flops=4 * size * size * quarter,
    )
    v3_xz = swap(v3, "col", 5)
    from_x = swap(to_x, "col", 1)
    v3_z = swap(v3, "col", 4)
    part_3 = inverse_3.shape[0]
    last = call(
        three, [((part_1 + part_2 + part_3, half), BF16)],
        v3, v3_z, v3_xz, from_x, inverse_3, sol1, sol2,
        scratch=[pltpu.VMEM((size, half), BF16)], flops=2 * inverse_3.size * half,
    )
    last_o = swap(last, "row", 1)
    rest = call(join, [((part, width), BF16) for part in (part_1, part_2, part_3)], last, last_o)
    return (out0, *rest)


def solution(mesh):
    return jax.shard_map(
        body,
        mesh=mesh,
        in_specs=(
            P(None, "col", "row", None),
            P(("col", "row"), None, None),
            P(("col", "row"), None, None),
            P(None, ("col", "row"), None, None),
            P("col", None),
            P("col", None),
            P("col", None),
            P("col", None),
            P(None, "row", "col"),
            P(None, "row", "col"),
            P(None, "row", "col"),
            P(None, "col", "row"),
        ),
        out_specs=(P("col", None), P("col", None), P("col", None), P("col", None)),
        check_vma=False,
    )
```

time: 38.3 us -> 38.1 us (level)
  starting transfers between devices: 17.3 us -> 13 us
  waiting for transfers between devices: 12.4 us -> 16.4 us
    ppermute x21 -> x14, starting transfers between devices: 17.3 us -> 13 us  [swap(): lax.ppermute(block, axis, [(low, low ^ stride) for low in range(count)])]
    ppermute x21 -> x14, waiting for transfers between devices: 12.4 us -> 16.4 us  [swap(): lax.ppermute(block, axis, [(low, low ^ stride) for low in range(count)])]
  transfers between devices with their start and end apart: 21 -> 14, of which waited for: 10 -> 7; matrix products, arithmetic and copies ran while one was open for 0% -> 0% of each run, Pallas kernels for 8% -> 8%
where the time goes in v4:
time: 38.1 us; the launch traced here: 37.9 us
  waiting for transfers between devices  16.4 us (43%)
  starting transfers between devices  13 us (34%)
  Pallas kernels  7.81 us (20%)
  between operations  0.74 us (2%)
    ppermute x14, waiting for transfers between devices, swap(): lax.ppermute(block, axis, [(low, low ^ stride) for low in range(count)])  16.4 us
    ppermute x14, starting transfers between devices, swap(): lax.ppermute(block, axis, [(low, low ^ stride) for low in range(count)])  13 us
    pallas_call x11, Pallas kernels, call(): pl.pallas_call(kernel, out_shape=outs[0] if single else outs, in_specs=sp...  7.81 us
  transfers between devices with their start and end apart: 14, of which 7 were waited for; matrix products, arithmetic and copies ran while one was open for 0% of the time, Pallas kernels for 8%

profile of v4, /device:TPU:0, one launch (start us, length us, event | category | flops | bytes accessed | tf_op | source)
XLA Modules:
  0.0 37.9 jit_solution(9602580639957919239)
XLA Ops:
  0.6 3.2 %shard_map.147 = (bf16[4,256,512]{2,1,0:T(8,128)(2,1)S(1)}, f32[2,256,256]{2,1,0:T(8,128)S(1)}, bf16[1056,256]{1,0:T(8,128)(2,1)S(1)}, bf16[288,256]{1,0:T(8,128...) custom-call(bf16[4,256,256]{2,1,0:T(8,128)(2,1)} %inverse.4, ...), custom_call_target="tpu_custom_call" | custom-call | flops 805306368 | bytes 8142944 | tf_op jit(solution)/shard_map/pallas_call | solution.py:25
  3.8 0.0 copy-start.1
  3.8 0.6 %collective-permute-start = (bf16[1056,256]{1,0:T(8,128)(2,1)S(1)}, bf16[1056,256]{1,0:T(8,128)(2,1)S(1)}, u32[]{:S(2)}, u32[]{:S(2)}) collective-permute-start(bf16[1056,256]{1,0:T(8,128)(2,1)S(1)} %get-tuple-element.27.pack), channel_id=1, source_target_pairs={{0,1},{1,0},{2,3},{3,2},{4,5},{5,4},{6,7},{7,6},{8,9},{9,8},{10,11... | collective-permute-start | bytes 1622024 | tf_op jit(solution)/shard_map/ppermute | solution.py:38
  4.4 0.9 %shard_map.150 = (f32[2,256,256]{2,1,0:T(8,128)S(1)}, bf16[512,256]{1,0:T(8,128)(2,1)S(1)}) custom-call(bf16[4,256,512]{2,1,0:T(8,128)(2,1)S(1)} %get-tuple-element.29.solved, bf16[2,4,256,256]{3,2,1,0:T(8,128)(2,1)S(1)} %get-tuple-element.30.lower, bf16[2,1,128,512]{3,2,1,0:T(8,128)(2,1)S(1)} %get-tuple-element.31.rhs), custom_call_target="tpu_custom_call" | custom-call | flops 536870912 | bytes 3145728 | tf_op jit(solution)/shard_map/pallas_call | solution.py:25
  5.3 0.0 copy-start
  5.3 0.1 collective-permute-start.2
  5.4 3.0 %collective-permute-start.5 = (bf16[288,256]{1,0:T(8,128)(2,1)S(1)}, bf16[288,256]{1,0:T(8,128)(2,1)S(1)}, u32[]{:S(2)}, u32[]{:S(2)}) collective-permute-start(bf16[288,256]{1,0:T(8,128)(2,1)S(1)} %get-tuple-element.38.along), channel_id=1, source_target_pairs={{0,2},{2,0},{4,6},{6,4},{8,10},{10,8},{12,14},{14,12},{16,18},{18,... | collective-permute-start | bytes 442376 | tf_op jit(solution)/shard_map/ppermute | solution.py:38
  8.4 4.1 %collective-permute-done.5.along_x = bf16[288,256]{1,0:T(8,128)(2,1)S(1)} collective-permute-done((bf16[288,256]{1,0:T(8,128)(2,1)S(1)}, bf16[288,256]{1,0:T(8,128)(2,1)S(1)}, u32[]{:S(2)}, u32[]{:S(2)}) %collective-permute-start.5) | collective-permute-done | bytes 147488 | tf_op jit(solution)/shard_map/ppermute | solution.py:38
  12.5 0.0 collective-permute-done.pack_o
  12.5 0.4 %shard_map.148 = (bf16[256,256]{1,0:T(8,128)(2,1)S(1)}, f32[256,128]{1,0:T(8,128)S(1)}, bf16[256,128]{1,0:T(8,128)(2,1)S(1)}) custom-call(f32[2,256,256]{2,1,0:T(8,128)S(1)} %get-tuple-element.26.keep, bf16[1056,256]{1,0:T(8,128)(2,1)S(1)} %get-tuple-element.27.pack, bf16[1056,256]{1,0:T(8,128)(2,1)S(1)} %collective-permute-done.pack_o, ...), custom_call_target="tpu_custom_call" | custom-call | flops 67108864 | bytes 2064384 | tf_op jit(solution)/shard_map/pallas_call | solution.py:25
  12.9 0.0 collective-permute-done.2.got
  12.9 0.4 %shard_map.151 = (f32[2,256,128]{2,1,0:T(8,128)S(1)}, bf16[2,256,128]{2,1,0:T(8,128)(2,1)S(1)}) custom-call(f32[2,256,256]{2,1,0:T(8,128)S(1)} %get-tuple-element.32.keep, bf16[512,256]{1,0:T(8,128)(2,1)S(1)} %collective-permute-done.2.got, bf16[256,256]{1,0:T(8,128)(2,1)S(1)} %get-tuple-element.28.own.solved, bf16[1056,256]{1,0:T(8,128)(2,1)S(1)} %get-tuple-element.27.pack, ...), custom_call_target="tpu_custom_call" | custom-call | flops 67108864 | bytes 2392064 | tf_op jit(solution)/shard_map/pallas_call | solution.py:25
  13.4 1.8 %collective-permute-start.3 = (bf16[2,256,128]{2,1,0:T(8,128)(2,1)S(1)}, bf16[2,256,128]{2,1,0:T(8,128)(2,1)S(1)}, u32[]{:S(2)}, u32[]{:S(2)}) collective-permute-start(bf16[2,256,128]{2,1,0:T(8,128)(2,1)S(1)} %get-tuple-element.35), channel_id=1, source_target_pairs={{0,2},{2,0},{4,6},{6,4},{8,10},{10,8},{12,14},{14,12},{16,18},{18,... | collective-permute-start | bytes 393224 | tf_op jit(solution)/shard_map/ppermute | solution.py:38
  15.2 0.3 collective-permute-start.4
  15.5 1.8 %collective-permute-start.8 = (bf16[192,256]{1,0:T(8,128)(2,1)S(1)}, bf16[192,256]{1,0:T(8,128)(2,1)S(1)}, u32[]{:S(2)}, u32[]{:S(2)}) collective-permute-start(bf16[192,256]{1,0:T(8,128)(2,1)S(1)} %shard_map.154), channel_id=1, source_target_pairs={{0,4},{2,6},{4,0},{6,2},{8,12},{10,14},{12,8},{14,10},{16,20},{18,... | collective-permute-start | bytes 294920 | tf_op jit(solution)/shard_map/ppermute | solution.py:38
  17.3 0.0 collective-permute-done.6.along_xo
  17.3 3.4 %collective-permute-done.4.got = bf16[256,128]{1,0:T(8,128)(2,1)S(1)} collective-permute-done((bf16[256,128]{1,0:T(8,128)(2,1)S(1)}, bf16[256,128]{1,0:T(8,128)(2,1)S(1)}, u32[]{:S(2)}, u32[]{:S(2)}) %collective-permute-start.4) | collective-permute-done | bytes 65568 | tf_op jit(solution)/shard_map/ppermute | solution.py:38
  20.7 0.4 %shard_map.152 = (bf16[128,128]{1,0:T(8,128)(2,1)S(1)}, bf16[128,128]{1,0:T(8,128)(2,1)S(1)}, f32[2,256,128]{2,1,0:T(8,128)S(1)}) custom-call(f32[256,128]{1,0:T(8,128)S(1)} %get-tuple-element.36.kept, bf16[256,128]{1,0:T(8,128)(2,1)S(1)} %collective-permute-done.4.got, bf16[128,256]{1,0:T(8,128)(2,1)S(1)} %copy-done, ...), custom_call_target="tpu_custom_call" | custom-call | flops 50331648 | bytes 2113536 | tf_op jit(solution)/shard_map/pallas_call | solution.py:25
  21.1 0.0 collective-permute-done.3.got
  21.2 1.8 %collective-permute-start.7 = (bf16[2,256,128]{2,1,0:T(8,128)(2,1)S(1)}, bf16[2,256,128]{2,1,0:T(8,128)(2,1)S(1)}, u32[]{:S(2)}, u32[]{:S(2)}) collective-permute-start(bf16[2,256,128]{2,1,0:T(8,128)(2,1)S(1)} %shard_map.153.w), channel_id=1, source_target_pairs={{0,4},{2,6},{4,0},{6,2},{8,12},{10,14},{12,8},{14,10},{16,20},{18,... | collective-permute-start | bytes 393224 | tf_op jit(solution)/shard_map/ppermute | solution.py:38
  23.0 1.3 %collective-permute-done.9.side_o = bf16[192,256]{1,0:T(8,128)(2,1)S(1)} collective-permute-done((bf16[192,256]{1,0:T(8,128)(2,1)S(1)}, bf16[192,256]{1,0:T(8,128)(2,1)S(1)}, u32[]{:S(2)}, u32[]{:S(2)}) %collective-permute-start.9) | collective-permute-done | bytes 98336 | tf_op jit(solution)/shard_map/ppermute | solution.py:38
  24.3 2.0 %collective-permute-done.7.w_y = bf16[2,256,128]{2,1,0:T(8,128)(2,1)S(1)} collective-permute-done((bf16[2,256,128]{2,1,0:T(8,128)(2,1)S(1)}, bf16[2,256,128]{2,1,0:T(8,128)(2,1)S(1)}, u32[]{:S(2)}, u32[]{:S(2)}) %collective-permute-start.7) | collective-permute-done | bytes 131104 | tf_op jit(solution)/shard_map/ppermute | solution.py:38
  26.3 0.8 %shard_map.155 = (bf16[64,128]{1,0:T(8,128)(2,1)S(1)}, bf16[256,128]{1,0:T(8,128)(2,1)S(1)}, bf16[448,128]{1,0:T(8,128)(2,1)S(1)}) custom-call(bf16[2,256,128]{2,1,0:T(8,128)(2,1)S(1)} %shard_map.153.w, bf16[2,256,128]{2,1,0:T(8,128)(2,1)S(1)} %collective-permute-done.7.w_y, bf16[1056,256]{1,0:T(8,128)(2,1)S(1)} %get-tuple-element.27.pack, ...), custom_call_target="tpu_custom_call" | custom-call | flops 33554432 | bytes 2211840 | tf_op jit(solution)/shard_map/pallas_call | solution.py:25
  27.2 1.8 %collective-permute-start.12 = (bf16[448,128]{1,0:T(8,128)(2,1)S(1)}, bf16[448,128]{1,0:T(8,128)(2,1)S(1)}, u32[]{:S(2)}, u32[]{:S(2)}) collective-permute-start(bf16[448,128]{1,0:T(8,128)(2,1)S(1)} %get-tuple-element.42), channel_id=1, source_target_pairs={{0,2},{2,0},{4,6},{6,4},{8,10},{10,8},{12,14},{14,12},{16,18},{18,... | collective-permute-start | bytes 344072 | tf_op jit(solution)/shard_map/ppermute | solution.py:38
  28.9 1.6 %collective-permute-start.10 = (bf16[256,128]{1,0:T(8,128)(2,1)S(1)}, bf16[256,128]{1,0:T(8,128)(2,1)S(1)}, u32[]{:S(2)}, u32[]{:S(2)}) collective-permute-start(bf16[256,128]{1,0:T(8,128)(2,1)S(1)} %get-tuple-element.41.v3), channel_id=1, source_target_pairs={{0,8},{2,10},{4,12},{6,14},{8,0},{10,2},{12,4},{14,6},{16,24},{18,... | collective-permute-start | bytes 196616 | tf_op jit(solution)/shard_map/ppermute | solution.py:38
  30.5 0.2 collective-permute-start.11
  30.7 2.5 %collective-permute-done.10.v3_z = bf16[256,128]{1,0:T(8,128)(2,1)S(1)} collective-permute-done((bf16[256,128]{1,0:T(8,128)(2,1)S(1)}, bf16[256,128]{1,0:T(8,128)(2,1)S(1)}, u32[]{:S(2)}, u32[]{:S(2)}) %collective-permute-start.10) | collective-permute-done | bytes 65568 | tf_op jit(solution)/shard_map/ppermute | solution.py:38
  33.2 2.5 %collective-permute-done.11.v3_xz = bf16[256,128]{1,0:T(8,128)(2,1)S(1)} collective-permute-done((bf16[256,128]{1,0:T(8,128)(2,1)S(1)}, bf16[256,128]{1,0:T(8,128)(2,1)S(1)}, u32[]{:S(2)}, u32[]{:S(2)}) %collective-permute-start.11) | collective-permute-done | bytes 65568 | tf_op jit(solution)/shard_map/ppermute | solution.py:38
  35.7 0.2 shard_map.156.own
  35.9 0.7 %shard_map.149 = bf16[256,512]{1,0:T(8,128)(2,1)} custom-call(bf16[256,256]{1,0:T(8,128)(2,1)S(1)} %get-tuple-element.28.own.solved, bf16[256,256]{1,0:T(8,128)(2,1)S(1)} %collective-permute-done.1.got), custom_call_target="tpu_custom_call" | custom-call | bytes 524288 | tf_op jit(solution)/shard_map/pallas_call | solution.py:25
  36.6 0.6 %collective-permute-done.13.got = bf16[224,256]{1,0:T(8,128)(2,1)S(1)} collective-permute-done((bf16[224,256]{1,0:T(8,128)(2,1)S(1)}, bf16[224,256]{1,0:T(8,128)(2,1)S(1)}, u32[]{:S(2)}, u32[]{:S(2)}) %collective-permute-start.13) | collective-permute-done | bytes 114720 | tf_op jit(solution)/shard_map/ppermute | solution.py:38
  37.2 0.7 %shard_map.157 = (bf16[128,512]{1,0:T(8,128)(2,1)}, bf16[64,512]{1,0:T(8,128)(2,1)}, bf16[32,512]{1,0:T(8,128)(2,1)}) custom-call(bf16[224,256]{1,0:T(8,128)(2,1)S(1)} %shard_map.156.own, bf16[224,256]{1,0:T(8,128)(2,1)S(1)} %collective-permute-done.13.got), custom_call_target="tpu_custom_call" | custom-call | bytes 458752 | tf_op jit(solution)/shard_map/pallas_call | solution.py:25
  (13 shorter events, 0.1 us)
Async XLA Ops:
  3.8 8.7 %copy-start.1 = (bf16[256,256]{1,0:T(8,128)(2,1)S(1)}, bf16[256,256]{1,0:T(8,128)(2,1)}, u32[]{:S(2)}) copy-start(bf16[256,256]{1,0:T(8,128)(2,1)} %inverse.5) | copy-start | bytes 393220
  3.8 8.6 %collective-permute-start = (bf16[1056,256]{1,0:T(8,128)(2,1)S(1)}, bf16[1056,256]{1,0:T(8,128)(2,1)S(1)}, u32[]{:S(2)}, u32[]{:S(2)}) collective-permute-start(bf16[1056,256]{1,0:T(8,128)(2,1)S(1)} %get-tuple-element.27.pack), channel_id=1, source_target_pairs={{0,1},{1,0},{2,3},{3,2},{4,5},{5,4},{6,7},{7,6},{8,9},{9,8},{10,11... | collective-permute-start | bytes 1622024 | tf_op jit(solution)/shard_map/ppermute | solution.py:38
  5.3 15.4 %copy-start = (bf16[128,256]{1,0:T(8,128)(2,1)S(1)}, bf16[128,256]{1,0:T(8,128)(2,1)}, u32[]{:S(2)}) copy-start(bf16[128,256]{1,0:T(8,128)(2,1)} %inverse.6) | copy-start | bytes 196612
  5.3 7.6 %collective-permute-start.2 = (bf16[512,256]{1,0:T(8,128)(2,1)S(1)}, bf16[512,256]{1,0:T(8,128)(2,1)S(1)}, u32[]{:S(2)}, u32[]{:S(2)}) collective-permute-start(bf16[512,256]{1,0:T(8,128)(2,1)S(1)} %get-tuple-element.33), channel_id=1, source_target_pairs={{0,1},{1,0},{2,3},{3,2},{4,5},{5,4},{6,7},{7,6},{8,9},{9,8},{10,11... | collective-permute-start | bytes 786440 | tf_op jit(solution)/shard_map/ppermute | solution.py:38
  5.4 7.1 %collective-permute-start.5 = (bf16[288,256]{1,0:T(8,128)(2,1)S(1)}, bf16[288,256]{1,0:T(8,128)(2,1)S(1)}, u32[]{:S(2)}, u32[]{:S(2)}) collective-permute-start(bf16[288,256]{1,0:T(8,128)(2,1)S(1)} %get-tuple-element.38.along), channel_id=1, source_target_pairs={{0,2},{2,0},{4,6},{6,4},{8,10},{10,8},{12,14},{14,12},{16,18},{18,... | collective-permute-start | bytes 442376 | tf_op jit(solution)/shard_map/ppermute | solution.py:38
  12.5 4.8 %collective-permute-start.6 = (bf16[288,256]{1,0:T(8,128)(2,1)S(1)}, bf16[288,256]{1,0:T(8,128)(2,1)S(1)}, u32[]{:S(2)}, u32[]{:S(2)}) collective-permute-start(bf16[288,256]{1,0:T(8,128)(2,1)S(1)} %collective-permute-done.5.along_x), channel_id=1, source_target_pairs={{0,1},{1,0},{2,3},{3,2},{4,5},{5,4},{6,7},{7,6},{8,9},{9,8},{10,11... | collective-permute-start | bytes 442376 | tf_op jit(solution)/shard_map/ppermute | solution.py:38
  13.4 7.8 %collective-permute-start.3 = (bf16[2,256,128]{2,1,0:T(8,128)(2,1)S(1)}, bf16[2,256,128]{2,1,0:T(8,128)(2,1)S(1)}, u32[]{:S(2)}, u32[]{:S(2)}) collective-permute-start(bf16[2,256,128]{2,1,0:T(8,128)(2,1)S(1)} %get-tuple-element.35), channel_id=1, source_target_pairs={{0,2},{2,0},{4,6},{6,4},{8,10},{10,8},{12,14},{14,12},{16,18},{18,... | collective-permute-start | bytes 393224 | tf_op jit(solution)/shard_map/ppermute | solution.py:38
  15.2 5.6 %collective-permute-start.4 = (bf16[256,128]{1,0:T(8,128)(2,1)S(1)}, bf16[256,128]{1,0:T(8,128)(2,1)S(1)}, u32[]{:S(2)}, u32[]{:S(2)}) collective-permute-start(bf16[256,128]{1,0:T(8,128)(2,1)S(1)} %get-tuple-element.37), channel_id=1, source_target_pairs={{0,2},{2,0},{4,6},{6,4},{8,10},{10,8},{12,14},{14,12},{16,18},{18,... | collective-permute-start | bytes 196616 | tf_op jit(solution)/shard_map/ppermute | solution.py:38
  15.5 7.6 %collective-permute-start.8 = (bf16[192,256]{1,0:T(8,128)(2,1)S(1)}, bf16[192,256]{1,0:T(8,128)(2,1)S(1)}, u32[]{:S(2)}, u32[]{:S(2)}) collective-permute-start(bf16[192,256]{1,0:T(8,128)(2,1)S(1)} %shard_map.154), channel_id=1, source_target_pairs={{0,4},{2,6},{4,0},{6,2},{8,12},{10,14},{12,8},{14,10},{16,20},{18,... | collective-permute-start | bytes 294920 | tf_op jit(solution)/shard_map/ppermute | solution.py:38
  20.7 14.9 %copy-start.2 = (bf16[32,256]{1,0:T(8,128)(2,1)S(1)}, bf16[32,256]{1,0:T(8,128)(2,1)}, u32[]{:S(2)}) copy-start(bf16[32,256]{1,0:T(8,128)(2,1)} %inverse.7) | copy-start | bytes 49156
  21.2 5.1 %collective-permute-start.7 = (bf16[2,256,128]{2,1,0:T(8,128)(2,1)S(1)}, bf16[2,256,128]{2,1,0:T(8,128)(2,1)S(1)}, u32[]{:S(2)}, u32[]{:S(2)}) collective-permute-start(bf16[2,256,128]{2,1,0:T(8,128)(2,1)S(1)} %shard_map.153.w), channel_id=1, source_target_pairs={{0,4},{2,6},{4,0},{6,2},{8,12},{10,14},{12,8},{14,10},{16,20},{18,... | collective-permute-start | bytes 393224 | tf_op jit(solution)/shard_map/ppermute | solution.py:38
  23.0 1.3 %collective-permute-start.9 = (bf16[192,256]{1,0:T(8,128)(2,1)S(1)}, bf16[192,256]{1,0:T(8,128)(2,1)S(1)}, u32[]{:S(2)}, u32[]{:S(2)}) collective-permute-start(bf16[192,256]{1,0:T(8,128)(2,1)S(1)} %collective-permute-done.8.side), channel_id=1, source_target_pairs={{0,1},{1,0},{2,3},{3,2},{4,5},{5,4},{6,7},{7,6},{8,9},{9,8},{10,11... | collective-permute-start | bytes 294920 | tf_op jit(solution)/shard_map/ppermute | solution.py:38
  27.2 8.5 %collective-permute-start.12 = (bf16[448,128]{1,0:T(8,128)(2,1)S(1)}, bf16[448,128]{1,0:T(8,128)(2,1)S(1)}, u32[]{:S(2)}, u32[]{:S(2)}) collective-permute-start(bf16[448,128]{1,0:T(8,128)(2,1)S(1)} %get-tuple-element.42), channel_id=1, source_target_pairs={{0,2},{2,0},{4,6},{6,4},{8,10},{10,8},{12,14},{14,12},{16,18},{18,... | collective-permute-start | bytes 344072 | tf_op jit(solution)/shard_map/ppermute | solution.py:38
  28.9 4.3 %collective-permute-start.10 = (bf16[256,128]{1,0:T(8,128)(2,1)S(1)}, bf16[256,128]{1,0:T(8,128)(2,1)S(1)}, u32[]{:S(2)}, u32[]{:S(2)}) collective-permute-start(bf16[256,128]{1,0:T(8,128)(2,1)S(1)} %get-tuple-element.41.v3), channel_id=1, source_target_pairs={{0,8},{2,10},{4,12},{6,14},{8,0},{10,2},{12,4},{14,6},{16,24},{18,... | collective-permute-start | bytes 196616 | tf_op jit(solution)/shard_map/ppermute | solution.py:38
  30.5 5.2 %collective-permute-start.11 = (bf16[256,128]{1,0:T(8,128)(2,1)S(1)}, bf16[256,128]{1,0:T(8,128)(2,1)S(1)}, u32[]{:S(2)}, u32[]{:S(2)}) collective-permute-start(bf16[256,128]{1,0:T(8,128)(2,1)S(1)} %get-tuple-element.41.v3), channel_id=1, source_target_pairs={{0,10},{2,8},{4,14},{6,12},{8,2},{10,0},{12,6},{14,4},{16,26},{18,... | collective-permute-start | bytes 196616 | tf_op jit(solution)/shard_map/ppermute | solution.py:38
  30.7 5.2 %collective-permute-start.1 = (bf16[256,256]{1,0:T(8,128)(2,1)S(1)}, bf16[256,256]{1,0:T(8,128)(2,1)S(1)}, u32[]{:S(2)}, u32[]{:S(2)}) collective-permute-start(bf16[256,256]{1,0:T(8,128)(2,1)S(1)} %get-tuple-element.28.own.solved), channel_id=1, source_target_pairs={{0,1},{1,0},{2,3},{3,2},{4,5},{5,4},{6,7},{7,6},{8,9},{9,8},{10,11... | collective-permute-start | bytes 393224 | tf_op jit(solution)/shard_map/ppermute | solution.py:38
  35.9 1.3 %collective-permute-start.13 = (bf16[224,256]{1,0:T(8,128)(2,1)S(1)}, bf16[224,256]{1,0:T(8,128)(2,1)S(1)}, u32[]{:S(2)}, u32[]{:S(2)}) collective-permute-start(bf16[224,256]{1,0:T(8,128)(2,1)S(1)} %shard_map.156.own), channel_id=1, source_target_pairs={{0,1},{1,0},{2,3},{3,2},{4,5},{5,4},{6,7},{7,6},{8,9},{9,8},{10,11... | collective-permute-start | bytes 344072 | tf_op jit(solution)/shard_map/ppermute | solution.py:38

commit v5 on v4

v5 whole, which is shorter than its diff:
```python
import jax
import jax.numpy as jnp
from jax import lax
from jax.experimental import pallas as pl
from jax.experimental.pallas import tpu as pltpu
from jax.sharding import PartitionSpec as P

F32, BF16 = jnp.float32, jnp.bfloat16
WHOLE = pl.BlockSpec(memory_space=pltpu.VMEM)
SCALARS = pl.BlockSpec(memory_space=pltpu.SMEM)


def dot(a, b):
    return jnp.dot(a, b, preferred_element_type=F32)


def dot_t(a, b):
    return lax.dot_general(a, b, (((0,), (0,)), ((), ())), preferred_element_type=F32)


def call(kernel, outs, *args, scratch=(), flops=0, specs=None):
    outs = [jax.ShapeDtypeStruct(shape, dtype) for shape, dtype in outs]
    moved = sum(a.size * a.dtype.itemsize for a in (*args, *outs))
    single = len(outs) == 1
    return pl.pallas_call(
        kernel,
        out_shape=outs[0] if single else outs,
        in_specs=specs or [WHOLE] * len(args),
        out_specs=WHOLE if single else [WHOLE] * len(outs),
        scratch_shapes=list(scratch),
        cost_estimate=pl.CostEstimate(flops=flops, bytes_accessed=moved, transcendentals=0),
        compiler_params=pltpu.CompilerParams(vmem_limit_bytes=16 << 20),
    )(*args)


def swap(block, axis, stride):
    count = lax.axis_size(axis)
    return lax.ppermute(block, axis, [(low, low ^ stride) for low in range(count)])


def own_and_other(part):
    me = lax.axis_index("row")
    return (
        pl.ds(pl.multiple_of(me * part, part), part),
        pl.ds(pl.multiple_of((1 - me) * part, part), part),
    )


def fetch_all(pairs, sems):
    copies = [pltpu.make_async_copy(source, target, sems.at[i]) for i, (source, target) in enumerate(pairs)]
    for copy in copies:
        copy.start()
    return copies


def prepare(
    lower_0h, lower_1h, lower_2h, pattern_h, inv_1h, inv_2h, pack, along,
    lower_0, lower_1, lower_2t, pattern, inv_1, inv_2, sems,
):
    first = 0
    for copy in fetch_all(
        (
            (pattern_h, pattern), (lower_1h, lower_1), (lower_2h, lower_2t), (inv_1h, inv_1), (inv_2h, inv_2),
            (lower_0h, lower_0),
        ),
        sems,
    ):
        copy.wait()
    rows = lower_0.shape[1]
    blocks = pattern.shape[1]
    spread = rows // blocks
    n0, n1 = lower_0.shape[0], lower_1.shape[0]
    part_1, part_2 = lower_1.shape[2], lower_2t.shape[1]
    for b in range(blocks):
        at = pl.ds(b * spread, spread)
        for m in range(n0):
            factor = pattern[0, b, m].astype(BF16)
            pack[pl.ds(first + m * rows + b * spread, spread), :] = lower_0[m, at, :] * factor
        for m in range(n1):
            factor = pattern[0, b, n0 + m].astype(BF16)
            masked = lower_1[m, at, :] * factor
            lanes = pl.ds(m * part_1, part_1)
            pack[pl.ds(first + n0 * rows + b * spread, spread), lanes] = masked
            along[at, lanes] = masked
    lane = lax.broadcasted_iota(jnp.int32, (1, rows), 1) // spread
    keep = jnp.zeros((1, rows), F32)
    for b in range(blocks):
        keep = jnp.where(lane == b, pattern[0, b, n0 + n1].astype(F32), keep)
    short = part_2 // 2
    cut = part_1 // 2
    last = rows + cut + part_2
    for i in range(2):
        masked = (lower_2t[0, pl.ds(i * short, short), :].astype(F32) * keep).astype(BF16)
        pack[pl.ds(first + (n0 + 1) * rows, short), pl.ds(i * rows, rows)] = masked
        along[pl.ds(last, short), pl.ds(i * rows, rows)] = masked
    mine, _ = own_and_other(cut)
    along[pl.ds(rows, cut), :] = inv_1[mine, :]
    along[pl.ds(rows + cut, part_2), :] = inv_2[...]


def leaf_sum(m, row, solved, lower, rhs, keep, send, total):
    leaves = lower.shape[1]
    mine, _ = own_and_other(rhs.shape[2])
    own, other = own_and_other(keep.shape[2])
    acc = dot(lower[row, 0], solved[0])
    for v in range(1, leaves):
        acc = acc + dot(lower[row, v], solved[v])
    total[...] = -acc
    total[mine, :] = total[mine, :] + rhs[row, 0].astype(F32)
    keep[m] = total[:, own]
    send[m] = total[:, other].astype(BF16)


def leaf_a(inverse, right, lower, rhs, solved, keep, send, total):
    for v in range(inverse.shape[0]):
        solved[v] = dot(inverse[v], right[v]).astype(BF16)
    for m in range(keep.shape[0]):
        leaf_sum(m, m, solved, lower, rhs, keep, send, total)


def leaf_b(solved, lower, rhs, keep, send, total):
    late = keep.shape[0]
    for m in range(late):
        leaf_sum(m, lower.shape[0] - late + m, solved, lower, rhs, keep, send, total)


def quarters(half):
    part = half // 2
    bit = lax.rem(lax.axis_index("col"), 2)
    return (
        pl.ds(pl.multiple_of(bit * part, part), part),
        pl.ds(pl.multiple_of((1 - bit) * part, part), part),
    )


def split(total, kept, sent):
    own, other = quarters(total.shape[1])
    kept[...] = total[:, own]
    sent[...] = total[:, other].astype(BF16)


def zero_a(keep, got, pack, pack_o, inverse, solved_out, kept, sent, total):
    size = inverse.shape[1]
    rows = size // 2
    residual = (keep[0] + got[0].astype(F32)).astype(BF16)
    solved = dot(inverse[...], residual).astype(BF16)
    solved_out[...] = solved
    total[...] = keep[1] + got[1].astype(F32)
    for ref, at in zip((pack, pack_o), own_and_other(rows)):
        total[at, :] = total[at, :] - dot(ref[pl.ds(0, rows), :], solved)
    split(total, kept, sent)


def zero_b(keep, got, solved, pack, pack_o, kept_2, sent_2, kept_3, sent_3, total):
    size = solved.shape[0]
    rows = size // 2
    for m, (kept, sent) in enumerate(((kept_2, sent_2), (kept_3, sent_3))):
        total[...] = keep[m] + got[m].astype(F32)
        for ref, at in zip((pack, pack_o), own_and_other(rows)):
            total[at, :] = total[at, :] - dot(ref[pl.ds((m + 1) * rows, rows), :], solved[...])
        split(total, kept, sent)


def one(kept, got, inverse, pack, pack_o, along, along_x, along_xo, solved_own, solved_x, *updates):
    size, part = kept.shape[0], inverse.shape[0]
    rows = size // 2
    first = 3 * rows
    residual = (kept[...] + got[...].astype(F32)).astype(BF16)
    solved_own[...] = dot(inverse[...], residual).astype(BF16)
    cut = part // 2
    for ref, at in zip((along_x, along_xo), own_and_other(cut)):
        solved_x[at, :] = dot(ref[pl.ds(rows, cut), :], residual).astype(BF16)
    own, other = solved_own[...], solved_x[...]
    for m, u in enumerate(updates):
        lanes = pl.ds(m * part, part)
        for ref, ref_x, at in zip((pack, pack_o), (along_x, along_xo), own_and_other(rows)):
            u[at, :] = dot(ref[pl.ds(first, rows), lanes], own) + dot(ref_x[pl.ds(0, rows), lanes], other)


def stack(along, along_x, out):
    part = out.shape[0] // 2
    at = pl.ds(along.shape[0] - part, part)
    out[pl.ds(0, part), :] = along[at, :]
    out[pl.ds(part, part), :] = along_x[at, :]


def difference(kept, got, update, out):
    out[...] = (kept[...] + got[...].astype(F32) - update[...]).astype(BF16)


def two(w2, w2_y, s3, s3_y, pack_o, along, along_x, along_xo, side, side_o, solved_own, v3, to_x):
    size = w2.shape[0]
    rows = size // 2
    part = solved_own.shape[0]
    short = part // 2
    residual = (w2[...].astype(F32) + w2_y[...].astype(F32)).astype(BF16)
    top = along.shape[0] - part - short
    step = part + short
    inverses = ((along, top), (along_x, top), (side, 0), (side, step))
    mine_at = ((along, top + part), (along_x, top + part), (side, part), (side, step + part))
    their_at = (
        (pack_o, pack_o.shape[0] - short), (along_xo, top + part), (side_o, part), (side_o, step + part),
    )
    ranges = own_and_other(rows)
    total = [s3[at, :].astype(F32) + s3_y[at, :].astype(F32) for at in ranges]
    for i, (ref, at) in enumerate(inverses):
        solved = dot(ref[pl.ds(at, part), :], residual).astype(BF16)
        if i == 0:
            solved_own[...] = solved
        if i == 1:
            to_x[pl.ds(size, part), :] = solved
        for j, (low, start) in enumerate((mine_at[i], their_at[i])):
            block = low[pl.ds(start, short), :]
            total[j] = total[j] - dot_t(block[:, :rows], solved[:short]) - dot_t(block[:, rows:], solved[short:])
    for at, value in zip(ranges, total):
        v3[at, :] = value.astype(BF16)
        to_x[at, :] = value.astype(BF16)


def three(v3, v3_z, v3_xz, from_x, inverse, sol1, sol1_x, sol2, out, full):
    size = v3.shape[0]
    own, other = quarters(out.shape[1])
    full[:, own] = (v3[...].astype(F32) + v3_z[...].astype(F32)).astype(BF16)
    full[:, other] = (from_x[pl.ds(0, size), :].astype(F32) + v3_xz[...].astype(F32)).astype(BF16)
    n1, n2 = sol1.shape[0], sol2.shape[0]
    out[pl.ds(0, n1), own] = sol1[...]
    out[pl.ds(0, n1), other] = sol1_x[...]
    out[pl.ds(n1, n2), own] = sol2[...]
    out[pl.ds(n1, n2), other] = from_x[pl.ds(size, n2), :]
    out[pl.ds(n1 + n2, inverse.shape[0]), :] = dot(inverse[...], full[...]).astype(BF16)


def join(own, got, *outs):
    mine, theirs = own_and_other(own.shape[1])
    first = 0
    for out in outs:
        at = pl.ds(first, out.shape[0])
        out[:, mine] = own[at, :]
        out[:, theirs] = got[at, :]
        first += out.shape[0]


PREPARE_FLOPS = 4 * 10**9


def body(
    rhs, leaf_rhs, leaf_inverse, leaf_lower,
    inverse_0, inverse_1, inverse_2, inverse_3,
    lower_0, lower_1, lower_2, sparsity,
):
    levels, _, rows, width = rhs.shape
    leaves, size, _ = leaf_inverse.shape
    half = width // lax.axis_size("row")
    n0 = lower_0.shape[0]
    part_1, part_2 = inverse_1.shape[0], inverse_2.shape[0]
    full = [pltpu.VMEM((size, width), F32)]

    early = 2
    late = levels - early
    short = part_2 // 2
    quarter = half // 2
    square = pltpu.VMEM((size, half), F32)
    kept, sent = ((size, quarter), F32), ((size, quarter), BF16)
    lower_2t, pattern = jnp.swapaxes(lower_2, 1, 2), jnp.transpose(sparsity, (1, 2, 0))
    sources = (lower_0, lower_1, lower_2t, pattern, inverse_1, inverse_2)
    pack, along = call(
        prepare,
        [
            (((n0 + 1) * rows + short, half), BF16),
            ((rows + part_1 // 2 + part_2 + short, half), BF16),
        ],
        *(pltpu.with_memory_space_constraint(x, pltpu.HBM) for x in sources),
        specs=[pl.BlockSpec(memory_space=pltpu.HBM)] * len(sources),
        scratch=[pltpu.VMEM(x.shape, BF16) for x in sources[:3]]
        + [pltpu.SMEM(pattern.shape, jnp.int32)]
        + [pltpu.VMEM(x.shape, BF16) for x in sources[4:]]
        + [pltpu.SemaphoreType.DMA((len(sources),))],
        flops=PREPARE_FLOPS,
    )
    along_x = swap(along, "col", 1)
    solved_leaf, keep_a, send_a = call(
        leaf_a,
        [((leaves, size, width), BF16), ((early, size, half), F32), ((early, size, half), BF16)],
        leaf_inverse, leaf_rhs, leaf_lower, rhs,
        scratch=full, flops=2 * (1 + early) * leaves * size * size * width,
    )
    got_a = swap(send_a, "row", 1)
    pack_o = swap(pack, "row", 1)
    keep_b, send_b = call(
        leaf_b,
        [((late, size, half), F32), ((late, size, half), BF16)],
        solved_leaf, leaf_lower, rhs,
        scratch=full, flops=2 * late * leaves * size * size * width,
    )
    got_b = swap(send_b, "row", 1)
    sol0, kept1, sent1 = call(
        zero_a, [((size, half), BF16), kept, sent],
        keep_a, got_a, pack, pack_o, inverse_0,
        scratch=[square], flops=4 * size * size * half,
    )
    got1 = swap(sent1, "col", 1)
    kept2, sent2, kept3, sent3 = call(
        zero_b, [kept, sent, kept, sent], keep_b, got_b, sol0, pack, pack_o,
        scratch=[square], flops=4 * size * size * half,
    )
    got2 = swap(sent2, "col", 1)
    got3 = swap(sent3, "col", 1)
    along_xo = swap(along_x, "row", 1)
    side = swap(call(stack, [((2 * (part_2 + short), half), BF16)], along, along_x), "col", 2)
    sol1, sol1_for_x, u2, u3 = call(
        one, [((part_1, quarter), BF16)] * 2 + [kept] * 2,
        kept1, got1, inverse_1, pack, pack_o, along, along_x, along_xo,
        flops=6 * size * size * quarter,
    )
    w2 = call(difference, [sent], kept2, got2, u2)
    w2_y = swap(w2, "col", 2)
    sol0_o = swap(sol0, "row", 1)
    side_o = swap(side, "row", 1)
    s3 = call(difference, [sent], kept3, got3, u3)
    s3_y = swap(s3, "col", 2)
    sol1_x = swap(sol1_for_x, "col", 1)
    out0 = call(join, [((size, width), BF16)], sol0, sol0_o)
    sol2, v3, to_x = call(
        two,
        [((part_2, quarter), BF16), sent, ((size + part_2, quarter), BF16)],
        w2, w2_y, s3, s3_y, pack_o, along, along_x, along_xo, side, side_o,
        flops=4 * size * size * quarter,
    )
    v3_xz = swap(v3, "col", 5)
    from_x = swap(to_x, "col", 1)
    v3_z = swap(v3, "col", 4)
    part_3 = inverse_3.shape[0]
    last = call(
        three, [((part_1 + part_2 + part_3, half), BF16)],
        v3, v3_z, v3_xz, from_x, inverse_3, sol1, sol1_x, sol2,
        scratch=[pltpu.VMEM((size, half), BF16)], flops=2 * inverse_3.size * half,
    )
    last_o = swap(last, "row", 1)
    rest = call(join, [((part, width), BF16) for part in (part_1, part_2, part_3)], last, last_o)
    return (out0, *rest)


def solution(mesh):
    return jax.shard_map(
        body,
        mesh=mesh,
        in_specs=(
            P(None, "col", "row", None),
            P(("col", "row"), None, None),
            P(("col", "row"), None, None),
            P(None, ("col", "row"), None, None),
            P("col", None),
            P("col", None),
            P("col", None),
            P("col", None),
            P(None, "row", "col"),
            P(None, "row", "col"),
            P(None, "row", "col"),
            P(None, "col", "row"),
        ),
        out_specs=(P("col", None), P("col", None), P("col", None), P("col", None)),
        check_vma=False,
    )
```

time: 38.1 us -> 42.8 us (1.12)
  local copies, waits for them, and re-layouts: 0.02 us -> 5.35 us
  waiting for transfers between devices: 16.4 us -> 13.2 us
  starting transfers between devices: 13 us -> 16.1 us
  Pallas kernels: 7.81 us -> 7.08 us
    unnamed x6 -> x18, local copies, waits for them, and re-layouts: 0.02 us -> 5.35 us
    ppermute x14 -> x18, waiting for transfers between devices: 16.4 us -> 13.2 us  [swap(): lax.ppermute(block, axis, [(low, low ^ stride) for low in range(count)])]
    ppermute x14 -> x18, starting transfers between devices: 13 us -> 16.1 us  [swap(): lax.ppermute(block, axis, [(low, low ^ stride) for low in range(count)])]
    pallas_call x11 -> x13, Pallas kernels: 7.81 us -> 7.08 us  [call(): pl.pallas_call(kernel, out_shape=outs[0] if single else outs, in_specs=sp...]
  transfers between devices with their start and end apart: 14 -> 18, of which waited for: 7 -> 8; matrix products, arithmetic and copies ran while one was open for 0% -> 0% of each run, Pallas kernels for 8% -> 10%
where the time goes in v5:
time: 42.8 us; the launch traced here: 42.5 us
  starting transfers between devices  16.1 us (38%)
  waiting for transfers between devices  13.2 us (31%)
  Pallas kernels  7.08 us (17%)
  local copies, waits for them, and re-layouts  5.35 us (12%)
  between operations  0.76 us (2%)
    ppermute x18, starting transfers between devices, swap(): lax.ppermute(block, axis, [(low, low ^ stride) for low in range(count)])  16.1 us
    ppermute x18, waiting for transfers between devices, swap(): lax.ppermute(block, axis, [(low, low ^ stride) for low in range(count)])  13.2 us
    pallas_call x13, Pallas kernels, call(): pl.pallas_call(kernel, out_shape=outs[0] if single else outs, in_specs=sp...  7.08 us
    unnamed x18, local copies, waits for them, and re-layouts  5.35 us
  transfers between devices with their start and end apart: 18, of which 8 were waited for; matrix products, arithmetic and copies ran while one was open for 0% of the time, Pallas kernels for 10%

profile of v5, /device:TPU:0, one launch (start us, length us, event | category | flops | bytes accessed | tf_op | source)
XLA Modules:
  0.0 42.5 jit_solution(9102229384469347741)
XLA Ops:
  0.6 1.6 %copy-done = bf16[4,4,256,256]{3,2,1,0:T(8,128)(2,1)S(1)} copy-done((bf16[4,4,256,256]{3,2,1,0:T(8,128)(2,1)S(1)}, bf16[4,4,256,256]{3,2,1,0:T(8,128)(2,1)}, u32[]{:S(2)}) %copy-start) | copy-done | bytes 2097176
  2.2 1.0 %copy-done.2 = bf16[4,1,128,512]{3,2,1,0:T(8,128)(2,1)S(1)} copy-done((bf16[4,1,128,512]{3,2,1,0:T(8,128)(2,1)S(1)}, bf16[4,1,128,512]{3,2,1,0:T(8,128)(2,1)}, u32[]{:S(2)}) %copy-start.2) | copy-done | bytes 524312
  3.3 1.2 %copy-done.4 = bf16[4,256,512]{2,1,0:T(8,128)(2,1)S(1)} copy-done((bf16[4,256,512]{2,1,0:T(8,128)(2,1)S(1)}, bf16[4,256,512]{2,1,0:T(8,128)(2,1)}, u32[]{:S(2)}) %copy-start.4) | copy-done | bytes 1048600
  4.5 1.0 %copy-done.5 = bf16[4,256,256]{2,1,0:T(8,128)(2,1)S(1)} copy-done((bf16[4,256,256]{2,1,0:T(8,128)(2,1)S(1)}, bf16[4,256,256]{2,1,0:T(8,128)(2,1)}, u32[]{:S(2)}) %copy-start.5) | copy-done | bytes 524312
  5.5 1.2 %shard_map.147 = (bf16[4,256,512]{2,1,0:T(8,128)(2,1)S(1)}, f32[2,256,256]{2,1,0:T(8,128)S(1)}, bf16[2,256,256]{2,1,0:T(8,128)(2,1)S(1)}) custom-call(bf16[4,256,256]{2,1,0:T(8,128)(2,1)S(1)} %copy-done.5, bf16[4,256,512]{2,1,0:T(8,128)(2,1)S(1)} %copy-done.4, bf16[4,4,256,256]{3,2,1,0:T(8,128)(2,1)S(1)} %copy-done, bf16[4,1,128,512]{3,2,1,0:T(8,128)(2,1)S(1)} %copy-done.2), custom_call_target="tpu_custom_call" | custom-call | flops 805306368 | bytes 6029312 | tf_op jit(solution)/shard_map/pallas_call | solution.py:25
  6.7 0.6 %collective-permute-start = (bf16[2,256,256]{2,1,0:T(8,128)(2,1)S(1)}, bf16[2,256,256]{2,1,0:T(8,128)(2,1)S(1)}, u32[]{:S(2)}, u32[]{:S(2)}) collective-permute-start(bf16[2,256,256]{2,1,0:T(8,128)(2,1)S(1)} %get-tuple-element.29), channel_id=1, source_target_pairs={{0,1},{1,0},{2,3},{3,2},{4,5},{5,4},{6,7},{7,6},{8,9},{9,8},{10,11... | collective-permute-start | bytes 786440 | tf_op jit(solution)/shard_map/ppermute | solution.py:38
  7.3 1.3 %shard_map.148 = (bf16[544,256]{1,0:T(8,128)(2,1)S(1)}, bf16[288,256]{1,0:T(8,128)(2,1)S(1)}) custom-call(bf16[3,128,256]{2,1,0:T(8,128)(2,1)} %lower_0h.1, bf16[2,128,128]{2,1,0:T(8,128)(2,1)} %lower_1h.1, bf16[1,64,128]{2,1,0:T(8,128)(2,1)} %bitcast.2, s32[1,4,6]{2,1,0:T(4,128)} %bitcast.3, bf16[128,256]{1,0:T(8,128)(2,1)} %inverse.6, bf16[64,256]{1,0:T(8,128)(2,1)} %inv_2h.1), custom_call_target="tpu_custom_call" | custom-call | flops 4000000000 | bytes 802912 | tf_op jit(solution)/shard_map/pallas_call | solution.py:25
  8.7 0.4 copy-done.1
  9.1 0.9 %shard_map.151 = (f32[2,256,256]{2,1,0:T(8,128)S(1)}, bf16[2,256,256]{2,1,0:T(8,128)(2,1)S(1)}) custom-call(bf16[4,256,512]{2,1,0:T(8,128)(2,1)S(1)} %get-tuple-element.32.solved, bf16[4,4,256,256]{3,2,1,0:T(8,128)(2,1)S(1)} %copy-done.1, bf16[4,1,128,512]{3,2,1,0:T(8,128)(2,1)S(1)} %copy-done.3), custom_call_target="tpu_custom_call" | custom-call | flops 536870912 | bytes 4456448 | tf_op jit(solution)/shard_map/pallas_call | solution.py:25
  10.2 2.9 %collective-permute-start.6 = (bf16[288,256]{1,0:T(8,128)(2,1)S(1)}, bf16[288,256]{1,0:T(8,128)(2,1)S(1)}, u32[]{:S(2)}, u32[]{:S(2)}) collective-permute-start(bf16[288,256]{1,0:T(8,128)(2,1)S(1)} %get-tuple-element.39.along), channel_id=1, source_target_pairs={{0,2},{2,0},{4,6},{6,4},{8,10},{10,8},{12,14},{14,12},{16,18},{18,... | collective-permute-start | bytes 442376 | tf_op jit(solution)/shard_map/ppermute | solution.py:38
  13.1 4.1 %collective-permute-done.6.along_x = bf16[288,256]{1,0:T(8,128)(2,1)S(1)} collective-permute-done((bf16[288,256]{1,0:T(8,128)(2,1)S(1)}, bf16[288,256]{1,0:T(8,128)(2,1)S(1)}, u32[]{:S(2)}, u32[]{:S(2)}) %collective-permute-start.6) | collective-permute-done | bytes 147488 | tf_op jit(solution)/shard_map/ppermute | solution.py:38
  17.2 1.8 %collective-permute-start.11 = (bf16[192,256]{1,0:T(8,128)(2,1)S(1)}, bf16[192,256]{1,0:T(8,128)(2,1)S(1)}, u32[]{:S(2)}, u32[]{:S(2)}) collective-permute-start(bf16[192,256]{1,0:T(8,128)(2,1)S(1)} %shard_map.156), channel_id=1, source_target_pairs={{0,4},{2,6},{4,0},{6,2},{8,12},{10,14},{12,8},{14,10},{16,20},{18,... | collective-permute-start | bytes 294920 | tf_op jit(solution)/shard_map/ppermute | solution.py:38
  19.0 0.4 %shard_map.149 = (bf16[256,256]{1,0:T(8,128)(2,1)S(1)}, f32[256,128]{1,0:T(8,128)S(1)}, bf16[256,128]{1,0:T(8,128)(2,1)S(1)}) custom-call(f32[2,256,256]{2,1,0:T(8,128)S(1)} %get-tuple-element.28.keep, bf16[2,256,256]{2,1,0:T(8,128)(2,1)S(1)} %collective-permute-done.got, bf16[544,256]{1,0:T(8,128)(2,1)S(1)} %get-tuple-element.30.pack, ...), custom_call_target="tpu_custom_call" | custom-call | flops 67108864 | bytes 1802240 | tf_op jit(solution)/shard_map/pallas_call | solution.py:25
  19.5 1.6 %collective-permute-start.5 = (bf16[256,128]{1,0:T(8,128)(2,1)S(1)}, bf16[256,128]{1,0:T(8,128)(2,1)S(1)}, u32[]{:S(2)}, u32[]{:S(2)}) collective-permute-start(bf16[256,128]{1,0:T(8,128)(2,1)S(1)} %get-tuple-element.38), channel_id=1, source_target_pairs={{0,2},{2,0},{4,6},{6,4},{8,10},{10,8},{12,14},{14,12},{16,18},{18,... | collective-permute-start | bytes 196616 | tf_op jit(solution)/shard_map/ppermute | solution.py:38
  21.0 0.4 shard_map.152
  21.5 0.6 %collective-permute-start.4 = (bf16[256,128]{1,0:T(8,128)(2,1)S(1)}, bf16[256,128]{1,0:T(8,128)(2,1)S(1)}, u32[]{:S(2)}, u32[]{:S(2)}) collective-permute-start(bf16[256,128]{1,0:T(8,128)(2,1)S(1)} %get-tuple-element.36), channel_id=1, source_target_pairs={{0,2},{2,0},{4,6},{6,4},{8,10},{10,8},{12,14},{14,12},{16,18},{18,... | collective-permute-start | bytes 196616 | tf_op jit(solution)/shard_map/ppermute | solution.py:38
  22.1 1.5 %collective-permute-start.9 = (bf16[256,128]{1,0:T(8,128)(2,1)S(1)}, bf16[256,128]{1,0:T(8,128)(2,1)S(1)}, u32[]{:S(2)}, u32[]{:S(2)}) collective-permute-start(bf16[256,128]{1,0:T(8,128)(2,1)S(1)} %get-tuple-element.42), channel_id=1, source_target_pairs={{0,2},{2,0},{4,6},{6,4},{8,10},{10,8},{12,14},{14,12},{16,18},{18,... | collective-permute-start | bytes 196616 | tf_op jit(solution)/shard_map/ppermute | solution.py:38
  23.8 0.4 shard_map.153
  24.2 1.9 %collective-permute-done.4.got = bf16[256,128]{1,0:T(8,128)(2,1)S(1)} collective-permute-done((bf16[256,128]{1,0:T(8,128)(2,1)S(1)}, bf16[256,128]{1,0:T(8,128)(2,1)S(1)}, u32[]{:S(2)}, u32[]{:S(2)}) %collective-permute-start.4) | collective-permute-done | bytes 65568 | tf_op jit(solution)/shard_map/ppermute | solution.py:38
  26.2 0.6 %collective-permute-start.8 = (bf16[256,128]{1,0:T(8,128)(2,1)S(1)}, bf16[256,128]{1,0:T(8,128)(2,1)S(1)}, u32[]{:S(2)}, u32[]{:S(2)}) collective-permute-start(bf16[256,128]{1,0:T(8,128)(2,1)S(1)} %shard_map.154.w2), channel_id=1, source_target_pairs={{0,4},{2,6},{4,0},{6,2},{8,12},{10,14},{12,8},{14,10},{16,20},{18,... | collective-permute-start | bytes 196616 | tf_op jit(solution)/shard_map/ppermute | solution.py:38
  26.9 1.5 %collective-permute-start.10 = (bf16[256,128]{1,0:T(8,128)(2,1)S(1)}, bf16[256,128]{1,0:T(8,128)(2,1)S(1)}, u32[]{:S(2)}, u32[]{:S(2)}) collective-permute-start(bf16[256,128]{1,0:T(8,128)(2,1)S(1)} %shard_map.155.s3), channel_id=1, source_target_pairs={{0,4},{2,6},{4,0},{6,2},{8,12},{10,14},{12,8},{14,10},{16,20},{18,... | collective-permute-start | bytes 196616 | tf_op jit(solution)/shard_map/ppermute | solution.py:38
  28.4 2.1 %collective-permute-done.8.w2_y = bf16[256,128]{1,0:T(8,128)(2,1)S(1)} collective-permute-done((bf16[256,128]{1,0:T(8,128)(2,1)S(1)}, bf16[256,128]{1,0:T(8,128)(2,1)S(1)}, u32[]{:S(2)}, u32[]{:S(2)}) %collective-permute-start.8) | collective-permute-done | bytes 65568 | tf_op jit(solution)/shard_map/ppermute | solution.py:38
  30.5 0.7 %collective-permute-done.10.s3_y = bf16[256,128]{1,0:T(8,128)(2,1)S(1)} collective-permute-done((bf16[256,128]{1,0:T(8,128)(2,1)S(1)}, bf16[256,128]{1,0:T(8,128)(2,1)S(1)}, u32[]{:S(2)}, u32[]{:S(2)}) %collective-permute-start.10) | collective-permute-done | bytes 65568 | tf_op jit(solution)/shard_map/ppermute | solution.py:38
  31.2 0.8 %shard_map.157 = (bf16[64,128]{1,0:T(8,128)(2,1)S(1)}, bf16[256,128]{1,0:T(8,128)(2,1)S(1)}, bf16[320,128]{1,0:T(8,128)(2,1)S(1)}) custom-call(bf16[256,128]{1,0:T(8,128)(2,1)S(1)} %shard_map.154.w2, bf16[256,128]{1,0:T(8,128)(2,1)S(1)} %collective-permute-done.8.w2_y, bf16[256,128]{1,0:T(8,128)(2,1)S(1)} %shard_map.155.s3, ...), custom_call_target="tpu_custom_call" | custom-call | flops 33554432 | bytes 1343488 | tf_op jit(solution)/shard_map/pallas_call | solution.py:25
  32.0 1.3 %collective-permute-start.15 = (bf16[320,128]{1,0:T(8,128)(2,1)S(1)}, bf16[320,128]{1,0:T(8,128)(2,1)S(1)}, u32[]{:S(2)}, u32[]{:S(2)}) collective-permute-start(bf16[320,128]{1,0:T(8,128)(2,1)S(1)} %get-tuple-element.45), channel_id=1, source_target_pairs={{0,2},{2,0},{4,6},{6,4},{8,10},{10,8},{12,14},{14,12},{16,18},{18,... | collective-permute-start | bytes 245768 | tf_op jit(solution)/shard_map/ppermute | solution.py:38
  33.3 1.6 %collective-permute-start.13 = (bf16[256,128]{1,0:T(8,128)(2,1)S(1)}, bf16[256,128]{1,0:T(8,128)(2,1)S(1)}, u32[]{:S(2)}, u32[]{:S(2)}) collective-permute-start(bf16[256,128]{1,0:T(8,128)(2,1)S(1)} %get-tuple-element.44.v3), channel_id=1, source_target_pairs={{0,8},{2,10},{4,12},{6,14},{8,0},{10,2},{12,4},{14,6},{16,24},{18,... | collective-permute-start | bytes 196616 | tf_op jit(solution)/shard_map/ppermute | solution.py:38
  34.9 0.7 %collective-permute-start.14 = (bf16[256,128]{1,0:T(8,128)(2,1)S(1)}, bf16[256,128]{1,0:T(8,128)(2,1)S(1)}, u32[]{:S(2)}, u32[]{:S(2)}) collective-permute-start(bf16[256,128]{1,0:T(8,128)(2,1)S(1)} %get-tuple-element.44.v3), channel_id=1, source_target_pairs={{0,10},{2,8},{4,14},{6,12},{8,2},{10,0},{12,6},{14,4},{16,26},{18,... | collective-permute-start | bytes 196616 | tf_op jit(solution)/shard_map/ppermute | solution.py:38
  35.6 1.3 %collective-permute-start.16 = (bf16[128,128]{1,0:T(8,128)(2,1)S(1)}, bf16[128,128]{1,0:T(8,128)(2,1)S(1)}, u32[]{:S(2)}, u32[]{:S(2)}) collective-permute-start(bf16[128,128]{1,0:T(8,128)(2,1)S(1)} %get-tuple-element.47), channel_id=1, source_target_pairs={{0,2},{2,0},{4,6},{6,4},{8,10},{10,8},{12,14},{14,12},{16,18},{18,... | collective-permute-start | bytes 98312 | tf_op jit(solution)/shard_map/ppermute | solution.py:38
  36.8 3.4 %collective-permute-done.16.sol1_x = bf16[128,128]{1,0:T(8,128)(2,1)S(1)} collective-permute-done((bf16[128,128]{1,0:T(8,128)(2,1)S(1)}, bf16[128,128]{1,0:T(8,128)(2,1)S(1)}, u32[]{:S(2)}, u32[]{:S(2)}) %collective-permute-start.16) | collective-permute-done | bytes 32800 | tf_op jit(solution)/shard_map/ppermute | solution.py:38
  40.4 0.7 %shard_map.150 = bf16[256,512]{1,0:T(8,128)(2,1)} custom-call(bf16[256,256]{1,0:T(8,128)(2,1)S(1)} %get-tuple-element.31.own.solved, bf16[256,256]{1,0:T(8,128)(2,1)S(1)} %collective-permute-done.2.got), custom_call_target="tpu_custom_call" | custom-call | bytes 524288 | tf_op jit(solution)/shard_map/pallas_call | solution.py:25
  41.2 0.6 %collective-permute-done.17.got = bf16[224,256]{1,0:T(8,128)(2,1)S(1)} collective-permute-done((bf16[224,256]{1,0:T(8,128)(2,1)S(1)}, bf16[224,256]{1,0:T(8,128)(2,1)S(1)}, u32[]{:S(2)}, u32[]{:S(2)}) %collective-permute-start.17) | collective-permute-done | bytes 114720 | tf_op jit(solution)/shard_map/ppermute | solution.py:38
  41.8 0.7 %shard_map.159 = (bf16[128,512]{1,0:T(8,128)(2,1)}, bf16[64,512]{1,0:T(8,128)(2,1)}, bf16[32,512]{1,0:T(8,128)(2,1)}) custom-call(bf16[224,256]{1,0:T(8,128)(2,1)S(1)} %shard_map.158.own, bf16[224,256]{1,0:T(8,128)(2,1)S(1)} %collective-permute-done.17.got), custom_call_target="tpu_custom_call" | custom-call | bytes 458752 | tf_op jit(solution)/shard_map/pallas_call | solution.py:25
  (35 shorter events, 1.0 us)
Async XLA Ops:
  0.6 1.6 %copy-start = (bf16[4,4,256,256]{3,2,1,0:T(8,128)(2,1)S(1)}, bf16[4,4,256,256]{3,2,1,0:T(8,128)(2,1)}, u32[]{:S(2)}) copy-start(bf16[4,4,256,256]{3,2,1,0:T(8,128)(2,1)} %lower.3) | copy-start | bytes 6291460
  2.2 1.0 %copy-start.2 = (bf16[4,1,128,512]{3,2,1,0:T(8,128)(2,1)S(1)}, bf16[4,1,128,512]{3,2,1,0:T(8,128)(2,1)}, u32[]{:S(2)}) copy-start(bf16[4,1,128,512]{3,2,1,0:T(8,128)(2,1)} %rhs.3) | copy-start | bytes 1572868
  3.3 1.2 %copy-start.4 = (bf16[4,256,512]{2,1,0:T(8,128)(2,1)S(1)}, bf16[4,256,512]{2,1,0:T(8,128)(2,1)}, u32[]{:S(2)}) copy-start(bf16[4,256,512]{2,1,0:T(8,128)(2,1)} %right.1) | copy-start | bytes 3145732
  4.5 1.0 %copy-start.5 = (bf16[4,256,256]{2,1,0:T(8,128)(2,1)S(1)}, bf16[4,256,256]{2,1,0:T(8,128)(2,1)}, u32[]{:S(2)}) copy-start(bf16[4,256,256]{2,1,0:T(8,128)(2,1)} %inverse.4) | copy-start | bytes 1572868
  6.7 12.3 %collective-permute-start = (bf16[2,256,256]{2,1,0:T(8,128)(2,1)S(1)}, bf16[2,256,256]{2,1,0:T(8,128)(2,1)S(1)}, u32[]{:S(2)}, u32[]{:S(2)}) collective-permute-start(bf16[2,256,256]{2,1,0:T(8,128)(2,1)S(1)} %get-tuple-element.29), channel_id=1, source_target_pairs={{0,1},{1,0},{2,3},{3,2},{4,5},{5,4},{6,7},{7,6},{8,9},{9,8},{10,11... | collective-permute-start | bytes 786440 | tf_op jit(solution)/shard_map/ppermute | solution.py:38
  7.3 1.8 %copy-start.1 = (bf16[4,4,256,256]{3,2,1,0:T(8,128)(2,1)S(1)}, bf16[4,4,256,256]{3,2,1,0:T(8,128)(2,1)}, u32[]{:S(2)}) copy-start(bf16[4,4,256,256]{3,2,1,0:T(8,128)(2,1)} %lower.3) | copy-start | bytes 6291460
  7.3 1.9 %copy-start.3 = (bf16[4,1,128,512]{3,2,1,0:T(8,128)(2,1)S(1)}, bf16[4,1,128,512]{3,2,1,0:T(8,128)(2,1)}, u32[]{:S(2)}) copy-start(bf16[4,1,128,512]{3,2,1,0:T(8,128)(2,1)} %rhs.3) | copy-start | bytes 1572868
  8.6 10.5 %copy-start.6 = (bf16[256,256]{1,0:T(8,128)(2,1)S(1)}, bf16[256,256]{1,0:T(8,128)(2,1)}, u32[]{:S(2)}) copy-start(bf16[256,256]{1,0:T(8,128)(2,1)} %inverse.5) | copy-start | bytes 393220
  8.6 10.4 %collective-permute-start.1 = (bf16[544,256]{1,0:T(8,128)(2,1)S(1)}, bf16[544,256]{1,0:T(8,128)(2,1)S(1)}, u32[]{:S(2)}, u32[]{:S(2)}) collective-permute-start(bf16[544,256]{1,0:T(8,128)(2,1)S(1)} %get-tuple-element.30.pack), channel_id=1, source_target_pairs={{0,1},{1,0},{2,3},{3,2},{4,5},{5,4},{6,7},{7,6},{8,9},{9,8},{10,11... | collective-permute-start | bytes 835592 | tf_op jit(solution)/shard_map/ppermute | solution.py:38
  10.0 13.8 %copy-start.7 = (bf16[128,256]{1,0:T(8,128)(2,1)S(1)}, bf16[128,256]{1,0:T(8,128)(2,1)}, u32[]{:S(2)}) copy-start(bf16[128,256]{1,0:T(8,128)(2,1)} %inverse.6) | copy-start | bytes 196612
  10.0 11.0 %collective-permute-start.3 = (bf16[2,256,256]{2,1,0:T(8,128)(2,1)S(1)}, bf16[2,256,256]{2,1,0:T(8,128)(2,1)S(1)}, u32[]{:S(2)}, u32[]{:S(2)}) collective-permute-start(bf16[2,256,256]{2,1,0:T(8,128)(2,1)S(1)} %get-tuple-element.34), channel_id=1, source_target_pairs={{0,1},{1,0},{2,3},{3,2},{4,5},{5,4},{6,7},{7,6},{8,9},{9,8},{10,11... | collective-permute-start | bytes 786440 | tf_op jit(solution)/shard_map/ppermute | solution.py:38
  10.2 7.0 %collective-permute-start.6 = (bf16[288,256]{1,0:T(8,128)(2,1)S(1)}, bf16[288,256]{1,0:T(8,128)(2,1)S(1)}, u32[]{:S(2)}, u32[]{:S(2)}) collective-permute-start(bf16[288,256]{1,0:T(8,128)(2,1)S(1)} %get-tuple-element.39.along), channel_id=1, source_target_pairs={{0,2},{2,0},{4,6},{6,4},{8,10},{10,8},{12,14},{14,12},{16,18},{18,... | collective-permute-start | bytes 442376 | tf_op jit(solution)/shard_map/ppermute | solution.py:38
  17.2 6.4 %collective-permute-start.7 = (bf16[288,256]{1,0:T(8,128)(2,1)S(1)}, bf16[288,256]{1,0:T(8,128)(2,1)S(1)}, u32[]{:S(2)}, u32[]{:S(2)}) collective-permute-start(bf16[288,256]{1,0:T(8,128)(2,1)S(1)} %collective-permute-done.6.along_x), channel_id=1, source_target_pairs={{0,1},{1,0},{2,3},{3,2},{4,5},{5,4},{6,7},{7,6},{8,9},{9,8},{10,11... | collective-permute-start | bytes 442376 | tf_op jit(solution)/shard_map/ppermute | solution.py:38
  17.2 6.3 %collective-permute-start.11 = (bf16[192,256]{1,0:T(8,128)(2,1)S(1)}, bf16[192,256]{1,0:T(8,128)(2,1)S(1)}, u32[]{:S(2)}, u32[]{:S(2)}) collective-permute-start(bf16[192,256]{1,0:T(8,128)(2,1)S(1)} %shard_map.156), channel_id=1, source_target_pairs={{0,4},{2,6},{4,0},{6,2},{8,12},{10,14},{12,8},{14,10},{16,20},{18,... | collective-permute-start | bytes 294920 | tf_op jit(solution)/shard_map/ppermute | solution.py:38
  19.5 4.3 %collective-permute-start.5 = (bf16[256,128]{1,0:T(8,128)(2,1)S(1)}, bf16[256,128]{1,0:T(8,128)(2,1)S(1)}, u32[]{:S(2)}, u32[]{:S(2)}) collective-permute-start(bf16[256,128]{1,0:T(8,128)(2,1)S(1)} %get-tuple-element.38), channel_id=1, source_target_pairs={{0,2},{2,0},{4,6},{6,4},{8,10},{10,8},{12,14},{14,12},{16,18},{18,... | collective-permute-start | bytes 196616 | tf_op jit(solution)/shard_map/ppermute | solution.py:38
  21.0 19.2 %copy-start.8 = (bf16[32,256]{1,0:T(8,128)(2,1)S(1)}, bf16[32,256]{1,0:T(8,128)(2,1)}, u32[]{:S(2)}) copy-start(bf16[32,256]{1,0:T(8,128)(2,1)} %inverse.7) | copy-start | bytes 49156
  21.5 4.7 %collective-permute-start.4 = (bf16[256,128]{1,0:T(8,128)(2,1)S(1)}, bf16[256,128]{1,0:T(8,128)(2,1)S(1)}, u32[]{:S(2)}, u32[]{:S(2)}) collective-permute-start(bf16[256,128]{1,0:T(8,128)(2,1)S(1)} %get-tuple-element.36), channel_id=1, source_target_pairs={{0,2},{2,0},{4,6},{6,4},{8,10},{10,8},{12,14},{14,12},{16,18},{18,... | collective-permute-start | bytes 196616 | tf_op jit(solution)/shard_map/ppermute | solution.py:38
  22.1 4.8 %collective-permute-start.9 = (bf16[256,128]{1,0:T(8,128)(2,1)S(1)}, bf16[256,128]{1,0:T(8,128)(2,1)S(1)}, u32[]{:S(2)}, u32[]{:S(2)}) collective-permute-start(bf16[256,128]{1,0:T(8,128)(2,1)S(1)} %get-tuple-element.42), channel_id=1, source_target_pairs={{0,2},{2,0},{4,6},{6,4},{8,10},{10,8},{12,14},{14,12},{16,18},{18,... | collective-permute-start | bytes 196616 | tf_op jit(solution)/shard_map/ppermute | solution.py:38
  23.5 4.8 %collective-permute-start.12 = (bf16[192,256]{1,0:T(8,128)(2,1)S(1)}, bf16[192,256]{1,0:T(8,128)(2,1)S(1)}, u32[]{:S(2)}, u32[]{:S(2)}) collective-permute-start(bf16[192,256]{1,0:T(8,128)(2,1)S(1)} %collective-permute-done.11.side), channel_id=1, source_target_pairs={{0,1},{1,0},{2,3},{3,2},{4,5},{5,4},{6,7},{7,6},{8,9},{9,8},{10,11... | collective-permute-start | bytes 294920 | tf_op jit(solution)/shard_map/ppermute | solution.py:38
  26.2 4.3 %collective-permute-start.8 = (bf16[256,128]{1,0:T(8,128)(2,1)S(1)}, bf16[256,128]{1,0:T(8,128)(2,1)S(1)}, u32[]{:S(2)}, u32[]{:S(2)}) collective-permute-start(bf16[256,128]{1,0:T(8,128)(2,1)S(1)} %shard_map.154.w2), channel_id=1, source_target_pairs={{0,4},{2,6},{4,0},{6,2},{8,12},{10,14},{12,8},{14,10},{16,20},{18,... | collective-permute-start | bytes 196616 | tf_op jit(solution)/shard_map/ppermute | solution.py:38
  26.9 4.3 %collective-permute-start.10 = (bf16[256,128]{1,0:T(8,128)(2,1)S(1)}, bf16[256,128]{1,0:T(8,128)(2,1)S(1)}, u32[]{:S(2)}, u32[]{:S(2)}) collective-permute-start(bf16[256,128]{1,0:T(8,128)(2,1)S(1)} %shard_map.155.s3), channel_id=1, source_target_pairs={{0,4},{2,6},{4,0},{6,2},{8,12},{10,14},{12,8},{14,10},{16,20},{18,... | collective-permute-start | bytes 196616 | tf_op jit(solution)/shard_map/ppermute | solution.py:38
  32.0 8.2 %collective-permute-start.15 = (bf16[320,128]{1,0:T(8,128)(2,1)S(1)}, bf16[320,128]{1,0:T(8,128)(2,1)S(1)}, u32[]{:S(2)}, u32[]{:S(2)}) collective-permute-start(bf16[320,128]{1,0:T(8,128)(2,1)S(1)} %get-tuple-element.45), channel_id=1, source_target_pairs={{0,2},{2,0},{4,6},{6,4},{8,10},{10,8},{12,14},{14,12},{16,18},{18,... | collective-permute-start | bytes 245768 | tf_op jit(solution)/shard_map/ppermute | solution.py:38
  33.3 6.9 %collective-permute-start.13 = (bf16[256,128]{1,0:T(8,128)(2,1)S(1)}, bf16[256,128]{1,0:T(8,128)(2,1)S(1)}, u32[]{:S(2)}, u32[]{:S(2)}) collective-permute-start(bf16[256,128]{1,0:T(8,128)(2,1)S(1)} %get-tuple-element.44.v3), channel_id=1, source_target_pairs={{0,8},{2,10},{4,12},{6,14},{8,0},{10,2},{12,4},{14,6},{16,24},{18,... | collective-permute-start | bytes 196616 | tf_op jit(solution)/shard_map/ppermute | solution.py:38
  34.9 5.3 %collective-permute-start.14 = (bf16[256,128]{1,0:T(8,128)(2,1)S(1)}, bf16[256,128]{1,0:T(8,128)(2,1)S(1)}, u32[]{:S(2)}, u32[]{:S(2)}) collective-permute-start(bf16[256,128]{1,0:T(8,128)(2,1)S(1)} %get-tuple-element.44.v3), channel_id=1, source_target_pairs={{0,10},{2,8},{4,14},{6,12},{8,2},{10,0},{12,6},{14,4},{16,26},{18,... | collective-permute-start | bytes 196616 | tf_op jit(solution)/shard_map/ppermute | solution.py:38
  35.6 4.6 %collective-permute-start.16 = (bf16[128,128]{1,0:T(8,128)(2,1)S(1)}, bf16[128,128]{1,0:T(8,128)(2,1)S(1)}, u32[]{:S(2)}, u32[]{:S(2)}) collective-permute-start(bf16[128,128]{1,0:T(8,128)(2,1)S(1)} %get-tuple-element.47), channel_id=1, source_target_pairs={{0,2},{2,0},{4,6},{6,4},{8,10},{10,8},{12,14},{14,12},{16,18},{18,... | collective-permute-start | bytes 98312 | tf_op jit(solution)/shard_map/ppermute | solution.py:38
  36.8 3.6 %collective-permute-start.2 = (bf16[256,256]{1,0:T(8,128)(2,1)S(1)}, bf16[256,256]{1,0:T(8,128)(2,1)S(1)}, u32[]{:S(2)}, u32[]{:S(2)}) collective-permute-start(bf16[256,256]{1,0:T(8,128)(2,1)S(1)} %get-tuple-element.31.own.solved), channel_id=1, source_target_pairs={{0,1},{1,0},{2,3},{3,2},{4,5},{5,4},{6,7},{7,6},{8,9},{9,8},{10,11... | collective-permute-start | bytes 393224 | tf_op jit(solution)/shard_map/ppermute | solution.py:38
  40.4 1.3 %collective-permute-start.17 = (bf16[224,256]{1,0:T(8,128)(2,1)S(1)}, bf16[224,256]{1,0:T(8,128)(2,1)S(1)}, u32[]{:S(2)}, u32[]{:S(2)}) collective-permute-start(bf16[224,256]{1,0:T(8,128)(2,1)S(1)} %shard_map.158.own), channel_id=1, source_target_pairs={{0,1},{1,0},{2,3},{3,2},{4,5},{5,4},{6,7},{7,6},{8,9},{9,8},{10,11... | collective-permute-start | bytes 344072 | tf_op jit(solution)/shard_map/ppermute | solution.py:38

commit v6 on v5

--- a/solution.py
+++ b/solution.py
@@ -118,10 +118,11 @@
         leaf_sum(m, m, solved, lower, rhs, keep, send, total)
 
 
-def leaf_b(solved, lower, rhs, keep, send, total):
-    late = keep.shape[0]
-    for m in range(late):
-        leaf_sum(m, lower.shape[0] - late + m, solved, lower, rhs, keep, send, total)
+def leaf_one(m):
+    def kernel(solved, lower, rhs, keep, send, total):
+        leaf_sum(0, m, solved, lower, rhs, keep, send, total)
+
+    return kernel
 
 
 def quarters(half):
@@ -151,14 +152,15 @@
     split(total, kept, sent)
 
 
-def zero_b(keep, got, solved, pack, pack_o, kept_2, sent_2, kept_3, sent_3, total):
-    size = solved.shape[0]
-    rows = size // 2
-    for m, (kept, sent) in enumerate(((kept_2, sent_2), (kept_3, sent_3))):
-        total[...] = keep[m] + got[m].astype(F32)
+def zero_next(m):
+    def kernel(keep, got, solved, pack, pack_o, kept, sent, total):
+        rows = solved.shape[0] // 2
+        total[...] = keep[0] + got[0].astype(F32)
         for ref, at in zip((pack, pack_o), own_and_other(rows)):
-            total[at, :] = total[at, :] - dot(ref[pl.ds((m + 1) * rows, rows), :], solved[...])
+            total[at, :] = total[at, :] - dot(ref[pl.ds((m - 1) * rows, rows), :], solved[...])
         split(total, kept, sent)
+
+    return kernel
 
 
 def one(kept, got, inverse, pack, pack_o, along, along_x, along_xo, solved_own, solved_x, *updates):
@@ -188,7 +190,7 @@
     out[...] = (kept[...] + got[...].astype(F32) - update[...]).astype(BF16)
 
 
-def two(w2, w2_y, s3, s3_y, pack_o, along, along_x, along_xo, side, side_o, solved_own, v3, to_x):
+def two(w2, w2_y, pack_o, along, along_x, along_xo, side, side_o, solved_own, solved_x, update):
     size = w2.shape[0]
     rows = size // 2
     part = solved_own.shape[0]
@@ -201,20 +203,24 @@
     their_at = (
         (pack_o, pack_o.shape[0] - short), (along_xo, top + part), (side_o, part), (side_o, step + part),
     )
-    ranges = own_and_other(rows)
-    total = [s3[at, :].astype(F32) + s3_y[at, :].astype(F32) for at in ranges]
+    total = [0.0, 0.0]
     for i, (ref, at) in enumerate(inverses):
         solved = dot(ref[pl.ds(at, part), :], residual).astype(BF16)
-        if i == 0:
-            solved_own[...] = solved
-        if i == 1:
-            to_x[pl.ds(size, part), :] = solved
+        if i < 2:
+            (solved_own, solved_x)[i][...] = solved
         for j, (low, start) in enumerate((mine_at[i], their_at[i])):
             block = low[pl.ds(start, short), :]
-            total[j] = total[j] - dot_t(block[:, :rows], solved[:short]) - dot_t(block[:, rows:], solved[short:])
-    for at, value in zip(ranges, total):
-        v3[at, :] = value.astype(BF16)
-        to_x[at, :] = value.astype(BF16)
+            total[j] = total[j] + dot_t(block[:, :rows], solved[:short]) + dot_t(block[:, rows:], solved[short:])
+    for at, value in zip(own_and_other(rows), total):
+        update[at, :] = value
+
+
+def top_share(s3, s3_y, update, solved_x, v3, to_x):
+    size = v3.shape[0]
+    value = (s3[...].astype(F32) + s3_y[...].astype(F32) - update[...]).astype(BF16)
+    v3[...] = value
+    to_x[pl.ds(0, size), :] = value
+    to_x[pl.ds(size, solved_x.shape[0]), :] = solved_x[...]
 
 
 def three(v3, v3_z, v3_xz, from_x, inverse, sol1, sol1_x, sol2, out, full):
@@ -256,7 +262,6 @@
     full = [pltpu.VMEM((size, width), F32)]
 
     early = 2
-    late = levels - early
     short = part_2 // 2
     quarter = half // 2
     square = pltpu.VMEM((size, half), F32)
@@ -286,25 +291,26 @@
     )
     got_a = swap(send_a, "row", 1)
     pack_o = swap(pack, "row", 1)
-    keep_b, send_b = call(
-        leaf_b,
-        [((late, size, half), F32), ((late, size, half), BF16)],
-        solved_leaf, leaf_lower, rhs,
-        scratch=full, flops=2 * late * leaves * size * size * width,
-    )
-    got_b = swap(send_b, "row", 1)
+    kept_m, got_m = {}, {}
+    for m in range(early, levels):
+        kept_m[m], send_m = call(
+            leaf_one(m), [((1, size, half), F32), ((1, size, half), BF16)],
+            solved_leaf, leaf_lower, rhs,
+            scratch=full, flops=2 * leaves * size * size * width,
+        )
+        got_m[m] = swap(send_m, "row", 1)
     sol0, kept1, sent1 = call(
         zero_a, [((size, half), BF16), kept, sent],
         keep_a, got_a, pack, pack_o, inverse_0,
         scratch=[square], flops=4 * size * size * half,
     )
     got1 = swap(sent1, "col", 1)
-    kept2, sent2, kept3, sent3 = call(
-        zero_b, [kept, sent, kept, sent], keep_b, got_b, sol0, pack, pack_o,
-        scratch=[square], flops=4 * size * size * half,
-    )
-    got2 = swap(sent2, "col", 1)
-    got3 = swap(sent3, "col", 1)
+    for m in range(early, levels):
+        kept_m[m], sent_m = call(
+            zero_next(m), [kept, sent], kept_m[m], got_m[m], sol0, pack, pack_o,
+            scratch=[square], flops=2 * size * size * half,
+        )
+        got_m[m] = swap(sent_m, "col", 1)
     along_xo = swap(along_x, "row", 1)
     side = swap(call(stack, [((2 * (part_2 + short), half), BF16)], along, along_x), "col", 2)
     sol1, sol1_for_x, u2, u3 = call(
@@ -312,20 +318,20 @@
         kept1, got1, inverse_1, pack, pack_o, along, along_x, along_xo,
         flops=6 * size * size * quarter,
     )
-    w2 = call(difference, [sent], kept2, got2, u2)
+    w2 = call(difference, [sent], kept_m[2], got_m[2], u2)
     w2_y = swap(w2, "col", 2)
     sol0_o = swap(sol0, "row", 1)
     side_o = swap(side, "row", 1)
-    s3 = call(difference, [sent], kept3, got3, u3)
+    s3 = call(difference, [sent], kept_m[3], got_m[3], u3)
     s3_y = swap(s3, "col", 2)
     sol1_x = swap(sol1_for_x, "col", 1)
     out0 = call(join, [((size, width), BF16)], sol0, sol0_o)
-    sol2, v3, to_x = call(
-        two,
-        [((part_2, quarter), BF16), sent, ((size + part_2, quarter), BF16)],
-        w2, w2_y, s3, s3_y, pack_o, along, along_x, along_xo, side, side_o,
+    sol2, sol2_for_x, u3_2 = call(
+        two, [((part_2, quarter), BF16)] * 2 + [kept],
+        w2, w2_y, pack_o, along, along_x, along_xo, side, side_o,
         flops=4 * size * size * quarter,
     )
+    v3, to_x = call(top_share, [sent, ((size + part_2, quarter), BF16)], s3, s3_y, u3_2, sol2_for_x)
     v3_xz = swap(v3, "col", 5)
     from_x = swap(to_x, "col", 1)
     v3_z = swap(v3, "col", 4)

time: 42.8 us -> 40.5 us (0.946)
  waiting for transfers between devices: 13.2 us -> 10.3 us
  starting transfers between devices: 16.1 us -> 16.8 us
  local copies, waits for them, and re-layouts: 5.35 us -> 4.92 us
    ppermute x18 -> x19, waiting for transfers between devices: 13.2 us -> 10.3 us  [swap(): lax.ppermute(block, axis, [(low, low ^ stride) for low in range(count)])]
    ppermute x18 -> x19, starting transfers between devices: 16.1 us -> 16.8 us  [swap(): lax.ppermute(block, axis, [(low, low ^ stride) for low in range(count)])]
    unnamed x18, local copies, waits for them, and re-layouts: 5.35 us -> 4.92 us
    pallas_call x13 -> x16, Pallas kernels: 7.08 us -> 7.39 us  [call(): pl.pallas_call(kernel, out_shape=outs[0] if single else outs, in_specs=sp...]
  transfers between devices with their start and end apart: 18 -> 19, of which waited for: 8 -> 8; matrix products, arithmetic and copies ran while one was open for 0% -> 0% of each run, Pallas kernels for 10% -> 14%
where the time goes in v6:
time: 40.5 us; the launch traced here: 40.2 us
  starting transfers between devices  16.8 us (41%)
  waiting for transfers between devices  10.3 us (25%)
  Pallas kernels  7.39 us (18%)
  local copies, waits for them, and re-layouts  4.92 us (12%)
  between operations  0.79 us (2%)
    ppermute x19, starting transfers between devices, swap(): lax.ppermute(block, axis, [(low, low ^ stride) for low in range(count)])  16.8 us
    ppermute x19, waiting for transfers between devices, swap(): lax.ppermute(block, axis, [(low, low ^ stride) for low in range(count)])  10.3 us
    pallas_call x16, Pallas kernels, call(): pl.pallas_call(kernel, out_shape=outs[0] if single else outs, in_specs=sp...  7.39 us
    unnamed x18, local copies, waits for them, and re-layouts  4.92 us
  transfers between devices with their start and end apart: 19, of which 8 were waited for; matrix products, arithmetic and copies ran while one was open for 0% of the time, Pallas kernels for 14%

profile of v6, /device:TPU:0, one launch (start us, length us, event | category | flops | bytes accessed | tf_op | source)
XLA Modules:
  0.0 40.2 jit_solution(7086048049319045733)
XLA Ops:
  0.6 1.6 %copy-done = bf16[4,4,256,256]{3,2,1,0:T(8,128)(2,1)S(1)} copy-done((bf16[4,4,256,256]{3,2,1,0:T(8,128)(2,1)S(1)}, bf16[4,4,256,256]{3,2,1,0:T(8,128)(2,1)}, u32[]{:S(2)}) %copy-start) | copy-done | bytes 2097176
  2.2 1.0 %copy-done.2 = bf16[4,1,128,512]{3,2,1,0:T(8,128)(2,1)S(1)} copy-done((bf16[4,1,128,512]{3,2,1,0:T(8,128)(2,1)S(1)}, bf16[4,1,128,512]{3,2,1,0:T(8,128)(2,1)}, u32[]{:S(2)}) %copy-start.2) | copy-done | bytes 524312
  3.3 1.2 %copy-done.4 = bf16[4,256,512]{2,1,0:T(8,128)(2,1)S(1)} copy-done((bf16[4,256,512]{2,1,0:T(8,128)(2,1)S(1)}, bf16[4,256,512]{2,1,0:T(8,128)(2,1)}, u32[]{:S(2)}) %copy-start.4) | copy-done | bytes 1048600
  4.5 1.0 %copy-done.5 = bf16[4,256,256]{2,1,0:T(8,128)(2,1)S(1)} copy-done((bf16[4,256,256]{2,1,0:T(8,128)(2,1)S(1)}, bf16[4,256,256]{2,1,0:T(8,128)(2,1)}, u32[]{:S(2)}) %copy-start.5) | copy-done | bytes 524312
  5.5 1.2 %shard_map.147 = (bf16[4,256,512]{2,1,0:T(8,128)(2,1)S(1)}, f32[2,256,256]{2,1,0:T(8,128)S(1)}, bf16[2,256,256]{2,1,0:T(8,128)(2,1)S(1)}) custom-call(bf16[4,256,256]{2,1,0:T(8,128)(2,1)S(1)} %copy-done.5, bf16[4,256,512]{2,1,0:T(8,128)(2,1)S(1)} %copy-done.4, bf16[4,4,256,256]{3,2,1,0:T(8,128)(2,1)S(1)} %copy-done, bf16[4,1,128,512]{3,2,1,0:T(8,128)(2,1)S(1)} %copy-done.2), custom_call_target="tpu_custom_call" | custom-call | flops 805306368 | bytes 6029312 | tf_op jit(solution)/shard_map/pallas_call | solution.py:25
  6.7 0.6 %collective-permute-start = (bf16[2,256,256]{2,1,0:T(8,128)(2,1)S(1)}, bf16[2,256,256]{2,1,0:T(8,128)(2,1)S(1)}, u32[]{:S(2)}, u32[]{:S(2)}) collective-permute-start(bf16[2,256,256]{2,1,0:T(8,128)(2,1)S(1)} %get-tuple-element.33), channel_id=1, source_target_pairs={{0,1},{1,0},{2,3},{3,2},{4,5},{5,4},{6,7},{7,6},{8,9},{9,8},{10,11... | collective-permute-start | bytes 786440 | tf_op jit(solution)/shard_map/ppermute | solution.py:38
  7.3 1.3 %shard_map.148 = (bf16[544,256]{1,0:T(8,128)(2,1)S(1)}, bf16[288,256]{1,0:T(8,128)(2,1)S(1)}) custom-call(bf16[3,128,256]{2,1,0:T(8,128)(2,1)} %lower_0h.1, bf16[2,128,128]{2,1,0:T(8,128)(2,1)} %lower_1h.1, bf16[1,64,128]{2,1,0:T(8,128)(2,1)} %bitcast.2, s32[1,4,6]{2,1,0:T(4,128)} %bitcast.3, bf16[128,256]{1,0:T(8,128)(2,1)} %inverse.6, bf16[64,256]{1,0:T(8,128)(2,1)} %inv_2h.1), custom_call_target="tpu_custom_call" | custom-call | flops 4000000000 | bytes 802912 | tf_op jit(solution)/shard_map/pallas_call | solution.py:25
  8.7 2.9 %collective-permute-start.6 = (bf16[288,256]{1,0:T(8,128)(2,1)S(1)}, bf16[288,256]{1,0:T(8,128)(2,1)S(1)}, u32[]{:S(2)}, u32[]{:S(2)}) collective-permute-start(bf16[288,256]{1,0:T(8,128)(2,1)S(1)} %get-tuple-element.43.along), channel_id=1, source_target_pairs={{0,2},{2,0},{4,6},{6,4},{8,10},{10,8},{12,14},{14,12},{16,18},{18,... | collective-permute-start | bytes 442376 | tf_op jit(solution)/shard_map/ppermute | solution.py:38
  11.6 0.5 %shard_map.155 = (f32[1,256,256]{2,1,0:T(8,128)S(1)}, bf16[1,256,256]{2,1,0:T(8,128)(2,1)S(1)}) custom-call(bf16[4,256,512]{2,1,0:T(8,128)(2,1)S(1)} %get-tuple-element.36.solved, bf16[4,4,256,256]{3,2,1,0:T(8,128)(2,1)S(1)} %copy-done.1, bf16[4,1,128,512]{3,2,1,0:T(8,128)(2,1)S(1)} %copy-done.3), custom_call_target="tpu_custom_call" | custom-call | flops 268435456 | bytes 4063232 | tf_op jit(solution)/shard_map/pallas_call | solution.py:25
  12.3 0.5 %shard_map.151 = (f32[1,256,256]{2,1,0:T(8,128)S(1)}, bf16[1,256,256]{2,1,0:T(8,128)(2,1)S(1)}) custom-call(bf16[4,256,512]{2,1,0:T(8,128)(2,1)S(1)} %get-tuple-element.36.solved, bf16[4,4,256,256]{3,2,1,0:T(8,128)(2,1)S(1)} %copy-done.1, bf16[4,1,128,512]{3,2,1,0:T(8,128)(2,1)S(1)} %copy-done.3), custom_call_target="tpu_custom_call" | custom-call | flops 268435456 | bytes 4063232 | tf_op jit(solution)/shard_map/pallas_call | solution.py:25
  12.8 0.6 %collective-permute-start.3 = (bf16[1,256,256]{2,1,0:T(8,128)(2,1)S(1)}, bf16[1,256,256]{2,1,0:T(8,128)(2,1)S(1)}, u32[]{:S(2)}, u32[]{:S(2)}) collective-permute-start(bf16[1,256,256]{2,1,0:T(8,128)(2,1)S(1)} %get-tuple-element.38), channel_id=1, source_target_pairs={{0,1},{1,0},{2,3},{3,2},{4,5},{5,4},{6,7},{7,6},{8,9},{9,8},{10,11... | collective-permute-start | bytes 393224 | tf_op jit(solution)/shard_map/ppermute | solution.py:38
  13.4 2.4 %collective-permute-done.6.along_x = bf16[288,256]{1,0:T(8,128)(2,1)S(1)} collective-permute-done((bf16[288,256]{1,0:T(8,128)(2,1)S(1)}, bf16[288,256]{1,0:T(8,128)(2,1)S(1)}, u32[]{:S(2)}, u32[]{:S(2)}) %collective-permute-start.6) | collective-permute-done | bytes 147488 | tf_op jit(solution)/shard_map/ppermute | solution.py:38
  15.7 1.8 %collective-permute-start.12 = (bf16[192,256]{1,0:T(8,128)(2,1)S(1)}, bf16[192,256]{1,0:T(8,128)(2,1)S(1)}, u32[]{:S(2)}, u32[]{:S(2)}) collective-permute-start(bf16[192,256]{1,0:T(8,128)(2,1)S(1)} %shard_map.158), channel_id=1, source_target_pairs={{0,4},{2,6},{4,0},{6,2},{8,12},{10,14},{12,8},{14,10},{16,20},{18,... | collective-permute-start | bytes 294920 | tf_op jit(solution)/shard_map/ppermute | solution.py:38
  17.6 0.4 %shard_map.149 = (bf16[256,256]{1,0:T(8,128)(2,1)S(1)}, f32[256,128]{1,0:T(8,128)S(1)}, bf16[256,128]{1,0:T(8,128)(2,1)S(1)}) custom-call(f32[2,256,256]{2,1,0:T(8,128)S(1)} %get-tuple-element.32.keep, bf16[2,256,256]{2,1,0:T(8,128)(2,1)S(1)} %collective-permute-done.got, bf16[544,256]{1,0:T(8,128)(2,1)S(1)} %get-tuple-element.34.pack, ...), custom_call_target="tpu_custom_call" | custom-call | flops 67108864 | bytes 1802240 | tf_op jit(solution)/shard_map/pallas_call | solution.py:25
  18.0 1.6 %collective-permute-start.5 = (bf16[256,128]{1,0:T(8,128)(2,1)S(1)}, bf16[256,128]{1,0:T(8,128)(2,1)S(1)}, u32[]{:S(2)}, u32[]{:S(2)}) collective-permute-start(bf16[256,128]{1,0:T(8,128)(2,1)S(1)} %get-tuple-element.42), channel_id=1, source_target_pairs={{0,2},{2,0},{4,6},{6,4},{8,10},{10,8},{12,14},{14,12},{16,18},{18,... | collective-permute-start | bytes 196616 | tf_op jit(solution)/shard_map/ppermute | solution.py:38
  19.8 0.6 %collective-permute-start.10 = (bf16[256,128]{1,0:T(8,128)(2,1)S(1)}, bf16[256,128]{1,0:T(8,128)(2,1)S(1)}, u32[]{:S(2)}, u32[]{:S(2)}) collective-permute-start(bf16[256,128]{1,0:T(8,128)(2,1)S(1)} %get-tuple-element.48), channel_id=1, source_target_pairs={{0,2},{2,0},{4,6},{6,4},{8,10},{10,8},{12,14},{14,12},{16,18},{18,... | collective-permute-start | bytes 196616 | tf_op jit(solution)/shard_map/ppermute | solution.py:38
  20.7 1.6 %collective-permute-start.4 = (bf16[256,128]{1,0:T(8,128)(2,1)S(1)}, bf16[256,128]{1,0:T(8,128)(2,1)S(1)}, u32[]{:S(2)}, u32[]{:S(2)}) collective-permute-start(bf16[256,128]{1,0:T(8,128)(2,1)S(1)} %get-tuple-element.40), channel_id=1, source_target_pairs={{0,2},{2,0},{4,6},{6,4},{8,10},{10,8},{12,14},{14,12},{16,18},{18,... | collective-permute-start | bytes 196616 | tf_op jit(solution)/shard_map/ppermute | solution.py:38
  22.4 0.4 shard_map.153
  22.8 1.8 %collective-permute-done.10.got = bf16[256,128]{1,0:T(8,128)(2,1)S(1)} collective-permute-done((bf16[256,128]{1,0:T(8,128)(2,1)S(1)}, bf16[256,128]{1,0:T(8,128)(2,1)S(1)}, u32[]{:S(2)}, u32[]{:S(2)}) %collective-permute-start.10) | collective-permute-done | bytes 65568 | tf_op jit(solution)/shard_map/ppermute | solution.py:38
  24.6 0.6 %collective-permute-start.11 = (bf16[256,128]{1,0:T(8,128)(2,1)S(1)}, bf16[256,128]{1,0:T(8,128)(2,1)S(1)}, u32[]{:S(2)}, u32[]{:S(2)}) collective-permute-start(bf16[256,128]{1,0:T(8,128)(2,1)S(1)} %shard_map.157.w2), channel_id=1, source_target_pairs={{0,4},{2,6},{4,0},{6,2},{8,12},{10,14},{12,8},{14,10},{16,20},{18,... | collective-permute-start | bytes 196616 | tf_op jit(solution)/shard_map/ppermute | solution.py:38
  25.3 1.5 %collective-permute-start.8 = (bf16[256,128]{1,0:T(8,128)(2,1)S(1)}, bf16[256,128]{1,0:T(8,128)(2,1)S(1)}, u32[]{:S(2)}, u32[]{:S(2)}) collective-permute-start(bf16[256,128]{1,0:T(8,128)(2,1)S(1)} %shard_map.154.s3), channel_id=1, source_target_pairs={{0,4},{2,6},{4,0},{6,2},{8,12},{10,14},{12,8},{14,10},{16,20},{18,... | collective-permute-start | bytes 196616 | tf_op jit(solution)/shard_map/ppermute | solution.py:38
  26.8 2.1 %collective-permute-done.11.w2_y = bf16[256,128]{1,0:T(8,128)(2,1)S(1)} collective-permute-done((bf16[256,128]{1,0:T(8,128)(2,1)S(1)}, bf16[256,128]{1,0:T(8,128)(2,1)S(1)}, u32[]{:S(2)}, u32[]{:S(2)}) %collective-permute-start.11) | collective-permute-done | bytes 65568 | tf_op jit(solution)/shard_map/ppermute | solution.py:38
  28.9 0.8 %shard_map.159 = (bf16[64,128]{1,0:T(8,128)(2,1)S(1)}, bf16[64,128]{1,0:T(8,128)(2,1)S(1)}, f32[256,128]{1,0:T(8,128)S(1)}) custom-call(bf16[256,128]{1,0:T(8,128)(2,1)S(1)} %shard_map.157.w2, bf16[256,128]{1,0:T(8,128)(2,1)S(1)} %collective-permute-done.11.w2_y, bf16[544,256]{1,0:T(8,128)(2,1)S(1)} %collective-permute-done.1.pack_o, ...), custom_call_target="tpu_custom_call" | custom-call | flops 33554432 | bytes 1212416 | tf_op jit(solution)/shard_map/pallas_call | solution.py:25
  29.8 1.4 %collective-permute-start.16 = (bf16[320,128]{1,0:T(8,128)(2,1)S(1)}, bf16[320,128]{1,0:T(8,128)(2,1)S(1)}, u32[]{:S(2)}, u32[]{:S(2)}) collective-permute-start(bf16[320,128]{1,0:T(8,128)(2,1)S(1)} %get-tuple-element.53), channel_id=1, source_target_pairs={{0,2},{2,0},{4,6},{6,4},{8,10},{10,8},{12,14},{14,12},{16,18},{18,... | collective-permute-start | bytes 245768 | tf_op jit(solution)/shard_map/ppermute | solution.py:38
  31.2 1.6 %collective-permute-start.14 = (bf16[256,128]{1,0:T(8,128)(2,1)S(1)}, bf16[256,128]{1,0:T(8,128)(2,1)S(1)}, u32[]{:S(2)}, u32[]{:S(2)}) collective-permute-start(bf16[256,128]{1,0:T(8,128)(2,1)S(1)} %get-tuple-element.52.v3), channel_id=1, source_target_pairs={{0,8},{2,10},{4,12},{6,14},{8,0},{10,2},{12,4},{14,6},{16,24},{18,... | collective-permute-start | bytes 196616 | tf_op jit(solution)/shard_map/ppermute | solution.py:38
  32.8 0.6 %collective-permute-start.15 = (bf16[256,128]{1,0:T(8,128)(2,1)S(1)}, bf16[256,128]{1,0:T(8,128)(2,1)S(1)}, u32[]{:S(2)}, u32[]{:S(2)}) collective-permute-start(bf16[256,128]{1,0:T(8,128)(2,1)S(1)} %get-tuple-element.52.v3), channel_id=1, source_target_pairs={{0,10},{2,8},{4,14},{6,12},{8,2},{10,0},{12,6},{14,4},{16,26},{18,... | collective-permute-start | bytes 196616 | tf_op jit(solution)/shard_map/ppermute | solution.py:38
  33.3 1.4 %collective-permute-start.17 = (bf16[128,128]{1,0:T(8,128)(2,1)S(1)}, bf16[128,128]{1,0:T(8,128)(2,1)S(1)}, u32[]{:S(2)}, u32[]{:S(2)}) collective-permute-start(bf16[128,128]{1,0:T(8,128)(2,1)S(1)} %get-tuple-element.55), channel_id=1, source_target_pairs={{0,2},{2,0},{4,6},{6,4},{8,10},{10,8},{12,14},{14,12},{16,18},{18,... | collective-permute-start | bytes 98312 | tf_op jit(solution)/shard_map/ppermute | solution.py:38
  34.7 2.6 %collective-permute-done.17.sol1_x = bf16[128,128]{1,0:T(8,128)(2,1)S(1)} collective-permute-done((bf16[128,128]{1,0:T(8,128)(2,1)S(1)}, bf16[128,128]{1,0:T(8,128)(2,1)S(1)}, u32[]{:S(2)}, u32[]{:S(2)}) %collective-permute-start.17) | collective-permute-done | bytes 32800 | tf_op jit(solution)/shard_map/ppermute | solution.py:38
  37.3 0.7 %collective-permute-done.15.v3_xz = bf16[256,128]{1,0:T(8,128)(2,1)S(1)} collective-permute-done((bf16[256,128]{1,0:T(8,128)(2,1)S(1)}, bf16[256,128]{1,0:T(8,128)(2,1)S(1)}, u32[]{:S(2)}, u32[]{:S(2)}) %collective-permute-start.15) | collective-permute-done | bytes 65568 | tf_op jit(solution)/shard_map/ppermute | solution.py:38
  38.2 0.7 %shard_map.150 = bf16[256,512]{1,0:T(8,128)(2,1)} custom-call(bf16[256,256]{1,0:T(8,128)(2,1)S(1)} %get-tuple-element.35.own.solved, bf16[256,256]{1,0:T(8,128)(2,1)S(1)} %collective-permute-done.2.got), custom_call_target="tpu_custom_call" | custom-call | bytes 524288 | tf_op jit(solution)/shard_map/pallas_call | solution.py:25
  38.9 0.6 %collective-permute-done.18.got = bf16[224,256]{1,0:T(8,128)(2,1)S(1)} collective-permute-done((bf16[224,256]{1,0:T(8,128)(2,1)S(1)}, bf16[224,256]{1,0:T(8,128)(2,1)S(1)}, u32[]{:S(2)}, u32[]{:S(2)}) %collective-permute-start.18) | collective-permute-done | bytes 114720 | tf_op jit(solution)/shard_map/ppermute | solution.py:38
  39.5 0.7 %shard_map.162 = (bf16[128,512]{1,0:T(8,128)(2,1)}, bf16[64,512]{1,0:T(8,128)(2,1)}, bf16[32,512]{1,0:T(8,128)(2,1)}) custom-call(bf16[224,256]{1,0:T(8,128)(2,1)S(1)} %shard_map.161.own, bf16[224,256]{1,0:T(8,128)(2,1)S(1)} %collective-permute-done.18.got), custom_call_target="tpu_custom_call" | custom-call | bytes 458752 | tf_op jit(solution)/shard_map/pallas_call | solution.py:25
  (40 shorter events, 1.2 us)
Async XLA Ops:
  0.6 1.6 %copy-start = (bf16[4,4,256,256]{3,2,1,0:T(8,128)(2,1)S(1)}, bf16[4,4,256,256]{3,2,1,0:T(8,128)(2,1)}, u32[]{:S(2)}) copy-start(bf16[4,4,256,256]{3,2,1,0:T(8,128)(2,1)} %lower.5) | copy-start | bytes 6291460
  2.2 1.0 %copy-start.2 = (bf16[4,1,128,512]{3,2,1,0:T(8,128)(2,1)S(1)}, bf16[4,1,128,512]{3,2,1,0:T(8,128)(2,1)}, u32[]{:S(2)}) copy-start(bf16[4,1,128,512]{3,2,1,0:T(8,128)(2,1)} %rhs.5) | copy-start | bytes 1572868
  3.3 1.2 %copy-start.4 = (bf16[4,256,512]{2,1,0:T(8,128)(2,1)S(1)}, bf16[4,256,512]{2,1,0:T(8,128)(2,1)}, u32[]{:S(2)}) copy-start(bf16[4,256,512]{2,1,0:T(8,128)(2,1)} %right.1) | copy-start | bytes 3145732
  4.5 1.0 %copy-start.5 = (bf16[4,256,256]{2,1,0:T(8,128)(2,1)S(1)}, bf16[4,256,256]{2,1,0:T(8,128)(2,1)}, u32[]{:S(2)}) copy-start(bf16[4,256,256]{2,1,0:T(8,128)(2,1)} %inverse.4) | copy-start | bytes 1572868
  6.7 9.0 %collective-permute-start = (bf16[2,256,256]{2,1,0:T(8,128)(2,1)S(1)}, bf16[2,256,256]{2,1,0:T(8,128)(2,1)S(1)}, u32[]{:S(2)}, u32[]{:S(2)}) collective-permute-start(bf16[2,256,256]{2,1,0:T(8,128)(2,1)S(1)} %get-tuple-element.33), channel_id=1, source_target_pairs={{0,1},{1,0},{2,3},{3,2},{4,5},{5,4},{6,7},{7,6},{8,9},{9,8},{10,11... | collective-permute-start | bytes 786440 | tf_op jit(solution)/shard_map/ppermute | solution.py:38
  7.3 4.4 %copy-start.1 = (bf16[4,4,256,256]{3,2,1,0:T(8,128)(2,1)S(1)}, bf16[4,4,256,256]{3,2,1,0:T(8,128)(2,1)}, u32[]{:S(2)}) copy-start(bf16[4,4,256,256]{3,2,1,0:T(8,128)(2,1)} %lower.5) | copy-start | bytes 6291460
  7.3 4.4 %copy-start.3 = (bf16[4,1,128,512]{3,2,1,0:T(8,128)(2,1)S(1)}, bf16[4,1,128,512]{3,2,1,0:T(8,128)(2,1)}, u32[]{:S(2)}) copy-start(bf16[4,1,128,512]{3,2,1,0:T(8,128)(2,1)} %rhs.5) | copy-start | bytes 1572868
  8.6 9.0 %collective-permute-start.1 = (bf16[544,256]{1,0:T(8,128)(2,1)S(1)}, bf16[544,256]{1,0:T(8,128)(2,1)S(1)}, u32[]{:S(2)}, u32[]{:S(2)}) collective-permute-start(bf16[544,256]{1,0:T(8,128)(2,1)S(1)} %get-tuple-element.34.pack), channel_id=1, source_target_pairs={{0,1},{1,0},{2,3},{3,2},{4,5},{5,4},{6,7},{7,6},{8,9},{9,8},{10,11... | collective-permute-start | bytes 835592 | tf_op jit(solution)/shard_map/ppermute | solution.py:38
  8.7 7.0 %collective-permute-start.6 = (bf16[288,256]{1,0:T(8,128)(2,1)S(1)}, bf16[288,256]{1,0:T(8,128)(2,1)S(1)}, u32[]{:S(2)}, u32[]{:S(2)}) collective-permute-start(bf16[288,256]{1,0:T(8,128)(2,1)S(1)} %get-tuple-element.43.along), channel_id=1, source_target_pairs={{0,2},{2,0},{4,6},{6,4},{8,10},{10,8},{12,14},{14,12},{16,18},{18,... | collective-permute-start | bytes 442376 | tf_op jit(solution)/shard_map/ppermute | solution.py:38
  12.2 5.4 %copy-start.6 = (bf16[256,256]{1,0:T(8,128)(2,1)S(1)}, bf16[256,256]{1,0:T(8,128)(2,1)}, u32[]{:S(2)}) copy-start(bf16[256,256]{1,0:T(8,128)(2,1)} %inverse.5) | copy-start | bytes 393220
  12.2 7.4 %collective-permute-start.9 = (bf16[1,256,256]{2,1,0:T(8,128)(2,1)S(1)}, bf16[1,256,256]{2,1,0:T(8,128)(2,1)S(1)}, u32[]{:S(2)}, u32[]{:S(2)}) collective-permute-start(bf16[1,256,256]{2,1,0:T(8,128)(2,1)S(1)} %get-tuple-element.46), channel_id=1, source_target_pairs={{0,1},{1,0},{2,3},{3,2},{4,5},{5,4},{6,7},{7,6},{8,9},{9,8},{10,11... | collective-permute-start | bytes 393224 | tf_op jit(solution)/shard_map/ppermute | solution.py:38
  12.8 9.6 %copy-start.7 = (bf16[128,256]{1,0:T(8,128)(2,1)S(1)}, bf16[128,256]{1,0:T(8,128)(2,1)}, u32[]{:S(2)}) copy-start(bf16[128,256]{1,0:T(8,128)(2,1)} %inverse.6) | copy-start | bytes 196612
  12.8 7.6 %collective-permute-start.3 = (bf16[1,256,256]{2,1,0:T(8,128)(2,1)S(1)}, bf16[1,256,256]{2,1,0:T(8,128)(2,1)S(1)}, u32[]{:S(2)}, u32[]{:S(2)}) collective-permute-start(bf16[1,256,256]{2,1,0:T(8,128)(2,1)S(1)} %get-tuple-element.38), channel_id=1, source_target_pairs={{0,1},{1,0},{2,3},{3,2},{4,5},{5,4},{6,7},{7,6},{8,9},{9,8},{10,11... | collective-permute-start | bytes 393224 | tf_op jit(solution)/shard_map/ppermute | solution.py:38
  15.7 6.5 %collective-permute-start.7 = (bf16[288,256]{1,0:T(8,128)(2,1)S(1)}, bf16[288,256]{1,0:T(8,128)(2,1)S(1)}, u32[]{:S(2)}, u32[]{:S(2)}) collective-permute-start(bf16[288,256]{1,0:T(8,128)(2,1)S(1)} %collective-permute-done.6.along_x), channel_id=1, source_target_pairs={{0,1},{1,0},{2,3},{3,2},{4,5},{5,4},{6,7},{7,6},{8,9},{9,8},{10,11... | collective-permute-start | bytes 442376 | tf_op jit(solution)/shard_map/ppermute | solution.py:38
  15.7 6.5 %collective-permute-start.12 = (bf16[192,256]{1,0:T(8,128)(2,1)S(1)}, bf16[192,256]{1,0:T(8,128)(2,1)S(1)}, u32[]{:S(2)}, u32[]{:S(2)}) collective-permute-start(bf16[192,256]{1,0:T(8,128)(2,1)S(1)} %shard_map.158), channel_id=1, source_target_pairs={{0,4},{2,6},{4,0},{6,2},{8,12},{10,14},{12,8},{14,10},{16,20},{18,... | collective-permute-start | bytes 294920 | tf_op jit(solution)/shard_map/ppermute | solution.py:38
  18.0 4.3 %collective-permute-start.5 = (bf16[256,128]{1,0:T(8,128)(2,1)S(1)}, bf16[256,128]{1,0:T(8,128)(2,1)S(1)}, u32[]{:S(2)}, u32[]{:S(2)}) collective-permute-start(bf16[256,128]{1,0:T(8,128)(2,1)S(1)} %get-tuple-element.42), channel_id=1, source_target_pairs={{0,2},{2,0},{4,6},{6,4},{8,10},{10,8},{12,14},{14,12},{16,18},{18,... | collective-permute-start | bytes 196616 | tf_op jit(solution)/shard_map/ppermute | solution.py:38
  19.8 4.7 %collective-permute-start.10 = (bf16[256,128]{1,0:T(8,128)(2,1)S(1)}, bf16[256,128]{1,0:T(8,128)(2,1)S(1)}, u32[]{:S(2)}, u32[]{:S(2)}) collective-permute-start(bf16[256,128]{1,0:T(8,128)(2,1)S(1)} %get-tuple-element.48), channel_id=1, source_target_pairs={{0,2},{2,0},{4,6},{6,4},{8,10},{10,8},{12,14},{14,12},{16,18},{18,... | collective-permute-start | bytes 196616 | tf_op jit(solution)/shard_map/ppermute | solution.py:38
  20.4 17.5 %copy-start.8 = (bf16[32,256]{1,0:T(8,128)(2,1)S(1)}, bf16[32,256]{1,0:T(8,128)(2,1)}, u32[]{:S(2)}) copy-start(bf16[32,256]{1,0:T(8,128)(2,1)} %inverse.7) | copy-start | bytes 49156
  20.7 4.5 %collective-permute-start.4 = (bf16[256,128]{1,0:T(8,128)(2,1)S(1)}, bf16[256,128]{1,0:T(8,128)(2,1)S(1)}, u32[]{:S(2)}, u32[]{:S(2)}) collective-permute-start(bf16[256,128]{1,0:T(8,128)(2,1)S(1)} %get-tuple-element.40), channel_id=1, source_target_pairs={{0,2},{2,0},{4,6},{6,4},{8,10},{10,8},{12,14},{14,12},{16,18},{18,... | collective-permute-start | bytes 196616 | tf_op jit(solution)/shard_map/ppermute | solution.py:38
  22.3 4.5 %collective-permute-start.13 = (bf16[192,256]{1,0:T(8,128)(2,1)S(1)}, bf16[192,256]{1,0:T(8,128)(2,1)S(1)}, u32[]{:S(2)}, u32[]{:S(2)}) collective-permute-start(bf16[192,256]{1,0:T(8,128)(2,1)S(1)} %collective-permute-done.12.side), channel_id=1, source_target_pairs={{0,1},{1,0},{2,3},{3,2},{4,5},{5,4},{6,7},{7,6},{8,9},{9,8},{10,11... | collective-permute-start | bytes 294920 | tf_op jit(solution)/shard_map/ppermute | solution.py:38
  24.6 4.3 %collective-permute-start.11 = (bf16[256,128]{1,0:T(8,128)(2,1)S(1)}, bf16[256,128]{1,0:T(8,128)(2,1)S(1)}, u32[]{:S(2)}, u32[]{:S(2)}) collective-permute-start(bf16[256,128]{1,0:T(8,128)(2,1)S(1)} %shard_map.157.w2), channel_id=1, source_target_pairs={{0,4},{2,6},{4,0},{6,2},{8,12},{10,14},{12,8},{14,10},{16,20},{18,... | collective-permute-start | bytes 196616 | tf_op jit(solution)/shard_map/ppermute | solution.py:38
  25.3 4.5 %collective-permute-start.8 = (bf16[256,128]{1,0:T(8,128)(2,1)S(1)}, bf16[256,128]{1,0:T(8,128)(2,1)S(1)}, u32[]{:S(2)}, u32[]{:S(2)}) collective-permute-start(bf16[256,128]{1,0:T(8,128)(2,1)S(1)} %shard_map.154.s3), channel_id=1, source_target_pairs={{0,4},{2,6},{4,0},{6,2},{8,12},{10,14},{12,8},{14,10},{16,20},{18,... | collective-permute-start | bytes 196616 | tf_op jit(solution)/shard_map/ppermute | solution.py:38
  29.8 8.2 %collective-permute-start.16 = (bf16[320,128]{1,0:T(8,128)(2,1)S(1)}, bf16[320,128]{1,0:T(8,128)(2,1)S(1)}, u32[]{:S(2)}, u32[]{:S(2)}) collective-permute-start(bf16[320,128]{1,0:T(8,128)(2,1)S(1)} %get-tuple-element.53), channel_id=1, source_target_pairs={{0,2},{2,0},{4,6},{6,4},{8,10},{10,8},{12,14},{14,12},{16,18},{18,... | collective-permute-start | bytes 245768 | tf_op jit(solution)/shard_map/ppermute | solution.py:38
  31.2 6.1 %collective-permute-start.14 = (bf16[256,128]{1,0:T(8,128)(2,1)S(1)}, bf16[256,128]{1,0:T(8,128)(2,1)S(1)}, u32[]{:S(2)}, u32[]{:S(2)}) collective-permute-start(bf16[256,128]{1,0:T(8,128)(2,1)S(1)} %get-tuple-element.52.v3), channel_id=1, source_target_pairs={{0,8},{2,10},{4,12},{6,14},{8,0},{10,2},{12,4},{14,6},{16,24},{18,... | collective-permute-start | bytes 196616 | tf_op jit(solution)/shard_map/ppermute | solution.py:38
  32.8 5.2 %collective-permute-start.15 = (bf16[256,128]{1,0:T(8,128)(2,1)S(1)}, bf16[256,128]{1,0:T(8,128)(2,1)S(1)}, u32[]{:S(2)}, u32[]{:S(2)}) collective-permute-start(bf16[256,128]{1,0:T(8,128)(2,1)S(1)} %get-tuple-element.52.v3), channel_id=1, source_target_pairs={{0,10},{2,8},{4,14},{6,12},{8,2},{10,0},{12,6},{14,4},{16,26},{18,... | collective-permute-start | bytes 196616 | tf_op jit(solution)/shard_map/ppermute | solution.py:38
  33.3 3.9 %collective-permute-start.17 = (bf16[128,128]{1,0:T(8,128)(2,1)S(1)}, bf16[128,128]{1,0:T(8,128)(2,1)S(1)}, u32[]{:S(2)}, u32[]{:S(2)}) collective-permute-start(bf16[128,128]{1,0:T(8,128)(2,1)S(1)} %get-tuple-element.55), channel_id=1, source_target_pairs={{0,2},{2,0},{4,6},{6,4},{8,10},{10,8},{12,14},{14,12},{16,18},{18,... | collective-permute-start | bytes 98312 | tf_op jit(solution)/shard_map/ppermute | solution.py:38
  34.7 3.5 %collective-permute-start.2 = (bf16[256,256]{1,0:T(8,128)(2,1)S(1)}, bf16[256,256]{1,0:T(8,128)(2,1)S(1)}, u32[]{:S(2)}, u32[]{:S(2)}) collective-permute-start(bf16[256,256]{1,0:T(8,128)(2,1)S(1)} %get-tuple-element.35.own.solved), channel_id=1, source_target_pairs={{0,1},{1,0},{2,3},{3,2},{4,5},{5,4},{6,7},{7,6},{8,9},{9,8},{10,11... | collective-permute-start | bytes 393224 | tf_op jit(solution)/shard_map/ppermute | solution.py:38
  38.1 1.3 %collective-permute-start.18 = (bf16[224,256]{1,0:T(8,128)(2,1)S(1)}, bf16[224,256]{1,0:T(8,128)(2,1)S(1)}, u32[]{:S(2)}, u32[]{:S(2)}) collective-permute-start(bf16[224,256]{1,0:T(8,128)(2,1)S(1)} %shard_map.161.own), channel_id=1, source_target_pairs={{0,1},{1,0},{2,3},{3,2},{4,5},{5,4},{6,7},{7,6},{8,9},{9,8},{10,11... | collective-permute-start | bytes 344072 | tf_op jit(solution)/shard_map/ppermute | solution.py:38

commit v7 on v6

--- a/solution.py
+++ b/solution.py
@@ -118,11 +118,10 @@
         leaf_sum(m, m, solved, lower, rhs, keep, send, total)
 
 
-def leaf_one(m):
-    def kernel(solved, lower, rhs, keep, send, total):
-        leaf_sum(0, m, solved, lower, rhs, keep, send, total)
-
-    return kernel
+def leaf_b(solved, lower, rhs, keep, send, total):
+    late = keep.shape[0]
+    for m in range(late):
+        leaf_sum(m, lower.shape[0] - late + m, solved, lower, rhs, keep, send, total)
 
 
 def quarters(half):
@@ -152,10 +151,10 @@
     split(total, kept, sent)
 
 
-def zero_next(m):
+def zero_next(m, row):
     def kernel(keep, got, solved, pack, pack_o, kept, sent, total):
         rows = solved.shape[0] // 2
-        total[...] = keep[0] + got[0].astype(F32)
+        total[...] = keep[row] + got[row].astype(F32)
         for ref, at in zip((pack, pack_o), own_and_other(rows)):
             total[at, :] = total[at, :] - dot(ref[pl.ds((m - 1) * rows, rows), :], solved[...])
         split(total, kept, sent)
@@ -223,17 +222,21 @@
     to_x[pl.ds(size, solved_x.shape[0]), :] = solved_x[...]
 
 
-def three(v3, v3_z, v3_xz, from_x, inverse, sol1, sol1_x, sol2, out, full):
+def half_of(own, got, out):
+    mine, theirs = quarters(out.shape[1])
+    out[:, mine] = own[...]
+    out[:, theirs] = got[...]
+
+
+def three(v3, v3_z, v3_xz, from_x, inverse, sol2, out, full):
     size = v3.shape[0]
     own, other = quarters(out.shape[1])
     full[:, own] = (v3[...].astype(F32) + v3_z[...].astype(F32)).astype(BF16)
     full[:, other] = (from_x[pl.ds(0, size), :].astype(F32) + v3_xz[...].astype(F32)).astype(BF16)
-    n1, n2 = sol1.shape[0], sol2.shape[0]
-    out[pl.ds(0, n1), own] = sol1[...]
-    out[pl.ds(0, n1), other] = sol1_x[...]
-    out[pl.ds(n1, n2), own] = sol2[...]
-    out[pl.ds(n1, n2), other] = from_x[pl.ds(size, n2), :]
-    out[pl.ds(n1 + n2, inverse.shape[0]), :] = dot(inverse[...], full[...]).astype(BF16)
+    part = sol2.shape[0]
+    out[pl.ds(0, part), own] = sol2[...]
+    out[pl.ds(0, part), other] = from_x[pl.ds(size, part), :]
+    out[pl.ds(part, inverse.shape[0]), :] = dot(inverse[...], full[...]).astype(BF16)
 
 
 def join(own, got, *outs):
@@ -291,23 +294,24 @@
     )
     got_a = swap(send_a, "row", 1)
     pack_o = swap(pack, "row", 1)
-    kept_m, got_m = {}, {}
-    for m in range(early, levels):
-        kept_m[m], send_m = call(
-            leaf_one(m), [((1, size, half), F32), ((1, size, half), BF16)],
-            solved_leaf, leaf_lower, rhs,
-            scratch=full, flops=2 * leaves * size * size * width,
-        )
-        got_m[m] = swap(send_m, "row", 1)
+    late = levels - early
+    keep_b, send_b = call(
+        leaf_b,
+        [((late, size, half), F32), ((late, size, half), BF16)],
+        solved_leaf, leaf_lower, rhs,
+        scratch=full, flops=2 * late * leaves * size * size * width,
+    )
+    got_b = swap(send_b, "row", 1)
     sol0, kept1, sent1 = call(
         zero_a, [((size, half), BF16), kept, sent],
         keep_a, got_a, pack, pack_o, inverse_0,
         scratch=[square], flops=4 * size * size * half,
     )
     got1 = swap(sent1, "col", 1)
+    kept_m, got_m = {}, {}
     for m in range(early, levels):
         kept_m[m], sent_m = call(
-            zero_next(m), [kept, sent], kept_m[m], got_m[m], sol0, pack, pack_o,
+            zero_next(m, m - early), [kept, sent], keep_b, got_b, sol0, pack, pack_o,
             scratch=[square], flops=2 * size * size * half,
         )
         got_m[m] = swap(sent_m, "col", 1)
@@ -325,6 +329,9 @@
     s3 = call(difference, [sent], kept_m[3], got_m[3], u3)
     s3_y = swap(s3, "col", 2)
     sol1_x = swap(sol1_for_x, "col", 1)
+    sol1_half = call(half_of, [((part_1, half), BF16)], sol1, sol1_x)
+    sol1_o = swap(sol1_half, "row", 1)
+    out1 = call(join, [((part_1, width), BF16)], sol1_half, sol1_o)
     out0 = call(join, [((size, width), BF16)], sol0, sol0_o)
     sol2, sol2_for_x, u3_2 = call(
         two, [((part_2, quarter), BF16)] * 2 + [kept],
@@ -337,13 +344,13 @@
     v3_z = swap(v3, "col", 4)
     part_3 = inverse_3.shape[0]
     last = call(
-        three, [((part_1 + part_2 + part_3, half), BF16)],
-        v3, v3_z, v3_xz, from_x, inverse_3, sol1, sol1_x, sol2,
+        three, [((part_2 + part_3, half), BF16)],
+        v3, v3_z, v3_xz, from_x, inverse_3, sol2,
         scratch=[pltpu.VMEM((size, half), BF16)], flops=2 * inverse_3.size * half,
     )
     last_o = swap(last, "row", 1)
-    rest = call(join, [((part, width), BF16) for part in (part_1, part_2, part_3)], last, last_o)
-    return (out0, *rest)
+    rest = call(join, [((part, width), BF16) for part in (part_2, part_3)], last, last_o)
+    return (out0, out1, *rest)
 
 
 def solution(mesh):

time: 40.5 us -> 38.3 us (0.946)
  local copies, waits for them, and re-layouts: 4.92 us -> 0.45 us
  waiting for transfers between devices: 10.3 us -> 11.8 us
  Pallas kernels: 7.39 us -> 7.85 us
    unnamed x18 -> x14, local copies, waits for them, and re-layouts: 4.92 us -> 0.45 us
    ppermute x19, waiting for transfers between devices: 10.3 us -> 11.8 us  [swap(): lax.ppermute(block, axis, [(low, low ^ stride) for low in range(count)])]
    ppermute x19, starting transfers between devices: 16.8 us -> 17.2 us  [swap(): lax.ppermute(block, axis, [(low, low ^ stride) for low in range(count)])]
    pallas_call x16 -> x17, Pallas kernels: 7.39 us -> 7.85 us  [call(): pl.pallas_call(kernel, out_shape=outs[0] if single else outs, in_specs=sp...]
  transfers between devices with their start and end apart: 19 -> 19, of which waited for: 8 -> 6; matrix products, arithmetic and copies ran while one was open for 0% -> 0% of each run, Pallas kernels for 14% -> 15%
where the time goes in v7:
time: 38.3 us; the launch traced here: 38.2 us
  starting transfers between devices  17.2 us (45%)
  waiting for transfers between devices  11.8 us (31%)
  Pallas kernels  7.85 us (20%)
  between operations  0.84 us (2%)
  local copies, waits for them, and re-layouts  0.45 us (1%)
    ppermute x19, starting transfers between devices, swap(): lax.ppermute(block, axis, [(low, low ^ stride) for low in range(count)])  17.2 us
    ppermute x19, waiting for transfers between devices, swap(): lax.ppermute(block, axis, [(low, low ^ stride) for low in range(count)])  11.8 us
    pallas_call x17, Pallas kernels, call(): pl.pallas_call(kernel, out_shape=outs[0] if single else outs, in_specs=sp...  7.85 us
  transfers between devices with their start and end apart: 19, of which 6 were waited for; matrix products, arithmetic and copies ran while one was open for 0% of the time, Pallas kernels for 15%

profile of v7, /device:TPU:0, one launch (start us, length us, event | category | flops | bytes accessed | tf_op | source)
XLA Modules:
  0.0 38.2 jit_solution(5089192300529210099)
XLA Ops:
  0.7 1.3 %shard_map.148 = (bf16[544,256]{1,0:T(8,128)(2,1)S(1)}, bf16[288,256]{1,0:T(8,128)(2,1)S(1)}) custom-call(bf16[3,128,256]{2,1,0:T(8,128)(2,1)} %lower_0h.1, bf16[2,128,128]{2,1,0:T(8,128)(2,1)} %lower_1h.1, bf16[1,64,128]{2,1,0:T(8,128)(2,1)} %bitcast.2, s32[1,4,6]{2,1,0:T(4,128)} %bitcast.3, bf16[128,256]{1,0:T(8,128)(2,1)} %inverse.6, bf16[64,256]{1,0:T(8,128)(2,1)} %inv_2h.1), custom_call_target="tpu_custom_call" | custom-call | flops 4000000000 | bytes 802912 | tf_op jit(solution)/shard_map/pallas_call | solution.py:25
  2.0 0.6 %collective-permute-start.1 = (bf16[544,256]{1,0:T(8,128)(2,1)S(1)}, bf16[544,256]{1,0:T(8,128)(2,1)S(1)}, u32[]{:S(2)}, u32[]{:S(2)}) collective-permute-start(bf16[544,256]{1,0:T(8,128)(2,1)S(1)} %get-tuple-element.31.pack), channel_id=1, source_target_pairs={{0,1},{1,0},{2,3},{3,2},{4,5},{5,4},{6,7},{7,6},{8,9},{9,8},{10,11... | collective-permute-start | bytes 835592 | tf_op jit(solution)/shard_map/ppermute | solution.py:38
  2.5 0.3 copy-done.2
  2.8 0.1 copy-done.3
  3.0 1.2 %shard_map.147 = (bf16[4,256,512]{2,1,0:T(8,128)(2,1)S(1)}, f32[2,256,256]{2,1,0:T(8,128)S(1)}, bf16[2,256,256]{2,1,0:T(8,128)(2,1)S(1)}) custom-call(bf16[4,256,256]{2,1,0:T(8,128)(2,1)S(1)} %copy-done.3, bf16[4,256,512]{2,1,0:T(8,128)(2,1)S(1)} %copy-done.2, bf16[4,4,256,256]{3,2,1,0:T(8,128)(2,1)S(1)} %copy-done, bf16[4,1,128,512]{3,2,1,0:T(8,128)(2,1)S(1)} %copy-done.1), custom_call_target="tpu_custom_call" | custom-call | flops 805306368 | bytes 6029312 | tf_op jit(solution)/shard_map/pallas_call | solution.py:25
  4.2 0.6 %collective-permute-start = (bf16[2,256,256]{2,1,0:T(8,128)(2,1)S(1)}, bf16[2,256,256]{2,1,0:T(8,128)(2,1)S(1)}, u32[]{:S(2)}, u32[]{:S(2)}) collective-permute-start(bf16[2,256,256]{2,1,0:T(8,128)(2,1)S(1)} %get-tuple-element.30), channel_id=1, source_target_pairs={{0,1},{1,0},{2,3},{3,2},{4,5},{5,4},{6,7},{7,6},{8,9},{9,8},{10,11... | collective-permute-start | bytes 786440 | tf_op jit(solution)/shard_map/ppermute | solution.py:38
  4.7 0.9 %shard_map.154 = (f32[2,256,256]{2,1,0:T(8,128)S(1)}, bf16[2,256,256]{2,1,0:T(8,128)(2,1)S(1)}) custom-call(bf16[4,256,512]{2,1,0:T(8,128)(2,1)S(1)} %get-tuple-element.38.solved, bf16[4,4,256,256]{3,2,1,0:T(8,128)(2,1)S(1)} %copy-done, bf16[4,1,128,512]{3,2,1,0:T(8,128)(2,1)S(1)} %copy-done.1), custom_call_target="tpu_custom_call" | custom-call | flops 536870912 | bytes 4456448 | tf_op jit(solution)/shard_map/pallas_call | solution.py:25
  5.7 3.0 %collective-permute-start.4 = (bf16[288,256]{1,0:T(8,128)(2,1)S(1)}, bf16[288,256]{1,0:T(8,128)(2,1)S(1)}, u32[]{:S(2)}, u32[]{:S(2)}) collective-permute-start(bf16[288,256]{1,0:T(8,128)(2,1)S(1)} %get-tuple-element.35.along), channel_id=1, source_target_pairs={{0,2},{2,0},{4,6},{6,4},{8,10},{10,8},{12,14},{14,12},{16,18},{18,... | collective-permute-start | bytes 442376 | tf_op jit(solution)/shard_map/ppermute | solution.py:38
  8.7 4.1 %collective-permute-done.4.along_x = bf16[288,256]{1,0:T(8,128)(2,1)S(1)} collective-permute-done((bf16[288,256]{1,0:T(8,128)(2,1)S(1)}, bf16[288,256]{1,0:T(8,128)(2,1)S(1)}, u32[]{:S(2)}, u32[]{:S(2)}) %collective-permute-start.4) | collective-permute-done | bytes 147488 | tf_op jit(solution)/shard_map/ppermute | solution.py:38
  12.8 1.8 %collective-permute-start.13 = (bf16[192,256]{1,0:T(8,128)(2,1)S(1)}, bf16[192,256]{1,0:T(8,128)(2,1)S(1)}, u32[]{:S(2)}, u32[]{:S(2)}) collective-permute-start(bf16[192,256]{1,0:T(8,128)(2,1)S(1)} %shard_map.159), channel_id=1, source_target_pairs={{0,4},{2,6},{4,0},{6,2},{8,12},{10,14},{12,8},{14,10},{16,20},{18,... | collective-permute-start | bytes 294920 | tf_op jit(solution)/shard_map/ppermute | solution.py:38
  14.6 0.4 %shard_map.149 = (bf16[256,256]{1,0:T(8,128)(2,1)S(1)}, f32[256,128]{1,0:T(8,128)S(1)}, bf16[256,128]{1,0:T(8,128)(2,1)S(1)}) custom-call(f32[2,256,256]{2,1,0:T(8,128)S(1)} %get-tuple-element.29.keep, bf16[2,256,256]{2,1,0:T(8,128)(2,1)S(1)} %collective-permute-done.got, bf16[544,256]{1,0:T(8,128)(2,1)S(1)} %get-tuple-element.31.pack, ...), custom_call_target="tpu_custom_call" | custom-call | flops 67108864 | bytes 1802240 | tf_op jit(solution)/shard_map/pallas_call | solution.py:25
  15.1 1.6 %collective-permute-start.3 = (bf16[256,128]{1,0:T(8,128)(2,1)S(1)}, bf16[256,128]{1,0:T(8,128)(2,1)S(1)}, u32[]{:S(2)}, u32[]{:S(2)}) collective-permute-start(bf16[256,128]{1,0:T(8,128)(2,1)S(1)} %get-tuple-element.34), channel_id=1, source_target_pairs={{0,2},{2,0},{4,6},{6,4},{8,10},{10,8},{12,14},{14,12},{16,18},{18,... | collective-permute-start | bytes 196616 | tf_op jit(solution)/shard_map/ppermute | solution.py:38
  16.6 0.2 shard_map.157
  16.9 0.6 %collective-permute-start.11 = (bf16[256,128]{1,0:T(8,128)(2,1)S(1)}, bf16[256,128]{1,0:T(8,128)(2,1)S(1)}, u32[]{:S(2)}, u32[]{:S(2)}) collective-permute-start(bf16[256,128]{1,0:T(8,128)(2,1)S(1)} %get-tuple-element.45), channel_id=1, source_target_pairs={{0,2},{2,0},{4,6},{6,4},{8,10},{10,8},{12,14},{14,12},{16,18},{18,... | collective-permute-start | bytes 196616 | tf_op jit(solution)/shard_map/ppermute | solution.py:38
  17.5 0.2 shard_map.155
  17.8 1.6 %collective-permute-start.9 = (bf16[256,128]{1,0:T(8,128)(2,1)S(1)}, bf16[256,128]{1,0:T(8,128)(2,1)S(1)}, u32[]{:S(2)}, u32[]{:S(2)}) collective-permute-start(bf16[256,128]{1,0:T(8,128)(2,1)S(1)} %get-tuple-element.42), channel_id=1, source_target_pairs={{0,2},{2,0},{4,6},{6,4},{8,10},{10,8},{12,14},{14,12},{16,18},{18,... | collective-permute-start | bytes 196616 | tf_op jit(solution)/shard_map/ppermute | solution.py:38
  19.4 0.4 %shard_map.151 = (bf16[128,128]{1,0:T(8,128)(2,1)S(1)}, bf16[128,128]{1,0:T(8,128)(2,1)S(1)}, f32[256,128]{1,0:T(8,128)S(1)}, f32[256,128]{1,0:T(8,128)S(1)}) custom-call(f32[256,128]{1,0:T(8,128)S(1)} %get-tuple-element.33.kept, bf16[256,128]{1,0:T(8,128)(2,1)S(1)} %collective-permute-done.3.got, bf16[128,256]{1,0:T(8,128)(2,1)S(1)} %copy-done.5, ...), custom_call_target="tpu_custom_call" | custom-call | flops 50331648 | bytes 1589248 | tf_op jit(solution)/shard_map/pallas_call | solution.py:25
  19.8 1.8 %collective-permute-done.11.got = bf16[256,128]{1,0:T(8,128)(2,1)S(1)} collective-permute-done((bf16[256,128]{1,0:T(8,128)(2,1)S(1)}, bf16[256,128]{1,0:T(8,128)(2,1)S(1)}, u32[]{:S(2)}, u32[]{:S(2)}) %collective-permute-start.11) | collective-permute-done | bytes 65568 | tf_op jit(solution)/shard_map/ppermute | solution.py:38
  21.6 0.6 %collective-permute-start.12 = (bf16[256,128]{1,0:T(8,128)(2,1)S(1)}, bf16[256,128]{1,0:T(8,128)(2,1)S(1)}, u32[]{:S(2)}, u32[]{:S(2)}) collective-permute-start(bf16[256,128]{1,0:T(8,128)(2,1)S(1)} %shard_map.158.w2), channel_id=1, source_target_pairs={{0,4},{2,6},{4,0},{6,2},{8,12},{10,14},{12,8},{14,10},{16,20},{18,... | collective-permute-start | bytes 196616 | tf_op jit(solution)/shard_map/ppermute | solution.py:38
  22.3 1.5 %collective-permute-start.10 = (bf16[256,128]{1,0:T(8,128)(2,1)S(1)}, bf16[256,128]{1,0:T(8,128)(2,1)S(1)}, u32[]{:S(2)}, u32[]{:S(2)}) collective-permute-start(bf16[256,128]{1,0:T(8,128)(2,1)S(1)} %shard_map.156.s3), channel_id=1, source_target_pairs={{0,4},{2,6},{4,0},{6,2},{8,12},{10,14},{12,8},{14,10},{16,20},{18,... | collective-permute-start | bytes 196616 | tf_op jit(solution)/shard_map/ppermute | solution.py:38
  23.8 2.1 %collective-permute-done.12.w2_y = bf16[256,128]{1,0:T(8,128)(2,1)S(1)} collective-permute-done((bf16[256,128]{1,0:T(8,128)(2,1)S(1)}, bf16[256,128]{1,0:T(8,128)(2,1)S(1)}, u32[]{:S(2)}, u32[]{:S(2)}) %collective-permute-start.12) | collective-permute-done | bytes 65568 | tf_op jit(solution)/shard_map/ppermute | solution.py:38
  26.0 0.8 %shard_map.160 = (bf16[64,128]{1,0:T(8,128)(2,1)S(1)}, bf16[64,128]{1,0:T(8,128)(2,1)S(1)}, f32[256,128]{1,0:T(8,128)S(1)}) custom-call(bf16[256,128]{1,0:T(8,128)(2,1)S(1)} %shard_map.158.w2, bf16[256,128]{1,0:T(8,128)(2,1)S(1)} %collective-permute-done.12.w2_y, bf16[544,256]{1,0:T(8,128)(2,1)S(1)} %collective-permute-done.1.pack_o, ...), custom_call_target="tpu_custom_call" | custom-call | flops 33554432 | bytes 1212416 | tf_op jit(solution)/shard_map/pallas_call | solution.py:25
  26.8 1.4 %collective-permute-start.17 = (bf16[320,128]{1,0:T(8,128)(2,1)S(1)}, bf16[320,128]{1,0:T(8,128)(2,1)S(1)}, u32[]{:S(2)}, u32[]{:S(2)}) collective-permute-start(bf16[320,128]{1,0:T(8,128)(2,1)S(1)} %get-tuple-element.50), channel_id=1, source_target_pairs={{0,2},{2,0},{4,6},{6,4},{8,10},{10,8},{12,14},{14,12},{16,18},{18,... | collective-permute-start | bytes 245768 | tf_op jit(solution)/shard_map/ppermute | solution.py:38
  28.2 1.6 %collective-permute-start.15 = (bf16[256,128]{1,0:T(8,128)(2,1)S(1)}, bf16[256,128]{1,0:T(8,128)(2,1)S(1)}, u32[]{:S(2)}, u32[]{:S(2)}) collective-permute-start(bf16[256,128]{1,0:T(8,128)(2,1)S(1)} %get-tuple-element.49.v3), channel_id=1, source_target_pairs={{0,8},{2,10},{4,12},{6,14},{8,0},{10,2},{12,4},{14,6},{16,24},{18,... | collective-permute-start | bytes 196616 | tf_op jit(solution)/shard_map/ppermute | solution.py:38
  29.8 0.6 %collective-permute-start.16 = (bf16[256,128]{1,0:T(8,128)(2,1)S(1)}, bf16[256,128]{1,0:T(8,128)(2,1)S(1)}, u32[]{:S(2)}, u32[]{:S(2)}) collective-permute-start(bf16[256,128]{1,0:T(8,128)(2,1)S(1)} %get-tuple-element.49.v3), channel_id=1, source_target_pairs={{0,10},{2,8},{4,14},{6,12},{8,2},{10,0},{12,6},{14,4},{16,26},{18,... | collective-permute-start | bytes 196616 | tf_op jit(solution)/shard_map/ppermute | solution.py:38
  30.4 1.4 %collective-permute-start.6 = (bf16[128,128]{1,0:T(8,128)(2,1)S(1)}, bf16[128,128]{1,0:T(8,128)(2,1)S(1)}, u32[]{:S(2)}, u32[]{:S(2)}) collective-permute-start(bf16[128,128]{1,0:T(8,128)(2,1)S(1)} %get-tuple-element.37), channel_id=1, source_target_pairs={{0,2},{2,0},{4,6},{6,4},{8,10},{10,8},{12,14},{14,12},{16,18},{18,... | collective-permute-start | bytes 98312 | tf_op jit(solution)/shard_map/ppermute | solution.py:38
  31.7 3.6 %collective-permute-done.6.got = bf16[128,128]{1,0:T(8,128)(2,1)S(1)} collective-permute-done((bf16[128,128]{1,0:T(8,128)(2,1)S(1)}, bf16[128,128]{1,0:T(8,128)(2,1)S(1)}, u32[]{:S(2)}, u32[]{:S(2)}) %collective-permute-start.6) | collective-permute-done | bytes 32800 | tf_op jit(solution)/shard_map/ppermute | solution.py:38
  35.4 0.2 shard_map.162.own
  35.6 0.5 %collective-permute-start.18 = (bf16[96,256]{1,0:T(8,128)(2,1)S(1)}, bf16[96,256]{1,0:T(8,128)(2,1)S(1)}, u32[]{:S(2)}, u32[]{:S(2)}) collective-permute-start(bf16[96,256]{1,0:T(8,128)(2,1)S(1)} %shard_map.162.own), channel_id=1, source_target_pairs={{0,1},{1,0},{2,3},{3,2},{4,5},{5,4},{6,7},{7,6},{8,9},{9,8},{10,11... | collective-permute-start | bytes 147464 | tf_op jit(solution)/shard_map/ppermute | solution.py:38
  36.1 0.7 %shard_map.150 = bf16[256,512]{1,0:T(8,128)(2,1)} custom-call(bf16[256,256]{1,0:T(8,128)(2,1)S(1)} %get-tuple-element.32.own.solved, bf16[256,256]{1,0:T(8,128)(2,1)S(1)} %collective-permute-done.2.got), custom_call_target="tpu_custom_call" | custom-call | bytes 524288 | tf_op jit(solution)/shard_map/pallas_call | solution.py:25
  36.9 0.7 %shard_map.153 = bf16[128,512]{1,0:T(8,128)(2,1)} custom-call(bf16[128,256]{1,0:T(8,128)(2,1)S(1)} %shard_map.152.own, bf16[128,256]{1,0:T(8,128)(2,1)S(1)} %collective-permute-done.7.got), custom_call_target="tpu_custom_call" | custom-call | bytes 262144 | tf_op jit(solution)/shard_map/pallas_call | solution.py:25
  37.5 0.7 %shard_map.163 = (bf16[64,512]{1,0:T(8,128)(2,1)}, bf16[32,512]{1,0:T(8,128)(2,1)}) custom-call(bf16[96,256]{1,0:T(8,128)(2,1)S(1)} %shard_map.162.own, bf16[96,256]{1,0:T(8,128)(2,1)S(1)} %collective-permute-done.18.got), custom_call_target="tpu_custom_call" | custom-call | bytes 196608 | tf_op jit(solution)/shard_map/pallas_call | solution.py:25
  (37 shorter events, 0.5 us)
Async XLA Ops:
  0.6 1.9 %copy-start = (bf16[4,4,256,256]{3,2,1,0:T(8,128)(2,1)S(1)}, bf16[4,4,256,256]{3,2,1,0:T(8,128)(2,1)}, u32[]{:S(2)}) copy-start(bf16[4,4,256,256]{3,2,1,0:T(8,128)(2,1)} %lower.3) | copy-start | bytes 6291460
  0.6 1.9 %copy-start.1 = (bf16[4,1,128,512]{3,2,1,0:T(8,128)(2,1)S(1)}, bf16[4,1,128,512]{3,2,1,0:T(8,128)(2,1)}, u32[]{:S(2)}) copy-start(bf16[4,1,128,512]{3,2,1,0:T(8,128)(2,1)} %rhs.3) | copy-start | bytes 1572868
  0.7 2.2 %copy-start.2 = (bf16[4,256,512]{2,1,0:T(8,128)(2,1)S(1)}, bf16[4,256,512]{2,1,0:T(8,128)(2,1)}, u32[]{:S(2)}) copy-start(bf16[4,256,512]{2,1,0:T(8,128)(2,1)} %right.1) | copy-start | bytes 3145732
  0.7 2.3 %copy-start.3 = (bf16[4,256,256]{2,1,0:T(8,128)(2,1)S(1)}, bf16[4,256,256]{2,1,0:T(8,128)(2,1)}, u32[]{:S(2)}) copy-start(bf16[4,256,256]{2,1,0:T(8,128)(2,1)} %inverse.4) | copy-start | bytes 1572868
  2.0 12.6 %collective-permute-start.1 = (bf16[544,256]{1,0:T(8,128)(2,1)S(1)}, bf16[544,256]{1,0:T(8,128)(2,1)S(1)}, u32[]{:S(2)}, u32[]{:S(2)}) collective-permute-start(bf16[544,256]{1,0:T(8,128)(2,1)S(1)} %get-tuple-element.31.pack), channel_id=1, source_target_pairs={{0,1},{1,0},{2,3},{3,2},{4,5},{5,4},{6,7},{7,6},{8,9},{9,8},{10,11... | collective-permute-start | bytes 835592 | tf_op jit(solution)/shard_map/ppermute | solution.py:38
  4.1 10.5 %copy-start.4 = (bf16[256,256]{1,0:T(8,128)(2,1)S(1)}, bf16[256,256]{1,0:T(8,128)(2,1)}, u32[]{:S(2)}) copy-start(bf16[256,256]{1,0:T(8,128)(2,1)} %inverse.5) | copy-start | bytes 393220
  4.2 10.5 %collective-permute-start = (bf16[2,256,256]{2,1,0:T(8,128)(2,1)S(1)}, bf16[2,256,256]{2,1,0:T(8,128)(2,1)S(1)}, u32[]{:S(2)}, u32[]{:S(2)}) collective-permute-start(bf16[2,256,256]{2,1,0:T(8,128)(2,1)S(1)} %get-tuple-element.30), channel_id=1, source_target_pairs={{0,1},{1,0},{2,3},{3,2},{4,5},{5,4},{6,7},{7,6},{8,9},{9,8},{10,11... | collective-permute-start | bytes 786440 | tf_op jit(solution)/shard_map/ppermute | solution.py:38
  5.6 11.0 %collective-permute-start.8 = (bf16[2,256,256]{2,1,0:T(8,128)(2,1)S(1)}, bf16[2,256,256]{2,1,0:T(8,128)(2,1)S(1)}, u32[]{:S(2)}, u32[]{:S(2)}) collective-permute-start(bf16[2,256,256]{2,1,0:T(8,128)(2,1)S(1)} %get-tuple-element.40), channel_id=1, source_target_pairs={{0,1},{1,0},{2,3},{3,2},{4,5},{5,4},{6,7},{7,6},{8,9},{9,8},{10,11... | collective-permute-start | bytes 786440 | tf_op jit(solution)/shard_map/ppermute | solution.py:38
  5.7 7.1 %collective-permute-start.4 = (bf16[288,256]{1,0:T(8,128)(2,1)S(1)}, bf16[288,256]{1,0:T(8,128)(2,1)S(1)}, u32[]{:S(2)}, u32[]{:S(2)}) collective-permute-start(bf16[288,256]{1,0:T(8,128)(2,1)S(1)} %get-tuple-element.35.along), channel_id=1, source_target_pairs={{0,2},{2,0},{4,6},{6,4},{8,10},{10,8},{12,14},{14,12},{16,18},{18,... | collective-permute-start | bytes 442376 | tf_op jit(solution)/shard_map/ppermute | solution.py:38
  12.8 6.6 %collective-permute-start.5 = (bf16[288,256]{1,0:T(8,128)(2,1)S(1)}, bf16[288,256]{1,0:T(8,128)(2,1)S(1)}, u32[]{:S(2)}, u32[]{:S(2)}) collective-permute-start(bf16[288,256]{1,0:T(8,128)(2,1)S(1)} %collective-permute-done.4.along_x), channel_id=1, source_target_pairs={{0,1},{1,0},{2,3},{3,2},{4,5},{5,4},{6,7},{7,6},{8,9},{9,8},{10,11... | collective-permute-start | bytes 442376 | tf_op jit(solution)/shard_map/ppermute | solution.py:38
  12.8 6.5 %collective-permute-start.13 = (bf16[192,256]{1,0:T(8,128)(2,1)S(1)}, bf16[192,256]{1,0:T(8,128)(2,1)S(1)}, u32[]{:S(2)}, u32[]{:S(2)}) collective-permute-start(bf16[192,256]{1,0:T(8,128)(2,1)S(1)} %shard_map.159), channel_id=1, source_target_pairs={{0,4},{2,6},{4,0},{6,2},{8,12},{10,14},{12,8},{14,10},{16,20},{18,... | collective-permute-start | bytes 294920 | tf_op jit(solution)/shard_map/ppermute | solution.py:38
  14.6 4.8 %copy-start.5 = (bf16[128,256]{1,0:T(8,128)(2,1)S(1)}, bf16[128,256]{1,0:T(8,128)(2,1)}, u32[]{:S(2)}) copy-start(bf16[128,256]{1,0:T(8,128)(2,1)} %inverse.6) | copy-start | bytes 196612
  15.1 4.3 %collective-permute-start.3 = (bf16[256,128]{1,0:T(8,128)(2,1)S(1)}, bf16[256,128]{1,0:T(8,128)(2,1)S(1)}, u32[]{:S(2)}, u32[]{:S(2)}) collective-permute-start(bf16[256,128]{1,0:T(8,128)(2,1)S(1)} %get-tuple-element.34), channel_id=1, source_target_pairs={{0,2},{2,0},{4,6},{6,4},{8,10},{10,8},{12,14},{14,12},{16,18},{18,... | collective-permute-start | bytes 196616 | tf_op jit(solution)/shard_map/ppermute | solution.py:38
  16.9 4.7 %collective-permute-start.11 = (bf16[256,128]{1,0:T(8,128)(2,1)S(1)}, bf16[256,128]{1,0:T(8,128)(2,1)S(1)}, u32[]{:S(2)}, u32[]{:S(2)}) collective-permute-start(bf16[256,128]{1,0:T(8,128)(2,1)S(1)} %get-tuple-element.45), channel_id=1, source_target_pairs={{0,2},{2,0},{4,6},{6,4},{8,10},{10,8},{12,14},{14,12},{16,18},{18,... | collective-permute-start | bytes 196616 | tf_op jit(solution)/shard_map/ppermute | solution.py:38
  17.7 17.7 %copy-start.6 = (bf16[32,256]{1,0:T(8,128)(2,1)S(1)}, bf16[32,256]{1,0:T(8,128)(2,1)}, u32[]{:S(2)}) copy-start(bf16[32,256]{1,0:T(8,128)(2,1)} %inverse.7) | copy-start | bytes 49156
  17.8 4.5 %collective-permute-start.9 = (bf16[256,128]{1,0:T(8,128)(2,1)S(1)}, bf16[256,128]{1,0:T(8,128)(2,1)S(1)}, u32[]{:S(2)}, u32[]{:S(2)}) collective-permute-start(bf16[256,128]{1,0:T(8,128)(2,1)S(1)} %get-tuple-element.42), channel_id=1, source_target_pairs={{0,2},{2,0},{4,6},{6,4},{8,10},{10,8},{12,14},{14,12},{16,18},{18,... | collective-permute-start | bytes 196616 | tf_op jit(solution)/shard_map/ppermute | solution.py:38
  19.3 4.5 %collective-permute-start.14 = (bf16[192,256]{1,0:T(8,128)(2,1)S(1)}, bf16[192,256]{1,0:T(8,128)(2,1)S(1)}, u32[]{:S(2)}, u32[]{:S(2)}) collective-permute-start(bf16[192,256]{1,0:T(8,128)(2,1)S(1)} %collective-permute-done.13.side), channel_id=1, source_target_pairs={{0,1},{1,0},{2,3},{3,2},{4,5},{5,4},{6,7},{7,6},{8,9},{9,8},{10,11... | collective-permute-start | bytes 294920 | tf_op jit(solution)/shard_map/ppermute | solution.py:38
  21.6 4.3 %collective-permute-start.12 = (bf16[256,128]{1,0:T(8,128)(2,1)S(1)}, bf16[256,128]{1,0:T(8,128)(2,1)S(1)}, u32[]{:S(2)}, u32[]{:S(2)}) collective-permute-start(bf16[256,128]{1,0:T(8,128)(2,1)S(1)} %shard_map.158.w2), channel_id=1, source_target_pairs={{0,4},{2,6},{4,0},{6,2},{8,12},{10,14},{12,8},{14,10},{16,20},{18,... | collective-permute-start | bytes 196616 | tf_op jit(solution)/shard_map/ppermute | solution.py:38
  22.3 4.5 %collective-permute-start.10 = (bf16[256,128]{1,0:T(8,128)(2,1)S(1)}, bf16[256,128]{1,0:T(8,128)(2,1)S(1)}, u32[]{:S(2)}, u32[]{:S(2)}) collective-permute-start(bf16[256,128]{1,0:T(8,128)(2,1)S(1)} %shard_map.156.s3), channel_id=1, source_target_pairs={{0,4},{2,6},{4,0},{6,2},{8,12},{10,14},{12,8},{14,10},{16,20},{18,... | collective-permute-start | bytes 196616 | tf_op jit(solution)/shard_map/ppermute | solution.py:38
  26.8 8.6 %collective-permute-start.17 = (bf16[320,128]{1,0:T(8,128)(2,1)S(1)}, bf16[320,128]{1,0:T(8,128)(2,1)S(1)}, u32[]{:S(2)}, u32[]{:S(2)}) collective-permute-start(bf16[320,128]{1,0:T(8,128)(2,1)S(1)} %get-tuple-element.50), channel_id=1, source_target_pairs={{0,2},{2,0},{4,6},{6,4},{8,10},{10,8},{12,14},{14,12},{16,18},{18,... | collective-permute-start | bytes 245768 | tf_op jit(solution)/shard_map/ppermute | solution.py:38
  28.2 7.9 %collective-permute-start.2 = (bf16[256,256]{1,0:T(8,128)(2,1)S(1)}, bf16[256,256]{1,0:T(8,128)(2,1)S(1)}, u32[]{:S(2)}, u32[]{:S(2)}) collective-permute-start(bf16[256,256]{1,0:T(8,128)(2,1)S(1)} %get-tuple-element.32.own.solved), channel_id=1, source_target_pairs={{0,1},{1,0},{2,3},{3,2},{4,5},{5,4},{6,7},{7,6},{8,9},{9,8},{10,11... | collective-permute-start | bytes 393224 | tf_op jit(solution)/shard_map/ppermute | solution.py:38
  28.2 7.2 %collective-permute-start.15 = (bf16[256,128]{1,0:T(8,128)(2,1)S(1)}, bf16[256,128]{1,0:T(8,128)(2,1)S(1)}, u32[]{:S(2)}, u32[]{:S(2)}) collective-permute-start(bf16[256,128]{1,0:T(8,128)(2,1)S(1)} %get-tuple-element.49.v3), channel_id=1, source_target_pairs={{0,8},{2,10},{4,12},{6,14},{8,0},{10,2},{12,4},{14,6},{16,24},{18,... | collective-permute-start | bytes 196616 | tf_op jit(solution)/shard_map/ppermute | solution.py:38
  29.8 5.6 %collective-permute-start.16 = (bf16[256,128]{1,0:T(8,128)(2,1)S(1)}, bf16[256,128]{1,0:T(8,128)(2,1)S(1)}, u32[]{:S(2)}, u32[]{:S(2)}) collective-permute-start(bf16[256,128]{1,0:T(8,128)(2,1)S(1)} %get-tuple-element.49.v3), channel_id=1, source_target_pairs={{0,10},{2,8},{4,14},{6,12},{8,2},{10,0},{12,6},{14,4},{16,26},{18,... | collective-permute-start | bytes 196616 | tf_op jit(solution)/shard_map/ppermute | solution.py:38
  30.4 4.9 %collective-permute-start.6 = (bf16[128,128]{1,0:T(8,128)(2,1)S(1)}, bf16[128,128]{1,0:T(8,128)(2,1)S(1)}, u32[]{:S(2)}, u32[]{:S(2)}) collective-permute-start(bf16[128,128]{1,0:T(8,128)(2,1)S(1)} %get-tuple-element.37), channel_id=1, source_target_pairs={{0,2},{2,0},{4,6},{6,4},{8,10},{10,8},{12,14},{14,12},{16,18},{18,... | collective-permute-start | bytes 98312 | tf_op jit(solution)/shard_map/ppermute | solution.py:38
  35.3 1.5 %collective-permute-start.7 = (bf16[128,256]{1,0:T(8,128)(2,1)S(1)}, bf16[128,256]{1,0:T(8,128)(2,1)S(1)}, u32[]{:S(2)}, u32[]{:S(2)}) collective-permute-start(bf16[128,256]{1,0:T(8,128)(2,1)S(1)} %shard_map.152.own), channel_id=1, source_target_pairs={{0,1},{1,0},{2,3},{3,2},{4,5},{5,4},{6,7},{7,6},{8,9},{9,8},{10,11... | collective-permute-start | bytes 196616 | tf_op jit(solution)/shard_map/ppermute | solution.py:38
  35.6 1.9 %collective-permute-start.18 = (bf16[96,256]{1,0:T(8,128)(2,1)S(1)}, bf16[96,256]{1,0:T(8,128)(2,1)S(1)}, u32[]{:S(2)}, u32[]{:S(2)}) collective-permute-start(bf16[96,256]{1,0:T(8,128)(2,1)S(1)} %shard_map.162.own), channel_id=1, source_target_pairs={{0,1},{1,0},{2,3},{3,2},{4,5},{5,4},{6,7},{7,6},{8,9},{9,8},{10,11... | collective-permute-start | bytes 147464 | tf_op jit(solution)/shard_map/ppermute | solution.py:38

commit v8 on v7

--- a/solution.py
+++ b/solution.py
@@ -12,10 +12,6 @@
 
 def dot(a, b):
     return jnp.dot(a, b, preferred_element_type=F32)
-
-
-def dot_t(a, b):
-    return lax.dot_general(a, b, (((0,), (0,)), ((), ())), preferred_element_type=F32)
 
 
 def call(kernel, outs, *args, scratch=(), flops=0, specs=None):
@@ -54,14 +50,14 @@
 
 
 def prepare(
-    lower_0h, lower_1h, lower_2h, pattern_h, inv_1h, inv_2h, pack, along,
-    lower_0, lower_1, lower_2t, pattern, inv_1, inv_2, sems,
+    lower_0h, lower_1h, lower_2h, pattern_h, inv_1h, inv_2h, inv_3h, pack, along,
+    lower_0, lower_1, lower_2t, pattern, inv_1, inv_2, inv_3, sems,
 ):
     first = 0
     for copy in fetch_all(
         (
             (pattern_h, pattern), (lower_1h, lower_1), (lower_2h, lower_2t), (inv_1h, inv_1), (inv_2h, inv_2),
-            (lower_0h, lower_0),
+            (inv_3h, inv_3), (lower_0h, lower_0),
         ),
         sems,
     ):
@@ -88,14 +84,16 @@
         keep = jnp.where(lane == b, pattern[0, b, n0 + n1].astype(F32), keep)
     short = part_2 // 2
     cut = part_1 // 2
-    last = rows + cut + part_2
+    last = rows + cut + short
     for i in range(2):
         masked = (lower_2t[0, pl.ds(i * short, short), :].astype(F32) * keep).astype(BF16)
         pack[pl.ds(first + (n0 + 1) * rows, short), pl.ds(i * rows, rows)] = masked
         along[pl.ds(last, short), pl.ds(i * rows, rows)] = masked
     mine, _ = own_and_other(cut)
     along[pl.ds(rows, cut), :] = inv_1[mine, :]
-    along[pl.ds(rows + cut, part_2), :] = inv_2[...]
+    mine, _ = own_and_other(short)
+    along[pl.ds(rows + cut, short), :] = inv_2[mine, :]
+    along[pl.ds(last + short, inv_3.shape[0]), :] = inv_3[...]
 
 
 def leaf_sum(m, row, solved, lower, rhs, keep, send, total):
@@ -180,7 +178,8 @@
 
 def stack(along, along_x, out):
     part = out.shape[0] // 2
-    at = pl.ds(along.shape[0] - part, part)
+    rows = along.shape[1] // 2
+    at = pl.ds(rows + rows // 2, part)
     out[pl.ds(0, part), :] = along[at, :]
     out[pl.ds(part, part), :] = along_x[at, :]
 
@@ -189,37 +188,43 @@
     out[...] = (kept[...] + got[...].astype(F32) - update[...]).astype(BF16)
 
 
-def two(w2, w2_y, pack_o, along, along_x, along_xo, side, side_o, solved_own, solved_x, update):
-    size = w2.shape[0]
-    rows = size // 2
+def whole_2(inverse, along, pack_o, along_x, along_xo, side, side_o, inv_out, low_out, low_t):
+    part, size = inverse.shape
+    rows, short = size // 2, part // 2
+    me = lax.axis_index("row")
+    inv_out[pl.ds(0, part), :] = inverse[...]
+    first = rows + rows // 2
+    halves = [(along_x, along_xo, first), (side, side_o, 0), (side, side_o, part)]
+    for i, (mine, theirs, at) in enumerate(halves):
+        for ref, which in ((mine, me), (theirs, 1 - me)):
+            start = pl.multiple_of((i + 1) * part + which * short, short)
+            inv_out[pl.ds(start, short), :] = ref[pl.ds(at, short), :]
+    own, other = own_and_other(rows)
+    lows = [((along, first + short), (pack_o, pack_o.shape[0] - short))]
+    lows += [((mine, at + short), (theirs, at + short)) for mine, theirs, at in halves]
+    for i, pair in enumerate(lows):
+        for (ref, at), lanes in zip(pair, (own, other)):
+            block = ref[pl.ds(at, short), :].astype(F32)
+            low_t[pl.ds(i * part, short), lanes] = block[:, :rows]
+            low_t[pl.ds(i * part + short, short), lanes] = block[:, rows:]
+    low_out[...] = jnp.transpose(low_t[...]).astype(BF16)
+
+
+def two(w2, w2_y, inverse, low, solved_own, solved_x, update):
     part = solved_own.shape[0]
-    short = part // 2
     residual = (w2[...].astype(F32) + w2_y[...].astype(F32)).astype(BF16)
-    top = along.shape[0] - part - short
-    step = part + short
-    inverses = ((along, top), (along_x, top), (side, 0), (side, step))
-    mine_at = ((along, top + part), (along_x, top + part), (side, part), (side, step + part))
-    their_at = (
-        (pack_o, pack_o.shape[0] - short), (along_xo, top + part), (side_o, part), (side_o, step + part),
-    )
-    total = [0.0, 0.0]
-    for i, (ref, at) in enumerate(inverses):
-        solved = dot(ref[pl.ds(at, part), :], residual).astype(BF16)
-        if i < 2:
-            (solved_own, solved_x)[i][...] = solved
-        for j, (low, start) in enumerate((mine_at[i], their_at[i])):
-            block = low[pl.ds(start, short), :]
-            total[j] = total[j] + dot_t(block[:, :rows], solved[:short]) + dot_t(block[:, rows:], solved[short:])
-    for at, value in zip(own_and_other(rows), total):
-        update[at, :] = value
-
-
-def top_share(s3, s3_y, update, solved_x, v3, to_x):
-    size = v3.shape[0]
+    solved = dot(inverse[...], residual).astype(BF16)
+    solved_own[...] = solved[:part]
+    solved_x[...] = solved[part : 2 * part]
+    update[...] = dot(low[...], solved)
+
+
+def top_share(s3, s3_y, update, solved_x, along_x, v3, to_x):
     value = (s3[...].astype(F32) + s3_y[...].astype(F32) - update[...]).astype(BF16)
     v3[...] = value
-    to_x[pl.ds(0, size), :] = value
-    to_x[pl.ds(size, solved_x.shape[0]), :] = solved_x[...]
+    part = to_x.shape[0] - solved_x.shape[0]
+    to_x[pl.ds(0, part), :] = dot(along_x[pl.ds(along_x.shape[0] - part, part), :], value).astype(BF16)
+    to_x[pl.ds(part, solved_x.shape[0]), :] = solved_x[...]
 
 
 def half_of(own, got, out):
@@ -228,15 +233,16 @@
     out[:, theirs] = got[...]
 
 
-def three(v3, v3_z, v3_xz, from_x, inverse, sol2, out, full):
-    size = v3.shape[0]
+def three(v3, v3_z, v3_xz, from_x, inverse, sol2, out, full, solved):
     own, other = quarters(out.shape[1])
     full[:, own] = (v3[...].astype(F32) + v3_z[...].astype(F32)).astype(BF16)
-    full[:, other] = (from_x[pl.ds(0, size), :].astype(F32) + v3_xz[...].astype(F32)).astype(BF16)
-    part = sol2.shape[0]
+    full[:, other] = v3_xz[...]
+    part, top = sol2.shape[0], inverse.shape[0]
+    solved[...] = dot(inverse[...], full[...])
+    solved[:, other] = solved[:, other] + from_x[pl.ds(0, top), :].astype(F32)
     out[pl.ds(0, part), own] = sol2[...]
-    out[pl.ds(0, part), other] = from_x[pl.ds(size, part), :]
-    out[pl.ds(part, inverse.shape[0]), :] = dot(inverse[...], full[...]).astype(BF16)
+    out[pl.ds(0, part), other] = from_x[pl.ds(top, part), :]
+    out[pl.ds(part, top), :] = solved[...].astype(BF16)
 
 
 def join(own, got, *outs):
@@ -270,12 +276,13 @@
     square = pltpu.VMEM((size, half), F32)
     kept, sent = ((size, quarter), F32), ((size, quarter), BF16)
     lower_2t, pattern = jnp.swapaxes(lower_2, 1, 2), jnp.transpose(sparsity, (1, 2, 0))
-    sources = (lower_0, lower_1, lower_2t, pattern, inverse_1, inverse_2)
+    sources = (lower_0, lower_1, lower_2t, pattern, inverse_1, inverse_2, inverse_3)
+    part_3 = inverse_3.shape[0]
     pack, along = call(
         prepare,
         [
             (((n0 + 1) * rows + short, half), BF16),
-            ((rows + part_1 // 2 + part_2 + short, half), BF16),
+            ((rows + part_1 // 2 + 2 * short + part_3, half), BF16),
         ],
         *(pltpu.with_memory_space_constraint(x, pltpu.HBM) for x in sources),
         specs=[pl.BlockSpec(memory_space=pltpu.HBM)] * len(sources),
@@ -316,7 +323,7 @@
         )
         got_m[m] = swap(sent_m, "col", 1)
     along_xo = swap(along_x, "row", 1)
-    side = swap(call(stack, [((2 * (part_2 + short), half), BF16)], along, along_x), "col", 2)
+    side = swap(call(stack, [((4 * short, half), BF16)], along, along_x), "col", 2)
     sol1, sol1_for_x, u2, u3 = call(
         one, [((part_1, quarter), BF16)] * 2 + [kept] * 2,
         kept1, got1, inverse_1, pack, pack_o, along, along_x, along_xo,
@@ -333,20 +340,22 @@
     sol1_o = swap(sol1_half, "row", 1)
     out1 = call(join, [((part_1, width), BF16)], sol1_half, sol1_o)
     out0 = call(join, [((size, width), BF16)], sol0, sol0_o)
+    inv2, low2 = call(
+        whole_2, [((size, size), BF16)] * 2,
+        inverse_2, along, pack_o, along_x, along_xo, side, side_o, scratch=[pltpu.VMEM((size, size), F32)],
+    )
     sol2, sol2_for_x, u3_2 = call(
-        two, [((part_2, quarter), BF16)] * 2 + [kept],
-        w2, w2_y, pack_o, along, along_x, along_xo, side, side_o,
+        two, [((part_2, quarter), BF16)] * 2 + [kept], w2, w2_y, inv2, low2,
         flops=4 * size * size * quarter,
     )
-    v3, to_x = call(top_share, [sent, ((size + part_2, quarter), BF16)], s3, s3_y, u3_2, sol2_for_x)
+    v3, to_x = call(top_share, [sent, ((part_3 + part_2, quarter), BF16)], s3, s3_y, u3_2, sol2_for_x, along_x)
     v3_xz = swap(v3, "col", 5)
     from_x = swap(to_x, "col", 1)
     v3_z = swap(v3, "col", 4)
-    part_3 = inverse_3.shape[0]
     last = call(
         three, [((part_2 + part_3, half), BF16)],
         v3, v3_z, v3_xz, from_x, inverse_3, sol2,
-        scratch=[pltpu.VMEM((size, half), BF16)], flops=2 * inverse_3.size * half,
+        scratch=[pltpu.VMEM((size, half), BF16), pltpu.VMEM((part_3, half), F32)], flops=2 * inverse_3.size * half,
     )
     last_o = swap(last, "row", 1)
     rest = call(join, [((part, width), BF16) for part in (part_2, part_3)], last, last_o)

time: 38.3 us -> 36.9 us (0.963)
  waiting for transfers between devices: 11.8 us -> 10.7 us
    ppermute x19, waiting for transfers between devices: 11.8 us -> 10.7 us  [swap(): lax.ppermute(block, axis, [(low, low ^ stride) for low in range(count)])]
    pallas_call x17 -> x18, Pallas kernels: 7.85 us -> 7.7 us  [call(): pl.pallas_call(kernel, out_shape=outs[0] if single else outs, in_specs=sp...]
  transfers between devices with their start and end apart: 19 -> 19, of which waited for: 6 -> 8; matrix products, arithmetic and copies ran while one was open for 0% -> 0% of each run, Pallas kernels for 15% -> 16%
where the time goes in v8:
time: 36.9 us; the launch traced here: 36.8 us
  starting transfers between devices  17.1 us (46%)
  waiting for transfers between devices  10.7 us (29%)
  Pallas kernels  7.7 us (21%)
  between operations  0.81 us (2%)
  local copies, waits for them, and re-layouts  0.45 us (1%)
    ppermute x19, starting transfers between devices, swap(): lax.ppermute(block, axis, [(low, low ^ stride) for low in range(count)])  17.1 us
    ppermute x19, waiting for transfers between devices, swap(): lax.ppermute(block, axis, [(low, low ^ stride) for low in range(count)])  10.7 us
    pallas_call x18, Pallas kernels, call(): pl.pallas_call(kernel, out_shape=outs[0] if single else outs, in_specs=sp...  7.7 us
  transfers between devices with their start and end apart: 19, of which 8 were waited for; matrix products, arithmetic and copies ran while one was open for 0% of the time, Pallas kernels for 16%

profile of v8, /device:TPU:0, one launch (start us, length us, event | category | flops | bytes accessed | tf_op | source)
XLA Modules:
  0.0 36.8 jit_solution(15816889724292024452)
XLA Ops:
  0.7 1.3 %shard_map.148 = (bf16[544,256]{1,0:T(8,128)(2,1)S(1)}, bf16[288,256]{1,0:T(8,128)(2,1)S(1)}) custom-call(bf16[3,128,256]{2,1,0:T(8,128)(2,1)} %lower_0h.1, bf16[2,128,128]{2,1,0:T(8,128)(2,1)} %lower_1h.1, bf16[1,64,128]{2,1,0:T(8,128)(2,1)} %bitcast.2, s32[1,4,6]{2,1,0:T(4,128)} %bitcast.3, bf16[128,256]{1,0:T(8,128)(2,1)} %inverse.7, ...), custom_call_target="tpu_custom_call" | custom-call | flops 4000000000 | bytes 819296 | tf_op jit(solution)/shard_map/pallas_call | solution.py:21
  2.0 0.6 %collective-permute-start.1 = (bf16[544,256]{1,0:T(8,128)(2,1)S(1)}, bf16[544,256]{1,0:T(8,128)(2,1)S(1)}, u32[]{:S(2)}, u32[]{:S(2)}) collective-permute-start(bf16[544,256]{1,0:T(8,128)(2,1)S(1)} %get-tuple-element.33.pack), channel_id=1, source_target_pairs={{0,1},{1,0},{2,3},{3,2},{4,5},{5,4},{6,7},{7,6},{8,9},{9,8},{10,11... | collective-permute-start | bytes 835592 | tf_op jit(solution)/shard_map/ppermute | solution.py:34
  2.6 0.3 copy-done.2
  3.0 1.2 %shard_map.147 = (bf16[4,256,512]{2,1,0:T(8,128)(2,1)S(1)}, f32[2,256,256]{2,1,0:T(8,128)S(1)}, bf16[2,256,256]{2,1,0:T(8,128)(2,1)S(1)}) custom-call(bf16[4,256,256]{2,1,0:T(8,128)(2,1)S(1)} %copy-done.3, bf16[4,256,512]{2,1,0:T(8,128)(2,1)S(1)} %copy-done.2, bf16[4,4,256,256]{3,2,1,0:T(8,128)(2,1)S(1)} %copy-done, bf16[4,1,128,512]{3,2,1,0:T(8,128)(2,1)S(1)} %copy-done.1), custom_call_target="tpu_custom_call" | custom-call | flops 805306368 | bytes 6029312 | tf_op jit(solution)/shard_map/pallas_call | solution.py:21
  4.2 0.6 %collective-permute-start = (bf16[2,256,256]{2,1,0:T(8,128)(2,1)S(1)}, bf16[2,256,256]{2,1,0:T(8,128)(2,1)S(1)}, u32[]{:S(2)}, u32[]{:S(2)}) collective-permute-start(bf16[2,256,256]{2,1,0:T(8,128)(2,1)S(1)} %get-tuple-element.32), channel_id=1, source_target_pairs={{0,1},{1,0},{2,3},{3,2},{4,5},{5,4},{6,7},{7,6},{8,9},{9,8},{10,11... | collective-permute-start | bytes 786440 | tf_op jit(solution)/shard_map/ppermute | solution.py:34
  4.7 0.9 %shard_map.154 = (f32[2,256,256]{2,1,0:T(8,128)S(1)}, bf16[2,256,256]{2,1,0:T(8,128)(2,1)S(1)}) custom-call(bf16[4,256,512]{2,1,0:T(8,128)(2,1)S(1)} %get-tuple-element.40.solved, bf16[4,4,256,256]{3,2,1,0:T(8,128)(2,1)S(1)} %copy-done, bf16[4,1,128,512]{3,2,1,0:T(8,128)(2,1)S(1)} %copy-done.1), custom_call_target="tpu_custom_call" | custom-call | flops 536870912 | bytes 4456448 | tf_op jit(solution)/shard_map/pallas_call | solution.py:21
  5.7 3.0 %collective-permute-start.4 = (bf16[288,256]{1,0:T(8,128)(2,1)S(1)}, bf16[288,256]{1,0:T(8,128)(2,1)S(1)}, u32[]{:S(2)}, u32[]{:S(2)}) collective-permute-start(bf16[288,256]{1,0:T(8,128)(2,1)S(1)} %get-tuple-element.37.along), channel_id=1, source_target_pairs={{0,2},{2,0},{4,6},{6,4},{8,10},{10,8},{12,14},{14,12},{16,18},{18,... | collective-permute-start | bytes 442376 | tf_op jit(solution)/shard_map/ppermute | solution.py:34
  8.7 4.1 %collective-permute-done.4.along_x = bf16[288,256]{1,0:T(8,128)(2,1)S(1)} collective-permute-done((bf16[288,256]{1,0:T(8,128)(2,1)S(1)}, bf16[288,256]{1,0:T(8,128)(2,1)S(1)}, u32[]{:S(2)}, u32[]{:S(2)}) %collective-permute-start.4) | collective-permute-done | bytes 147488 | tf_op jit(solution)/shard_map/ppermute | solution.py:34
  12.8 1.8 %collective-permute-start.13 = (bf16[128,256]{1,0:T(8,128)(2,1)S(1)}, bf16[128,256]{1,0:T(8,128)(2,1)S(1)}, u32[]{:S(2)}, u32[]{:S(2)}) collective-permute-start(bf16[128,256]{1,0:T(8,128)(2,1)S(1)} %shard_map.159), channel_id=1, source_target_pairs={{0,4},{2,6},{4,0},{6,2},{8,12},{10,14},{12,8},{14,10},{16,20},{18,... | collective-permute-start | bytes 196616 | tf_op jit(solution)/shard_map/ppermute | solution.py:34
  14.6 0.4 %shard_map.149 = (bf16[256,256]{1,0:T(8,128)(2,1)S(1)}, f32[256,128]{1,0:T(8,128)S(1)}, bf16[256,128]{1,0:T(8,128)(2,1)S(1)}) custom-call(f32[2,256,256]{2,1,0:T(8,128)S(1)} %get-tuple-element.31.keep, bf16[2,256,256]{2,1,0:T(8,128)(2,1)S(1)} %collective-permute-done.got, bf16[544,256]{1,0:T(8,128)(2,1)S(1)} %get-tuple-element.33.pack, ...), custom_call_target="tpu_custom_call" | custom-call | flops 67108864 | bytes 1802240 | tf_op jit(solution)/shard_map/pallas_call | solution.py:21
  15.1 1.6 %collective-permute-start.3 = (bf16[256,128]{1,0:T(8,128)(2,1)S(1)}, bf16[256,128]{1,0:T(8,128)(2,1)S(1)}, u32[]{:S(2)}, u32[]{:S(2)}) collective-permute-start(bf16[256,128]{1,0:T(8,128)(2,1)S(1)} %get-tuple-element.36), channel_id=1, source_target_pairs={{0,2},{2,0},{4,6},{6,4},{8,10},{10,8},{12,14},{14,12},{16,18},{18,... | collective-permute-start | bytes 196616 | tf_op jit(solution)/shard_map/ppermute | solution.py:34
  16.6 0.2 shard_map.157
  16.9 0.6 %collective-permute-start.11 = (bf16[256,128]{1,0:T(8,128)(2,1)S(1)}, bf16[256,128]{1,0:T(8,128)(2,1)S(1)}, u32[]{:S(2)}, u32[]{:S(2)}) collective-permute-start(bf16[256,128]{1,0:T(8,128)(2,1)S(1)} %get-tuple-element.47), channel_id=1, source_target_pairs={{0,2},{2,0},{4,6},{6,4},{8,10},{10,8},{12,14},{14,12},{16,18},{18,... | collective-permute-start | bytes 196616 | tf_op jit(solution)/shard_map/ppermute | solution.py:34
  17.5 0.2 shard_map.155
  17.8 1.6 %collective-permute-start.9 = (bf16[256,128]{1,0:T(8,128)(2,1)S(1)}, bf16[256,128]{1,0:T(8,128)(2,1)S(1)}, u32[]{:S(2)}, u32[]{:S(2)}) collective-permute-start(bf16[256,128]{1,0:T(8,128)(2,1)S(1)} %get-tuple-element.44), channel_id=1, source_target_pairs={{0,2},{2,0},{4,6},{6,4},{8,10},{10,8},{12,14},{14,12},{16,18},{18,... | collective-permute-start | bytes 196616 | tf_op jit(solution)/shard_map/ppermute | solution.py:34
  19.4 0.4 %shard_map.151 = (bf16[128,128]{1,0:T(8,128)(2,1)S(1)}, bf16[128,128]{1,0:T(8,128)(2,1)S(1)}, f32[256,128]{1,0:T(8,128)S(1)}, f32[256,128]{1,0:T(8,128)S(1)}) custom-call(f32[256,128]{1,0:T(8,128)S(1)} %get-tuple-element.35.kept, bf16[256,128]{1,0:T(8,128)(2,1)S(1)} %collective-permute-done.3.got, bf16[128,256]{1,0:T(8,128)(2,1)S(1)} %copy-done.5, ...), custom_call_target="tpu_custom_call" | custom-call | flops 50331648 | bytes 1589248 | tf_op jit(solution)/shard_map/pallas_call | solution.py:21
  19.8 1.7 %collective-permute-done.11.got = bf16[256,128]{1,0:T(8,128)(2,1)S(1)} collective-permute-done((bf16[256,128]{1,0:T(8,128)(2,1)S(1)}, bf16[256,128]{1,0:T(8,128)(2,1)S(1)}, u32[]{:S(2)}, u32[]{:S(2)}) %collective-permute-start.11) | collective-permute-done | bytes 65568 | tf_op jit(solution)/shard_map/ppermute | solution.py:34
  21.6 0.6 %collective-permute-start.12 = (bf16[256,128]{1,0:T(8,128)(2,1)S(1)}, bf16[256,128]{1,0:T(8,128)(2,1)S(1)}, u32[]{:S(2)}, u32[]{:S(2)}) collective-permute-start(bf16[256,128]{1,0:T(8,128)(2,1)S(1)} %shard_map.158.w2), channel_id=1, source_target_pairs={{0,4},{2,6},{4,0},{6,2},{8,12},{10,14},{12,8},{14,10},{16,20},{18,... | collective-permute-start | bytes 196616 | tf_op jit(solution)/shard_map/ppermute | solution.py:34
  22.3 1.5 %collective-permute-start.10 = (bf16[256,128]{1,0:T(8,128)(2,1)S(1)}, bf16[256,128]{1,0:T(8,128)(2,1)S(1)}, u32[]{:S(2)}, u32[]{:S(2)}) collective-permute-start(bf16[256,128]{1,0:T(8,128)(2,1)S(1)} %shard_map.156.s3), channel_id=1, source_target_pairs={{0,4},{2,6},{4,0},{6,2},{8,12},{10,14},{12,8},{14,10},{16,20},{18,... | collective-permute-start | bytes 196616 | tf_op jit(solution)/shard_map/ppermute | solution.py:34
  23.9 2.0 %collective-permute-done.12.w2_y = bf16[256,128]{1,0:T(8,128)(2,1)S(1)} collective-permute-done((bf16[256,128]{1,0:T(8,128)(2,1)S(1)}, bf16[256,128]{1,0:T(8,128)(2,1)S(1)}, u32[]{:S(2)}, u32[]{:S(2)}) %collective-permute-start.12) | collective-permute-done | bytes 65568 | tf_op jit(solution)/shard_map/ppermute | solution.py:34
  25.9 0.4 %shard_map.161 = (bf16[64,128]{1,0:T(8,128)(2,1)S(1)}, bf16[64,128]{1,0:T(8,128)(2,1)S(1)}, f32[256,128]{1,0:T(8,128)S(1)}) custom-call(bf16[256,128]{1,0:T(8,128)(2,1)S(1)} %shard_map.158.w2, bf16[256,128]{1,0:T(8,128)(2,1)S(1)} %collective-permute-done.12.w2_y, bf16[256,256]{1,0:T(8,128)(2,1)S(1)} %get-tuple-element.49.inverse, ...), custom_call_target="tpu_custom_call" | custom-call | flops 33554432 | bytes 557056 | tf_op jit(solution)/shard_map/pallas_call | solution.py:21
  26.3 0.3 collective-permute-done.10.s3_y
  26.7 1.6 %collective-permute-start.15 = (bf16[256,128]{1,0:T(8,128)(2,1)S(1)}, bf16[256,128]{1,0:T(8,128)(2,1)S(1)}, u32[]{:S(2)}, u32[]{:S(2)}) collective-permute-start(bf16[256,128]{1,0:T(8,128)(2,1)S(1)} %get-tuple-element.53.v3), channel_id=1, source_target_pairs={{0,8},{2,10},{4,12},{6,14},{8,0},{10,2},{12,4},{14,6},{16,24},{18,... | collective-permute-start | bytes 196616 | tf_op jit(solution)/shard_map/ppermute | solution.py:34
  28.3 1.2 %collective-permute-start.16 = (bf16[256,128]{1,0:T(8,128)(2,1)S(1)}, bf16[256,128]{1,0:T(8,128)(2,1)S(1)}, u32[]{:S(2)}, u32[]{:S(2)}) collective-permute-start(bf16[256,128]{1,0:T(8,128)(2,1)S(1)} %get-tuple-element.53.v3), channel_id=1, source_target_pairs={{0,10},{2,8},{4,14},{6,12},{8,2},{10,0},{12,6},{14,4},{16,26},{18,... | collective-permute-start | bytes 196616 | tf_op jit(solution)/shard_map/ppermute | solution.py:34
  29.6 0.7 %collective-permute-start.6 = (bf16[128,128]{1,0:T(8,128)(2,1)S(1)}, bf16[128,128]{1,0:T(8,128)(2,1)S(1)}, u32[]{:S(2)}, u32[]{:S(2)}) collective-permute-start(bf16[128,128]{1,0:T(8,128)(2,1)S(1)} %get-tuple-element.39), channel_id=1, source_target_pairs={{0,2},{2,0},{4,6},{6,4},{8,10},{10,8},{12,14},{14,12},{16,18},{18,... | collective-permute-start | bytes 98312 | tf_op jit(solution)/shard_map/ppermute | solution.py:34
  30.2 1.4 %collective-permute-start.17 = (bf16[96,128]{1,0:T(8,128)(2,1)S(1)}, bf16[96,128]{1,0:T(8,128)(2,1)S(1)}, u32[]{:S(2)}, u32[]{:S(2)}) collective-permute-start(bf16[96,128]{1,0:T(8,128)(2,1)S(1)} %get-tuple-element.54), channel_id=1, source_target_pairs={{0,2},{2,0},{4,6},{6,4},{8,10},{10,8},{12,14},{14,12},{16,18},{18,... | collective-permute-start | bytes 73736 | tf_op jit(solution)/shard_map/ppermute | solution.py:34
  31.6 2.3 %collective-permute-done.6.got = bf16[128,128]{1,0:T(8,128)(2,1)S(1)} collective-permute-done((bf16[128,128]{1,0:T(8,128)(2,1)S(1)}, bf16[128,128]{1,0:T(8,128)(2,1)S(1)}, u32[]{:S(2)}, u32[]{:S(2)}) %collective-permute-start.6) | collective-permute-done | bytes 32800 | tf_op jit(solution)/shard_map/ppermute | solution.py:34
  34.1 0.2 shard_map.163.own
  34.3 0.4 collective-permute-start.18
  34.7 0.7 %shard_map.150 = bf16[256,512]{1,0:T(8,128)(2,1)} custom-call(bf16[256,256]{1,0:T(8,128)(2,1)S(1)} %get-tuple-element.34.own.solved, bf16[256,256]{1,0:T(8,128)(2,1)S(1)} %collective-permute-done.2.got), custom_call_target="tpu_custom_call" | custom-call | bytes 524288 | tf_op jit(solution)/shard_map/pallas_call | solution.py:21
  35.4 0.7 %shard_map.153 = bf16[128,512]{1,0:T(8,128)(2,1)} custom-call(bf16[128,256]{1,0:T(8,128)(2,1)S(1)} %shard_map.152.own, bf16[128,256]{1,0:T(8,128)(2,1)S(1)} %collective-permute-done.7.got), custom_call_target="tpu_custom_call" | custom-call | bytes 262144 | tf_op jit(solution)/shard_map/pallas_call | solution.py:21
  36.1 0.7 %shard_map.164 = (bf16[64,512]{1,0:T(8,128)(2,1)}, bf16[32,512]{1,0:T(8,128)(2,1)}) custom-call(bf16[96,256]{1,0:T(8,128)(2,1)S(1)} %shard_map.163.own, bf16[96,256]{1,0:T(8,128)(2,1)S(1)} %collective-permute-done.18.got), custom_call_target="tpu_custom_call" | custom-call | bytes 196608 | tf_op jit(solution)/shard_map/pallas_call | solution.py:21
  (40 shorter events, 1.1 us)
Async XLA Ops:
  0.6 1.9 %copy-start = (bf16[4,4,256,256]{3,2,1,0:T(8,128)(2,1)S(1)}, bf16[4,4,256,256]{3,2,1,0:T(8,128)(2,1)}, u32[]{:S(2)}) copy-start(bf16[4,4,256,256]{3,2,1,0:T(8,128)(2,1)} %lower.3) | copy-start | bytes 6291460
  0.6 1.9 %copy-start.1 = (bf16[4,1,128,512]{3,2,1,0:T(8,128)(2,1)S(1)}, bf16[4,1,128,512]{3,2,1,0:T(8,128)(2,1)}, u32[]{:S(2)}) copy-start(bf16[4,1,128,512]{3,2,1,0:T(8,128)(2,1)} %rhs.3) | copy-start | bytes 1572868
  0.7 2.2 %copy-start.2 = (bf16[4,256,512]{2,1,0:T(8,128)(2,1)S(1)}, bf16[4,256,512]{2,1,0:T(8,128)(2,1)}, u32[]{:S(2)}) copy-start(bf16[4,256,512]{2,1,0:T(8,128)(2,1)} %right.1) | copy-start | bytes 3145732
  0.7 2.3 %copy-start.3 = (bf16[4,256,256]{2,1,0:T(8,128)(2,1)S(1)}, bf16[4,256,256]{2,1,0:T(8,128)(2,1)}, u32[]{:S(2)}) copy-start(bf16[4,256,256]{2,1,0:T(8,128)(2,1)} %inverse.5) | copy-start | bytes 1572868
  2.0 12.6 %collective-permute-start.1 = (bf16[544,256]{1,0:T(8,128)(2,1)S(1)}, bf16[544,256]{1,0:T(8,128)(2,1)S(1)}, u32[]{:S(2)}, u32[]{:S(2)}) collective-permute-start(bf16[544,256]{1,0:T(8,128)(2,1)S(1)} %get-tuple-element.33.pack), channel_id=1, source_target_pairs={{0,1},{1,0},{2,3},{3,2},{4,5},{5,4},{6,7},{7,6},{8,9},{9,8},{10,11... | collective-permute-start | bytes 835592 | tf_op jit(solution)/shard_map/ppermute | solution.py:34
  4.2 10.5 %copy-start.4 = (bf16[256,256]{1,0:T(8,128)(2,1)S(1)}, bf16[256,256]{1,0:T(8,128)(2,1)}, u32[]{:S(2)}) copy-start(bf16[256,256]{1,0:T(8,128)(2,1)} %inverse.6) | copy-start | bytes 393220
  4.2 10.4 %collective-permute-start = (bf16[2,256,256]{2,1,0:T(8,128)(2,1)S(1)}, bf16[2,256,256]{2,1,0:T(8,128)(2,1)S(1)}, u32[]{:S(2)}, u32[]{:S(2)}) collective-permute-start(bf16[2,256,256]{2,1,0:T(8,128)(2,1)S(1)} %get-tuple-element.32), channel_id=1, source_target_pairs={{0,1},{1,0},{2,3},{3,2},{4,5},{5,4},{6,7},{7,6},{8,9},{9,8},{10,11... | collective-permute-start | bytes 786440 | tf_op jit(solution)/shard_map/ppermute | solution.py:34
  5.6 11.0 %collective-permute-start.8 = (bf16[2,256,256]{2,1,0:T(8,128)(2,1)S(1)}, bf16[2,256,256]{2,1,0:T(8,128)(2,1)S(1)}, u32[]{:S(2)}, u32[]{:S(2)}) collective-permute-start(bf16[2,256,256]{2,1,0:T(8,128)(2,1)S(1)} %get-tuple-element.42), channel_id=1, source_target_pairs={{0,1},{1,0},{2,3},{3,2},{4,5},{5,4},{6,7},{7,6},{8,9},{9,8},{10,11... | collective-permute-start | bytes 786440 | tf_op jit(solution)/shard_map/ppermute | solution.py:34
  5.7 7.0 %collective-permute-start.4 = (bf16[288,256]{1,0:T(8,128)(2,1)S(1)}, bf16[288,256]{1,0:T(8,128)(2,1)S(1)}, u32[]{:S(2)}, u32[]{:S(2)}) collective-permute-start(bf16[288,256]{1,0:T(8,128)(2,1)S(1)} %get-tuple-element.37.along), channel_id=1, source_target_pairs={{0,2},{2,0},{4,6},{6,4},{8,10},{10,8},{12,14},{14,12},{16,18},{18,... | collective-permute-start | bytes 442376 | tf_op jit(solution)/shard_map/ppermute | solution.py:34
  12.8 6.6 %collective-permute-start.5 = (bf16[288,256]{1,0:T(8,128)(2,1)S(1)}, bf16[288,256]{1,0:T(8,128)(2,1)S(1)}, u32[]{:S(2)}, u32[]{:S(2)}) collective-permute-start(bf16[288,256]{1,0:T(8,128)(2,1)S(1)} %collective-permute-done.4.along_x), channel_id=1, source_target_pairs={{0,1},{1,0},{2,3},{3,2},{4,5},{5,4},{6,7},{7,6},{8,9},{9,8},{10,11... | collective-permute-start | bytes 442376 | tf_op jit(solution)/shard_map/ppermute | solution.py:34
  12.8 6.5 %collective-permute-start.13 = (bf16[128,256]{1,0:T(8,128)(2,1)S(1)}, bf16[128,256]{1,0:T(8,128)(2,1)S(1)}, u32[]{:S(2)}, u32[]{:S(2)}) collective-permute-start(bf16[128,256]{1,0:T(8,128)(2,1)S(1)} %shard_map.159), channel_id=1, source_target_pairs={{0,4},{2,6},{4,0},{6,2},{8,12},{10,14},{12,8},{14,10},{16,20},{18,... | collective-permute-start | bytes 196616 | tf_op jit(solution)/shard_map/ppermute | solution.py:34
  14.6 4.8 %copy-start.5 = (bf16[128,256]{1,0:T(8,128)(2,1)S(1)}, bf16[128,256]{1,0:T(8,128)(2,1)}, u32[]{:S(2)}) copy-start(bf16[128,256]{1,0:T(8,128)(2,1)} %inverse.7) | copy-start | bytes 196612
  15.1 4.3 %collective-permute-start.3 = (bf16[256,128]{1,0:T(8,128)(2,1)S(1)}, bf16[256,128]{1,0:T(8,128)(2,1)S(1)}, u32[]{:S(2)}, u32[]{:S(2)}) collective-permute-start(bf16[256,128]{1,0:T(8,128)(2,1)S(1)} %get-tuple-element.36), channel_id=1, source_target_pairs={{0,2},{2,0},{4,6},{6,4},{8,10},{10,8},{12,14},{14,12},{16,18},{18,... | collective-permute-start | bytes 196616 | tf_op jit(solution)/shard_map/ppermute | solution.py:34
  16.9 6.9 %copy-start.6 = (bf16[64,256]{1,0:T(8,128)(2,1)S(1)}, bf16[64,256]{1,0:T(8,128)(2,1)}, u32[]{:S(2)}) copy-start(bf16[64,256]{1,0:T(8,128)(2,1)} %inverse.8) | copy-start | bytes 98308
  16.9 4.6 %collective-permute-start.11 = (bf16[256,128]{1,0:T(8,128)(2,1)S(1)}, bf16[256,128]{1,0:T(8,128)(2,1)S(1)}, u32[]{:S(2)}, u32[]{:S(2)}) collective-permute-start(bf16[256,128]{1,0:T(8,128)(2,1)S(1)} %get-tuple-element.47), channel_id=1, source_target_pairs={{0,2},{2,0},{4,6},{6,4},{8,10},{10,8},{12,14},{14,12},{16,18},{18,... | collective-permute-start | bytes 196616 | tf_op jit(solution)/shard_map/ppermute | solution.py:34
  17.8 16.4 %copy-start.7 = (bf16[32,256]{1,0:T(8,128)(2,1)S(1)}, bf16[32,256]{1,0:T(8,128)(2,1)}, u32[]{:S(2)}) copy-start(bf16[32,256]{1,0:T(8,128)(2,1)} %inverse.9) | copy-start | bytes 49156
  17.8 4.5 %collective-permute-start.9 = (bf16[256,128]{1,0:T(8,128)(2,1)S(1)}, bf16[256,128]{1,0:T(8,128)(2,1)S(1)}, u32[]{:S(2)}, u32[]{:S(2)}) collective-permute-start(bf16[256,128]{1,0:T(8,128)(2,1)S(1)} %get-tuple-element.44), channel_id=1, source_target_pairs={{0,2},{2,0},{4,6},{6,4},{8,10},{10,8},{12,14},{14,12},{16,18},{18,... | collective-permute-start | bytes 196616 | tf_op jit(solution)/shard_map/ppermute | solution.py:34
  19.3 4.4 %collective-permute-start.14 = (bf16[128,256]{1,0:T(8,128)(2,1)S(1)}, bf16[128,256]{1,0:T(8,128)(2,1)S(1)}, u32[]{:S(2)}, u32[]{:S(2)}) collective-permute-start(bf16[128,256]{1,0:T(8,128)(2,1)S(1)} %collective-permute-done.13.side), channel_id=1, source_target_pairs={{0,1},{1,0},{2,3},{3,2},{4,5},{5,4},{6,7},{7,6},{8,9},{9,8},{10,11... | collective-permute-start | bytes 196616 | tf_op jit(solution)/shard_map/ppermute | solution.py:34
  21.6 4.3 %collective-permute-start.12 = (bf16[256,128]{1,0:T(8,128)(2,1)S(1)}, bf16[256,128]{1,0:T(8,128)(2,1)S(1)}, u32[]{:S(2)}, u32[]{:S(2)}) collective-permute-start(bf16[256,128]{1,0:T(8,128)(2,1)S(1)} %shard_map.158.w2), channel_id=1, source_target_pairs={{0,4},{2,6},{4,0},{6,2},{8,12},{10,14},{12,8},{14,10},{16,20},{18,... | collective-permute-start | bytes 196616 | tf_op jit(solution)/shard_map/ppermute | solution.py:34
  22.3 4.3 %collective-permute-start.10 = (bf16[256,128]{1,0:T(8,128)(2,1)S(1)}, bf16[256,128]{1,0:T(8,128)(2,1)S(1)}, u32[]{:S(2)}, u32[]{:S(2)}) collective-permute-start(bf16[256,128]{1,0:T(8,128)(2,1)S(1)} %shard_map.156.s3), channel_id=1, source_target_pairs={{0,4},{2,6},{4,0},{6,2},{8,12},{10,14},{12,8},{14,10},{16,20},{18,... | collective-permute-start | bytes 196616 | tf_op jit(solution)/shard_map/ppermute | solution.py:34
  23.7 10.9 %collective-permute-start.2 = (bf16[256,256]{1,0:T(8,128)(2,1)S(1)}, bf16[256,256]{1,0:T(8,128)(2,1)S(1)}, u32[]{:S(2)}, u32[]{:S(2)}) collective-permute-start(bf16[256,256]{1,0:T(8,128)(2,1)S(1)} %get-tuple-element.34.own.solved), channel_id=1, source_target_pairs={{0,1},{1,0},{2,3},{3,2},{4,5},{5,4},{6,7},{7,6},{8,9},{9,8},{10,11... | collective-permute-start | bytes 393224 | tf_op jit(solution)/shard_map/ppermute | solution.py:34
  26.7 7.4 %collective-permute-start.15 = (bf16[256,128]{1,0:T(8,128)(2,1)S(1)}, bf16[256,128]{1,0:T(8,128)(2,1)S(1)}, u32[]{:S(2)}, u32[]{:S(2)}) collective-permute-start(bf16[256,128]{1,0:T(8,128)(2,1)S(1)} %get-tuple-element.53.v3), channel_id=1, source_target_pairs={{0,8},{2,10},{4,12},{6,14},{8,0},{10,2},{12,4},{14,6},{16,24},{18,... | collective-permute-start | bytes 196616 | tf_op jit(solution)/shard_map/ppermute | solution.py:34
  28.3 5.8 %collective-permute-start.16 = (bf16[256,128]{1,0:T(8,128)(2,1)S(1)}, bf16[256,128]{1,0:T(8,128)(2,1)S(1)}, u32[]{:S(2)}, u32[]{:S(2)}) collective-permute-start(bf16[256,128]{1,0:T(8,128)(2,1)S(1)} %get-tuple-element.53.v3), channel_id=1, source_target_pairs={{0,10},{2,8},{4,14},{6,12},{8,2},{10,0},{12,6},{14,4},{16,26},{18,... | collective-permute-start | bytes 196616 | tf_op jit(solution)/shard_map/ppermute | solution.py:34
  29.6 4.3 %collective-permute-start.6 = (bf16[128,128]{1,0:T(8,128)(2,1)S(1)}, bf16[128,128]{1,0:T(8,128)(2,1)S(1)}, u32[]{:S(2)}, u32[]{:S(2)}) collective-permute-start(bf16[128,128]{1,0:T(8,128)(2,1)S(1)} %get-tuple-element.39), channel_id=1, source_target_pairs={{0,2},{2,0},{4,6},{6,4},{8,10},{10,8},{12,14},{14,12},{16,18},{18,... | collective-permute-start | bytes 98312 | tf_op jit(solution)/shard_map/ppermute | solution.py:34
  30.2 3.9 %collective-permute-start.17 = (bf16[96,128]{1,0:T(8,128)(2,1)S(1)}, bf16[96,128]{1,0:T(8,128)(2,1)S(1)}, u32[]{:S(2)}, u32[]{:S(2)}) collective-permute-start(bf16[96,128]{1,0:T(8,128)(2,1)S(1)} %get-tuple-element.54), channel_id=1, source_target_pairs={{0,2},{2,0},{4,6},{6,4},{8,10},{10,8},{12,14},{14,12},{16,18},{18,... | collective-permute-start | bytes 73736 | tf_op jit(solution)/shard_map/ppermute | solution.py:34
  33.9 1.6 %collective-permute-start.7 = (bf16[128,256]{1,0:T(8,128)(2,1)S(1)}, bf16[128,256]{1,0:T(8,128)(2,1)S(1)}, u32[]{:S(2)}, u32[]{:S(2)}) collective-permute-start(bf16[128,256]{1,0:T(8,128)(2,1)S(1)} %shard_map.152.own), channel_id=1, source_target_pairs={{0,1},{1,0},{2,3},{3,2},{4,5},{5,4},{6,7},{7,6},{8,9},{9,8},{10,11... | collective-permute-start | bytes 196616 | tf_op jit(solution)/shard_map/ppermute | solution.py:34
  34.3 1.8 %collective-permute-start.18 = (bf16[96,256]{1,0:T(8,128)(2,1)S(1)}, bf16[96,256]{1,0:T(8,128)(2,1)S(1)}, u32[]{:S(2)}, u32[]{:S(2)}) collective-permute-start(bf16[96,256]{1,0:T(8,128)(2,1)S(1)} %shard_map.163.own), channel_id=1, source_target_pairs={{0,1},{1,0},{2,3},{3,2},{4,5},{5,4},{6,7},{7,6},{8,9},{9,8},{10,11... | collective-permute-start | bytes 147464 | tf_op jit(solution)/shard_map/ppermute | solution.py:34

commit v9 on v8

--- a/solution.py
+++ b/solution.py
@@ -96,30 +96,32 @@
     along[pl.ds(last + short, inv_3.shape[0]), :] = inv_3[...]
 
 
-def leaf_sum(m, row, solved, lower, rhs, keep, send, total):
-    leaves = lower.shape[1]
-    mine, _ = own_and_other(rhs.shape[2])
+def leaf_sum(m, row, solved, lower, rhs, keep, send):
+    leaves, size = lower.shape[1], lower.shape[2]
+    rows = rhs.shape[2]
+    first = lax.axis_index("row") == 0
     own, other = own_and_other(keep.shape[2])
-    acc = dot(lower[row, 0], solved[0])
-    for v in range(1, leaves):
-        acc = acc + dot(lower[row, v], solved[v])
-    total[...] = -acc
-    total[mine, :] = total[mine, :] + rhs[row, 0].astype(F32)
-    keep[m] = total[:, own]
-    send[m] = total[:, other].astype(BF16)
-
-
-def leaf_a(inverse, right, lower, rhs, solved, keep, send, total):
+    for lanes, out in ((other, send), (own, keep)):
+        acc = dot(lower[row, 0], solved[0, :, lanes])
+        for v in range(1, leaves):
+            acc = acc + dot(lower[row, v], solved[v, :, lanes])
+        piece = rhs[row, 0, :, lanes].astype(F32)
+        none = jnp.zeros_like(piece)
+        out[m, pl.ds(0, rows), :] = (jnp.where(first, piece, none) - acc[:rows]).astype(out.dtype)
+        out[m, pl.ds(rows, size - rows), :] = (jnp.where(first, none, piece) - acc[rows:]).astype(out.dtype)
+
+
+def leaf_a(inverse, right, lower, rhs, solved, keep, send):
     for v in range(inverse.shape[0]):
         solved[v] = dot(inverse[v], right[v]).astype(BF16)
     for m in range(keep.shape[0]):
-        leaf_sum(m, m, solved, lower, rhs, keep, send, total)
-
-
-def leaf_b(solved, lower, rhs, keep, send, total):
+        leaf_sum(m, m, solved, lower, rhs, keep, send)
+
+
+def leaf_b(solved, lower, rhs, keep, send):
     late = keep.shape[0]
     for m in range(late):
-        leaf_sum(m, lower.shape[0] - late + m, solved, lower, rhs, keep, send, total)
+        leaf_sum(m, lower.shape[0] - late + m, solved, lower, rhs, keep, send)
 
 
 def quarters(half):
@@ -132,30 +134,32 @@
 
 
 def split(total, kept, sent):
-    own, other = quarters(total.shape[1])
-    kept[...] = total[:, own]
-    sent[...] = total[:, other].astype(BF16)
-
-
-def zero_a(keep, got, pack, pack_o, inverse, solved_out, kept, sent, total):
-    size = inverse.shape[1]
-    rows = size // 2
+    part = kept.shape[1]
+    low, high = total[:, :part], total[:, part:]
+    first = lax.rem(lax.axis_index("col"), 2) == 0
+    kept[...] = jnp.where(first, low, high)
+    sent[...] = jnp.where(first, high, low).astype(BF16)
+
+
+def lower_block(pack, pack_o, m, rows):
+    at = pl.ds(m * rows, rows)
+    mine, theirs = pack[at, :], pack_o[at, :]
+    first = lax.axis_index("row") == 0
+    return jnp.concatenate([jnp.where(first, mine, theirs), jnp.where(first, theirs, mine)], axis=0)
+
+
+def zero_a(keep, got, pack, pack_o, inverse, solved_out, kept, sent):
     residual = (keep[0] + got[0].astype(F32)).astype(BF16)
     solved = dot(inverse[...], residual).astype(BF16)
     solved_out[...] = solved
-    total[...] = keep[1] + got[1].astype(F32)
-    for ref, at in zip((pack, pack_o), own_and_other(rows)):
-        total[at, :] = total[at, :] - dot(ref[pl.ds(0, rows), :], solved)
-    split(total, kept, sent)
+    low = lower_block(pack, pack_o, 0, inverse.shape[1] // 2)
+    split(keep[1] + got[1].astype(F32) - dot(low, solved), kept, sent)
 
 
 def zero_next(m, row):
-    def kernel(keep, got, solved, pack, pack_o, kept, sent, total):
-        rows = solved.shape[0] // 2
-        total[...] = keep[row] + got[row].astype(F32)
-        for ref, at in zip((pack, pack_o), own_and_other(rows)):
-            total[at, :] = total[at, :] - dot(ref[pl.ds((m - 1) * rows, rows), :], solved[...])
-        split(total, kept, sent)
+    def kernel(keep, got, solved, pack, pack_o, kept, sent):
+        low = lower_block(pack, pack_o, m - 1, solved.shape[0] // 2)
+        split(keep[row] + got[row].astype(F32) - dot(low, solved[...]), kept, sent)
 
     return kernel
 
@@ -268,12 +272,10 @@
     half = width // lax.axis_size("row")
     n0 = lower_0.shape[0]
     part_1, part_2 = inverse_1.shape[0], inverse_2.shape[0]
-    full = [pltpu.VMEM((size, width), F32)]
 
     early = 2
     short = part_2 // 2
     quarter = half // 2
-    square = pltpu.VMEM((size, half), F32)
     kept, sent = ((size, quarter), F32), ((size, quarter), BF16)
     lower_2t, pattern = jnp.swapaxes(lower_2, 1, 2), jnp.transpose(sparsity, (1, 2, 0))
     sources = (lower_0, lower_1, lower_2t, pattern, inverse_1, inverse_2, inverse_3)
@@ -297,7 +299,7 @@
         leaf_a,
         [((leaves, size, width), BF16), ((early, size, half), F32), ((early, size, half), BF16)],
         leaf_inverse, leaf_rhs, leaf_lower, rhs,
-        scratch=full, flops=2 * (1 + early) * leaves * size * size * width,
+        flops=2 * (1 + early) * leaves * size * size * width,
     )
     got_a = swap(send_a, "row", 1)
     pack_o = swap(pack, "row", 1)
@@ -306,20 +308,20 @@
         leaf_b,
         [((late, size, half), F32), ((late, size, half), BF16)],
         solved_leaf, leaf_lower, rhs,
-        scratch=full, flops=2 * late * leaves * size * size * width,
+        flops=2 * late * leaves * size * size * width,
     )
     got_b = swap(send_b, "row", 1)
     sol0, kept1, sent1 = call(
         zero_a, [((size, half), BF16), kept, sent],
         keep_a, got_a, pack, pack_o, inverse_0,
-        scratch=[square], flops=4 * size * size * half,
+        flops=4 * size * size * half,
     )
     got1 = swap(sent1, "col", 1)
     kept_m, got_m = {}, {}
     for m in range(early, levels):
         kept_m[m], sent_m = call(
             zero_next(m, m - early), [kept, sent], keep_b, got_b, sol0, pack, pack_o,
-            scratch=[square], flops=2 * size * size * half,
+            flops=2 * size * size * half,
         )
         got_m[m] = swap(sent_m, "col", 1)
     along_xo = swap(along_x, "row", 1)

time: 36.9 us -> 36.5 us (0.989)
  Pallas kernels: 7.7 us -> 7.22 us
    pallas_call x18, Pallas kernels: 7.7 us -> 7.22 us  [call(): pl.pallas_call(kernel, out_shape=outs[0] if single else outs, in_specs=sp...]
  transfers between devices with their start and end apart: 19 -> 19, of which waited for: 8 -> 8; matrix products, arithmetic and copies ran while one was open for 0% -> 0% of each run, Pallas kernels for 16% -> 14%
where the time goes in v9:
time: 36.5 us; the launch traced here: 36.4 us
  starting transfers between devices  17 us (47%)
  waiting for transfers between devices  10.8 us (30%)
  Pallas kernels  7.22 us (20%)
  between operations  0.82 us (2%)
  local copies, waits for them, and re-layouts  0.45 us (1%)
    ppermute x19, starting transfers between devices, swap(): lax.ppermute(block, axis, [(low, low ^ stride) for low in range(count)])  17 us
    ppermute x19, waiting for transfers between devices, swap(): lax.ppermute(block, axis, [(low, low ^ stride) for low in range(count)])  10.8 us
    pallas_call x18, Pallas kernels, call(): pl.pallas_call(kernel, out_shape=outs[0] if single else outs, in_specs=sp...  7.22 us
  transfers between devices with their start and end apart: 19, of which 8 were waited for; matrix products, arithmetic and copies ran while one was open for 0% of the time, Pallas kernels for 14%

profile of v9, /device:TPU:0, one launch (start us, length us, event | category | flops | bytes accessed | tf_op | source)
XLA Modules:
  0.0 36.4 jit_solution(6748092883225054486)
XLA Ops:
  0.7 1.3 %shard_map.148 = (bf16[544,256]{1,0:T(8,128)(2,1)S(1)}, bf16[288,256]{1,0:T(8,128)(2,1)S(1)}) custom-call(bf16[3,128,256]{2,1,0:T(8,128)(2,1)} %lower_0h.1, bf16[2,128,128]{2,1,0:T(8,128)(2,1)} %lower_1h.1, bf16[1,64,128]{2,1,0:T(8,128)(2,1)} %bitcast.2, s32[1,4,6]{2,1,0:T(4,128)} %bitcast.3, bf16[128,256]{1,0:T(8,128)(2,1)} %inverse.7, ...), custom_call_target="tpu_custom_call" | custom-call | flops 4000000000 | bytes 819296 | tf_op jit(solution)/shard_map/pallas_call | solution.py:21
  2.0 0.6 %collective-permute-start.1 = (bf16[544,256]{1,0:T(8,128)(2,1)S(1)}, bf16[544,256]{1,0:T(8,128)(2,1)S(1)}, u32[]{:S(2)}, u32[]{:S(2)}) collective-permute-start(bf16[544,256]{1,0:T(8,128)(2,1)S(1)} %get-tuple-element.33.pack), channel_id=1, source_target_pairs={{0,1},{1,0},{2,3},{3,2},{4,5},{5,4},{6,7},{7,6},{8,9},{9,8},{10,11... | collective-permute-start | bytes 835592 | tf_op jit(solution)/shard_map/ppermute | solution.py:34
  2.6 0.3 copy-done.2
  3.0 1.0 %shard_map.147 = (bf16[4,256,512]{2,1,0:T(8,128)(2,1)S(1)}, f32[2,256,256]{2,1,0:T(8,128)S(1)}, bf16[2,256,256]{2,1,0:T(8,128)(2,1)S(1)}) custom-call(bf16[4,256,256]{2,1,0:T(8,128)(2,1)S(1)} %copy-done.3, bf16[4,256,512]{2,1,0:T(8,128)(2,1)S(1)} %copy-done.2, bf16[4,4,256,256]{3,2,1,0:T(8,128)(2,1)S(1)} %copy-done, bf16[4,1,128,512]{3,2,1,0:T(8,128)(2,1)S(1)} %copy-done.1), custom_call_target="tpu_custom_call" | custom-call | flops 805306368 | bytes 6029312 | tf_op jit(solution)/shard_map/pallas_call | solution.py:21
  4.0 0.6 %collective-permute-start = (bf16[2,256,256]{2,1,0:T(8,128)(2,1)S(1)}, bf16[2,256,256]{2,1,0:T(8,128)(2,1)S(1)}, u32[]{:S(2)}, u32[]{:S(2)}) collective-permute-start(bf16[2,256,256]{2,1,0:T(8,128)(2,1)S(1)} %get-tuple-element.32), channel_id=1, source_target_pairs={{0,1},{1,0},{2,3},{3,2},{4,5},{5,4},{6,7},{7,6},{8,9},{9,8},{10,11... | collective-permute-start | bytes 786440 | tf_op jit(solution)/shard_map/ppermute | solution.py:34
  4.6 0.7 %shard_map.154 = (f32[2,256,256]{2,1,0:T(8,128)S(1)}, bf16[2,256,256]{2,1,0:T(8,128)(2,1)S(1)}) custom-call(bf16[4,256,512]{2,1,0:T(8,128)(2,1)S(1)} %get-tuple-element.40.solved, bf16[4,4,256,256]{3,2,1,0:T(8,128)(2,1)S(1)} %copy-done, bf16[4,1,128,512]{3,2,1,0:T(8,128)(2,1)S(1)} %copy-done.1), custom_call_target="tpu_custom_call" | custom-call | flops 536870912 | bytes 4456448 | tf_op jit(solution)/shard_map/pallas_call | solution.py:21
  5.4 3.0 %collective-permute-start.4 = (bf16[288,256]{1,0:T(8,128)(2,1)S(1)}, bf16[288,256]{1,0:T(8,128)(2,1)S(1)}, u32[]{:S(2)}, u32[]{:S(2)}) collective-permute-start(bf16[288,256]{1,0:T(8,128)(2,1)S(1)} %get-tuple-element.37.along), channel_id=1, source_target_pairs={{0,2},{2,0},{4,6},{6,4},{8,10},{10,8},{12,14},{14,12},{16,18},{18,... | collective-permute-start | bytes 442376 | tf_op jit(solution)/shard_map/ppermute | solution.py:34
  8.3 4.1 %collective-permute-done.4.along_x = bf16[288,256]{1,0:T(8,128)(2,1)S(1)} collective-permute-done((bf16[288,256]{1,0:T(8,128)(2,1)S(1)}, bf16[288,256]{1,0:T(8,128)(2,1)S(1)}, u32[]{:S(2)}, u32[]{:S(2)}) %collective-permute-start.4) | collective-permute-done | bytes 147488 | tf_op jit(solution)/shard_map/ppermute | solution.py:34
  12.4 1.8 %collective-permute-start.13 = (bf16[128,256]{1,0:T(8,128)(2,1)S(1)}, bf16[128,256]{1,0:T(8,128)(2,1)S(1)}, u32[]{:S(2)}, u32[]{:S(2)}) collective-permute-start(bf16[128,256]{1,0:T(8,128)(2,1)S(1)} %shard_map.159), channel_id=1, source_target_pairs={{0,4},{2,6},{4,0},{6,2},{8,12},{10,14},{12,8},{14,10},{16,20},{18,... | collective-permute-start | bytes 196616 | tf_op jit(solution)/shard_map/ppermute | solution.py:34
  14.3 0.4 %shard_map.149 = (bf16[256,256]{1,0:T(8,128)(2,1)S(1)}, f32[256,128]{1,0:T(8,128)S(1)}, bf16[256,128]{1,0:T(8,128)(2,1)S(1)}) custom-call(f32[2,256,256]{2,1,0:T(8,128)S(1)} %get-tuple-element.31.keep, bf16[2,256,256]{2,1,0:T(8,128)(2,1)S(1)} %collective-permute-done.got, bf16[544,256]{1,0:T(8,128)(2,1)S(1)} %get-tuple-element.33.pack, ...), custom_call_target="tpu_custom_call" | custom-call | flops 67108864 | bytes 1802240 | tf_op jit(solution)/shard_map/pallas_call | solution.py:21
  14.7 1.6 %collective-permute-start.3 = (bf16[256,128]{1,0:T(8,128)(2,1)S(1)}, bf16[256,128]{1,0:T(8,128)(2,1)S(1)}, u32[]{:S(2)}, u32[]{:S(2)}) collective-permute-start(bf16[256,128]{1,0:T(8,128)(2,1)S(1)} %get-tuple-element.36), channel_id=1, source_target_pairs={{0,2},{2,0},{4,6},{6,4},{8,10},{10,8},{12,14},{14,12},{16,18},{18,... | collective-permute-start | bytes 196616 | tf_op jit(solution)/shard_map/ppermute | solution.py:34
  16.3 0.2 shard_map.157
  16.5 0.6 %collective-permute-start.11 = (bf16[256,128]{1,0:T(8,128)(2,1)S(1)}, bf16[256,128]{1,0:T(8,128)(2,1)S(1)}, u32[]{:S(2)}, u32[]{:S(2)}) collective-permute-start(bf16[256,128]{1,0:T(8,128)(2,1)S(1)} %get-tuple-element.47), channel_id=1, source_target_pairs={{0,2},{2,0},{4,6},{6,4},{8,10},{10,8},{12,14},{14,12},{16,18},{18,... | collective-permute-start | bytes 196616 | tf_op jit(solution)/shard_map/ppermute | solution.py:34
  17.3 1.6 %collective-permute-start.9 = (bf16[256,128]{1,0:T(8,128)(2,1)S(1)}, bf16[256,128]{1,0:T(8,128)(2,1)S(1)}, u32[]{:S(2)}, u32[]{:S(2)}) collective-permute-start(bf16[256,128]{1,0:T(8,128)(2,1)S(1)} %get-tuple-element.44), channel_id=1, source_target_pairs={{0,2},{2,0},{4,6},{6,4},{8,10},{10,8},{12,14},{14,12},{16,18},{18,... | collective-permute-start | bytes 196616 | tf_op jit(solution)/shard_map/ppermute | solution.py:34
  18.8 0.2 collective-permute-done.3.got
  19.1 0.4 %shard_map.151 = (bf16[128,128]{1,0:T(8,128)(2,1)S(1)}, bf16[128,128]{1,0:T(8,128)(2,1)S(1)}, f32[256,128]{1,0:T(8,128)S(1)}, f32[256,128]{1,0:T(8,128)S(1)}) custom-call(f32[256,128]{1,0:T(8,128)S(1)} %get-tuple-element.35.kept, bf16[256,128]{1,0:T(8,128)(2,1)S(1)} %collective-permute-done.3.got, bf16[128,256]{1,0:T(8,128)(2,1)S(1)} %copy-done.5, ...), custom_call_target="tpu_custom_call" | custom-call | flops 50331648 | bytes 1589248 | tf_op jit(solution)/shard_map/pallas_call | solution.py:21
  19.5 1.7 %collective-permute-done.11.got = bf16[256,128]{1,0:T(8,128)(2,1)S(1)} collective-permute-done((bf16[256,128]{1,0:T(8,128)(2,1)S(1)}, bf16[256,128]{1,0:T(8,128)(2,1)S(1)}, u32[]{:S(2)}, u32[]{:S(2)}) %collective-permute-start.11) | collective-permute-done | bytes 65568 | tf_op jit(solution)/shard_map/ppermute | solution.py:34
  21.2 0.5 %collective-permute-start.12 = (bf16[256,128]{1,0:T(8,128)(2,1)S(1)}, bf16[256,128]{1,0:T(8,128)(2,1)S(1)}, u32[]{:S(2)}, u32[]{:S(2)}) collective-permute-start(bf16[256,128]{1,0:T(8,128)(2,1)S(1)} %shard_map.158.w2), channel_id=1, source_target_pairs={{0,4},{2,6},{4,0},{6,2},{8,12},{10,14},{12,8},{14,10},{16,20},{18,... | collective-permute-start | bytes 196616 | tf_op jit(solution)/shard_map/ppermute | solution.py:34
  21.9 1.5 %collective-permute-start.10 = (bf16[256,128]{1,0:T(8,128)(2,1)S(1)}, bf16[256,128]{1,0:T(8,128)(2,1)S(1)}, u32[]{:S(2)}, u32[]{:S(2)}) collective-permute-start(bf16[256,128]{1,0:T(8,128)(2,1)S(1)} %shard_map.156.s3), channel_id=1, source_target_pairs={{0,4},{2,6},{4,0},{6,2},{8,12},{10,14},{12,8},{14,10},{16,20},{18,... | collective-permute-start | bytes 196616 | tf_op jit(solution)/shard_map/ppermute | solution.py:34
  23.5 2.0 %collective-permute-done.12.w2_y = bf16[256,128]{1,0:T(8,128)(2,1)S(1)} collective-permute-done((bf16[256,128]{1,0:T(8,128)(2,1)S(1)}, bf16[256,128]{1,0:T(8,128)(2,1)S(1)}, u32[]{:S(2)}, u32[]{:S(2)}) %collective-permute-start.12) | collective-permute-done | bytes 65568 | tf_op jit(solution)/shard_map/ppermute | solution.py:34
  25.5 0.4 %shard_map.161 = (bf16[64,128]{1,0:T(8,128)(2,1)S(1)}, bf16[64,128]{1,0:T(8,128)(2,1)S(1)}, f32[256,128]{1,0:T(8,128)S(1)}) custom-call(bf16[256,128]{1,0:T(8,128)(2,1)S(1)} %shard_map.158.w2, bf16[256,128]{1,0:T(8,128)(2,1)S(1)} %collective-permute-done.12.w2_y, bf16[256,256]{1,0:T(8,128)(2,1)S(1)} %get-tuple-element.49.inverse, ...), custom_call_target="tpu_custom_call" | custom-call | flops 33554432 | bytes 557056 | tf_op jit(solution)/shard_map/pallas_call | solution.py:21
  25.9 0.3 collective-permute-done.10.s3_y
  26.3 1.6 %collective-permute-start.15 = (bf16[256,128]{1,0:T(8,128)(2,1)S(1)}, bf16[256,128]{1,0:T(8,128)(2,1)S(1)}, u32[]{:S(2)}, u32[]{:S(2)}) collective-permute-start(bf16[256,128]{1,0:T(8,128)(2,1)S(1)} %get-tuple-element.53.v3), channel_id=1, source_target_pairs={{0,8},{2,10},{4,12},{6,14},{8,0},{10,2},{12,4},{14,6},{16,24},{18,... | collective-permute-start | bytes 196616 | tf_op jit(solution)/shard_map/ppermute | solution.py:34
  27.9 1.3 %collective-permute-start.16 = (bf16[256,128]{1,0:T(8,128)(2,1)S(1)}, bf16[256,128]{1,0:T(8,128)(2,1)S(1)}, u32[]{:S(2)}, u32[]{:S(2)}) collective-permute-start(bf16[256,128]{1,0:T(8,128)(2,1)S(1)} %get-tuple-element.53.v3), channel_id=1, source_target_pairs={{0,10},{2,8},{4,14},{6,12},{8,2},{10,0},{12,6},{14,4},{16,26},{18,... | collective-permute-start | bytes 196616 | tf_op jit(solution)/shard_map/ppermute | solution.py:34
  29.2 0.6 %collective-permute-start.6 = (bf16[128,128]{1,0:T(8,128)(2,1)S(1)}, bf16[128,128]{1,0:T(8,128)(2,1)S(1)}, u32[]{:S(2)}, u32[]{:S(2)}) collective-permute-start(bf16[128,128]{1,0:T(8,128)(2,1)S(1)} %get-tuple-element.39), channel_id=1, source_target_pairs={{0,2},{2,0},{4,6},{6,4},{8,10},{10,8},{12,14},{14,12},{16,18},{18,... | collective-permute-start | bytes 98312 | tf_op jit(solution)/shard_map/ppermute | solution.py:34
  29.8 1.4 %collective-permute-start.17 = (bf16[96,128]{1,0:T(8,128)(2,1)S(1)}, bf16[96,128]{1,0:T(8,128)(2,1)S(1)}, u32[]{:S(2)}, u32[]{:S(2)}) collective-permute-start(bf16[96,128]{1,0:T(8,128)(2,1)S(1)} %get-tuple-element.54), channel_id=1, source_target_pairs={{0,2},{2,0},{4,6},{6,4},{8,10},{10,8},{12,14},{14,12},{16,18},{18,... | collective-permute-start | bytes 73736 | tf_op jit(solution)/shard_map/ppermute | solution.py:34
  31.2 2.2 %collective-permute-done.6.got = bf16[128,128]{1,0:T(8,128)(2,1)S(1)} collective-permute-done((bf16[128,128]{1,0:T(8,128)(2,1)S(1)}, bf16[128,128]{1,0:T(8,128)(2,1)S(1)}, u32[]{:S(2)}, u32[]{:S(2)}) %collective-permute-start.6) | collective-permute-done | bytes 32800 | tf_op jit(solution)/shard_map/ppermute | solution.py:34
  33.7 0.2 shard_map.163.own
  33.9 0.4 collective-permute-start.18
  34.3 0.7 %shard_map.150 = bf16[256,512]{1,0:T(8,128)(2,1)} custom-call(bf16[256,256]{1,0:T(8,128)(2,1)S(1)} %get-tuple-element.34.own.solved, bf16[256,256]{1,0:T(8,128)(2,1)S(1)} %collective-permute-done.2.got), custom_call_target="tpu_custom_call" | custom-call | bytes 524288 | tf_op jit(solution)/shard_map/pallas_call | solution.py:21
  35.0 0.7 %shard_map.153 = bf16[128,512]{1,0:T(8,128)(2,1)} custom-call(bf16[128,256]{1,0:T(8,128)(2,1)S(1)} %shard_map.152.own, bf16[128,256]{1,0:T(8,128)(2,1)S(1)} %collective-permute-done.7.got), custom_call_target="tpu_custom_call" | custom-call | bytes 262144 | tf_op jit(solution)/shard_map/pallas_call | solution.py:21
  35.7 0.7 %shard_map.164 = (bf16[64,512]{1,0:T(8,128)(2,1)}, bf16[32,512]{1,0:T(8,128)(2,1)}) custom-call(bf16[96,256]{1,0:T(8,128)(2,1)S(1)} %shard_map.163.own, bf16[96,256]{1,0:T(8,128)(2,1)S(1)} %collective-permute-done.18.got), custom_call_target="tpu_custom_call" | custom-call | bytes 196608 | tf_op jit(solution)/shard_map/pallas_call | solution.py:21
  (40 shorter events, 1.2 us)
Async XLA Ops:
  0.6 1.9 %copy-start = (bf16[4,4,256,256]{3,2,1,0:T(8,128)(2,1)S(1)}, bf16[4,4,256,256]{3,2,1,0:T(8,128)(2,1)}, u32[]{:S(2)}) copy-start(bf16[4,4,256,256]{3,2,1,0:T(8,128)(2,1)} %lower.3) | copy-start | bytes 6291460
  0.6 1.9 %copy-start.1 = (bf16[4,1,128,512]{3,2,1,0:T(8,128)(2,1)S(1)}, bf16[4,1,128,512]{3,2,1,0:T(8,128)(2,1)}, u32[]{:S(2)}) copy-start(bf16[4,1,128,512]{3,2,1,0:T(8,128)(2,1)} %rhs.3) | copy-start | bytes 1572868
  0.7 2.2 %copy-start.2 = (bf16[4,256,512]{2,1,0:T(8,128)(2,1)S(1)}, bf16[4,256,512]{2,1,0:T(8,128)(2,1)}, u32[]{:S(2)}) copy-start(bf16[4,256,512]{2,1,0:T(8,128)(2,1)} %right.1) | copy-start | bytes 3145732
  0.7 2.3 %copy-start.3 = (bf16[4,256,256]{2,1,0:T(8,128)(2,1)S(1)}, bf16[4,256,256]{2,1,0:T(8,128)(2,1)}, u32[]{:S(2)}) copy-start(bf16[4,256,256]{2,1,0:T(8,128)(2,1)} %inverse.5) | copy-start | bytes 1572868
  2.0 12.3 %collective-permute-start.1 = (bf16[544,256]{1,0:T(8,128)(2,1)S(1)}, bf16[544,256]{1,0:T(8,128)(2,1)S(1)}, u32[]{:S(2)}, u32[]{:S(2)}) collective-permute-start(bf16[544,256]{1,0:T(8,128)(2,1)S(1)} %get-tuple-element.33.pack), channel_id=1, source_target_pairs={{0,1},{1,0},{2,3},{3,2},{4,5},{5,4},{6,7},{7,6},{8,9},{9,8},{10,11... | collective-permute-start | bytes 835592 | tf_op jit(solution)/shard_map/ppermute | solution.py:34
  4.0 10.3 %copy-start.4 = (bf16[256,256]{1,0:T(8,128)(2,1)S(1)}, bf16[256,256]{1,0:T(8,128)(2,1)}, u32[]{:S(2)}) copy-start(bf16[256,256]{1,0:T(8,128)(2,1)} %inverse.6) | copy-start | bytes 393220
  4.0 10.3 %collective-permute-start = (bf16[2,256,256]{2,1,0:T(8,128)(2,1)S(1)}, bf16[2,256,256]{2,1,0:T(8,128)(2,1)S(1)}, u32[]{:S(2)}, u32[]{:S(2)}) collective-permute-start(bf16[2,256,256]{2,1,0:T(8,128)(2,1)S(1)} %get-tuple-element.32), channel_id=1, source_target_pairs={{0,1},{1,0},{2,3},{3,2},{4,5},{5,4},{6,7},{7,6},{8,9},{9,8},{10,11... | collective-permute-start | bytes 786440 | tf_op jit(solution)/shard_map/ppermute | solution.py:34
  5.3 11.0 %collective-permute-start.8 = (bf16[2,256,256]{2,1,0:T(8,128)(2,1)S(1)}, bf16[2,256,256]{2,1,0:T(8,128)(2,1)S(1)}, u32[]{:S(2)}, u32[]{:S(2)}) collective-permute-start(bf16[2,256,256]{2,1,0:T(8,128)(2,1)S(1)} %get-tuple-element.42), channel_id=1, source_target_pairs={{0,1},{1,0},{2,3},{3,2},{4,5},{5,4},{6,7},{7,6},{8,9},{9,8},{10,11... | collective-permute-start | bytes 786440 | tf_op jit(solution)/shard_map/ppermute | solution.py:34
  5.4 7.1 %collective-permute-start.4 = (bf16[288,256]{1,0:T(8,128)(2,1)S(1)}, bf16[288,256]{1,0:T(8,128)(2,1)S(1)}, u32[]{:S(2)}, u32[]{:S(2)}) collective-permute-start(bf16[288,256]{1,0:T(8,128)(2,1)S(1)} %get-tuple-element.37.along), channel_id=1, source_target_pairs={{0,2},{2,0},{4,6},{6,4},{8,10},{10,8},{12,14},{14,12},{16,18},{18,... | collective-permute-start | bytes 442376 | tf_op jit(solution)/shard_map/ppermute | solution.py:34
  12.4 6.4 %collective-permute-start.5 = (bf16[288,256]{1,0:T(8,128)(2,1)S(1)}, bf16[288,256]{1,0:T(8,128)(2,1)S(1)}, u32[]{:S(2)}, u32[]{:S(2)}) collective-permute-start(bf16[288,256]{1,0:T(8,128)(2,1)S(1)} %collective-permute-done.4.along_x), channel_id=1, source_target_pairs={{0,1},{1,0},{2,3},{3,2},{4,5},{5,4},{6,7},{7,6},{8,9},{9,8},{10,11... | collective-permute-start | bytes 442376 | tf_op jit(solution)/shard_map/ppermute | solution.py:34
  12.4 6.4 %collective-permute-start.13 = (bf16[128,256]{1,0:T(8,128)(2,1)S(1)}, bf16[128,256]{1,0:T(8,128)(2,1)S(1)}, u32[]{:S(2)}, u32[]{:S(2)}) collective-permute-start(bf16[128,256]{1,0:T(8,128)(2,1)S(1)} %shard_map.159), channel_id=1, source_target_pairs={{0,4},{2,6},{4,0},{6,2},{8,12},{10,14},{12,8},{14,10},{16,20},{18,... | collective-permute-start | bytes 196616 | tf_op jit(solution)/shard_map/ppermute | solution.py:34
  14.3 4.8 %copy-start.5 = (bf16[128,256]{1,0:T(8,128)(2,1)S(1)}, bf16[128,256]{1,0:T(8,128)(2,1)}, u32[]{:S(2)}) copy-start(bf16[128,256]{1,0:T(8,128)(2,1)} %inverse.7) | copy-start | bytes 196612
  14.7 4.4 %collective-permute-start.3 = (bf16[256,128]{1,0:T(8,128)(2,1)S(1)}, bf16[256,128]{1,0:T(8,128)(2,1)S(1)}, u32[]{:S(2)}, u32[]{:S(2)}) collective-permute-start(bf16[256,128]{1,0:T(8,128)(2,1)S(1)} %get-tuple-element.36), channel_id=1, source_target_pairs={{0,2},{2,0},{4,6},{6,4},{8,10},{10,8},{12,14},{14,12},{16,18},{18,... | collective-permute-start | bytes 196616 | tf_op jit(solution)/shard_map/ppermute | solution.py:34
  16.5 6.9 %copy-start.6 = (bf16[64,256]{1,0:T(8,128)(2,1)S(1)}, bf16[64,256]{1,0:T(8,128)(2,1)}, u32[]{:S(2)}) copy-start(bf16[64,256]{1,0:T(8,128)(2,1)} %inverse.8) | copy-start | bytes 98308
  16.5 4.7 %collective-permute-start.11 = (bf16[256,128]{1,0:T(8,128)(2,1)S(1)}, bf16[256,128]{1,0:T(8,128)(2,1)S(1)}, u32[]{:S(2)}, u32[]{:S(2)}) collective-permute-start(bf16[256,128]{1,0:T(8,128)(2,1)S(1)} %get-tuple-element.47), channel_id=1, source_target_pairs={{0,2},{2,0},{4,6},{6,4},{8,10},{10,8},{12,14},{14,12},{16,18},{18,... | collective-permute-start | bytes 196616 | tf_op jit(solution)/shard_map/ppermute | solution.py:34
  17.3 16.4 %copy-start.7 = (bf16[32,256]{1,0:T(8,128)(2,1)S(1)}, bf16[32,256]{1,0:T(8,128)(2,1)}, u32[]{:S(2)}) copy-start(bf16[32,256]{1,0:T(8,128)(2,1)} %inverse.9) | copy-start | bytes 49156
  17.3 4.6 %collective-permute-start.9 = (bf16[256,128]{1,0:T(8,128)(2,1)S(1)}, bf16[256,128]{1,0:T(8,128)(2,1)S(1)}, u32[]{:S(2)}, u32[]{:S(2)}) collective-permute-start(bf16[256,128]{1,0:T(8,128)(2,1)S(1)} %get-tuple-element.44), channel_id=1, source_target_pairs={{0,2},{2,0},{4,6},{6,4},{8,10},{10,8},{12,14},{14,12},{16,18},{18,... | collective-permute-start | bytes 196616 | tf_op jit(solution)/shard_map/ppermute | solution.py:34
  18.8 4.5 %collective-permute-start.14 = (bf16[128,256]{1,0:T(8,128)(2,1)S(1)}, bf16[128,256]{1,0:T(8,128)(2,1)S(1)}, u32[]{:S(2)}, u32[]{:S(2)}) collective-permute-start(bf16[128,256]{1,0:T(8,128)(2,1)S(1)} %collective-permute-done.13.side), channel_id=1, source_target_pairs={{0,1},{1,0},{2,3},{3,2},{4,5},{5,4},{6,7},{7,6},{8,9},{9,8},{10,11... | collective-permute-start | bytes 196616 | tf_op jit(solution)/shard_map/ppermute | solution.py:34
  21.2 4.3 %collective-permute-start.12 = (bf16[256,128]{1,0:T(8,128)(2,1)S(1)}, bf16[256,128]{1,0:T(8,128)(2,1)S(1)}, u32[]{:S(2)}, u32[]{:S(2)}) collective-permute-start(bf16[256,128]{1,0:T(8,128)(2,1)S(1)} %shard_map.158.w2), channel_id=1, source_target_pairs={{0,4},{2,6},{4,0},{6,2},{8,12},{10,14},{12,8},{14,10},{16,20},{18,... | collective-permute-start | bytes 196616 | tf_op jit(solution)/shard_map/ppermute | solution.py:34
  21.9 4.3 %collective-permute-start.10 = (bf16[256,128]{1,0:T(8,128)(2,1)S(1)}, bf16[256,128]{1,0:T(8,128)(2,1)S(1)}, u32[]{:S(2)}, u32[]{:S(2)}) collective-permute-start(bf16[256,128]{1,0:T(8,128)(2,1)S(1)} %shard_map.156.s3), channel_id=1, source_target_pairs={{0,4},{2,6},{4,0},{6,2},{8,12},{10,14},{12,8},{14,10},{16,20},{18,... | collective-permute-start | bytes 196616 | tf_op jit(solution)/shard_map/ppermute | solution.py:34
  23.3 10.9 %collective-permute-start.2 = (bf16[256,256]{1,0:T(8,128)(2,1)S(1)}, bf16[256,256]{1,0:T(8,128)(2,1)S(1)}, u32[]{:S(2)}, u32[]{:S(2)}) collective-permute-start(bf16[256,256]{1,0:T(8,128)(2,1)S(1)} %get-tuple-element.34.own.solved), channel_id=1, source_target_pairs={{0,1},{1,0},{2,3},{3,2},{4,5},{5,4},{6,7},{7,6},{8,9},{9,8},{10,11... | collective-permute-start | bytes 393224 | tf_op jit(solution)/shard_map/ppermute | solution.py:34
  26.3 7.4 %collective-permute-start.15 = (bf16[256,128]{1,0:T(8,128)(2,1)S(1)}, bf16[256,128]{1,0:T(8,128)(2,1)S(1)}, u32[]{:S(2)}, u32[]{:S(2)}) collective-permute-start(bf16[256,128]{1,0:T(8,128)(2,1)S(1)} %get-tuple-element.53.v3), channel_id=1, source_target_pairs={{0,8},{2,10},{4,12},{6,14},{8,0},{10,2},{12,4},{14,6},{16,24},{18,... | collective-permute-start | bytes 196616 | tf_op jit(solution)/shard_map/ppermute | solution.py:34
  27.9 5.8 %collective-permute-start.16 = (bf16[256,128]{1,0:T(8,128)(2,1)S(1)}, bf16[256,128]{1,0:T(8,128)(2,1)S(1)}, u32[]{:S(2)}, u32[]{:S(2)}) collective-permute-start(bf16[256,128]{1,0:T(8,128)(2,1)S(1)} %get-tuple-element.53.v3), channel_id=1, source_target_pairs={{0,10},{2,8},{4,14},{6,12},{8,2},{10,0},{12,6},{14,4},{16,26},{18,... | collective-permute-start | bytes 196616 | tf_op jit(solution)/shard_map/ppermute | solution.py:34
  29.2 4.2 %collective-permute-start.6 = (bf16[128,128]{1,0:T(8,128)(2,1)S(1)}, bf16[128,128]{1,0:T(8,128)(2,1)S(1)}, u32[]{:S(2)}, u32[]{:S(2)}) collective-permute-start(bf16[128,128]{1,0:T(8,128)(2,1)S(1)} %get-tuple-element.39), channel_id=1, source_target_pairs={{0,2},{2,0},{4,6},{6,4},{8,10},{10,8},{12,14},{14,12},{16,18},{18,... | collective-permute-start | bytes 98312 | tf_op jit(solution)/shard_map/ppermute | solution.py:34
  29.8 3.9 %collective-permute-start.17 = (bf16[96,128]{1,0:T(8,128)(2,1)S(1)}, bf16[96,128]{1,0:T(8,128)(2,1)S(1)}, u32[]{:S(2)}, u32[]{:S(2)}) collective-permute-start(bf16[96,128]{1,0:T(8,128)(2,1)S(1)} %get-tuple-element.54), channel_id=1, source_target_pairs={{0,2},{2,0},{4,6},{6,4},{8,10},{10,8},{12,14},{14,12},{16,18},{18,... | collective-permute-start | bytes 73736 | tf_op jit(solution)/shard_map/ppermute | solution.py:34
  33.5 1.6 %collective-permute-start.7 = (bf16[128,256]{1,0:T(8,128)(2,1)S(1)}, bf16[128,256]{1,0:T(8,128)(2,1)S(1)}, u32[]{:S(2)}, u32[]{:S(2)}) collective-permute-start(bf16[128,256]{1,0:T(8,128)(2,1)S(1)} %shard_map.152.own), channel_id=1, source_target_pairs={{0,1},{1,0},{2,3},{3,2},{4,5},{5,4},{6,7},{7,6},{8,9},{9,8},{10,11... | collective-permute-start | bytes 196616 | tf_op jit(solution)/shard_map/ppermute | solution.py:34
  33.9 1.8 %collective-permute-start.18 = (bf16[96,256]{1,0:T(8,128)(2,1)S(1)}, bf16[96,256]{1,0:T(8,128)(2,1)S(1)}, u32[]{:S(2)}, u32[]{:S(2)}) collective-permute-start(bf16[96,256]{1,0:T(8,128)(2,1)S(1)} %shard_map.163.own), channel_id=1, source_target_pairs={{0,1},{1,0},{2,3},{3,2},{4,5},{5,4},{6,7},{7,6},{8,9},{9,8},{10,11... | collective-permute-start | bytes 147464 | tf_op jit(solution)/shard_map/ppermute | solution.py:34

commit v10 on v9

--- a/solution.py
+++ b/solution.py
@@ -237,16 +237,21 @@
     out[:, theirs] = got[...]
 
 
-def three(v3, v3_z, v3_xz, from_x, inverse, sol2, out, full, solved):
-    own, other = quarters(out.shape[1])
+def three(v3, v3_z, v3_xz, inverse, solved, full):
+    own, other = quarters(solved.shape[1])
     full[:, own] = (v3[...].astype(F32) + v3_z[...].astype(F32)).astype(BF16)
     full[:, other] = v3_xz[...]
-    part, top = sol2.shape[0], inverse.shape[0]
     solved[...] = dot(inverse[...], full[...])
-    solved[:, other] = solved[:, other] + from_x[pl.ds(0, top), :].astype(F32)
+
+
+def lay(solved, from_x, sol2, out):
+    own, other = quarters(out.shape[1])
+    part, top = sol2.shape[0], solved.shape[0]
     out[pl.ds(0, part), own] = sol2[...]
     out[pl.ds(0, part), other] = from_x[pl.ds(top, part), :]
-    out[pl.ds(part, top), :] = solved[...].astype(BF16)
+    low = pl.ds(part, top)
+    out[low, own] = solved[:, own].astype(BF16)
+    out[low, other] = (solved[:, other] + from_x[pl.ds(0, top), :].astype(F32)).astype(BF16)
 
 
 def join(own, got, *outs):
@@ -354,11 +359,11 @@
     v3_xz = swap(v3, "col", 5)
     from_x = swap(to_x, "col", 1)
     v3_z = swap(v3, "col", 4)
-    last = call(
-        three, [((part_2 + part_3, half), BF16)],
-        v3, v3_z, v3_xz, from_x, inverse_3, sol2,
-        scratch=[pltpu.VMEM((size, half), BF16), pltpu.VMEM((part_3, half), F32)], flops=2 * inverse_3.size * half,
-    )
+    solved3 = call(
+        three, [((part_3, half), F32)], v3, v3_z, v3_xz, inverse_3,
+        scratch=[pltpu.VMEM((size, half), BF16)], flops=2 * inverse_3.size * half,
+    )
+    last = call(lay, [((part_2 + part_3, half), BF16)], solved3, from_x, sol2)
     last_o = swap(last, "row", 1)
     rest = call(join, [((part, width), BF16) for part in (part_2, part_3)], last, last_o)
     return (out0, out1, *rest)

time: 36.5 us -> 36.6 us (level)
    pallas_call x18 -> x19, Pallas kernels: 7.22 us -> 7.22 us  [call(): pl.pallas_call(kernel, out_shape=outs[0] if single else outs, in_specs=sp...]
  transfers between devices with their start and end apart: 19 -> 19, of which waited for: 8 -> 7; matrix products, arithmetic and copies ran while one was open for 0% -> 0% of each run, Pallas kernels for 14% -> 14%
where the time goes in v10:
time: 36.6 us; the launch traced here: 36.4 us
  starting transfers between devices  17.2 us (47%)
  waiting for transfers between devices  10.7 us (29%)
  Pallas kernels  7.22 us (20%)
  between operations  0.85 us (2%)
  local copies, waits for them, and re-layouts  0.45 us (1%)
    ppermute x19, starting transfers between devices, swap(): lax.ppermute(block, axis, [(low, low ^ stride) for low in range(count)])  17.2 us
    ppermute x19, waiting for transfers between devices, swap(): lax.ppermute(block, axis, [(low, low ^ stride) for low in range(count)])  10.7 us
    pallas_call x19, Pallas kernels, call(): pl.pallas_call(kernel, out_shape=outs[0] if single else outs, in_specs=sp...  7.22 us
  transfers between devices with their start and end apart: 19, of which 7 were waited for; matrix products, arithmetic and copies ran while one was open for 0% of the time, Pallas kernels for 14%

profile of v10, /device:TPU:0, one launch (start us, length us, event | category | flops | bytes accessed | tf_op | source)
XLA Modules:
  0.0 36.4 jit_solution(8692122997795951229)
XLA Ops:
  0.7 1.3 %shard_map.148 = (bf16[544,256]{1,0:T(8,128)(2,1)S(1)}, bf16[288,256]{1,0:T(8,128)(2,1)S(1)}) custom-call(bf16[3,128,256]{2,1,0:T(8,128)(2,1)} %lower_0h.1, bf16[2,128,128]{2,1,0:T(8,128)(2,1)} %lower_1h.1, bf16[1,64,128]{2,1,0:T(8,128)(2,1)} %bitcast.2, s32[1,4,6]{2,1,0:T(4,128)} %bitcast.3, bf16[128,256]{1,0:T(8,128)(2,1)} %inverse.7, ...), custom_call_target="tpu_custom_call" | custom-call | flops 4000000000 | bytes 819296 | tf_op jit(solution)/shard_map/pallas_call | solution.py:21
  2.0 0.6 %collective-permute-start.1 = (bf16[544,256]{1,0:T(8,128)(2,1)S(1)}, bf16[544,256]{1,0:T(8,128)(2,1)S(1)}, u32[]{:S(2)}, u32[]{:S(2)}) collective-permute-start(bf16[544,256]{1,0:T(8,128)(2,1)S(1)} %get-tuple-element.33.pack), channel_id=1, source_target_pairs={{0,1},{1,0},{2,3},{3,2},{4,5},{5,4},{6,7},{7,6},{8,9},{9,8},{10,11... | collective-permute-start | bytes 835592 | tf_op jit(solution)/shard_map/ppermute | solution.py:34
  2.6 0.3 copy-done.2
  3.0 1.0 %shard_map.147 = (bf16[4,256,512]{2,1,0:T(8,128)(2,1)S(1)}, f32[2,256,256]{2,1,0:T(8,128)S(1)}, bf16[2,256,256]{2,1,0:T(8,128)(2,1)S(1)}) custom-call(bf16[4,256,256]{2,1,0:T(8,128)(2,1)S(1)} %copy-done.3, bf16[4,256,512]{2,1,0:T(8,128)(2,1)S(1)} %copy-done.2, bf16[4,4,256,256]{3,2,1,0:T(8,128)(2,1)S(1)} %copy-done, bf16[4,1,128,512]{3,2,1,0:T(8,128)(2,1)S(1)} %copy-done.1), custom_call_target="tpu_custom_call" | custom-call | flops 805306368 | bytes 6029312 | tf_op jit(solution)/shard_map/pallas_call | solution.py:21
  4.0 0.6 %collective-permute-start = (bf16[2,256,256]{2,1,0:T(8,128)(2,1)S(1)}, bf16[2,256,256]{2,1,0:T(8,128)(2,1)S(1)}, u32[]{:S(2)}, u32[]{:S(2)}) collective-permute-start(bf16[2,256,256]{2,1,0:T(8,128)(2,1)S(1)} %get-tuple-element.32), channel_id=1, source_target_pairs={{0,1},{1,0},{2,3},{3,2},{4,5},{5,4},{6,7},{7,6},{8,9},{9,8},{10,11... | collective-permute-start | bytes 786440 | tf_op jit(solution)/shard_map/ppermute | solution.py:34
  4.6 0.7 %shard_map.154 = (f32[2,256,256]{2,1,0:T(8,128)S(1)}, bf16[2,256,256]{2,1,0:T(8,128)(2,1)S(1)}) custom-call(bf16[4,256,512]{2,1,0:T(8,128)(2,1)S(1)} %get-tuple-element.40.solved, bf16[4,4,256,256]{3,2,1,0:T(8,128)(2,1)S(1)} %copy-done, bf16[4,1,128,512]{3,2,1,0:T(8,128)(2,1)S(1)} %copy-done.1), custom_call_target="tpu_custom_call" | custom-call | flops 536870912 | bytes 4456448 | tf_op jit(solution)/shard_map/pallas_call | solution.py:21
  5.4 3.0 %collective-permute-start.4 = (bf16[288,256]{1,0:T(8,128)(2,1)S(1)}, bf16[288,256]{1,0:T(8,128)(2,1)S(1)}, u32[]{:S(2)}, u32[]{:S(2)}) collective-permute-start(bf16[288,256]{1,0:T(8,128)(2,1)S(1)} %get-tuple-element.37.along), channel_id=1, source_target_pairs={{0,2},{2,0},{4,6},{6,4},{8,10},{10,8},{12,14},{14,12},{16,18},{18,... | collective-permute-start | bytes 442376 | tf_op jit(solution)/shard_map/ppermute | solution.py:34
  8.3 4.1 %collective-permute-done.4.along_x = bf16[288,256]{1,0:T(8,128)(2,1)S(1)} collective-permute-done((bf16[288,256]{1,0:T(8,128)(2,1)S(1)}, bf16[288,256]{1,0:T(8,128)(2,1)S(1)}, u32[]{:S(2)}, u32[]{:S(2)}) %collective-permute-start.4) | collective-permute-done | bytes 147488 | tf_op jit(solution)/shard_map/ppermute | solution.py:34
  12.4 1.8 %collective-permute-start.13 = (bf16[128,256]{1,0:T(8,128)(2,1)S(1)}, bf16[128,256]{1,0:T(8,128)(2,1)S(1)}, u32[]{:S(2)}, u32[]{:S(2)}) collective-permute-start(bf16[128,256]{1,0:T(8,128)(2,1)S(1)} %shard_map.159), channel_id=1, source_target_pairs={{0,4},{2,6},{4,0},{6,2},{8,12},{10,14},{12,8},{14,10},{16,20},{18,... | collective-permute-start | bytes 196616 | tf_op jit(solution)/shard_map/ppermute | solution.py:34
  14.3 0.4 %shard_map.149 = (bf16[256,256]{1,0:T(8,128)(2,1)S(1)}, f32[256,128]{1,0:T(8,128)S(1)}, bf16[256,128]{1,0:T(8,128)(2,1)S(1)}) custom-call(f32[2,256,256]{2,1,0:T(8,128)S(1)} %get-tuple-element.31.keep, bf16[2,256,256]{2,1,0:T(8,128)(2,1)S(1)} %collective-permute-done.got, bf16[544,256]{1,0:T(8,128)(2,1)S(1)} %get-tuple-element.33.pack, ...), custom_call_target="tpu_custom_call" | custom-call | flops 67108864 | bytes 1802240 | tf_op jit(solution)/shard_map/pallas_call | solution.py:21
  14.7 1.6 %collective-permute-start.3 = (bf16[256,128]{1,0:T(8,128)(2,1)S(1)}, bf16[256,128]{1,0:T(8,128)(2,1)S(1)}, u32[]{:S(2)}, u32[]{:S(2)}) collective-permute-start(bf16[256,128]{1,0:T(8,128)(2,1)S(1)} %get-tuple-element.36), channel_id=1, source_target_pairs={{0,2},{2,0},{4,6},{6,4},{8,10},{10,8},{12,14},{14,12},{16,18},{18,... | collective-permute-start | bytes 196616 | tf_op jit(solution)/shard_map/ppermute | solution.py:34
  16.3 0.2 shard_map.157
  16.5 0.6 %collective-permute-start.11 = (bf16[256,128]{1,0:T(8,128)(2,1)S(1)}, bf16[256,128]{1,0:T(8,128)(2,1)S(1)}, u32[]{:S(2)}, u32[]{:S(2)}) collective-permute-start(bf16[256,128]{1,0:T(8,128)(2,1)S(1)} %get-tuple-element.47), channel_id=1, source_target_pairs={{0,2},{2,0},{4,6},{6,4},{8,10},{10,8},{12,14},{14,12},{16,18},{18,... | collective-permute-start | bytes 196616 | tf_op jit(solution)/shard_map/ppermute | solution.py:34
  17.1 0.2 shard_map.155
  17.3 1.6 %collective-permute-start.9 = (bf16[256,128]{1,0:T(8,128)(2,1)S(1)}, bf16[256,128]{1,0:T(8,128)(2,1)S(1)}, u32[]{:S(2)}, u32[]{:S(2)}) collective-permute-start(bf16[256,128]{1,0:T(8,128)(2,1)S(1)} %get-tuple-element.44), channel_id=1, source_target_pairs={{0,2},{2,0},{4,6},{6,4},{8,10},{10,8},{12,14},{14,12},{16,18},{18,... | collective-permute-start | bytes 196616 | tf_op jit(solution)/shard_map/ppermute | solution.py:34
  18.8 0.2 collective-permute-done.3.got
  19.1 0.4 %shard_map.151 = (bf16[128,128]{1,0:T(8,128)(2,1)S(1)}, bf16[128,128]{1,0:T(8,128)(2,1)S(1)}, f32[256,128]{1,0:T(8,128)S(1)}, f32[256,128]{1,0:T(8,128)S(1)}) custom-call(f32[256,128]{1,0:T(8,128)S(1)} %get-tuple-element.35.kept, bf16[256,128]{1,0:T(8,128)(2,1)S(1)} %collective-permute-done.3.got, bf16[128,256]{1,0:T(8,128)(2,1)S(1)} %copy-done.5, ...), custom_call_target="tpu_custom_call" | custom-call | flops 50331648 | bytes 1589248 | tf_op jit(solution)/shard_map/pallas_call | solution.py:21
  19.5 1.7 %collective-permute-done.11.got = bf16[256,128]{1,0:T(8,128)(2,1)S(1)} collective-permute-done((bf16[256,128]{1,0:T(8,128)(2,1)S(1)}, bf16[256,128]{1,0:T(8,128)(2,1)S(1)}, u32[]{:S(2)}, u32[]{:S(2)}) %collective-permute-start.11) | collective-permute-done | bytes 65568 | tf_op jit(solution)/shard_map/ppermute | solution.py:34
  21.2 0.5 %collective-permute-start.12 = (bf16[256,128]{1,0:T(8,128)(2,1)S(1)}, bf16[256,128]{1,0:T(8,128)(2,1)S(1)}, u32[]{:S(2)}, u32[]{:S(2)}) collective-permute-start(bf16[256,128]{1,0:T(8,128)(2,1)S(1)} %shard_map.158.w2), channel_id=1, source_target_pairs={{0,4},{2,6},{4,0},{6,2},{8,12},{10,14},{12,8},{14,10},{16,20},{18,... | collective-permute-start | bytes 196616 | tf_op jit(solution)/shard_map/ppermute | solution.py:34
  21.9 1.5 %collective-permute-start.10 = (bf16[256,128]{1,0:T(8,128)(2,1)S(1)}, bf16[256,128]{1,0:T(8,128)(2,1)S(1)}, u32[]{:S(2)}, u32[]{:S(2)}) collective-permute-start(bf16[256,128]{1,0:T(8,128)(2,1)S(1)} %shard_map.156.s3), channel_id=1, source_target_pairs={{0,4},{2,6},{4,0},{6,2},{8,12},{10,14},{12,8},{14,10},{16,20},{18,... | collective-permute-start | bytes 196616 | tf_op jit(solution)/shard_map/ppermute | solution.py:34
  23.5 2.0 %collective-permute-done.12.w2_y = bf16[256,128]{1,0:T(8,128)(2,1)S(1)} collective-permute-done((bf16[256,128]{1,0:T(8,128)(2,1)S(1)}, bf16[256,128]{1,0:T(8,128)(2,1)S(1)}, u32[]{:S(2)}, u32[]{:S(2)}) %collective-permute-start.12) | collective-permute-done | bytes 65568 | tf_op jit(solution)/shard_map/ppermute | solution.py:34
  25.5 0.4 %shard_map.161 = (bf16[64,128]{1,0:T(8,128)(2,1)S(1)}, bf16[64,128]{1,0:T(8,128)(2,1)S(1)}, f32[256,128]{1,0:T(8,128)S(1)}) custom-call(bf16[256,128]{1,0:T(8,128)(2,1)S(1)} %shard_map.158.w2, bf16[256,128]{1,0:T(8,128)(2,1)S(1)} %collective-permute-done.12.w2_y, bf16[256,256]{1,0:T(8,128)(2,1)S(1)} %get-tuple-element.49.inverse, ...), custom_call_target="tpu_custom_call" | custom-call | flops 33554432 | bytes 557056 | tf_op jit(solution)/shard_map/pallas_call | solution.py:21
  25.9 0.3 collective-permute-done.10.s3_y
  26.3 1.6 %collective-permute-start.15 = (bf16[256,128]{1,0:T(8,128)(2,1)S(1)}, bf16[256,128]{1,0:T(8,128)(2,1)S(1)}, u32[]{:S(2)}, u32[]{:S(2)}) collective-permute-start(bf16[256,128]{1,0:T(8,128)(2,1)S(1)} %get-tuple-element.53.v3), channel_id=1, source_target_pairs={{0,8},{2,10},{4,12},{6,14},{8,0},{10,2},{12,4},{14,6},{16,24},{18,... | collective-permute-start | bytes 196616 | tf_op jit(solution)/shard_map/ppermute | solution.py:34
  27.9 1.3 %collective-permute-start.16 = (bf16[256,128]{1,0:T(8,128)(2,1)S(1)}, bf16[256,128]{1,0:T(8,128)(2,1)S(1)}, u32[]{:S(2)}, u32[]{:S(2)}) collective-permute-start(bf16[256,128]{1,0:T(8,128)(2,1)S(1)} %get-tuple-element.53.v3), channel_id=1, source_target_pairs={{0,10},{2,8},{4,14},{6,12},{8,2},{10,0},{12,6},{14,4},{16,26},{18,... | collective-permute-start | bytes 196616 | tf_op jit(solution)/shard_map/ppermute | solution.py:34
  29.2 0.6 %collective-permute-start.6 = (bf16[128,128]{1,0:T(8,128)(2,1)S(1)}, bf16[128,128]{1,0:T(8,128)(2,1)S(1)}, u32[]{:S(2)}, u32[]{:S(2)}) collective-permute-start(bf16[128,128]{1,0:T(8,128)(2,1)S(1)} %get-tuple-element.39), channel_id=1, source_target_pairs={{0,2},{2,0},{4,6},{6,4},{8,10},{10,8},{12,14},{14,12},{16,18},{18,... | collective-permute-start | bytes 98312 | tf_op jit(solution)/shard_map/ppermute | solution.py:34
  29.8 1.4 %collective-permute-start.17 = (bf16[96,128]{1,0:T(8,128)(2,1)S(1)}, bf16[96,128]{1,0:T(8,128)(2,1)S(1)}, u32[]{:S(2)}, u32[]{:S(2)}) collective-permute-start(bf16[96,128]{1,0:T(8,128)(2,1)S(1)} %get-tuple-element.54), channel_id=1, source_target_pairs={{0,2},{2,0},{4,6},{6,4},{8,10},{10,8},{12,14},{14,12},{16,18},{18,... | collective-permute-start | bytes 73736 | tf_op jit(solution)/shard_map/ppermute | solution.py:34
  31.2 2.2 %collective-permute-done.6.got = bf16[128,128]{1,0:T(8,128)(2,1)S(1)} collective-permute-done((bf16[128,128]{1,0:T(8,128)(2,1)S(1)}, bf16[128,128]{1,0:T(8,128)(2,1)S(1)}, u32[]{:S(2)}, u32[]{:S(2)}) %collective-permute-start.6) | collective-permute-done | bytes 32800 | tf_op jit(solution)/shard_map/ppermute | solution.py:34
  33.8 0.5 %collective-permute-start.18 = (bf16[96,256]{1,0:T(8,128)(2,1)S(1)}, bf16[96,256]{1,0:T(8,128)(2,1)S(1)}, u32[]{:S(2)}, u32[]{:S(2)}) collective-permute-start(bf16[96,256]{1,0:T(8,128)(2,1)S(1)} %shard_map.164.own), channel_id=1, source_target_pairs={{0,1},{1,0},{2,3},{3,2},{4,5},{5,4},{6,7},{7,6},{8,9},{9,8},{10,11... | collective-permute-start | bytes 147464 | tf_op jit(solution)/shard_map/ppermute | solution.py:34
  34.3 0.7 %shard_map.150 = bf16[256,512]{1,0:T(8,128)(2,1)} custom-call(bf16[256,256]{1,0:T(8,128)(2,1)S(1)} %get-tuple-element.34.own.solved, bf16[256,256]{1,0:T(8,128)(2,1)S(1)} %collective-permute-done.2.got), custom_call_target="tpu_custom_call" | custom-call | bytes 524288 | tf_op jit(solution)/shard_map/pallas_call | solution.py:21
  35.1 0.7 %shard_map.153 = bf16[128,512]{1,0:T(8,128)(2,1)} custom-call(bf16[128,256]{1,0:T(8,128)(2,1)S(1)} %shard_map.152.own, bf16[128,256]{1,0:T(8,128)(2,1)S(1)} %collective-permute-done.7.got), custom_call_target="tpu_custom_call" | custom-call | bytes 262144 | tf_op jit(solution)/shard_map/pallas_call | solution.py:21
  35.8 0.7 %shard_map.165 = (bf16[64,512]{1,0:T(8,128)(2,1)}, bf16[32,512]{1,0:T(8,128)(2,1)}) custom-call(bf16[96,256]{1,0:T(8,128)(2,1)S(1)} %shard_map.164.own, bf16[96,256]{1,0:T(8,128)(2,1)S(1)} %collective-permute-done.18.got), custom_call_target="tpu_custom_call" | custom-call | bytes 196608 | tf_op jit(solution)/shard_map/pallas_call | solution.py:21
  (41 shorter events, 1.1 us)
Async XLA Ops:
  0.6 1.9 %copy-start = (bf16[4,4,256,256]{3,2,1,0:T(8,128)(2,1)S(1)}, bf16[4,4,256,256]{3,2,1,0:T(8,128)(2,1)}, u32[]{:S(2)}) copy-start(bf16[4,4,256,256]{3,2,1,0:T(8,128)(2,1)} %lower.3) | copy-start | bytes 6291460
  0.6 1.9 %copy-start.1 = (bf16[4,1,128,512]{3,2,1,0:T(8,128)(2,1)S(1)}, bf16[4,1,128,512]{3,2,1,0:T(8,128)(2,1)}, u32[]{:S(2)}) copy-start(bf16[4,1,128,512]{3,2,1,0:T(8,128)(2,1)} %rhs.3) | copy-start | bytes 1572868
  0.7 2.2 %copy-start.2 = (bf16[4,256,512]{2,1,0:T(8,128)(2,1)S(1)}, bf16[4,256,512]{2,1,0:T(8,128)(2,1)}, u32[]{:S(2)}) copy-start(bf16[4,256,512]{2,1,0:T(8,128)(2,1)} %right.1) | copy-start | bytes 3145732
  0.7 2.3 %copy-start.3 = (bf16[4,256,256]{2,1,0:T(8,128)(2,1)S(1)}, bf16[4,256,256]{2,1,0:T(8,128)(2,1)}, u32[]{:S(2)}) copy-start(bf16[4,256,256]{2,1,0:T(8,128)(2,1)} %inverse.5) | copy-start | bytes 1572868
  2.0 12.3 %collective-permute-start.1 = (bf16[544,256]{1,0:T(8,128)(2,1)S(1)}, bf16[544,256]{1,0:T(8,128)(2,1)S(1)}, u32[]{:S(2)}, u32[]{:S(2)}) collective-permute-start(bf16[544,256]{1,0:T(8,128)(2,1)S(1)} %get-tuple-element.33.pack), channel_id=1, source_target_pairs={{0,1},{1,0},{2,3},{3,2},{4,5},{5,4},{6,7},{7,6},{8,9},{9,8},{10,11... | collective-permute-start | bytes 835592 | tf_op jit(solution)/shard_map/ppermute | solution.py:34
  4.0 10.3 %copy-start.4 = (bf16[256,256]{1,0:T(8,128)(2,1)S(1)}, bf16[256,256]{1,0:T(8,128)(2,1)}, u32[]{:S(2)}) copy-start(bf16[256,256]{1,0:T(8,128)(2,1)} %inverse.6) | copy-start | bytes 393220
  4.0 10.3 %collective-permute-start = (bf16[2,256,256]{2,1,0:T(8,128)(2,1)S(1)}, bf16[2,256,256]{2,1,0:T(8,128)(2,1)S(1)}, u32[]{:S(2)}, u32[]{:S(2)}) collective-permute-start(bf16[2,256,256]{2,1,0:T(8,128)(2,1)S(1)} %get-tuple-element.32), channel_id=1, source_target_pairs={{0,1},{1,0},{2,3},{3,2},{4,5},{5,4},{6,7},{7,6},{8,9},{9,8},{10,11... | collective-permute-start | bytes 786440 | tf_op jit(solution)/shard_map/ppermute | solution.py:34
  5.3 11.0 %collective-permute-start.8 = (bf16[2,256,256]{2,1,0:T(8,128)(2,1)S(1)}, bf16[2,256,256]{2,1,0:T(8,128)(2,1)S(1)}, u32[]{:S(2)}, u32[]{:S(2)}) collective-permute-start(bf16[2,256,256]{2,1,0:T(8,128)(2,1)S(1)} %get-tuple-element.42), channel_id=1, source_target_pairs={{0,1},{1,0},{2,3},{3,2},{4,5},{5,4},{6,7},{7,6},{8,9},{9,8},{10,11... | collective-permute-start | bytes 786440 | tf_op jit(solution)/shard_map/ppermute | solution.py:34
  5.4 7.1 %collective-permute-start.4 = (bf16[288,256]{1,0:T(8,128)(2,1)S(1)}, bf16[288,256]{1,0:T(8,128)(2,1)S(1)}, u32[]{:S(2)}, u32[]{:S(2)}) collective-permute-start(bf16[288,256]{1,0:T(8,128)(2,1)S(1)} %get-tuple-element.37.along), channel_id=1, source_target_pairs={{0,2},{2,0},{4,6},{6,4},{8,10},{10,8},{12,14},{14,12},{16,18},{18,... | collective-permute-start | bytes 442376 | tf_op jit(solution)/shard_map/ppermute | solution.py:34
  12.4 6.4 %collective-permute-start.5 = (bf16[288,256]{1,0:T(8,128)(2,1)S(1)}, bf16[288,256]{1,0:T(8,128)(2,1)S(1)}, u32[]{:S(2)}, u32[]{:S(2)}) collective-permute-start(bf16[288,256]{1,0:T(8,128)(2,1)S(1)} %collective-permute-done.4.along_x), channel_id=1, source_target_pairs={{0,1},{1,0},{2,3},{3,2},{4,5},{5,4},{6,7},{7,6},{8,9},{9,8},{10,11... | collective-permute-start | bytes 442376 | tf_op jit(solution)/shard_map/ppermute | solution.py:34
  12.4 6.4 %collective-permute-start.13 = (bf16[128,256]{1,0:T(8,128)(2,1)S(1)}, bf16[128,256]{1,0:T(8,128)(2,1)S(1)}, u32[]{:S(2)}, u32[]{:S(2)}) collective-permute-start(bf16[128,256]{1,0:T(8,128)(2,1)S(1)} %shard_map.159), channel_id=1, source_target_pairs={{0,4},{2,6},{4,0},{6,2},{8,12},{10,14},{12,8},{14,10},{16,20},{18,... | collective-permute-start | bytes 196616 | tf_op jit(solution)/shard_map/ppermute | solution.py:34
  14.3 4.8 %copy-start.5 = (bf16[128,256]{1,0:T(8,128)(2,1)S(1)}, bf16[128,256]{1,0:T(8,128)(2,1)}, u32[]{:S(2)}) copy-start(bf16[128,256]{1,0:T(8,128)(2,1)} %inverse.7) | copy-start | bytes 196612
  14.7 4.4 %collective-permute-start.3 = (bf16[256,128]{1,0:T(8,128)(2,1)S(1)}, bf16[256,128]{1,0:T(8,128)(2,1)S(1)}, u32[]{:S(2)}, u32[]{:S(2)}) collective-permute-start(bf16[256,128]{1,0:T(8,128)(2,1)S(1)} %get-tuple-element.36), channel_id=1, source_target_pairs={{0,2},{2,0},{4,6},{6,4},{8,10},{10,8},{12,14},{14,12},{16,18},{18,... | collective-permute-start | bytes 196616 | tf_op jit(solution)/shard_map/ppermute | solution.py:34
  16.5 6.9 %copy-start.6 = (bf16[64,256]{1,0:T(8,128)(2,1)S(1)}, bf16[64,256]{1,0:T(8,128)(2,1)}, u32[]{:S(2)}) copy-start(bf16[64,256]{1,0:T(8,128)(2,1)} %inverse.8) | copy-start | bytes 98308
  16.5 4.7 %collective-permute-start.11 = (bf16[256,128]{1,0:T(8,128)(2,1)S(1)}, bf16[256,128]{1,0:T(8,128)(2,1)S(1)}, u32[]{:S(2)}, u32[]{:S(2)}) collective-permute-start(bf16[256,128]{1,0:T(8,128)(2,1)S(1)} %get-tuple-element.47), channel_id=1, source_target_pairs={{0,2},{2,0},{4,6},{6,4},{8,10},{10,8},{12,14},{14,12},{16,18},{18,... | collective-permute-start | bytes 196616 | tf_op jit(solution)/shard_map/ppermute | solution.py:34
  17.3 16.3 %copy-start.7 = (bf16[32,256]{1,0:T(8,128)(2,1)S(1)}, bf16[32,256]{1,0:T(8,128)(2,1)}, u32[]{:S(2)}) copy-start(bf16[32,256]{1,0:T(8,128)(2,1)} %inverse.9) | copy-start | bytes 49156
  17.3 4.6 %collective-permute-start.9 = (bf16[256,128]{1,0:T(8,128)(2,1)S(1)}, bf16[256,128]{1,0:T(8,128)(2,1)S(1)}, u32[]{:S(2)}, u32[]{:S(2)}) collective-permute-start(bf16[256,128]{1,0:T(8,128)(2,1)S(1)} %get-tuple-element.44), channel_id=1, source_target_pairs={{0,2},{2,0},{4,6},{6,4},{8,10},{10,8},{12,14},{14,12},{16,18},{18,... | collective-permute-start | bytes 196616 | tf_op jit(solution)/shard_map/ppermute | solution.py:34
  18.8 4.5 %collective-permute-start.14 = (bf16[128,256]{1,0:T(8,128)(2,1)S(1)}, bf16[128,256]{1,0:T(8,128)(2,1)S(1)}, u32[]{:S(2)}, u32[]{:S(2)}) collective-permute-start(bf16[128,256]{1,0:T(8,128)(2,1)S(1)} %collective-permute-done.13.side), channel_id=1, source_target_pairs={{0,1},{1,0},{2,3},{3,2},{4,5},{5,4},{6,7},{7,6},{8,9},{9,8},{10,11... | collective-permute-start | bytes 196616 | tf_op jit(solution)/shard_map/ppermute | solution.py:34
  21.2 4.3 %collective-permute-start.12 = (bf16[256,128]{1,0:T(8,128)(2,1)S(1)}, bf16[256,128]{1,0:T(8,128)(2,1)S(1)}, u32[]{:S(2)}, u32[]{:S(2)}) collective-permute-start(bf16[256,128]{1,0:T(8,128)(2,1)S(1)} %shard_map.158.w2), channel_id=1, source_target_pairs={{0,4},{2,6},{4,0},{6,2},{8,12},{10,14},{12,8},{14,10},{16,20},{18,... | collective-permute-start | bytes 196616 | tf_op jit(solution)/shard_map/ppermute | solution.py:34
  21.9 4.3 %collective-permute-start.10 = (bf16[256,128]{1,0:T(8,128)(2,1)S(1)}, bf16[256,128]{1,0:T(8,128)(2,1)S(1)}, u32[]{:S(2)}, u32[]{:S(2)}) collective-permute-start(bf16[256,128]{1,0:T(8,128)(2,1)S(1)} %shard_map.156.s3), channel_id=1, source_target_pairs={{0,4},{2,6},{4,0},{6,2},{8,12},{10,14},{12,8},{14,10},{16,20},{18,... | collective-permute-start | bytes 196616 | tf_op jit(solution)/shard_map/ppermute | solution.py:34
  23.3 11.0 %collective-permute-start.2 = (bf16[256,256]{1,0:T(8,128)(2,1)S(1)}, bf16[256,256]{1,0:T(8,128)(2,1)S(1)}, u32[]{:S(2)}, u32[]{:S(2)}) collective-permute-start(bf16[256,256]{1,0:T(8,128)(2,1)S(1)} %get-tuple-element.34.own.solved), channel_id=1, source_target_pairs={{0,1},{1,0},{2,3},{3,2},{4,5},{5,4},{6,7},{7,6},{8,9},{9,8},{10,11... | collective-permute-start | bytes 393224 | tf_op jit(solution)/shard_map/ppermute | solution.py:34
  26.3 7.2 %collective-permute-start.15 = (bf16[256,128]{1,0:T(8,128)(2,1)S(1)}, bf16[256,128]{1,0:T(8,128)(2,1)S(1)}, u32[]{:S(2)}, u32[]{:S(2)}) collective-permute-start(bf16[256,128]{1,0:T(8,128)(2,1)S(1)} %get-tuple-element.53.v3), channel_id=1, source_target_pairs={{0,8},{2,10},{4,12},{6,14},{8,0},{10,2},{12,4},{14,6},{16,24},{18,... | collective-permute-start | bytes 196616 | tf_op jit(solution)/shard_map/ppermute | solution.py:34
  27.9 5.6 %collective-permute-start.16 = (bf16[256,128]{1,0:T(8,128)(2,1)S(1)}, bf16[256,128]{1,0:T(8,128)(2,1)S(1)}, u32[]{:S(2)}, u32[]{:S(2)}) collective-permute-start(bf16[256,128]{1,0:T(8,128)(2,1)S(1)} %get-tuple-element.53.v3), channel_id=1, source_target_pairs={{0,10},{2,8},{4,14},{6,12},{8,2},{10,0},{12,6},{14,4},{16,26},{18,... | collective-permute-start | bytes 196616 | tf_op jit(solution)/shard_map/ppermute | solution.py:34
  29.2 4.2 %collective-permute-start.6 = (bf16[128,128]{1,0:T(8,128)(2,1)S(1)}, bf16[128,128]{1,0:T(8,128)(2,1)S(1)}, u32[]{:S(2)}, u32[]{:S(2)}) collective-permute-start(bf16[128,128]{1,0:T(8,128)(2,1)S(1)} %get-tuple-element.39), channel_id=1, source_target_pairs={{0,2},{2,0},{4,6},{6,4},{8,10},{10,8},{12,14},{14,12},{16,18},{18,... | collective-permute-start | bytes 98312 | tf_op jit(solution)/shard_map/ppermute | solution.py:34
  29.8 3.9 %collective-permute-start.17 = (bf16[96,128]{1,0:T(8,128)(2,1)S(1)}, bf16[96,128]{1,0:T(8,128)(2,1)S(1)}, u32[]{:S(2)}, u32[]{:S(2)}) collective-permute-start(bf16[96,128]{1,0:T(8,128)(2,1)S(1)} %get-tuple-element.54), channel_id=1, source_target_pairs={{0,2},{2,0},{4,6},{6,4},{8,10},{10,8},{12,14},{14,12},{16,18},{18,... | collective-permute-start | bytes 73736 | tf_op jit(solution)/shard_map/ppermute | solution.py:34
  33.5 1.6 %collective-permute-start.7 = (bf16[128,256]{1,0:T(8,128)(2,1)S(1)}, bf16[128,256]{1,0:T(8,128)(2,1)S(1)}, u32[]{:S(2)}, u32[]{:S(2)}) collective-permute-start(bf16[128,256]{1,0:T(8,128)(2,1)S(1)} %shard_map.152.own), channel_id=1, source_target_pairs={{0,1},{1,0},{2,3},{3,2},{4,5},{5,4},{6,7},{7,6},{8,9},{9,8},{10,11... | collective-permute-start | bytes 196616 | tf_op jit(solution)/shard_map/ppermute | solution.py:34
  33.8 2.0 %collective-permute-start.18 = (bf16[96,256]{1,0:T(8,128)(2,1)S(1)}, bf16[96,256]{1,0:T(8,128)(2,1)S(1)}, u32[]{:S(2)}, u32[]{:S(2)}) collective-permute-start(bf16[96,256]{1,0:T(8,128)(2,1)S(1)} %shard_map.164.own), channel_id=1, source_target_pairs={{0,1},{1,0},{2,3},{3,2},{4,5},{5,4},{6,7},{7,6},{8,9},{9,8},{10,11... | collective-permute-start | bytes 147464 | tf_op jit(solution)/shard_map/ppermute | solution.py:34
